TPU v7x, 32 devices: a whole 2x2x4 slice. The times are simulated.
32 devices in a mesh: block: 16 (over z, y, core), tok: 2 (over x).
Axes of the slice: x: 2, y: 2, z: 4, core: 2. Of those that a mesh axis runs over, the one named last changes fastest.
Arguments:
- keys: bfloat16 [2, 24576, 768], P(None, ('block', 'tok')), may hold values from -6 to 6
- values: bfloat16 [2, 24576, 768], P(None, ('block', 'tok')), may hold values from -6 to 6
- queries: bfloat16 [2, 24576, 768], P(None, ('block', 'tok')), may hold values from -6 to 6
- fast_in: bfloat16 [16, 3, 2, 384, 384], P('block', None, None, None, 'tok'), may hold values from -0.3125 to 0.3125
- moment_in: float32 [16, 3, 2, 384, 384], P('block', None, None, None, 'tok'), may hold values from -0.06 to 0.06
- initial_fast: bfloat16 [3, 2, 384, 384], P(None, None, None, 'tok'), may hold values from -0.3125 to 0.3125
- rates: float32 [3, 2], replicated, may hold values from 0.5 to 4
- decays: float32 [2], replicated, may hold values from 0.3 to 0.9
Outputs:
- outputs: bfloat16 [2, 24576, 768], P(None, ('block', 'tok'))
- fast_out: bfloat16 [16, 3, 2, 384, 384], P('block', None, None, None, 'tok')
- moment_out: float32 [16, 3, 2, 384, 384], P('block', None, None, None, 'tok')
All inputs are finite; a program needn't handle non-finite values.
Results may differ from a plain program's by a relative error of at most 0.0091.
Values may be sent and summed in bfloat16 or wider, within the bound.
No kernel may reach another device: no remote copies, remote signals or barrier semaphores. Data moves between devices by JAX's collectives and lax.ppermute only.
A program may use at most 64 MiB of HBM per device.

v0:
```python
import jax
import jax.numpy as jnp
from jax import lax
from jax.sharding import PartitionSpec as P


def shifted(block, axis, distance):
    devices = range(lax.axis_size(axis))
    route = [(i - distance, i) for i in devices if i - distance in devices]
    return lax.ppermute(block, axis, route)


def swiglu_parts(rows, weights):
    gate = jnp.einsum("rhi,hio->rho", rows, weights[0], preferred_element_type=jnp.float32)
    upper = jnp.einsum("rhi,hio->rho", rows, weights[1], preferred_element_type=jnp.float32)
    return (gate, upper)


def local_grad(whole, kin, vin, divisor):
    gate, upper = swiglu_parts(kin, whole)
    silu_gate = jax.nn.silu(gate)
    hidden = (silu_gate * upper).astype(jnp.bfloat16)
    dout = (-vin.astype(jnp.float32) / divisor).astype(jnp.bfloat16)
    grad_down = jnp.einsum("rhi,rho->hio", hidden, dout, preferred_element_type=jnp.float32)
    dhid = jnp.einsum("rho,hio->rhi", dout, whole[2], preferred_element_type=jnp.float32)
    sigma = jax.nn.sigmoid(gate)
    dgate = (dhid * upper * sigma * (1.0 + gate * (1.0 - sigma))).astype(jnp.bfloat16)
    dup = (dhid * silu_gate).astype(jnp.bfloat16)
    grad_gate = jnp.einsum("rhi,rho->hio", kin, dgate, preferred_element_type=jnp.float32)
    grad_up = jnp.einsum("rhi,rho->hio", kin, dup, preferred_element_type=jnp.float32)
    return jnp.stack([grad_gate, grad_up, grad_down])


def update_apply(whole, shard_w, shard_m, kin, vin, qin, rates, decays, divisor):
    grad = local_grad(whole, kin, vin, divisor)
    grad_shard = lax.psum_scatter(grad, "tok", scatter_dimension=3, tiled=True)
    new_moment = decays[None, :, None, None] * shard_m + grad_shard
    old = shard_w.astype(jnp.float32)
    moved = old - rates[:, :, None, None] * new_moment
    old_norm = jnp.sqrt(jnp.mean(old * old, axis=-2, keepdims=True) + 1e-06)
    new_norm = jnp.sqrt(jnp.mean(moved * moved, axis=-2, keepdims=True) + 1e-06)
    new_shard = (moved * (old_norm / new_norm)).astype(jnp.bfloat16)
    new_whole = lax.all_gather(new_shard, "tok", axis=3, tiled=True)
    qgate, qup = swiglu_parts(qin, new_whole)
    qhid = (jax.nn.silu(qgate) * qup).astype(jnp.bfloat16)
    result = jnp.einsum("rhi,hio->rho", qhid, new_whole[2], preferred_element_type=jnp.float32)
    return (new_shard, new_moment, new_whole, result.astype(jnp.bfloat16))


def on_device(keys, values, queries, fast_in, moment_in, initial_fast, rates, decays):
    count = keys.shape[1]
    heads = rates.shape[1]
    width = keys.shape[2] // heads
    divisor = float(count * lax.axis_size("tok"))
    columns = fast_in.shape[4]

    def rows_of(arr, step):
        return arr[step].reshape(count, heads, width)

    first_whole = lax.all_gather(fast_in[0], "tok", axis=3, tiled=True)
    shard_one, moment_one, whole_one, out_one = update_apply(
        first_whole,
        fast_in[0],
        moment_in[0],
        rows_of(keys, 0),
        rows_of(values, 0),
        rows_of(queries, 0),
        rates,
        decays,
        divisor,
    )
    leading = lax.axis_index("block") == 0
    arrived_moment = shifted(moment_one.astype(jnp.bfloat16), "block", 1).astype(moment_one.dtype)
    moment_two = jnp.where(leading, jnp.zeros_like(arrived_moment), arrived_moment)
    start_whole = lax.all_gather(initial_fast, "tok", axis=3, tiled=True)
    arrived_whole = shifted(whole_one, "block", 1)
    whole_two = jnp.where(leading, start_whole, arrived_whole)
    shard_two = lax.dynamic_slice_in_dim(whole_two, lax.axis_index("tok") * columns, columns, 3)
    shard_fin, moment_fin, unused_whole, out_two = update_apply(
        whole_two,
        shard_two,
        moment_two,
        rows_of(keys, 1),
        rows_of(values, 1),
        rows_of(queries, 1),
        rates,
        decays,
        divisor,
    )
    outputs = jnp.stack(
        [out_one.reshape(count, heads * width), out_two.reshape(count, heads * width)]
    )
    return (outputs, shard_fin[None], moment_fin[None])


def solution(mesh):
    placed = (
        P(None, ("block", "tok"), None),
        P(None, ("block", "tok"), None),
        P(None, ("block", "tok"), None),
        P("block", None, None, None, "tok"),
        P("block", None, None, None, "tok"),
        P(None, None, None, "tok"),
        P(),
        P(),
    )
    return jax.shard_map(
        on_device,
        mesh=mesh,
        in_specs=placed,
        out_specs=(
            P(None, ("block", "tok"), None),
            P("block", None, None, None, "tok"),
            P("block", None, None, None, "tok"),
        ),
        check_vma=False,
    )
```

profile of v0, /device:TPU:1, one launch (start us, length us, event | category | flops | bytes accessed | tf_op | source)
XLA Modules:
  0.0 278.7 jit_solution(12824303113874475939)
XLA Ops:
  7.2 3.0 %copy.77 = bf16[1,3,2,384,192]{3,2,1,0,4:T(2,128)(2,1)} copy(bf16[1,3,2,384,192]{3,4,2,1,0:T(8,128)(2,1)} %param.11) | data formatting | bytes 1769472 | tf_op args[3]
  10.3 2.8 %fusion.58 = (bf16[1,768,768]{2,1,0:T(8,128)(2,1)}, bf16[1,768,768]{2,1,0:T(8,128)(2,1)S(1)}) fusion(bf16[2,768,768]{2,1,0:T(8,128)(2,1)} %param.8), kind=kLoop, calls=%fused_computation.106 | loop fusion | bytes 4718592 | tf_op jit(solution)/shard_map/slice | solution.py:58
  13.7 2.8 %fusion.59 = (bf16[1,768,768]{2,1,0:T(8,128)(2,1)}, bf16[1,768,768]{2,1,0:T(8,128)(2,1)S(1)}) fusion(bf16[2,768,768]{2,1,0:T(8,128)(2,1)} %param.9), kind=kLoop, calls=%fused_computation.107 | loop fusion | bytes 4718592 | tf_op jit(solution)/shard_map/slice | solution.py:58
  17.4 24.3 %all-gather.12.cloned.1.call-done = bf16[1,3,2,384,384]{3,2,1,0,4:T(2,128)(2,1)} async-done(((bf16[1,3,2,384,192]{3,2,1,0,4:T(2,128)(2,1)}), bf16[1,3,2,384,384]{3,2,1,0,4:T(2,128)(2,1)}) %all-gather.12.cloned.1.call-update) | async-done | bytes 1769488 | tf_op jit(solution)/shard_map/all_gather | solution.py:60
  41.7 3.4 %fusion.60 = (bf16[1,1,2,384,384]{3,2,1,0,4:T(2,128)(2,1)S(1)}, bf16[1,1,2,384,384]{3,2,1,0,4:T(2,128)(2,1)S(1)}, bf16[1,1,2,384,384]{3,2,1,0,4:T(2,128)(2,1)}) fusion(bf16[1,3,2,384,384]{3,2,1,0,4:T(2,128)(2,1)} %all-gather.12.cloned.1.call-done), kind=kLoop, calls=%fused_computation.108 | loop fusion | bytes 3538944 | tf_op jit(solution)/shard_map/slice | solution.py:25
  45.1 1.9 copy.157
  47.1 2.0 fusion.42
  55.0 2.0 pad_maximum_fusion
  57.8 47.1 %reduce-scatter.3.cloned.1.call-done = f32[3,2,384,192]{2,3,1,0:T(8,128)} async-done(((f32[3,2,384,384]{2,3,1,0:T(8,128)}), f32[3,2,384,192]{2,3,1,0:T(8,128)}) %reduce-scatter.3.cloned.1.call-update) | async-done | bytes 1769488 | tf_op jit(solution)/shard_map/reduce_scatter | solution.py:36
  104.9 2.7 fusion.55
  110.2 28.9 %all-gather.6.cloned.1.call-done = bf16[3,2,384,384]{2,3,1,0:T(8,128)(2,1)} async-done(((bf16[3,2,384,192]{2,3,1,0:T(8,128)(2,1)}), bf16[3,2,384,384]{2,3,1,0:T(8,128)(2,1)}) %all-gather.6.cloned.1.call-update) | async-done | bytes 1769488 | tf_op jit(solution)/shard_map/all_gather | solution.py:43
  139.1 3.8 %collective-permute-start = (bf16[3,2,384,384]{2,3,1,0:T(8,128)(2,1)}, bf16[3,2,384,384]{2,3,1,0:T(8,128)(2,1)}, u32[]{:S(2)}, u32[]{:S(2)}) collective-permute-start(bf16[3,2,384,384]{2,3,1,0:T(8,128)(2,1)} %all-gather.6.cloned.1.call-done), channel_id=1, source_target_pairs={{0,2},{2,4},{4,6},{6,8},{8,10},{10,12},{12,14},{14,16},{16,18},{18... | collective-permute-start | bytes 5308424 | tf_op jit(solution)/shard_map/ppermute | solution.py:10
  146.5 23.5 %all-gather.8.cloned.1.call-done = bf16[3,2,384,384]{2,3,1,0:T(8,128)(2,1)} async-done(((bf16[3,2,384,192]{2,3,1,0:T(8,128)(2,1)}), bf16[3,2,384,384]{2,3,1,0:T(8,128)(2,1)}) %all-gather.8.cloned.1.call-update) | async-done | bytes 1769488 | tf_op jit(solution)/shard_map/all_gather | solution.py:75
  178.6 2.0 pad_maximum_fusion.1
  181.8 4.0 %collective-permute-start.1 = (bf16[3,2,384,192]{2,3,1,0:T(8,128)(2,1)S(1)}, bf16[3,2,384,192]{2,3,1,0:T(8,128)(2,1)S(1)}, u32[]{:S(2)}, u32[]{:S(2)}) collective-permute-start(bf16[3,2,384,192]{2,3,1,0:T(8,128)(2,1)S(1)} %copy-done.6), channel_id=1, source_target_pairs={{0,2},{2,4},{4,6},{6,8},{8,10},{10,12},{12,14},{14,16},{16,18},{18... | collective-permute-start | bytes 2654216 | tf_op jit(solution)/shard_map/ppermute | solution.py:10
  185.8 9.7 %collective-permute-done.1 = bf16[3,2,384,192]{2,3,1,0:T(8,128)(2,1)S(1)} collective-permute-done((bf16[3,2,384,192]{2,3,1,0:T(8,128)(2,1)S(1)}, bf16[3,2,384,192]{2,3,1,0:T(8,128)(2,1)S(1)}, u32[]{:S(2)}, u32[]{:S(2)}) %collective-permute-start.1) | collective-permute-done | bytes 884768 | tf_op jit(solution)/shard_map/ppermute | solution.py:10
  195.5 33.0 %reduce-scatter.5.cloned.1.call-done = f32[3,2,384,192]{2,3,1,0:T(8,128)} async-done(((f32[3,2,384,384]{2,3,1,0:T(8,128)}), f32[3,2,384,192]{2,3,1,0:T(8,128)}) %reduce-scatter.5.cloned.1.call-update) | async-done | bytes 1769488 | tf_op jit(solution)/shard_map/reduce_scatter | solution.py:36
  228.5 2.3 fusion.26
  230.9 2.1 fusion.54
  236.1 3.4 %fusion.41 = f32[2,384,768]{1,2,0:T(8,128)} fusion(bf16[768,2,384]{0,2,1:T(8,128)(2,1)S(1)} %bitcast.245, bf16[3,2,384,384]{2,3,1,0:T(8,128)(2,1)} %all-gather.6.cloned.1.call-done), kind=kOutput, calls=%fused_computation.85 | convolution fusion | flops 452984832 | bytes 4128768 | tf_op jit(solution)/shard_map/rhi,hio->rho/dot_general | solution.py:14
  239.5 4.0 %convolution_convert_fusion.1 = bf16[2,384,768]{2,1,0:T(8,128)(2,1)S(1)} fusion(f32[2,384,768]{1,2,0:T(8,128)} %fusion.41, bf16[768,2,384]{0,2,1:T(8,128)(2,1)S(1)} %bitcast.246, bf16[3,2,384,384]{2,3,1,0:T(8,128)(2,1)} %all-gather.6.cloned.1.call-done), kind=kOutput, calls=%fused_computation.64 | convolution fusion | flops 910098432 | bytes 5898240 | tf_op jit(solution)/shard_map/rhi,hio->rho/dot_general | solution.py:46
  244.1 18.4 %all-gather.10.cloned.1.call-done = bf16[3,2,384,384]{2,3,1,0:T(8,128)(2,1)} async-done(((bf16[3,2,384,192]{2,3,1,0:T(8,128)(2,1)}), bf16[3,2,384,384]{2,3,1,0:T(8,128)(2,1)}) %all-gather.10.cloned.1.call-update) | async-done | bytes 1769488 | tf_op jit(solution)/shard_map/all_gather | solution.py:43
  262.5 3.4 %fusion.37 = f32[2,384,768]{1,2,0:T(8,128)} fusion(bf16[768,2,384]{0,2,1:T(8,128)(2,1)S(1)} %bitcast.243, bf16[3,2,384,384]{2,3,1,0:T(8,128)(2,1)} %all-gather.10.cloned.1.call-done), kind=kOutput, calls=%fused_computation.75 | convolution fusion | flops 452984832 | bytes 4128768 | tf_op jit(solution)/shard_map/rhi,hio->rho/dot_general | solution.py:14
  266.0 3.6 %convolution_convert_fusion = bf16[2,384,768]{2,1,0:T(8,128)(2,1)S(1)} fusion(f32[2,384,768]{1,2,0:T(8,128)} %fusion.37, bf16[768,2,384]{0,2,1:T(8,128)(2,1)S(1)} %bitcast.244, bf16[3,2,384,384]{2,3,1,0:T(8,128)(2,1)} %all-gather.10.cloned.1.call-done), kind=kOutput, calls=%fused_computation.63 | convolution fusion | flops 910098432 | bytes 5898240 | tf_op jit(solution)/shard_map/rhi,hio->rho/dot_general | solution.py:46
  (60 shorter events, 29.9 us)
Async XLA Ops:
  7.2 34.5 %all-gather.12.cloned.1.call-start = ((), (), s32[]{:S(2)}) async-start(), calls=%async_computation.7 | async-start | bytes 2654208 | tf_op jit(solution)/shard_map/all_gather | solution.py:60
  10.2 94.7 %reduce-scatter.3.cloned.1.call-start = ((), (), s32[]{:S(2)}) async-start(), calls=%async_computation.2 | async-start | bytes 5308416 | tf_op jit(solution)/shard_map/reduce_scatter | solution.py:36
  49.1 1.1 copy-start.4
  57.0 0.7 copy-start.8
  57.0 47.9 %copy-start.5 = (f32[1,3,2,384,192]{3,4,2,1,0:T(8,128)S(1)}, f32[1,3,2,384,192]{3,4,2,1,0:T(8,128)}, u32[]{:S(2)}) copy-start(f32[1,3,2,384,192]{3,4,2,1,0:T(8,128)} %param.12) | copy-start | bytes 5308420
  57.0 47.9 %copy-start.7 = (f32[2]{0:T(128)S(1)}, f32[2]{0:T(128)}, u32[]{:S(2)}) copy-start(f32[2]{0:T(128)} %param.15) | copy-start | bytes 28
  57.0 82.1 %all-gather.6.cloned.1.call-start = ((), (), s32[]{:S(2)}) async-start(), calls=%async_computation.3 | async-start | bytes 2654208 | tf_op jit(solution)/shard_map/all_gather | solution.py:43
  57.8 49.9 %copy-start = (bf16[1,3,2,384,192]{3,4,2,1,0:T(8,128)(2,1)S(1)}, bf16[1,3,2,384,192]{3,4,2,1,0:T(8,128)(2,1)}, u32[]{:S(2)}) copy-start(bf16[1,3,2,384,192]{3,4,2,1,0:T(8,128)(2,1)} %param.11) | copy-start | bytes 2654212
  109.6 33.4 %copy-start.2 = (bf16[1,768,768]{2,1,0:T(8,128)(2,1)S(1)}, bf16[1,768,768]{2,1,0:T(8,128)(2,1)}, u32[]{:S(2)}) copy-start(bf16[1,768,768]{2,1,0:T(8,128)(2,1)} %get-tuple-element.13) | copy-start | bytes 3538948
  109.6 60.4 %all-gather.8.cloned.1.call-start = ((), (), s32[]{:S(2)}) async-start(), calls=%async_computation.4 | async-start | bytes 2654208 | tf_op jit(solution)/shard_map/all_gather | solution.py:75
  110.2 118.3 %reduce-scatter.5.cloned.1.call-start = ((), (), s32[]{:S(2)}) async-start(), calls=%async_computation.5 | async-start | bytes 5308416 | tf_op jit(solution)/shard_map/reduce_scatter | solution.py:36
  139.1 30.8 %collective-permute-start = (bf16[3,2,384,384]{2,3,1,0:T(8,128)(2,1)}, bf16[3,2,384,384]{2,3,1,0:T(8,128)(2,1)}, u32[]{:S(2)}, u32[]{:S(2)}) collective-permute-start(bf16[3,2,384,384]{2,3,1,0:T(8,128)(2,1)} %all-gather.6.cloned.1.call-done), channel_id=1, source_target_pairs={{0,2},{2,4},{4,6},{6,8},{8,10},{10,12},{12,14},{14,16},{16,18},{18... | collective-permute-start | bytes 5308424 | tf_op jit(solution)/shard_map/ppermute | solution.py:10
  172.6 1.3 copy-start.3
  180.6 1.2 copy-start.6
  180.6 81.9 %all-gather.10.cloned.1.call-start = ((), (), s32[]{:S(2)}) async-start(), calls=%async_computation.6 | async-start | bytes 2654208 | tf_op jit(solution)/shard_map/all_gather | solution.py:43
  181.8 13.8 %collective-permute-start.1 = (bf16[3,2,384,192]{2,3,1,0:T(8,128)(2,1)S(1)}, bf16[3,2,384,192]{2,3,1,0:T(8,128)(2,1)S(1)}, u32[]{:S(2)}, u32[]{:S(2)}) collective-permute-start(bf16[3,2,384,192]{2,3,1,0:T(8,128)(2,1)S(1)} %copy-done.6), channel_id=1, source_target_pairs={{0,2},{2,4},{4,6},{6,8},{8,10},{10,12},{12,14},{14,16},{16,18},{18... | collective-permute-start | bytes 2654216 | tf_op jit(solution)/shard_map/ppermute | solution.py:10
  228.5 2.4 copy-start.1
Sparse Core Ops, SparseCore 0:
  10.3 31.2 all-gather.11
  57.1 47.7 reduce-scatter.2
  109.7 29.3 all-gather.5
  140.5 29.3 all-gather.7
  180.7 47.7 reduce-scatter.4
  233.1 29.3 all-gather.9
where the time goes:
time: 280 us; the launch traced here: 279 us
  waiting for transfers between devices  186 us (66%)
  matrix products  28.8 us (10%)
  local copies, waits for them, and re-layouts  23.9 us (9%)
  other arithmetic  17.8 us (6%)
  between operations  14.4 us (5%)
  starting transfers between devices  8.27 us (3%)
    reduce_scatter x2, waiting for transfers between devices, update_apply(): grad_shard = lax.psum_scatter(grad, 'tok', scatter_dimension=3, tiled=True)  80.1 us
    all_gather x2, waiting for transfers between devices, update_apply(): new_whole = lax.all_gather(new_shard, 'tok', axis=3, tiled=True)  47.3 us
    all_gather x1, waiting for transfers between devices, on_device(): first_whole = lax.all_gather(fast_in[0], 'tok', axis=3, tiled=True)  24.3 us
    all_gather x1, waiting for transfers between devices, on_device(): start_whole = lax.all_gather(initial_fast, 'tok', axis=3, tiled=True)  23.5 us
    unnamed x27, local copies, waits for them, and re-layouts  11.8 us
    dot_general x4, matrix products, swiglu_parts(): jnp.einsum('rhi,hio->rho', rows, weights[0], preferred_element_type=jnp.f...  9.79 us
    ppermute x2, waiting for transfers between devices, shifted(): return lax.ppermute(block, axis, route)  9.74 us
    ppermute x2, starting transfers between devices, shifted(): return lax.ppermute(block, axis, route)  7.85 us
  transfers between devices with their start and end apart: 8, of which 7 were waited for; matrix products, arithmetic and copies ran while one was open for 8% of the time, Pallas kernels for 0%

commit v1 on v0

v1 whole, which is shorter than its diff:
```python
import functools

import jax
import jax.numpy as jnp
from jax import lax
from jax.experimental import pallas as pl
from jax.experimental.pallas import tpu as pltpu
from jax.sharding import PartitionSpec as P

F32 = jnp.float32
BF16 = jnp.bfloat16
VMEM = pl.BlockSpec(memory_space=pltpu.VMEM)
SMEM = pl.BlockSpec(memory_space=pltpu.SMEM)


def mm(a, b, dims):
    return lax.dot_general(a, b, (dims, ((), ())), preferred_element_type=F32)


def call(kernel, name, out, in_specs, out_specs=None, scratch=(), aliases=None):
    return pl.pallas_call(
        kernel,
        name=name,
        grid=(1,),
        out_shape=out,
        in_specs=in_specs,
        out_specs=out_specs,
        scratch_shapes=list(scratch),
        input_output_aliases=aliases or {},
    )


def whole_spec(*shape):
    return pl.BlockSpec(shape, lambda i: (0,) * len(shape))


def row_chunk(rows):
    for size in (256, 384, 128):
        if rows % size == 0:
            return size
    return rows


def spread(shards, own, width):
    n = len(shards)
    part = shards[0].shape[-1]
    owner = lax.broadcasted_iota(jnp.int32, (shards[0].shape[0], width), 1) // part
    total = None
    for r, shard in enumerate(shards):
        tiled = jnp.concatenate([shard] * n, axis=1)
        source = lax.rem(own - r + n, n)
        total = tiled if total is None else jnp.where(owner == source, tiled, total)
    return total


def grads_core(divisor, k_ref, v_ref, gu_ref, down_ref, hid_s, dout_s, dgu_s):
    rows, width = k_ref.shape
    size = row_chunk(rows)
    for first in range(0, rows, size):
        at = pl.ds(first, size)
        both = mm(k_ref[at, :], gu_ref[...], ((1,), (0,)))
        gate, upper = both[:, :width], both[:, width:]
        dout = (-v_ref[at, :].astype(F32) / divisor).astype(BF16)
        dhid = mm(dout, down_ref[...], ((1,), (1,)))
        sigma = jax.nn.sigmoid(gate)
        silu = gate * sigma
        hid_s[at, :] = (silu * upper).astype(BF16)
        dout_s[at, :] = dout
        dgu_s[at, :width] = (dhid * upper * sigma * (1.0 + gate * (1.0 - sigma))).astype(BF16)
        dgu_s[at, width:] = (dhid * silu).astype(BF16)
    grad_down = mm(hid_s[...], dout_s[...], ((0,), (0,)))
    grad_gu = mm(k_ref[...], dgu_s[...], ((0,), (0,)))
    return grad_gu, grad_down


def grads_one(n, head, divisor, tok_ref, decay_ref, k_ref, v_ref, m_ref, *refs):
    shards = refs[:n]
    gu_ref, down_ref, send_gu, send_down, own_gu, own_down, hid_s, dout_s, dgu_s = refs[n:]
    width = down_ref.shape[1]
    me = tok_ref[0]
    gu_ref[:, :width] = spread([s[0] for s in shards], me, width)
    gu_ref[:, width:] = spread([s[1] for s in shards], me, width)
    down_ref[...] = spread([s[2] for s in shards], me, width)
    grad_gu, grad_down = grads_core(
        divisor, k_ref, v_ref, gu_ref, down_ref, hid_s, dout_s, dgu_s
    )
    decay = decay_ref[head]
    part = m_ref.shape[-1]
    mine = lax.broadcasted_iota(jnp.int32, (width, width), 1) // part == me

    def folded(grad, m):
        tiled = jnp.concatenate([m_ref[m]] * n, axis=1)
        return grad + jnp.where(mine, decay * tiled, 0.0)

    for m in range(2):
        cols = slice(m * width, (m + 1) * width)
        total = folded(grad_gu[:, cols], m)
        own_gu[:, cols] = total
        send_gu[:, cols] = total.astype(BF16)
    total = folded(grad_down, 2)
    own_down[...] = total
    send_down[...] = total.astype(BF16)


def grads_two(head, divisor, tok_ref, decay_ref, k_ref, v_ref, pgu_ref, pdown_ref, *refs):
    send_gu, send_down, own_gu, own_down, hid_s, dout_s, dgu_s = refs
    width = k_ref.shape[1]
    grad_gu, grad_down = grads_core(
        divisor,
        k_ref,
        v_ref,
        pgu_ref.at[pl.ds(0, width), :],
        pdown_ref.at[pl.ds(0, width), :],
        hid_s,
        dout_s,
        dgu_s,
    )
    decay = decay_ref[head]
    held = pgu_ref.shape[0] - width
    mine = pl.ds(pl.multiple_of(tok_ref[0] * held, held), held)
    old = pl.ds(width, held)
    own_gu[...] = grad_gu
    own_gu[mine, :] += decay * pgu_ref[old, :].astype(F32)
    send_gu[...] = own_gu[...].astype(BF16)
    own_down[...] = grad_down
    own_down[mine, :] += decay * pdown_ref[old, :].astype(F32)
    send_down[...] = own_down[...].astype(BF16)


def updated(rate, old_ref, own_ref, recvs, cols):
    width = own_ref.shape[0]
    moment = own_ref[:, cols]
    for recv in recvs:
        moment = moment + recv[:, cols].astype(F32)
    old = old_ref[pl.ds(0, width), cols].astype(F32)
    moved = old - rate * moment
    old_norm = jnp.sqrt(jnp.mean(old * old, axis=0, keepdims=True) + 1e-06)
    new_norm = jnp.sqrt(jnp.mean(moved * moved, axis=0, keepdims=True) + 1e-06)
    return (moved * (old_norm / new_norm)).astype(BF16), moment


def update_one(n, head, mats, tok_ref, rate_ref, old_ref, own_ref, *refs):
    recvs = refs[: n - 1]
    pack_ref, moment_s = refs[n - 1 :]
    width = own_ref.shape[0]
    held = width // n
    for i, m in enumerate(mats):
        cols = slice(i * width, (i + 1) * width)
        new, moment = updated(rate_ref[m, head], old_ref, own_ref, recvs, cols)
        pack_ref[:width, cols] = new
        moment_s[:, cols] = moment
    mine = pl.ds(pl.multiple_of(tok_ref[0] * held, held), held)
    pack_ref[width:, :] = moment_s[mine, :].astype(BF16)


def columns_of(n, me, x):
    part = x.shape[1] // n
    picked = x[:, :part]
    for j in range(1, n):
        picked = jnp.where(me == j, x[:, j * part : (j + 1) * part], picked)
    return picked


def update_two_gu(n, head, tok_ref, rate_ref, old_ref, own_ref, q_ref, *refs):
    recvs = refs[: n - 1]
    hq_ref, fast_ref, moment_ref, gu_s = refs[-4:]
    width = own_ref.shape[0]
    me = tok_ref[0]
    for m in range(2):
        cols = slice(m * width, (m + 1) * width)
        new, moment = updated(rate_ref[m, head], old_ref, own_ref, recvs, cols)
        gu_s[:, cols] = new
        fast_ref[m] = columns_of(n, me, new)
        moment_ref[m] = columns_of(n, me, moment)
    rows = q_ref.shape[0]
    size = row_chunk(rows)
    for first in range(0, rows, size):
        at = pl.ds(first, size)
        both = mm(q_ref[at, :], gu_s[...], ((1,), (0,)))
        hq_ref[at, :] = (jax.nn.silu(both[:, :width]) * both[:, width:]).astype(BF16)


def update_two_down(n, head, tok_ref, rate_ref, old_ref, own_ref, hq_ref, *refs):
    recvs = refs[: n - 1]
    out_ref, fast_ref, moment_ref = refs[-3:]
    me = tok_ref[0]
    new, moment = updated(rate_ref[2, head], old_ref, own_ref, recvs, slice(None))
    fast_ref[0] = columns_of(n, me, new)
    moment_ref[0] = columns_of(n, me, moment)
    out_ref[...] = mm(hq_ref[...], new, ((1,), (0,))).astype(BF16)


def apply_one(q_ref, pgu_ref, pdown_ref, *refs):
    out_ref = refs[-1]
    rows, width = q_ref.shape
    size = row_chunk(rows)
    for first in range(0, rows, size):
        at = pl.ds(first, size)
        both = mm(q_ref[at, :], pgu_ref[pl.ds(0, width), :], ((1,), (0,)))
        hq = (jax.nn.silu(both[:, :width]) * both[:, width:]).astype(BF16)
        out_ref[at, :] = mm(hq, pdown_ref[pl.ds(0, width), :], ((1,), (0,))).astype(BF16)


def on_device(keys, values, queries, fast_in, moment_in, initial_fast, rates, decays):
    n = lax.axis_size("tok")
    blocks = lax.axis_size("block")
    steps, rows, features = keys.shape
    heads = rates.shape[1]
    width = features // heads
    part = fast_in.shape[4]
    held = width // n
    divisor = float(rows * n)
    me = lax.axis_index("tok").astype(jnp.int32)
    tok = me.reshape(1)
    leading = lax.axis_index("block") == 0

    def others(x):
        return [
            lax.ppermute(x, "tok", [(i, (i + r) % n) for i in range(n)]) for r in range(1, n)
        ]

    def forward(x):
        return lax.ppermute(x, "block", [(i, i + 1) for i in range(blocks - 1)])

    def rows_spec(step, head):
        return pl.BlockSpec((None, rows, width), lambda i: (step, 0, head))

    def shape(*dims, dtype=BF16):
        return jax.ShapeDtypeStruct(dims, dtype)

    w1 = whole_spec(width, width)
    w2 = whole_spec(width, 2 * width)
    p1 = whole_spec(width + held, width)
    p2 = whole_spec(width + held, 2 * width)
    scratch = (
        pltpu.VMEM((rows, width), BF16),
        pltpu.VMEM((rows, width), BF16),
        pltpu.VMEM((rows, 2 * width), BF16),
    )
    grad_out = (
        shape(width, 2 * width),
        shape(width, width),
        shape(width, 2 * width, dtype=F32),
        shape(width, width, dtype=F32),
    )

    owned = [fast_in[0, :, h] for h in range(heads)]
    shards = [[owned[h]] + others(owned[h]) for h in range(heads)]
    first = []
    for h in range(heads):
        first.append(
            call(
                functools.partial(grads_one, n, h, divisor),
                "grads_one",
                (shape(width, 2 * width), shape(width, width)) + grad_out,
                [
                    SMEM,
                    SMEM,
                    rows_spec(0, h),
                    rows_spec(0, h),
                    pl.BlockSpec((None, 3, None, width, part), lambda i, h=h: (0, 0, h, 0, 0)),
                ]
                + [whole_spec(3, width, part)] * n,
                (w2, w1, w2, w1, w2, w1),
                scratch,
            )(tok, decays, keys, values, moment_in, *shards[h])
        )
    start = [[initial_fast[:, h]] + others(initial_fast[:, h]) for h in range(heads)]

    packs = []
    for h in range(heads):
        gu, down, send_gu, send_down, own_gu, own_down = first[h]
        recv_gu, recv_down = others(send_gu), others(send_down)
        pair = []
        for mats, old, own, recvs, w, p in (
            ((0, 1), gu, own_gu, recv_gu, w2, p2),
            ((2,), down, own_down, recv_down, w1, p1),
        ):
            cols = len(mats) * width
            pair.append(
                call(
                    functools.partial(update_one, n, h, mats),
                    "update_one",
                    shape(width + held, cols),
                    [SMEM, SMEM, w, w] + [w] * (n - 1),
                    p,
                    (pltpu.VMEM((width, cols), F32),),
                )(tok, rates, old, own, *recvs)
            )
        packs.append(pair)

    second, seeds = [], []
    for h in range(heads):
        shard_list = start[h]
        order = [
            sum(jnp.where(lax.rem(me - r + n, n) == j, s, 0) for r, s in enumerate(shard_list))
            for j in range(n)
        ]
        begin = jnp.concatenate(order, axis=2)
        blank = jnp.zeros((held, width), BF16)
        begin_gu = jnp.concatenate(
            [
                jnp.concatenate([begin[0], begin[1]], axis=1),
                jnp.concatenate([blank, blank], axis=1),
            ],
            axis=0,
        )
        begin_down = jnp.concatenate([begin[2], blank], axis=0)
        seed_gu = jnp.where(leading, begin_gu, forward(packs[h][0]))
        seed_down = jnp.where(leading, begin_down, forward(packs[h][1]))
        seeds.append((seed_gu, seed_down))
        second.append(
            call(
                functools.partial(grads_two, h, divisor),
                "grads_two",
                grad_out,
                [SMEM, SMEM, rows_spec(1, h), rows_spec(1, h), p2, p1],
                (w2, w1, w2, w1),
                scratch,
            )(tok, decays, keys, values, seed_gu, seed_down)
        )

    out_shape = jax.ShapeDtypeStruct(keys.shape, BF16)
    any_spec = pl.BlockSpec(memory_space=pl.ANY)
    outputs = None
    for h in range(heads):
        prior = [] if outputs is None else [outputs]
        outputs = call(
            apply_one,
            "apply_one",
            out_shape,
            [rows_spec(0, h), p2, p1] + [any_spec] * len(prior),
            rows_spec(0, h),
            aliases={3: 0} if prior else None,
        )(queries, packs[h][0], packs[h][1], *prior)

    fast_shape = jax.ShapeDtypeStruct(fast_in.shape, BF16)
    moment_shape = jax.ShapeDtypeStruct(moment_in.shape, F32)
    fast_out = moment_out = None
    for h in range(heads):
        send_gu, send_down, own_gu, own_down = second[h]
        recv_gu, recv_down = others(send_gu), others(send_down)
        pair_spec = pl.BlockSpec((None, 2, None, width, part), lambda i, h=h: (0, 0, h, 0, 0))
        lone_spec = pl.BlockSpec((None, 1, None, width, part), lambda i, h=h: (0, 2, h, 0, 0))
        prior = [] if fast_out is None else [fast_out, moment_out]
        at = 5 + (n - 1)
        hq, fast_out, moment_out = call(
            functools.partial(update_two_gu, n, h),
            "update_two_gu",
            (shape(rows, width), fast_shape, moment_shape),
            [SMEM, SMEM, w2, w2, rows_spec(1, h)]
            + [w2] * (n - 1)
            + [any_spec] * len(prior),
            (whole_spec(rows, width), pair_spec, pair_spec),
            (pltpu.VMEM((width, 2 * width), BF16),),
            aliases={at: 1, at + 1: 2} if prior else None,
        )(tok, rates, seeds[h][0], own_gu, queries, *recv_gu, *prior)
        outputs, fast_out, moment_out = call(
            functools.partial(update_two_down, n, h),
            "update_two_down",
            (out_shape, fast_shape, moment_shape),
            [SMEM, SMEM, w1, w1, whole_spec(rows, width)]
            + [w1] * (n - 1)
            + [any_spec] * 3,
            (rows_spec(1, h), lone_spec, lone_spec),
            aliases={at: 0, at + 1: 1, at + 2: 2},
        )(
            tok,
            rates,
            seeds[h][1],
            own_down,
            hq,
            *recv_down,
            outputs,
            fast_out,
            moment_out,
        )
    return (outputs, fast_out, moment_out)


def solution(mesh):
    placed = (
        P(None, ("block", "tok"), None),
        P(None, ("block", "tok"), None),
        P(None, ("block", "tok"), None),
        P("block", None, None, None, "tok"),
        P("block", None, None, None, "tok"),
        P(None, None, None, "tok"),
        P(),
        P(),
    )
    step = jax.shard_map(
        on_device,
        mesh=mesh,
        in_specs=placed,
        out_specs=(
            P(None, ("block", "tok"), None),
            P("block", None, None, None, "tok"),
            P("block", None, None, None, "tok"),
        ),
        check_vma=False,
    )

    def run(*args):
        with jax.sharding.use_abstract_mesh(mesh.abstract_mesh):
            return step(*args)

    return run
```

time: 280 us -> 157 us (0.56)
  waiting for transfers between devices: 186 us -> 42.7 us
  Pallas kernels: 0 us -> 54.4 us
  matrix products: 28.8 us -> 0 us
  starting transfers between devices: 8.27 us -> 27.5 us
  between operations: 14.4 us -> 0.78 us
  other arithmetic: 17.8 us -> 10.3 us
  local copies, waits for them, and re-layouts: 23.9 us -> 20.6 us
    all_gather x4 -> x0, waiting for transfers between devices: 95.2 us -> none  [the longest x2 47.3 us: update_apply(): new_whole = lax.all_gather(new_shard, 'tok', axis=3, tiled=True)]
    reduce_scatter x2 -> x0, waiting for transfers between devices: 80.1 us -> none  [update_apply(): grad_shard = lax.psum_scatter(grad, 'tok', scatter_dimension=3, tiled=True)]
    pallas_call x0 -> x14, Pallas kernels: none -> 54.4 us  [the longest x2 11.3 us: on_device(): call(functools.partial(grads_one, n, h, divisor), 'grads_one', (shape(wid...]
    ppermute x2 -> x16, waiting for transfers between devices: 9.74 us -> 42.7 us  [the longest x12 42.7 us: others(): lax.ppermute(x, 'tok', [(i, (i + r) % n) for i in range(n)])]
    dot_general x16 -> x0, matrix products: 28.8 us -> none  [the longest x4 9.79 us: swiglu_parts(): jnp.einsum('rhi,hio->rho', rows, weights[0], preferred_element_type=jnp.f...]
    ppermute x2 -> x16, starting transfers between devices: 7.85 us -> 27.5 us  [the longest x4 17.3 us: forward(): return lax.ppermute(x, 'block', [(i, i + 1) for i in range(blocks - 1)])]
    slice x4 -> x0, local copies, waits for them, and re-layouts: 10.8 us -> none  [the longest x3 7.37 us: rows_of(): return arr[step].reshape(count, heads, width)]
    select_n x1 -> x4, other arithmetic: 1.69 us -> 8.37 us  [the longest x2 4.58 us: on_device(): seed_gu = jnp.where(leading, begin_gu, forward(packs[h][0]))]
  transfers between devices with their start and end apart: 8 -> 16, of which waited for: 7 -> 6; matrix products, arithmetic and copies ran while one was open for 8% -> 14% of each run, Pallas kernels for 0% -> 33%
where the time goes in v1:
time: 157 us; the launch traced here: 156 us
  Pallas kernels  54.4 us (35%)
  waiting for transfers between devices  42.7 us (27%)
  starting transfers between devices  27.5 us (18%)
  local copies, waits for them, and re-layouts  20.6 us (13%)
  other arithmetic  10.3 us (7%)
    ppermute x12, waiting for transfers between devices, others(): lax.ppermute(x, 'tok', [(i, (i + r) % n) for i in range(n)])  42.7 us
    ppermute x4, starting transfers between devices, forward(): return lax.ppermute(x, 'block', [(i, i + 1) for i in range(blocks - 1)])  17.3 us
    pallas_call x2, Pallas kernels, on_device(): call(functools.partial(grads_one, n, h, divisor), 'grads_one', (shape(wid...  11.3 us
    pallas_call x4, Pallas kernels, on_device(): call(functools.partial(update_one, n, h, mats), 'update_one', shape(width...  10.7 us
    ppermute x12, starting transfers between devices, others(): lax.ppermute(x, 'tok', [(i, (i + r) % n) for i in range(n)])  10.3 us
    pallas_call x2, Pallas kernels, on_device(): call(functools.partial(grads_two, h, divisor), 'grads_two', grad_out, [SM...  10.2 us
    pallas_call x2, Pallas kernels, on_device(): call(functools.partial(update_two_gu, n, h), 'update_two_gu', (shape(rows...  8.45 us
    unnamed x28, local copies, waits for them, and re-layouts  8.25 us
  transfers between devices with their start and end apart: 16, of which 6 were waited for; matrix products, arithmetic and copies ran while one was open for 14% of the time, Pallas kernels for 33%

profile of v1, /device:TPU:1, one launch (start us, length us, event | category | flops | bytes accessed | tf_op | source)
XLA Modules:
  0.0 156.3 jit_solution(9778587899197883429)
XLA Ops:
  7.9 6.9 %collective-permute-done.8 = bf16[3,384,192]{1,2,0:T(8,128)(2,1)S(1)} collective-permute-done((bf16[3,384,192]{1,2,0:T(8,128)(2,1)S(1)}, bf16[3,384,192]{1,2,0:T(8,128)(2,1)S(1)}, u32[]{:S(2)}, u32[]{:S(2)}) %collective-permute-start.8) | collective-permute-done | bytes 442400 | tf_op jit(solution)/shard_map/ppermute | solution.py:219
  15.9 5.7 %grads_one.3 = (bf16[384,768]{1,0:T(8,128)(2,1)}, bf16[384,384]{1,0:T(8,128)(2,1)}, bf16[384,768]{1,0:T(8,128)(2,1)}, bf16[384,384]{1,0:T(8,128)(2,1)}, f32[384,768]{1,0:T(8,128)}, /*index=5*/f32[384,384]{1,0:T(8,128)}) custom-call(s32[1]{0:T(128)} %bitcast.tok_ref, f32[2]{0:T(128)} %decay_ref.7, bf16[2,768,768]{2,1,0:T(8,128)(2,1)} %k_ref.7, ...), custom_call_target="tpu_custom_call" | custom-call | tf_op jit(solution)/shard_map/grads_one/pallas_call | solution.py:252
  28.7 5.6 %grads_one.2 = (bf16[384,768]{1,0:T(8,128)(2,1)}, bf16[384,384]{1,0:T(8,128)(2,1)}, bf16[384,768]{1,0:T(8,128)(2,1)}, bf16[384,384]{1,0:T(8,128)(2,1)}, f32[384,768]{1,0:T(8,128)}, /*index=5*/f32[384,384]{1,0:T(8,128)}) custom-call(s32[1]{0:T(128)} %bitcast.tok_ref, f32[2]{0:T(128)} %decay_ref.7, bf16[2,768,768]{2,1,0:T(8,128)(2,1)} %k_ref.7, ...), custom_call_target="tpu_custom_call" | custom-call | tf_op jit(solution)/shard_map/grads_one/pallas_call | solution.py:252
  36.7 8.7 %collective-permute-done = bf16[3,384,192]{1,2,0:T(8,128)(2,1)S(1)} collective-permute-done((bf16[3,384,192]{1,2,0:T(8,128)(2,1)}, bf16[3,384,192]{1,2,0:T(8,128)(2,1)S(1)}, u32[]{:S(2)}, u32[]{:S(2)}) %collective-permute-start) | collective-permute-done | bytes 442400 | tf_op jit(solution)/shard_map/ppermute | solution.py:219
  46.8 8.2 %collective-permute-done.7 = bf16[3,384,192]{1,2,0:T(8,128)(2,1)} collective-permute-done((bf16[3,384,192]{1,2,0:T(8,128)(2,1)}, bf16[3,384,192]{1,2,0:T(8,128)(2,1)}, u32[]{:S(2)}, u32[]{:S(2)}) %collective-permute-start.7) | collective-permute-done | bytes 442400 | tf_op jit(solution)/shard_map/ppermute | solution.py:219
  56.2 5.1 %collective-permute-done.9.refs_0_ = bf16[384,384]{1,0:T(8,128)(2,1)} collective-permute-done((bf16[384,384]{1,0:T(8,128)(2,1)}, bf16[384,384]{1,0:T(8,128)(2,1)}, u32[]{:S(2)}, u32[]{:S(2)}) %collective-permute-start.9) | collective-permute-done | bytes 294944 | tf_op jit(solution)/shard_map/ppermute | solution.py:219
  61.3 2.3 %update_one.6.pdown_ref = bf16[576,384]{1,0:T(8,128)(2,1)} custom-call(s32[1]{0:T(128)} %bitcast.tok_ref, f32[3,2]{1,0:T(4,128)} %copy.59.rate_ref, bf16[384,384]{1,0:T(8,128)(2,1)} %get-tuple-element.41.old_ref, f32[384,384]{1,0:T(8,128)} %get-tuple-element.42.own_ref, bf16[384,384]{1,0:T(8,128)(2,1)} %collective-permute-done.9.refs_0_), custom_call_target="tpu_custom_call" | custom-call | tf_op jit(solution)/shard_map/update_one/pallas_call | solution.py:281
  63.6 7.7 %collective-permute-start.10 = (bf16[576,384]{1,0:T(8,128)(2,1)}, bf16[576,384]{1,0:T(8,128)(2,1)}, u32[]{:S(2)}, u32[]{:S(2)}) collective-permute-start(bf16[576,384]{1,0:T(8,128)(2,1)} %update_one.6.pdown_ref), channel_id=1, source_target_pairs={{0,2},{2,4},{4,6},{6,8},{8,10},{10,12},{12,14},{14,16},{16,18},{18... | collective-permute-start | bytes 1327112 | tf_op jit(solution)/shard_map/ppermute | solution.py:223
  71.3 3.0 %update_one.7.pgu_ref = bf16[576,768]{1,0:T(8,128)(2,1)} custom-call(s32[1]{0:T(128)} %bitcast.tok_ref, f32[3,2]{1,0:T(4,128)} %copy.59.rate_ref, bf16[384,768]{1,0:T(8,128)(2,1)} %get-tuple-element.44.old_ref, f32[384,768]{1,0:T(8,128)} %get-tuple-element.45.own_ref, bf16[384,768]{1,0:T(8,128)(2,1)} %collective-permute-done.11.refs_0_), custom_call_target="tpu_custom_call" | custom-call | tf_op jit(solution)/shard_map/update_one/pallas_call | solution.py:281
  77.5 2.7 %collective-permute-done.2.refs_0_ = bf16[384,384]{1,0:T(8,128)(2,1)} collective-permute-done((bf16[384,384]{1,0:T(8,128)(2,1)}, bf16[384,384]{1,0:T(8,128)(2,1)}, u32[]{:S(2)}, u32[]{:S(2)}) %collective-permute-start.2) | collective-permute-done | bytes 294944 | tf_op jit(solution)/shard_map/ppermute | solution.py:219
  80.2 2.3 %update_one.4.pdown_ref = bf16[576,384]{1,0:T(8,128)(2,1)} custom-call(s32[1]{0:T(128)} %bitcast.tok_ref, f32[3,2]{1,0:T(4,128)} %copy.59.rate_ref, bf16[384,384]{1,0:T(8,128)(2,1)} %get-tuple-element.32.old_ref, f32[384,384]{1,0:T(8,128)} %get-tuple-element.33.own_ref, bf16[384,384]{1,0:T(8,128)(2,1)} %collective-permute-done.2.refs_0_), custom_call_target="tpu_custom_call" | custom-call | tf_op jit(solution)/shard_map/update_one/pallas_call | solution.py:281
  82.5 5.6 %collective-permute-start.3 = (bf16[576,384]{1,0:T(8,128)(2,1)}, bf16[576,384]{1,0:T(8,128)(2,1)}, u32[]{:S(2)}, u32[]{:S(2)}) collective-permute-start(bf16[576,384]{1,0:T(8,128)(2,1)} %update_one.4.pdown_ref), channel_id=1, source_target_pairs={{0,2},{2,4},{4,6},{6,8},{8,10},{10,12},{12,14},{14,16},{16,18},{18... | collective-permute-start | bytes 1327112 | tf_op jit(solution)/shard_map/ppermute | solution.py:223
  88.4 3.0 %update_one.5.pgu_ref = bf16[576,768]{1,0:T(8,128)(2,1)} custom-call(s32[1]{0:T(128)} %bitcast.tok_ref, f32[3,2]{1,0:T(4,128)} %copy.59.rate_ref, bf16[384,768]{1,0:T(8,128)(2,1)} %get-tuple-element.35.old_ref, f32[384,768]{1,0:T(8,128)} %get-tuple-element.36.own_ref, bf16[384,768]{1,0:T(8,128)(2,1)} %collective-permute-done.4.refs_0_), custom_call_target="tpu_custom_call" | custom-call | tf_op jit(solution)/shard_map/update_one/pallas_call | solution.py:281
  100.0 5.1 %grads_two.3 = (bf16[384,768]{1,0:T(8,128)(2,1)}, bf16[384,384]{1,0:T(8,128)(2,1)}, f32[384,768]{1,0:T(8,128)}, f32[384,384]{1,0:T(8,128)}) custom-call(s32[1]{0:T(128)} %bitcast.tok_ref, f32[2]{0:T(128)} %decay_ref.7, bf16[2,768,768]{2,1,0:T(8,128)(2,1)} %k_ref.7, bf16[2,768,768]{2,1,0:T(8,128)(2,1)} %v_ref.7, bf16[576,768]{1,0:T(8,128)(2,1)} %fusion.7.pgu_ref.old_ref, ...), custom_call_target="tpu_custom_call" | custom-call | tf_op jit(solution)/shard_map/grads_two/pallas_call | solution.py:313
  106.3 2.3 %fusion.5.pgu_ref.old_ref = bf16[576,768]{1,0:T(8,128)(2,1)} fusion(bf16[576,768]{1,0:T(8,128)(2,1)} %collective-permute-done.5, bf16[384,384]{1,0:T(8,128)(2,1)S(1)} %get-tuple-element.74, bf16[384,384]{1,0:T(8,128)(2,1)S(1)} %get-tuple-element.72, pred[]{:T(512)S(6)} %eq.19), kind=kLoop, calls=%fused_computation.14 | loop fusion | flops 3538944 | bytes 2359297 | tf_op jit(solution)/shard_map/jit(_where)/select_n | solution.py:309
  108.6 5.1 %grads_two.2 = (bf16[384,768]{1,0:T(8,128)(2,1)}, bf16[384,384]{1,0:T(8,128)(2,1)}, f32[384,768]{1,0:T(8,128)}, f32[384,384]{1,0:T(8,128)}) custom-call(s32[1]{0:T(128)} %bitcast.tok_ref, f32[2]{0:T(128)} %decay_ref.7, bf16[2,768,768]{2,1,0:T(8,128)(2,1)} %k_ref.7, bf16[2,768,768]{2,1,0:T(8,128)(2,1)} %v_ref.7, bf16[576,768]{1,0:T(8,128)(2,1)} %fusion.5.pgu_ref.old_ref, ...), custom_call_target="tpu_custom_call" | custom-call | tf_op jit(solution)/shard_map/grads_two/pallas_call | solution.py:313
  115.5 4.0 %apply_one.2.refs_0_ = bf16[2,768,768]{2,1,0:T(8,128)(2,1)} custom-call(bf16[2,768,768]{2,1,0:T(8,128)(2,1)} %q_ref.7, bf16[576,768]{1,0:T(8,128)(2,1)} %update_one.7.pgu_ref, bf16[576,384]{1,0:T(8,128)(2,1)} %update_one.6.pdown_ref), custom_call_target="tpu_custom_call" | custom-call | tf_op jit(solution)/shard_map/apply_one/pallas_call | solution.py:328
  119.4 4.0 %apply_one.3.refs_1_ = bf16[2,768,768]{2,1,0:T(8,128)(2,1)} custom-call(bf16[2,768,768]{2,1,0:T(8,128)(2,1)} %q_ref.7, bf16[576,768]{1,0:T(8,128)(2,1)} %update_one.5.pgu_ref, bf16[576,384]{1,0:T(8,128)(2,1)} %update_one.4.pdown_ref, bf16[2,768,768]{2,1,0:T(8,128)(2,1)} %apply_one.2.refs_0_), custom_call_target="tpu_custom_call", output_to_operand_aliasing={{}: (3, {})} | custom-call | tf_op jit(solution)/shard_map/apply_one/pallas_call | solution.py:328
  124.2 4.2 %update_two_gu.2 = (bf16[768,384]{1,0:T(8,128)(2,1)}, bf16[1,3,2,384,192]{4,3,2,1,0:T(8,128)(2,1)}, f32[1,3,2,384,192]{4,3,2,1,0:T(8,128)}) custom-call(s32[1]{0:T(128)} %bitcast.tok_ref, f32[3,2]{1,0:T(4,128)} %copy.59.rate_ref, bf16[576,768]{1,0:T(8,128)(2,1)} %fusion.7.pgu_ref.old_ref, f32[384,768]{1,0:T(8,128)} %get-tuple-element.48.own_ref, ...), custom_call_target="tpu_custom_call" | custom-call | tf_op jit(solution)/shard_map/update_two_gu/pallas_call | solution.py:347
  128.4 11.2 %collective-permute-done.14.refs_0_ = bf16[384,384]{1,0:T(8,128)(2,1)S(1)} collective-permute-done((bf16[384,384]{1,0:T(8,128)(2,1)S(1)}, bf16[384,384]{1,0:T(8,128)(2,1)S(1)}, u32[]{:S(2)}, u32[]{:S(2)}) %collective-permute-start.14) | collective-permute-done | bytes 294944 | tf_op jit(solution)/shard_map/ppermute | solution.py:219
  140.3 3.0 %update_two_down.2 = (bf16[2,768,768]{2,1,0:T(8,128)(2,1)}, bf16[1,3,2,384,192]{4,3,2,1,0:T(8,128)(2,1)}, f32[1,3,2,384,192]{4,3,2,1,0:T(8,128)}) custom-call(s32[1]{0:T(128)} %bitcast.tok_ref, f32[3,2]{1,0:T(4,128)} %copy.59.rate_ref, bf16[576,384]{1,0:T(8,128)(2,1)} %pad_select_fusion.pdown_ref.old_ref, ...), custom_call_target="tpu_custom_call", output_to_operand_aliasing={{0}: (6, {}), {1}: (7, {}), {2}: (8, {})} | custom-call | tf_op jit(solution)/shard_map/update_two_down/pallas_call | solution.py:358
  144.1 4.2 %update_two_gu.3 = (bf16[768,384]{1,0:T(8,128)(2,1)}, bf16[1,3,2,384,192]{4,3,2,1,0:T(8,128)(2,1)}, f32[1,3,2,384,192]{4,3,2,1,0:T(8,128)}) custom-call(s32[1]{0:T(128)} %bitcast.tok_ref, f32[3,2]{1,0:T(4,128)} %copy.59.rate_ref, bf16[576,768]{1,0:T(8,128)(2,1)} %fusion.5.pgu_ref.old_ref, ...), custom_call_target="tpu_custom_call", output_to_operand_aliasing={{1}: (6, {}), {2}: (7, {})} | custom-call | tf_op jit(solution)/shard_map/update_two_gu/pallas_call | solution.py:347
  149.0 3.0 %update_two_down.3 = (bf16[2,768,768]{2,1,0:T(8,128)(2,1)}, bf16[1,3,2,384,192]{4,3,2,1,0:T(8,128)(2,1)}, f32[1,3,2,384,192]{4,3,2,1,0:T(8,128)}) custom-call(s32[1]{0:T(128)} %bitcast.tok_ref, f32[3,2]{1,0:T(4,128)} %copy.59.rate_ref, ...), custom_call_target="tpu_custom_call", output_to_operand_aliasing={{0}: (6, {}), {1}: (7, {}), {2}: (8, {})} | custom-call | tf_op jit(solution)/shard_map/update_two_down/pallas_call | solution.py:358
  152.0 3.0 %copy.61 = f32[1,3,2,384,192]{3,4,2,1,0:T(8,128)} copy(f32[1,3,2,384,192]{4,3,2,1,0:T(8,128)} %get-tuple-element.66) | data formatting | bytes 3538944 | tf_op jit(solution)/shard_map/update_two_down/pallas_call | solution.py:358
  (65 shorter events, 39.9 us)
Async XLA Ops:
  0.6 5.4 %copy-start.3 = (f32[1,3,2,384,192]{3,4,2,1,0:T(8,128)S(1)}, f32[1,3,2,384,192]{3,4,2,1,0:T(8,128)}, u32[]{:S(2)}) copy-start(f32[1,3,2,384,192]{3,4,2,1,0:T(8,128)} %param.12) | copy-start | bytes 5308420
  2.9 11.9 %collective-permute-start.8 = (bf16[3,384,192]{1,2,0:T(8,128)(2,1)S(1)}, bf16[3,384,192]{1,2,0:T(8,128)(2,1)S(1)}, u32[]{:S(2)}, u32[]{:S(2)}) collective-permute-start(bf16[3,384,192]{1,2,0:T(8,128)(2,1)S(1)} %get-tuple-element.81), channel_id=1, source_target_pairs={{0,1},{1,0},{2,3},{3,2},{4,5},{5,4},{6,7},{7,6},{8,9},{9,8},{10,11... | collective-permute-start | bytes 1327112 | tf_op jit(solution)/shard_map/ppermute | solution.py:219
  4.9 21.7 %collective-permute-start.1 = (bf16[3,384,192]{1,2,0:T(8,128)(2,1)}, bf16[3,384,192]{1,2,0:T(8,128)(2,1)}, u32[]{:S(2)}, u32[]{:S(2)}) collective-permute-start(bf16[3,384,192]{1,2,0:T(8,128)(2,1)} %get-tuple-element.82), channel_id=1, source_target_pairs={{0,1},{1,0},{2,3},{3,2},{4,5},{5,4},{6,7},{7,6},{8,9},{9,8},{10,11... | collective-permute-start | bytes 1327112 | tf_op jit(solution)/shard_map/ppermute | solution.py:219
  15.9 6.9 %copy-start.4 = (bf16[3,2,384,192]{2,3,1,0:T(8,128)(2,1)S(1)}, bf16[3,2,384,192]{2,3,1,0:T(8,128)(2,1)}, u32[]{:S(2)}) copy-start(bf16[3,2,384,192]{2,3,1,0:T(8,128)(2,1)} %param.13) | copy-start | bytes 2654212
  21.5 49.8 %collective-permute-start.11 = (bf16[384,768]{1,0:T(8,128)(2,1)}, bf16[384,768]{1,0:T(8,128)(2,1)}, u32[]{:S(2)}, u32[]{:S(2)}) collective-permute-start(bf16[384,768]{1,0:T(8,128)(2,1)} %get-tuple-element.46), channel_id=1, source_target_pairs={{0,1},{1,0},{2,3},{3,2},{4,5},{5,4},{6,7},{7,6},{8,9},{9,8},{10,11... | collective-permute-start | bytes 1769480 | tf_op jit(solution)/shard_map/ppermute | solution.py:219
  23.8 21.5 %collective-permute-start = (bf16[3,384,192]{1,2,0:T(8,128)(2,1)}, bf16[3,384,192]{1,2,0:T(8,128)(2,1)S(1)}, u32[]{:S(2)}, u32[]{:S(2)}) collective-permute-start(bf16[3,384,192]{1,2,0:T(8,128)(2,1)} %get-tuple-element.78), channel_id=1, source_target_pairs={{0,1},{1,0},{2,3},{3,2},{4,5},{5,4},{6,7},{7,6},{8,9},{9,8},{10,11... | collective-permute-start | bytes 1327112 | tf_op jit(solution)/shard_map/ppermute | solution.py:219
  24.1 30.8 %collective-permute-start.7 = (bf16[3,384,192]{1,2,0:T(8,128)(2,1)}, bf16[3,384,192]{1,2,0:T(8,128)(2,1)}, u32[]{:S(2)}, u32[]{:S(2)}) collective-permute-start(bf16[3,384,192]{1,2,0:T(8,128)(2,1)} %get-tuple-element.77), channel_id=1, source_target_pairs={{0,1},{1,0},{2,3},{3,2},{4,5},{5,4},{6,7},{7,6},{8,9},{9,8},{10,11... | collective-permute-start | bytes 1327112 | tf_op jit(solution)/shard_map/ppermute | solution.py:219
  25.3 36.0 %collective-permute-start.9 = (bf16[384,384]{1,0:T(8,128)(2,1)}, bf16[384,384]{1,0:T(8,128)(2,1)}, u32[]{:S(2)}, u32[]{:S(2)}) collective-permute-start(bf16[384,384]{1,0:T(8,128)(2,1)} %get-tuple-element.43), channel_id=1, source_target_pairs={{0,1},{1,0},{2,3},{3,2},{4,5},{5,4},{6,7},{7,6},{8,9},{9,8},{10,11... | collective-permute-start | bytes 884744 | tf_op jit(solution)/shard_map/ppermute | solution.py:219
  28.7 6.8 %copy-start.9 = (f32[3,2]{0,1:T(2,128)S(1)}, f32[3,2]{0,1:T(2,128)}, u32[]{:S(2)}) copy-start(f32[3,2]{0,1:T(2,128)} %param.14) | copy-start | bytes 76
  34.3 54.1 %collective-permute-start.4 = (bf16[384,768]{1,0:T(8,128)(2,1)}, bf16[384,768]{1,0:T(8,128)(2,1)}, u32[]{:S(2)}, u32[]{:S(2)}) collective-permute-start(bf16[384,768]{1,0:T(8,128)(2,1)} %get-tuple-element.37), channel_id=1, source_target_pairs={{0,1},{1,0},{2,3},{3,2},{4,5},{5,4},{6,7},{7,6},{8,9},{9,8},{10,11... | collective-permute-start | bytes 1769480 | tf_op jit(solution)/shard_map/ppermute | solution.py:219
  45.4 34.9 %collective-permute-start.2 = (bf16[384,384]{1,0:T(8,128)(2,1)}, bf16[384,384]{1,0:T(8,128)(2,1)}, u32[]{:S(2)}, u32[]{:S(2)}) collective-permute-start(bf16[384,384]{1,0:T(8,128)(2,1)} %get-tuple-element.34), channel_id=1, source_target_pairs={{0,1},{1,0},{2,3},{3,2},{4,5},{5,4},{6,7},{7,6},{8,9},{9,8},{10,11... | collective-permute-start | bytes 884744 | tf_op jit(solution)/shard_map/ppermute | solution.py:219
  63.6 30.3 %collective-permute-start.10 = (bf16[576,384]{1,0:T(8,128)(2,1)}, bf16[576,384]{1,0:T(8,128)(2,1)}, u32[]{:S(2)}, u32[]{:S(2)}) collective-permute-start(bf16[576,384]{1,0:T(8,128)(2,1)} %update_one.6.pdown_ref), channel_id=1, source_target_pairs={{0,2},{2,4},{4,6},{6,8},{8,10},{10,12},{12,14},{14,16},{16,18},{18... | collective-permute-start | bytes 1327112 | tf_op jit(solution)/shard_map/ppermute | solution.py:223
  74.4 23.3 %collective-permute-start.12 = (bf16[576,768]{1,0:T(8,128)(2,1)}, bf16[576,768]{1,0:T(8,128)(2,1)}, u32[]{:S(2)}, u32[]{:S(2)}) collective-permute-start(bf16[576,768]{1,0:T(8,128)(2,1)} %update_one.7.pgu_ref), channel_id=1, source_target_pairs={{0,2},{2,4},{4,6},{6,8},{8,10},{10,12},{12,14},{14,16},{16,18},{18... | collective-permute-start | bytes 2654216 | tf_op jit(solution)/shard_map/ppermute | solution.py:223
  77.5 10.5 %copy-start.1 = (bf16[3,384,192]{2,1,0:T(8,128)(2,1)S(1)}, bf16[3,384,192]{2,1,0:T(8,128)(2,1)}, u32[]{:S(2)}) copy-start(bf16[3,384,192]{2,1,0:T(8,128)(2,1)} %get-tuple-element.70) | copy-start | bytes 1327108
  77.5 10.5 %copy-start.2 = (bf16[3,384,192]{2,1,0:T(8,128)(2,1)S(1)}, bf16[3,384,192]{2,1,0:T(8,128)(2,1)}, u32[]{:S(2)}) copy-start(bf16[3,384,192]{2,1,0:T(8,128)(2,1)} %get-tuple-element.71) | copy-start | bytes 1327108
  82.5 13.3 %collective-permute-start.3 = (bf16[576,384]{1,0:T(8,128)(2,1)}, bf16[576,384]{1,0:T(8,128)(2,1)}, u32[]{:S(2)}, u32[]{:S(2)}) collective-permute-start(bf16[576,384]{1,0:T(8,128)(2,1)} %update_one.4.pdown_ref), channel_id=1, source_target_pairs={{0,2},{2,4},{4,6},{6,8},{8,10},{10,12},{12,14},{14,16},{16,18},{18... | collective-permute-start | bytes 1327112 | tf_op jit(solution)/shard_map/ppermute | solution.py:223
  91.5 14.8 %collective-permute-start.5 = (bf16[576,768]{1,0:T(8,128)(2,1)}, bf16[576,768]{1,0:T(8,128)(2,1)}, u32[]{:S(2)}, u32[]{:S(2)}) collective-permute-start(bf16[576,768]{1,0:T(8,128)(2,1)} %update_one.5.pgu_ref), channel_id=1, source_target_pairs={{0,2},{2,4},{4,6},{6,8},{8,10},{10,12},{12,14},{14,16},{16,18},{18... | collective-permute-start | bytes 2654216 | tf_op jit(solution)/shard_map/ppermute | solution.py:223
  105.1 18.3 %collective-permute-start.13 = (bf16[384,768]{1,0:T(8,128)(2,1)}, bf16[384,768]{1,0:T(8,128)(2,1)S(1)}, u32[]{:S(2)}, u32[]{:S(2)}) collective-permute-start(bf16[384,768]{1,0:T(8,128)(2,1)} %get-tuple-element.49), channel_id=1, source_target_pairs={{0,1},{1,0},{2,3},{3,2},{4,5},{5,4},{6,7},{7,6},{8,9},{9,8},{10,11... | collective-permute-start | bytes 1769480 | tf_op jit(solution)/shard_map/ppermute | solution.py:219
  108.6 5.4 %copy-start.10 = (bf16[384,384]{1,0:T(8,128)(2,1)S(1)}, bf16[384,384]{1,0:T(8,128)(2,1)}, u32[]{:S(2)}) copy-start(bf16[384,384]{1,0:T(8,128)(2,1)} %get-tuple-element.51) | copy-start | bytes 884740
  113.8 29.5 %collective-permute-start.6 = (bf16[384,768]{1,0:T(8,128)(2,1)}, bf16[384,768]{1,0:T(8,128)(2,1)S(1)}, u32[]{:S(2)}, u32[]{:S(2)}) collective-permute-start(bf16[384,768]{1,0:T(8,128)(2,1)} %get-tuple-element.40), channel_id=1, source_target_pairs={{0,1},{1,0},{2,3},{3,2},{4,5},{5,4},{6,7},{7,6},{8,9},{9,8},{10,11... | collective-permute-start | bytes 1769480 | tf_op jit(solution)/shard_map/ppermute | solution.py:219
  114.0 25.6 %collective-permute-start.14 = (bf16[384,384]{1,0:T(8,128)(2,1)S(1)}, bf16[384,384]{1,0:T(8,128)(2,1)S(1)}, u32[]{:S(2)}, u32[]{:S(2)}) collective-permute-start(bf16[384,384]{1,0:T(8,128)(2,1)S(1)} %copy-done.10), channel_id=1, source_target_pairs={{0,1},{1,0},{2,3},{3,2},{4,5},{5,4},{6,7},{7,6},{8,9},{9,8},{10,11... | collective-permute-start | bytes 884744 | tf_op jit(solution)/shard_map/ppermute | solution.py:219
  115.2 33.1 %collective-permute-start.15 = (bf16[384,384]{1,0:T(8,128)(2,1)}, bf16[384,384]{1,0:T(8,128)(2,1)S(1)}, u32[]{:S(2)}, u32[]{:S(2)}) collective-permute-start(bf16[384,384]{1,0:T(8,128)(2,1)} %get-tuple-element.57), channel_id=1, source_target_pairs={{0,1},{1,0},{2,3},{3,2},{4,5},{5,4},{6,7},{7,6},{8,9},{9,8},{10,11... | collective-permute-start | bytes 884744 | tf_op jit(solution)/shard_map/ppermute | solution.py:219
  143.3 0.8 copy-start.5
  152.0 3.0 %copy-start = (bf16[1,3,2,384,192]{4,3,2,1,0:T(8,128)(2,1)S(1)}, bf16[1,3,2,384,192]{4,3,2,1,0:T(8,128)(2,1)}, u32[]{:S(2)}) copy-start(bf16[1,3,2,384,192]{4,3,2,1,0:T(8,128)(2,1)} %get-tuple-element.65) | copy-start | bytes 2654212
  (3 other events, 2.2 us)

commit v2 on v0

v2 whole, which is shorter than its diff:
```python
import functools

import jax
import jax.numpy as jnp
from jax import lax
from jax.experimental import pallas as pl
from jax.experimental.pallas import tpu as pltpu
from jax.sharding import PartitionSpec as P


F32 = jnp.float32
BF16 = jnp.bfloat16
VMEM = pl.BlockSpec(memory_space=pltpu.VMEM)
SMEM = pl.BlockSpec(memory_space=pltpu.SMEM)


def mm(a, b, dims):
    return lax.dot_general(a, b, (dims, ((), ())), preferred_element_type=F32)


def call(kernel, out, in_specs, out_specs, scratch=(), aliases=None, grid=()):
    return pl.pallas_call(
        kernel,
        grid=grid,
        out_shape=out,
        in_specs=in_specs,
        out_specs=out_specs,
        scratch_shapes=list(scratch),
        input_output_aliases=aliases or {},
        compiler_params=pltpu.CompilerParams(vmem_limit_bytes=12 << 20),
    )


def row_chunk(rows):
    for size in (256, 384, 128):
        if rows % size == 0:
            return size
    return rows


def shard_rows(me, r, n, part):
    source = lax.rem(me - r + n, n)
    return pl.multiple_of(source * part, part)


def assemble(me, shards, gu_ref, down_ref):
    n = len(shards)
    width = down_ref.shape[0]
    part = width // n
    for r, shard in enumerate(shards):
        at = shard_rows(me, r, n, part)
        gu_ref[pl.ds(at, part), :] = shard(0)
        gu_ref[pl.ds(width + at, part), :] = shard(1)
        down_ref[pl.ds(at, part), :] = shard(2)


def grads_core(divisor, keys, values, gu_ref, down_ref, own_gu, own_down, hid_s, dout_s, dgu_s):
    rows, width = hid_s.shape
    size = row_chunk(rows)
    for first in range(0, rows, size):
        at = pl.ds(first, size)
        both = mm(keys(at), gu_ref[...], ((1,), (1,)))
        gate, upper = both[:, :width], both[:, width:]
        dout = (-values(at).astype(F32) / divisor).astype(BF16)
        dhid = mm(dout, down_ref[...], ((1,), (0,)))
        sigma = jax.nn.sigmoid(gate)
        silu = gate * sigma
        hid_s[at, :] = (silu * upper).astype(BF16)
        dout_s[at, :] = dout
        dgu_s[at, :width] = (dhid * upper * sigma * (1.0 + gate * (1.0 - sigma))).astype(BF16)
        dgu_s[at, width:] = (dhid * silu).astype(BF16)
    own_gu[...] = mm(dgu_s[...], keys(pl.ds(0, rows)), ((0,), (0,)))
    own_down[...] = mm(dout_s[...], hid_s[...], ((0,), (0,)))


def take_head(head, fast_ref, own_ref):
    pltpu.sync_copy(fast_ref.at[0, :, head], own_ref)


def grads_one(n, head, divisor, tok_ref, decay_ref, k_ref, v_ref, m_ref, *refs):
    shards = refs[:n]
    gu_ref, down_ref, send_gu, send_down, own_gu, own_down, hid_s, dout_s, dgu_s = refs[n:]
    width = down_ref.shape[0]
    part = width // n
    me = tok_ref[0]
    assemble(me, [lambda m, ref=ref: ref[m] for ref in shards], gu_ref, down_ref)
    cols = pl.ds(head * width, width)
    grads_core(
        divisor,
        lambda at: k_ref[0, at, cols],
        lambda at: v_ref[0, at, cols],
        gu_ref,
        down_ref,
        own_gu,
        own_down,
        hid_s,
        dout_s,
        dgu_s,
    )
    decay = decay_ref[head]
    mine = pl.multiple_of(me * part, part)
    own_gu[pl.ds(mine, part), :] += decay * m_ref[0, 0, head]
    own_gu[pl.ds(width + mine, part), :] += decay * m_ref[0, 1, head]
    own_down[pl.ds(mine, part), :] += decay * m_ref[0, 2, head]
    send_gu[...] = own_gu[...].astype(BF16)
    send_down[...] = own_down[...].astype(BF16)


def grads_two(n, head, divisor, tok_ref, lead_ref, decay_ref, k_ref, v_ref, pgu_ref, pdown_ref, *refs):
    begins = refs[:n]
    gu_ref, down_ref, send_gu, send_down, own_gu, own_down, hid_s, dout_s, dgu_s = refs[n:]
    width = down_ref.shape[0]
    part = width // n
    me = tok_ref[0]
    leading = lead_ref[0] == 1

    @pl.when(leading)
    def _():
        assemble(me, [lambda m, ref=ref: ref[m, head] for ref in begins], gu_ref, down_ref)

    @pl.when(jnp.logical_not(leading))
    def _():
        gu_ref[...] = pgu_ref[: 2 * width, :]
        down_ref[...] = pdown_ref[:width, :]

    cols = pl.ds(head * width, width)
    grads_core(
        divisor,
        lambda at: k_ref[1, at, cols],
        lambda at: v_ref[1, at, cols],
        gu_ref,
        down_ref,
        own_gu,
        own_down,
        hid_s,
        dout_s,
        dgu_s,
    )
    decay = decay_ref[head]
    mine = pl.multiple_of(me * part, part)

    @pl.when(jnp.logical_not(leading))
    def _():
        for m in range(2):
            old = pgu_ref[2 * width + m * part : 2 * width + (m + 1) * part, :]
            own_gu[pl.ds(m * width + mine, part), :] += decay * old.astype(F32)
        own_down[pl.ds(mine, part), :] += decay * pdown_ref[width:, :].astype(F32)

    send_gu[...] = own_gu[...].astype(BF16)
    send_down[...] = own_down[...].astype(BF16)


def updated(rate, old_ref, own_ref, recvs, at):
    moment = own_ref[at, :]
    for recv in recvs:
        moment = moment + recv[at, :].astype(F32)
    old = old_ref[at, :].astype(F32)
    moved = old - rate * moment
    old_norm = jnp.sqrt(jnp.mean(old * old, axis=1, keepdims=True) + 1e-06)
    new_norm = jnp.sqrt(jnp.mean(moved * moved, axis=1, keepdims=True) + 1e-06)
    return (moved * (old_norm / new_norm)).astype(BF16), moment


def update_one(n, head, mats, tok_ref, rate_ref, old_ref, own_ref, *refs):
    recvs = refs[: n - 1]
    pack_ref, moment_s = refs[n - 1 :]
    width = own_ref.shape[1]
    part = width // n
    total = len(mats) * width
    mine = pl.multiple_of(tok_ref[0] * part, part)
    for i, m in enumerate(mats):
        at = pl.ds(i * width, width)
        new, moment = updated(rate_ref[head, m], old_ref, own_ref, recvs, at)
        pack_ref[at, :] = new
        moment_s[...] = moment
        pack_ref[pl.ds(total + i * part, part), :] = moment_s[pl.ds(mine, part), :].astype(BF16)


def update_two_gu(n, head, tok_ref, rate_ref, old_ref, own_ref, q_ref, *refs):
    recvs = refs[: n - 1]
    hq_ref, fast_ref, moment_ref, gu_s, moment_s = refs[-5:]
    width = own_ref.shape[1]
    part = width // n
    mine = pl.multiple_of(tok_ref[0] * part, part)
    for m in range(2):
        at = pl.ds(m * width, width)
        new, moment = updated(rate_ref[head, m], old_ref, own_ref, recvs, at)
        gu_s[at, :] = new
        moment_s[...] = moment
        fast_ref[m] = gu_s[pl.ds(m * width + mine, part), :]
        moment_ref[m] = moment_s[pl.ds(mine, part), :]
    cols = pl.ds(head * width, width)
    rows = q_ref.shape[1]
    size = row_chunk(rows)
    for first in range(0, rows, size):
        at = pl.ds(first, size)
        both = mm(q_ref[1, at, cols], gu_s[...], ((1,), (1,)))
        hq_ref[at, :] = (jax.nn.silu(both[:, :width]) * both[:, width:]).astype(BF16)


def update_two_down(n, head, tok_ref, rate_ref, old_ref, own_ref, hq_ref, *refs):
    recvs = refs[: n - 1]
    out_ref, fast_ref, moment_ref, down_s, moment_s = refs[-5:]
    width = own_ref.shape[1]
    part = width // n
    mine = pl.multiple_of(tok_ref[0] * part, part)
    new, moment = updated(rate_ref[head, 2], old_ref, own_ref, recvs, pl.ds(0, width))
    down_s[...] = new
    moment_s[...] = moment
    fast_ref[...] = down_s[pl.ds(mine, part), :]
    moment_ref[...] = moment_s[pl.ds(mine, part), :]
    out_ref[...] = mm(hq_ref[...], down_s[...], ((1,), (1,))).astype(BF16)


def apply_one(head, q_ref, pgu_ref, pdown_ref, *refs):
    out_ref = refs[-1]
    rows, width = out_ref.shape
    cols = pl.ds(head * width, width)
    size = row_chunk(rows)
    for first in range(0, rows, size):
        at = pl.ds(first, size)
        both = mm(q_ref[0, at, cols], pgu_ref[: 2 * width, :], ((1,), (1,)))
        hq = (jax.nn.silu(both[:, :width]) * both[:, width:]).astype(BF16)
        out_ref[at, :] = mm(hq, pdown_ref[:width, :], ((1,), (1,))).astype(BF16)


def on_device(keys, values, queries, fast_in, moment_in, initial_fast, rates, decays):
    n = lax.axis_size("tok")
    blocks = lax.axis_size("block")
    _, rows, features = keys.shape
    heads = rates.shape[1]
    width = features // heads
    part = width // n
    divisor = float(rows * n)
    tok = lax.axis_index("tok").astype(jnp.int32).reshape(1)
    lead = (lax.axis_index("block") == 0).astype(jnp.int32).reshape(1)
    fast_t = jnp.swapaxes(fast_in, 3, 4)
    moment_t = jnp.swapaxes(moment_in, 3, 4)
    begin_t = jnp.swapaxes(initial_fast, 2, 3)
    rates = rates.T

    def others(x):
        return [lax.ppermute(x, "tok", [(i, (i + r) % n) for i in range(n)]) for r in range(1, n)]

    def forward(x):
        return lax.ppermute(x, "block", [(i, i + 1) for i in range(blocks - 1)])

    def shape(*dims, dtype=BF16):
        return jax.ShapeDtypeStruct(dims, dtype)

    def out_spec(step, head):
        return pl.BlockSpec((None, rows, width), lambda i: (step, 0, head))

    scratch = (
        pltpu.VMEM((rows, width), BF16),
        pltpu.VMEM((rows, width), BF16),
        pltpu.VMEM((rows, 2 * width), BF16),
    )
    grad_out = (
        shape(2 * width, width),
        shape(width, width),
        shape(2 * width, width),
        shape(width, width),
        shape(2 * width, width, dtype=F32),
        shape(width, width, dtype=F32),
    )

    owned = [
        call(
            functools.partial(take_head, h),
            shape(3, part, width),
            [pl.BlockSpec(memory_space=pl.ANY)],
            VMEM,
        )(fast_t)
        for h in range(heads)
    ]
    recv_fast = [others(x) for x in owned]
    first = [
        call(
            functools.partial(grads_one, n, h, divisor),
            grad_out,
            [SMEM, SMEM] + [VMEM] * (4 + n - 1),
            (VMEM,) * 6,
            scratch,
        )(tok, decays, keys, values, moment_t, owned[h], *recv_fast[h])
        for h in range(heads)
    ]
    begins = [begin_t] + [
        lax.ppermute(begin_t, ("block", "tok"), [(i, (i + r) % n) for i in range(n)])
        for r in range(1, n)
    ]

    packs = []
    for h in range(heads):
        gu, down, send_gu, send_down, own_gu, own_down = first[h]
        recv_gu, recv_down = others(send_gu), others(send_down)
        pair = []
        for mats, old, own, recvs in (
            ((0, 1), gu, own_gu, recv_gu), ((2,), down, own_down, recv_down)
        ):
            pair.append(
                call(
                    functools.partial(update_one, n, h, mats),
                    shape(len(mats) * (width + part), width),
                    [SMEM, SMEM] + [VMEM] * (2 + n - 1),
                    VMEM,
                    (pltpu.VMEM((width, width), F32),),
                )(tok, rates, old, own, *recvs)
            )
        packs.append(pair)

    second = [
        call(
            functools.partial(grads_two, n, h, divisor),
            grad_out,
            [SMEM, SMEM, SMEM] + [VMEM] * (4 + n),
            (VMEM,) * 6,
            scratch,
        )(tok, lead, decays, keys, values, forward(packs[h][0]), forward(packs[h][1]), *begins)
        for h in range(heads)
    ]

    out_shape = jax.ShapeDtypeStruct(keys.shape, BF16)
    any_spec = pl.BlockSpec(memory_space=pl.ANY)
    outputs = None
    for h in range(heads):
        prior = [] if outputs is None else [outputs]
        outputs = call(
            functools.partial(apply_one, h),
            out_shape,
            [VMEM] * 3 + [any_spec] * len(prior),
            out_spec(0, h),
            aliases={3: 0} if prior else None,
            grid=(1,),
        )(queries, packs[h][0], packs[h][1], *prior)

    fast_shape = jax.ShapeDtypeStruct(fast_t.shape, BF16)
    moment_shape = jax.ShapeDtypeStruct(moment_t.shape, F32)
    fast_out = moment_out = None
    for h in range(heads):
        gu, down, send_gu, send_down, own_gu, own_down = second[h]
        recv_gu, recv_down = others(send_gu), others(send_down)
        pair_spec = pl.BlockSpec((None, 2, None, part, width), lambda i, h=h: (0, 0, h, 0, 0))
        lone_spec = pl.BlockSpec((None, None, None, part, width), lambda i, h=h: (0, 2, h, 0, 0))
        prior = [] if fast_out is None else [fast_out, moment_out]
        at = 5 + (n - 1)
        hq, fast_out, moment_out = call(
            functools.partial(update_two_gu, n, h),
            (shape(rows, width), fast_shape, moment_shape),
            [SMEM, SMEM] + [VMEM] * (3 + n - 1) + [any_spec] * len(prior),
            (VMEM, pair_spec, pair_spec),
            (pltpu.VMEM((2 * width, width), BF16), pltpu.VMEM((width, width), F32)),
            aliases={at: 1, at + 1: 2} if prior else None,
            grid=(1,),
        )(tok, rates, gu, own_gu, queries, *recv_gu, *prior)
        outputs, fast_out, moment_out = call(
            functools.partial(update_two_down, n, h),
            (out_shape, fast_shape, moment_shape),
            [SMEM, SMEM] + [VMEM] * (3 + n - 1) + [any_spec] * 3,
            (out_spec(1, h), lone_spec, lone_spec),
            (pltpu.VMEM((width, width), BF16), pltpu.VMEM((width, width), F32)),
            aliases={at: 0, at + 1: 1, at + 2: 2},
            grid=(1,),
        )(tok, rates, down, own_down, hq, *recv_down, outputs, fast_out, moment_out)
    return (outputs, jnp.swapaxes(fast_out, 3, 4), jnp.swapaxes(moment_out, 3, 4))


def solution(mesh):
    placed = (
        P(None, ("block", "tok"), None),
        P(None, ("block", "tok"), None),
        P(None, ("block", "tok"), None),
        P("block", None, None, None, "tok"),
        P("block", None, None, None, "tok"),
        P(None, None, None, "tok"),
        P(),
        P(),
    )
    step = jax.shard_map(
        on_device,
        mesh=mesh,
        in_specs=placed,
        out_specs=(
            P(None, ("block", "tok"), None),
            P("block", None, None, None, "tok"),
            P("block", None, None, None, "tok"),
        ),
        check_vma=False,
    )

    def run(*args):
        with jax.sharding.use_abstract_mesh(mesh.abstract_mesh):
            return step(*args)

    return run
```

time: 280 us -> 125 us (0.45)
  the two profiles are of different devices: /device:TPU:1 before, /device:TPU:0 now
where the time goes in v2:
time: 125 us
  waiting for transfers between devices  52.8 us (42%)
  Pallas kernels  40.7 us (33%)
  starting transfers between devices  24.1 us (19%)
  local copies, waits for them, and re-layouts  6.14 us (5%)
    ppermute x10, waiting for transfers between devices, others(): lax.ppermute(x, 'tok', [(i, (i + r) % n) for i in range(n)])  52.8 us
    ppermute x10, starting transfers between devices, others(): lax.ppermute(x, 'tok', [(i, (i + r) % n) for i in range(n)])  13.7 us
    pallas_call x2, Pallas kernels, on_device(): call(functools.partial(grads_two, n, h, divisor), grad_out, [SMEM, SMEM,...  9.01 us
    ppermute x4, starting transfers between devices, forward(): return lax.ppermute(x, 'block', [(i, i + 1) for i in range(blocks - 1)])  8.53 us
    pallas_call x2, Pallas kernels, on_device(): call(functools.partial(grads_one, n, h, divisor), grad_out, [SMEM, SMEM]...  7.5 us
    pallas_call x2, Pallas kernels, on_device(): call(functools.partial(apply_one, h), out_shape, [VMEM] * 3 + [any_spec]...  7.07 us
    pallas_call x4, Pallas kernels, on_device(): call(functools.partial(update_one, n, h, mats), shape(len(mats) * (width...  6.73 us
    unnamed x18, local copies, waits for them, and re-layouts  6.14 us
  transfers between devices with their start and end apart: 15, of which 7 were waited for; matrix products, arithmetic and copies ran while one was open for 0% of the time, Pallas kernels for 31%

profile of v2, /device:TPU:0, one launch (start us, length us, event | category | flops | bytes accessed | tf_op | source)
XLA Modules:
  0.0 124.5 jit_solution(14172699233950703433)
XLA Ops:
  2.0 3.0 %collective-permute-start.7 = (bf16[3,192,384]{2,1,0:T(8,128)(2,1)S(1)}, bf16[3,192,384]{2,1,0:T(8,128)(2,1)}, u32[]{:S(2)}, u32[]{:S(2)}) collective-permute-start(bf16[3,192,384]{2,1,0:T(8,128)(2,1)S(1)} %shard_map.108.refs_0_), channel_id=1, source_target_pairs={{0,1},{1,0},{2,3},{3,2},{4,5},{5,4},{6,7},{7,6},{8,9},{9,8},{10,11... | collective-permute-start | bytes 1327112 | tf_op jit(solution)/shard_map/ppermute | solution.py:243
  5.3 10.9 %collective-permute-done.7.refs_1_ = bf16[3,192,384]{2,1,0:T(8,128)(2,1)} collective-permute-done((bf16[3,192,384]{2,1,0:T(8,128)(2,1)S(1)}, bf16[3,192,384]{2,1,0:T(8,128)(2,1)}, u32[]{:S(2)}, u32[]{:S(2)}) %collective-permute-start.7) | collective-permute-done | bytes 442400 | tf_op jit(solution)/shard_map/ppermute | solution.py:243
  19.4 3.8 %shard_map.109 = (bf16[768,384]{1,0:T(8,128)(2,1)S(1)}, bf16[384,384]{1,0:T(8,128)(2,1)S(1)}, bf16[768,384]{1,0:T(8,128)(2,1)S(1)}, bf16[384,384]{1,0:T(8,128)(2...) custom-call(s32[1]{0:T(128)} %bitcast.tok_ref, f32[2]{0:T(128)S(1)} %copy-done.8, ...), custom_call_target="tpu_custom_call" | custom-call | tf_op jit(solution)/shard_map/pallas_call | solution.py:279
  23.2 2.1 %collective-permute-start.8 = (bf16[768,384]{1,0:T(8,128)(2,1)S(1)}, bf16[768,384]{1,0:T(8,128)(2,1)S(1)}, u32[]{:S(2)}, u32[]{:S(2)}) collective-permute-start(bf16[768,384]{1,0:T(8,128)(2,1)S(1)} %get-tuple-element.52), channel_id=1, source_target_pairs={{0,1},{1,0},{2,3},{3,2},{4,5},{5,4},{6,7},{7,6},{8,9},{9,8},{10,11... | collective-permute-start | bytes 1769480 | tf_op jit(solution)/shard_map/ppermute | solution.py:243
  25.3 3.7 %shard_map.104 = (bf16[768,384]{1,0:T(8,128)(2,1)S(1)}, bf16[384,384]{1,0:T(8,128)(2,1)S(1)}, bf16[768,384]{1,0:T(8,128)(2,1)S(1)}, bf16[384,384]{1,0:T(8,128)(2...) custom-call(s32[1]{0:T(128)} %bitcast.tok_ref, f32[2]{0:T(128)S(1)} %copy-done.8, ...), custom_call_target="tpu_custom_call" | custom-call | tf_op jit(solution)/shard_map/pallas_call | solution.py:279
  29.0 2.1 %collective-permute-start.1 = (bf16[768,384]{1,0:T(8,128)(2,1)S(1)}, bf16[768,384]{1,0:T(8,128)(2,1)S(1)}, u32[]{:S(2)}, u32[]{:S(2)}) collective-permute-start(bf16[768,384]{1,0:T(8,128)(2,1)S(1)} %get-tuple-element.41), channel_id=1, source_target_pairs={{0,1},{1,0},{2,3},{3,2},{4,5},{5,4},{6,7},{7,6},{8,9},{9,8},{10,11... | collective-permute-start | bytes 1769480 | tf_op jit(solution)/shard_map/ppermute | solution.py:243
  31.1 1.9 %collective-permute-start.5 = (bf16[3,2,192,384]{3,2,1,0:T(8,128)(2,1)}, bf16[3,2,192,384]{3,2,1,0:T(8,128)(2,1)}, u32[]{:S(2)}, u32[]{:S(2)}) collective-permute-start(bf16[3,2,192,384]{3,2,1,0:T(8,128)(2,1)} %bitcast.5.refs_0_), channel_id=1, source_target_pairs={{0,1},{1,0}} | collective-permute-start | bytes 2654216 | tf_op jit(solution)/shard_map/ppermute | solution.py:289
  33.0 6.5 %collective-permute-done.8.refs_0_ = bf16[768,384]{1,0:T(8,128)(2,1)S(1)} collective-permute-done((bf16[768,384]{1,0:T(8,128)(2,1)S(1)}, bf16[768,384]{1,0:T(8,128)(2,1)S(1)}, u32[]{:S(2)}, u32[]{:S(2)}) %collective-permute-start.8) | collective-permute-done | bytes 589856 | tf_op jit(solution)/shard_map/ppermute | solution.py:243
  40.7 2.2 %collective-permute-start.9 = (bf16[1152,384]{1,0:T(8,128)(2,1)S(1)}, bf16[1152,384]{1,0:T(8,128)(2,1)}, u32[]{:S(2)}, u32[]{:S(2)}) collective-permute-start(bf16[1152,384]{1,0:T(8,128)(2,1)S(1)} %shard_map.110.pgu_ref), channel_id=1, source_target_pairs={{0,2},{2,4},{4,6},{6,8},{8,10},{10,12},{12,14},{14,16},{16,18},{18... | collective-permute-start | bytes 2654216 | tf_op jit(solution)/shard_map/ppermute | solution.py:246
  43.0 7.0 %collective-permute-done.1.refs_0_ = bf16[768,384]{1,0:T(8,128)(2,1)S(1)} collective-permute-done((bf16[768,384]{1,0:T(8,128)(2,1)S(1)}, bf16[768,384]{1,0:T(8,128)(2,1)S(1)}, u32[]{:S(2)}, u32[]{:S(2)}) %collective-permute-start.1) | collective-permute-done | bytes 589856 | tf_op jit(solution)/shard_map/ppermute | solution.py:243
  50.0 2.2 %shard_map.105.pgu_ref = bf16[1152,384]{1,0:T(8,128)(2,1)} custom-call(s32[1]{0:T(128)} %bitcast.tok_ref, f32[2,3]{1,0:T(2,128)S(1)} %bitcast.13, bf16[768,384]{1,0:T(8,128)(2,1)S(1)} %get-tuple-element.39.old_ref, f32[768,384]{1,0:T(8,128)S(1)} %get-tuple-element.40.own_ref, bf16[768,384]{1,0:T(8,128)(2,1)S(1)} %collective-permute-done.1.refs_0_), custom_call_target="tpu_custom_call" | custom-call | tf_op jit(solution)/shard_map/pallas_call | solution.py:302
  52.2 2.2 %collective-permute-start.2 = (bf16[1152,384]{1,0:T(8,128)(2,1)}, bf16[1152,384]{1,0:T(8,128)(2,1)}, u32[]{:S(2)}, u32[]{:S(2)}) collective-permute-start(bf16[1152,384]{1,0:T(8,128)(2,1)} %shard_map.105.pgu_ref), channel_id=1, source_target_pairs={{0,2},{2,4},{4,6},{6,8},{8,10},{10,12},{12,14},{14,16},{16,18},{18... | collective-permute-start | bytes 2654216 | tf_op jit(solution)/shard_map/ppermute | solution.py:246
  56.4 10.3 %collective-permute-done.10.refs_0_ = bf16[384,384]{1,0:T(8,128)(2,1)S(1)} collective-permute-done((bf16[384,384]{1,0:T(8,128)(2,1)S(1)}, bf16[384,384]{1,0:T(8,128)(2,1)S(1)}, u32[]{:S(2)}, u32[]{:S(2)}) %collective-permute-start.10) | collective-permute-done | bytes 294944 | tf_op jit(solution)/shard_map/ppermute | solution.py:243
  68.3 2.0 %collective-permute-start.11 = (bf16[576,384]{1,0:T(8,128)(2,1)}, bf16[576,384]{1,0:T(8,128)(2,1)}, u32[]{:S(2)}, u32[]{:S(2)}) collective-permute-start(bf16[576,384]{1,0:T(8,128)(2,1)} %shard_map.111.pdown_ref), channel_id=1, source_target_pairs={{0,2},{2,4},{4,6},{6,8},{8,10},{10,12},{12,14},{14,16},{16,18},{18... | collective-permute-start | bytes 1327112 | tf_op jit(solution)/shard_map/ppermute | solution.py:246
  73.8 2.0 %collective-permute-start.4 = (bf16[576,384]{1,0:T(8,128)(2,1)}, bf16[576,384]{1,0:T(8,128)(2,1)}, u32[]{:S(2)}, u32[]{:S(2)}) collective-permute-start(bf16[576,384]{1,0:T(8,128)(2,1)} %shard_map.106.pdown_ref), channel_id=1, source_target_pairs={{0,2},{2,4},{4,6},{6,8},{8,10},{10,12},{12,14},{14,16},{16,18},{18... | collective-permute-start | bytes 1327112 | tf_op jit(solution)/shard_map/ppermute | solution.py:246
  77.5 4.4 %shard_map.112 = (bf16[768,384]{1,0:T(8,128)(2,1)S(1)}, bf16[384,384]{1,0:T(8,128)(2,1)S(1)}, bf16[768,384]{1,0:T(8,128)(2,1)S(1)}, bf16[384,384]{1,0:T(8,128)(2...) custom-call(s32[1]{0:T(128)} %bitcast.tok_ref, s32[1]{0:T(128)} %bitcast.2.lead_ref, f32[2]{0:T(128)S(1)} %copy-done.8, ...), custom_call_target="tpu_custom_call" | custom-call | tf_op jit(solution)/shard_map/pallas_call | solution.py:313
  83.8 4.6 %shard_map.107 = (bf16[768,384]{1,0:T(8,128)(2,1)S(1)}, bf16[384,384]{1,0:T(8,128)(2,1)S(1)}, bf16[768,384]{1,0:T(8,128)(2,1)S(1)}, bf16[384,384]{1,0:T(8,128)(2...) custom-call(s32[1]{0:T(128)} %bitcast.tok_ref, s32[1]{0:T(128)} %bitcast.2.lead_ref, f32[2]{0:T(128)S(1)} %copy-done.8, ...), custom_call_target="tpu_custom_call" | custom-call | tf_op jit(solution)/shard_map/pallas_call | solution.py:313
  90.9 3.4 %shard_map.114.refs_0_ = bf16[2,768,768]{2,1,0:T(8,128)(2,1)} custom-call(bf16[2,768,768]{2,1,0:T(8,128)(2,1)S(1)} %copy-done.4, bf16[1152,384]{1,0:T(8,128)(2,1)S(1)} %shard_map.110.pgu_ref, bf16[576,384]{1,0:T(8,128)(2,1)} %shard_map.111.pdown_ref), custom_call_target="tpu_custom_call" | custom-call | tf_op jit(solution)/shard_map/pallas_call | solution.py:328
  94.3 3.7 %shard_map.115.refs_1_ = bf16[2,768,768]{2,1,0:T(8,128)(2,1)} custom-call(bf16[2,768,768]{2,1,0:T(8,128)(2,1)S(1)} %copy-done.4, bf16[1152,384]{1,0:T(8,128)(2,1)} %shard_map.105.pgu_ref, bf16[576,384]{1,0:T(8,128)(2,1)} %shard_map.106.pdown_ref, bf16[2,768,768]{2,1,0:T(8,128)(2,1)} %shard_map.114.refs_0_), custom_call_target="tpu_custom_call", output_to_operand_aliasing={{}: (3, {})} | custom-call | tf_op jit(solution)/shard_map/pallas_call | solution.py:328
  98.2 2.9 %shard_map.113 = (bf16[768,384]{1,0:T(8,128)(2,1)S(1)}, bf16[1,3,2,192,384]{4,3,2,1,0:T(8,128)(2,1)}, f32[1,3,2,192,384]{4,3,2,1,0:T(8,128)}) custom-call(s32[1]{0:T(128)} %bitcast.tok_ref, f32[2,3]{1,0:T(2,128)S(1)} %bitcast.16, bf16[768,384]{1,0:T(8,128)(2,1)S(1)} %get-tuple-element.58.old_ref, f32[768,384]{1,0:T(8,128)S(1)} %get-tuple-element.59.own_ref, ...), custom_call_target="tpu_custom_call" | custom-call | tf_op jit(solution)/shard_map/pallas_call | solution.py:347
  101.1 16.1 %collective-permute-done.13.refs_0_ = bf16[384,384]{1,0:T(8,128)(2,1)S(1)} collective-permute-done((bf16[384,384]{1,0:T(8,128)(2,1)S(1)}, bf16[384,384]{1,0:T(8,128)(2,1)S(1)}, u32[]{:S(2)}, u32[]{:S(2)}) %collective-permute-start.13) | collective-permute-done | bytes 294944 | tf_op jit(solution)/shard_map/ppermute | solution.py:243
  117.2 2.2 %shard_map.116 = (bf16[2,768,768]{2,1,0:T(8,128)(2,1)}, bf16[1,3,2,192,384]{4,3,2,1,0:T(8,128)(2,1)}, f32[1,3,2,192,384]{4,3,2,1,0:T(8,128)}) custom-call(s32[1]{0:T(128)} %bitcast.tok_ref, f32[2,3]{1,0:T(2,128)S(1)} %bitcast.17, bf16[384,384]{1,0:T(8,128)(2,1)S(1)} %get-tuple-element.56.old_ref, ...), custom_call_target="tpu_custom_call", output_to_operand_aliasing={{0}: (6, {}), {1}: (7, {}), {2}: (8, {})} | custom-call | tf_op jit(solution)/shard_map/pallas_call | solution.py:356
  119.4 2.9 %shard_map.117 = (bf16[768,384]{1,0:T(8,128)(2,1)S(1)}, bf16[1,3,2,192,384]{4,3,2,1,0:T(8,128)(2,1)}, f32[1,3,2,192,384]{4,3,2,1,0:T(8,128)}) custom-call(s32[1]{0:T(128)} %bitcast.tok_ref, f32[2,3]{1,0:T(2,128)S(1)} %bitcast.18, bf16[768,384]{1,0:T(8,128)(2,1)S(1)} %get-tuple-element.47.old_ref, ...), custom_call_target="tpu_custom_call", output_to_operand_aliasing={{1}: (6, {}), {2}: (7, {})} | custom-call | tf_op jit(solution)/shard_map/pallas_call | solution.py:347
  122.3 2.2 %shard_map.118 = (bf16[2,768,768]{2,1,0:T(8,128)(2,1)}, bf16[1,3,2,192,384]{4,3,2,1,0:T(8,128)(2,1)}, f32[1,3,2,192,384]{4,3,2,1,0:T(8,128)}) custom-call(s32[1]{0:T(128)} %bitcast.tok_ref, f32[2,3]{1,0:T(2,128)S(1)} %bitcast.19, bf16[384,384]{1,0:T(8,128)(2,1)S(1)} %get-tuple-element.45.old_ref, ...), custom_call_target="tpu_custom_call", output_to_operand_aliasing={{0}: (6, {}), {1}: (7, {}), {2}: (8, {})} | custom-call | tf_op jit(solution)/shard_map/pallas_call | solution.py:356
  (40 shorter events, 19.4 us)
Async XLA Ops:
  0.6 15.6 %copy-start = (bf16[2,768,768]{2,1,0:T(8,128)(2,1)S(1)}, bf16[2,768,768]{2,1,0:T(8,128)(2,1)}, u32[]{:S(2)}) copy-start(bf16[2,768,768]{2,1,0:T(8,128)(2,1)} %k_ref.7) | copy-start | bytes 7077892
  0.6 1.3 %copy-start.6 = (bf16[1,3,2,384,192]{3,4,2,1,0:T(8,128)(2,1)S(1)}, bf16[1,3,2,384,192]{3,4,2,1,0:T(8,128)(2,1)}, u32[]{:S(2)}) copy-start(bf16[1,3,2,384,192]{3,4,2,1,0:T(8,128)(2,1)} %param.11) | copy-start | bytes 2654212
  2.0 14.3 %copy-start.8 = (f32[2]{0:T(128)S(1)}, f32[2]{0:T(128)}, u32[]{:S(2)}) copy-start(f32[2]{0:T(128)} %decay_ref.7) | copy-start | bytes 28
  2.0 14.2 %collective-permute-start.7 = (bf16[3,192,384]{2,1,0:T(8,128)(2,1)S(1)}, bf16[3,192,384]{2,1,0:T(8,128)(2,1)}, u32[]{:S(2)}, u32[]{:S(2)}) collective-permute-start(bf16[3,192,384]{2,1,0:T(8,128)(2,1)S(1)} %shard_map.108.refs_0_), channel_id=1, source_target_pairs={{0,1},{1,0},{2,3},{3,2},{4,5},{5,4},{6,7},{7,6},{8,9},{9,8},{10,11... | collective-permute-start | bytes 1327112 | tf_op jit(solution)/shard_map/ppermute | solution.py:243
  5.2 20.1 %collective-permute-start = (bf16[3,192,384]{2,1,0:T(8,128)(2,1)S(1)}, bf16[3,192,384]{2,1,0:T(8,128)(2,1)}, u32[]{:S(2)}, u32[]{:S(2)}) collective-permute-start(bf16[3,192,384]{2,1,0:T(8,128)(2,1)S(1)} %shard_map.103.refs_0_), channel_id=1, source_target_pairs={{0,1},{1,0},{2,3},{3,2},{4,5},{5,4},{6,7},{7,6},{8,9},{9,8},{10,11... | collective-permute-start | bytes 1327112 | tf_op jit(solution)/shard_map/ppermute | solution.py:243
  16.2 1.7 %copy-start.1 = (bf16[2,768,768]{2,1,0:T(8,128)(2,1)S(1)}, bf16[2,768,768]{2,1,0:T(8,128)(2,1)}, u32[]{:S(2)}) copy-start(bf16[2,768,768]{2,1,0:T(8,128)(2,1)} %v_ref.7) | copy-start | bytes 7077892
  17.9 1.5 %copy-start.5 = (f32[1,3,2,384,192]{3,4,2,1,0:T(8,128)S(1)}, f32[1,3,2,384,192]{3,4,2,1,0:T(8,128)}, u32[]{:S(2)}) copy-start(f32[1,3,2,384,192]{3,4,2,1,0:T(8,128)} %param.12) | copy-start | bytes 5308420
  19.4 5.9 %copy-start.2 = (bf16[2,768,768]{2,1,0:T(8,128)(2,1)S(1)}, bf16[2,768,768]{2,1,0:T(8,128)(2,1)}, u32[]{:S(2)}) copy-start(bf16[2,768,768]{2,1,0:T(8,128)(2,1)} %v_ref.7) | copy-start | bytes 7077892
  23.2 16.3 %copy-start.7 = (f32[3,2]{0,1:T(2,128)S(1)}, f32[3,2]{0,1:T(2,128)}, u32[]{:S(2)}) copy-start(f32[3,2]{0,1:T(2,128)} %param.14) | copy-start | bytes 76
  23.2 16.3 %collective-permute-start.8 = (bf16[768,384]{1,0:T(8,128)(2,1)S(1)}, bf16[768,384]{1,0:T(8,128)(2,1)S(1)}, u32[]{:S(2)}, u32[]{:S(2)}) collective-permute-start(bf16[768,384]{1,0:T(8,128)(2,1)S(1)} %get-tuple-element.52), channel_id=1, source_target_pairs={{0,1},{1,0},{2,3},{3,2},{4,5},{5,4},{6,7},{7,6},{8,9},{9,8},{10,11... | collective-permute-start | bytes 1769480 | tf_op jit(solution)/shard_map/ppermute | solution.py:243
  29.0 21.0 %collective-permute-start.1 = (bf16[768,384]{1,0:T(8,128)(2,1)S(1)}, bf16[768,384]{1,0:T(8,128)(2,1)S(1)}, u32[]{:S(2)}, u32[]{:S(2)}) collective-permute-start(bf16[768,384]{1,0:T(8,128)(2,1)S(1)} %get-tuple-element.41), channel_id=1, source_target_pairs={{0,1},{1,0},{2,3},{3,2},{4,5},{5,4},{6,7},{7,6},{8,9},{9,8},{10,11... | collective-permute-start | bytes 1769480 | tf_op jit(solution)/shard_map/ppermute | solution.py:243
  31.1 44.8 %collective-permute-start.5 = (bf16[3,2,192,384]{3,2,1,0:T(8,128)(2,1)}, bf16[3,2,192,384]{3,2,1,0:T(8,128)(2,1)}, u32[]{:S(2)}, u32[]{:S(2)}) collective-permute-start(bf16[3,2,192,384]{3,2,1,0:T(8,128)(2,1)} %bitcast.5.refs_0_), channel_id=1, source_target_pairs={{0,1},{1,0}} | collective-permute-start | bytes 2654216 | tf_op jit(solution)/shard_map/ppermute | solution.py:289
  40.7 35.1 %collective-permute-start.9 = (bf16[1152,384]{1,0:T(8,128)(2,1)S(1)}, bf16[1152,384]{1,0:T(8,128)(2,1)}, u32[]{:S(2)}, u32[]{:S(2)}) collective-permute-start(bf16[1152,384]{1,0:T(8,128)(2,1)S(1)} %shard_map.110.pgu_ref), channel_id=1, source_target_pairs={{0,2},{2,4},{4,6},{6,8},{8,10},{10,12},{12,14},{14,16},{16,18},{18... | collective-permute-start | bytes 2654216 | tf_op jit(solution)/shard_map/ppermute | solution.py:246
  52.2 31.6 %collective-permute-start.2 = (bf16[1152,384]{1,0:T(8,128)(2,1)}, bf16[1152,384]{1,0:T(8,128)(2,1)}, u32[]{:S(2)}, u32[]{:S(2)}) collective-permute-start(bf16[1152,384]{1,0:T(8,128)(2,1)} %shard_map.105.pgu_ref), channel_id=1, source_target_pairs={{0,2},{2,4},{4,6},{6,8},{8,10},{10,12},{12,14},{14,16},{16,18},{18... | collective-permute-start | bytes 2654216 | tf_op jit(solution)/shard_map/ppermute | solution.py:246
  54.4 12.3 %collective-permute-start.10 = (bf16[384,384]{1,0:T(8,128)(2,1)S(1)}, bf16[384,384]{1,0:T(8,128)(2,1)S(1)}, u32[]{:S(2)}, u32[]{:S(2)}) collective-permute-start(bf16[384,384]{1,0:T(8,128)(2,1)S(1)} %get-tuple-element.55), channel_id=1, source_target_pairs={{0,1},{1,0},{2,3},{3,2},{4,5},{5,4},{6,7},{7,6},{8,9},{9,8},{10,11... | collective-permute-start | bytes 884744 | tf_op jit(solution)/shard_map/ppermute | solution.py:243
  56.1 16.0 %collective-permute-start.3 = (bf16[384,384]{1,0:T(8,128)(2,1)S(1)}, bf16[384,384]{1,0:T(8,128)(2,1)S(1)}, u32[]{:S(2)}, u32[]{:S(2)}) collective-permute-start(bf16[384,384]{1,0:T(8,128)(2,1)S(1)} %get-tuple-element.44), channel_id=1, source_target_pairs={{0,1},{1,0},{2,3},{3,2},{4,5},{5,4},{6,7},{7,6},{8,9},{9,8},{10,11... | collective-permute-start | bytes 884744 | tf_op jit(solution)/shard_map/ppermute | solution.py:243
  68.3 7.5 %collective-permute-start.11 = (bf16[576,384]{1,0:T(8,128)(2,1)}, bf16[576,384]{1,0:T(8,128)(2,1)}, u32[]{:S(2)}, u32[]{:S(2)}) collective-permute-start(bf16[576,384]{1,0:T(8,128)(2,1)} %shard_map.111.pdown_ref), channel_id=1, source_target_pairs={{0,2},{2,4},{4,6},{6,8},{8,10},{10,12},{12,14},{14,16},{16,18},{18... | collective-permute-start | bytes 1327112 | tf_op jit(solution)/shard_map/ppermute | solution.py:246
  73.8 10.0 %collective-permute-start.4 = (bf16[576,384]{1,0:T(8,128)(2,1)}, bf16[576,384]{1,0:T(8,128)(2,1)}, u32[]{:S(2)}, u32[]{:S(2)}) collective-permute-start(bf16[576,384]{1,0:T(8,128)(2,1)} %shard_map.106.pdown_ref), channel_id=1, source_target_pairs={{0,2},{2,4},{4,6},{6,8},{8,10},{10,12},{12,14},{14,16},{16,18},{18... | collective-permute-start | bytes 1327112 | tf_op jit(solution)/shard_map/ppermute | solution.py:246
  75.8 1.7 %copy-start.3 = (bf16[2,768,768]{2,1,0:T(8,128)(2,1)S(1)}, bf16[2,768,768]{2,1,0:T(8,128)(2,1)}, u32[]{:S(2)}) copy-start(bf16[2,768,768]{2,1,0:T(8,128)(2,1)} %v_ref.7) | copy-start | bytes 7077892
  81.9 9.0 %copy-start.4 = (bf16[2,768,768]{2,1,0:T(8,128)(2,1)S(1)}, bf16[2,768,768]{2,1,0:T(8,128)(2,1)}, u32[]{:S(2)}) copy-start(bf16[2,768,768]{2,1,0:T(8,128)(2,1)} %q_ref.7) | copy-start | bytes 7077892
  81.9 16.3 %collective-permute-start.12 = (bf16[768,384]{1,0:T(8,128)(2,1)S(1)}, bf16[768,384]{1,0:T(8,128)(2,1)S(1)}, u32[]{:S(2)}, u32[]{:S(2)}) collective-permute-start(bf16[768,384]{1,0:T(8,128)(2,1)S(1)} %get-tuple-element.60), channel_id=1, source_target_pairs={{0,1},{1,0},{2,3},{3,2},{4,5},{5,4},{6,7},{7,6},{8,9},{9,8},{10,11... | collective-permute-start | bytes 1769480 | tf_op jit(solution)/shard_map/ppermute | solution.py:243
  88.4 31.1 %collective-permute-start.6 = (bf16[768,384]{1,0:T(8,128)(2,1)S(1)}, bf16[768,384]{1,0:T(8,128)(2,1)S(1)}, u32[]{:S(2)}, u32[]{:S(2)}) collective-permute-start(bf16[768,384]{1,0:T(8,128)(2,1)S(1)} %get-tuple-element.49), channel_id=1, source_target_pairs={{0,1},{1,0},{2,3},{3,2},{4,5},{5,4},{6,7},{7,6},{8,9},{9,8},{10,11... | collective-permute-start | bytes 1769480 | tf_op jit(solution)/shard_map/ppermute | solution.py:243
  88.9 28.3 %collective-permute-start.13 = (bf16[384,384]{1,0:T(8,128)(2,1)S(1)}, bf16[384,384]{1,0:T(8,128)(2,1)S(1)}, u32[]{:S(2)}, u32[]{:S(2)}) collective-permute-start(bf16[384,384]{1,0:T(8,128)(2,1)S(1)} %get-tuple-element.62), channel_id=1, source_target_pairs={{0,1},{1,0},{2,3},{3,2},{4,5},{5,4},{6,7},{7,6},{8,9},{9,8},{10,11... | collective-permute-start | bytes 884744 | tf_op jit(solution)/shard_map/ppermute | solution.py:243
  90.4 31.9 %collective-permute-start.14 = (bf16[384,384]{1,0:T(8,128)(2,1)S(1)}, bf16[384,384]{1,0:T(8,128)(2,1)S(1)}, u32[]{:S(2)}, u32[]{:S(2)}) collective-permute-start(bf16[384,384]{1,0:T(8,128)(2,1)S(1)} %get-tuple-element.68), channel_id=1, source_target_pairs={{0,1},{1,0},{2,3},{3,2},{4,5},{5,4},{6,7},{7,6},{8,9},{9,8},{10,11... | collective-permute-start | bytes 884744 | tf_op jit(solution)/shard_map/ppermute | solution.py:243

commit v3 on v2

v3 whole, which is shorter than its diff:
```python
import functools

import jax
import jax.numpy as jnp
from jax import lax
from jax.experimental import pallas as pl
from jax.experimental.pallas import tpu as pltpu
from jax.sharding import PartitionSpec as P


F32 = jnp.float32
BF16 = jnp.bfloat16
VMEM = pl.BlockSpec(memory_space=pltpu.VMEM)
SMEM = pl.BlockSpec(memory_space=pltpu.SMEM)
HBM = pl.BlockSpec(memory_space=pltpu.HBM)
DMA = pltpu.SemaphoreType.DMA


def mm(a, b, dims):
    return lax.dot_general(a, b, (dims, ((), ())), preferred_element_type=F32)


def call(kernel, out, in_specs, out_specs, scratch=(), aliases=None):
    return pl.pallas_call(
        kernel,
        out_shape=out,
        in_specs=in_specs,
        out_specs=out_specs,
        scratch_shapes=list(scratch),
        input_output_aliases=aliases or {},
        compiler_params=pltpu.CompilerParams(vmem_limit_bytes=12 << 20),
    )


def row_chunks(rows):
    for size in (256, 384, 128):
        if rows % size == 0:
            return [pl.ds(first, size) for first in range(0, rows, size)]
    return [pl.ds(0, rows)]


def fetch_rows(step, head, ref, scratch, sems, which):
    rows, width = scratch.shape
    copies = [
        pltpu.make_async_copy(
            ref.at[step, at, pl.ds(head * width, width)], scratch.at[at, :], sems.at[which, i]
        )
        for i, at in enumerate(row_chunks(rows))
    ]
    for copy in copies:
        copy.start()
    return copies


def assemble(me, shards, gu_ref, down_ref):
    n = len(shards)
    width = down_ref.shape[0]
    part = width // n
    for r, shard in enumerate(shards):
        at = pl.multiple_of(lax.rem(me - r + n, n) * part, part)
        gu_ref[pl.ds(at, part), :] = shard(0)
        gu_ref[pl.ds(width + at, part), :] = shard(1)
        down_ref[pl.ds(at, part), :] = shard(2)


def grads_core(divisor, loads, k_s, v_s, gu_ref, down_ref, own_gu, own_down, hid_s, dout_s, dgu_s):
    rows, width = k_s.shape
    for at, load_k, load_v in zip(row_chunks(rows), *loads):
        load_k.wait()
        both = mm(k_s[at, :], gu_ref[...], ((1,), (1,)))
        gate, upper = both[:, :width], both[:, width:]
        load_v.wait()
        dout = (-v_s[at, :].astype(F32) / divisor).astype(BF16)
        dhid = mm(dout, down_ref[...], ((1,), (0,)))
        sigma = jax.nn.sigmoid(gate)
        silu = gate * sigma
        hid_s[at, :] = (silu * upper).astype(BF16)
        dout_s[at, :] = dout
        dgu_s[at, :width] = (dhid * upper * sigma * (1.0 + gate * (1.0 - sigma))).astype(BF16)
        dgu_s[at, width:] = (dhid * silu).astype(BF16)
    own_gu[...] = mm(dgu_s[...], k_s[...], ((0,), (0,)))
    own_down[...] = mm(dout_s[...], hid_s[...], ((0,), (0,)))


def round_out(own_gu, own_down, send_gate, send_up, send_down):
    width = own_down.shape[0]
    send_gate[...] = own_gu[:width, :].astype(BF16)
    send_up[...] = own_gu[width:, :].astype(BF16)
    send_down[...] = own_down[...].astype(BF16)


def take_head(head, fast_ref, own_ref):
    pltpu.sync_copy(fast_ref.at[0, :, head], own_ref)


def take_piece(sources, block_ref, begin_ref, piece_ref):
    block = block_ref[0]
    piece = jnp.int32(0)
    for p, source in enumerate(sources):
        piece = jnp.where(block == source, jnp.int32(p), piece)
    heads = begin_ref.shape[1]
    pltpu.sync_copy(begin_ref.at[piece // heads, lax.rem(piece, heads)], piece_ref)


def grads_one(n, head, divisor, tok_ref, decay_ref, k_ref, v_ref, m_ref, *refs):
    shards = refs[:n]
    gu_ref, down_ref, send_gate, send_up, send_down, own_gu, own_down = refs[n : n + 7]
    k_s, v_s, m_s, hid_s, dout_s, dgu_s, sems, m_sem = refs[n + 7 :]
    loads = (
        fetch_rows(0, head, k_ref, k_s, sems, 0),
        fetch_rows(0, head, v_ref, v_s, sems, 1),
    )
    load_m = pltpu.make_async_copy(m_ref.at[0, :, head], m_s, m_sem)
    load_m.start()
    width = down_ref.shape[0]
    part = width // n
    me = tok_ref[0]
    assemble(me, [lambda m, ref=ref: ref[m] for ref in shards], gu_ref, down_ref)
    grads_core(
        divisor, loads, k_s, v_s, gu_ref, down_ref, own_gu, own_down, hid_s, dout_s, dgu_s
    )
    decay = decay_ref[head]
    mine = pl.multiple_of(me * part, part)
    load_m.wait()
    own_gu[pl.ds(mine, part), :] += decay * m_s[0]
    own_gu[pl.ds(width + mine, part), :] += decay * m_s[1]
    own_down[pl.ds(mine, part), :] += decay * m_s[2]
    round_out(own_gu, own_down, send_gate, send_up, send_down)


def grads_two(n, head, divisor, tok_ref, block_ref, decay_ref, k_ref, v_ref, begin_ref, *refs):
    packs, pieces = refs[:3], refs[3 : 3 * n]
    gu_ref, down_ref, send_gate, send_up, send_down, own_gu, own_down = refs[3 * n : 3 * n + 7]
    k_s, v_s, b_s, hid_s, dout_s, dgu_s, sems, b_sem = refs[3 * n + 7 :]
    loads = (
        fetch_rows(1, head, k_ref, k_s, sems, 0),
        fetch_rows(1, head, v_ref, v_s, sems, 1),
    )
    load_b = pltpu.make_async_copy(begin_ref.at[:, head], b_s, b_sem)
    load_b.start()
    width = down_ref.shape[0]
    part = width // n
    me = tok_ref[0]
    leading = block_ref[0] == 0
    load_b.wait()

    @pl.when(leading)
    def _():
        shards = [lambda m: b_s[m]]
        for r in range(n - 1):
            shards.append(lambda m, r=r: pieces[3 * r + m][...])
        assemble(me, shards, gu_ref, down_ref)

    @pl.when(jnp.logical_not(leading))
    def _():
        gu_ref[:width, :] = packs[0][:width, :]
        gu_ref[width:, :] = packs[1][:width, :]
        down_ref[...] = packs[2][:width, :]

    grads_core(
        divisor, loads, k_s, v_s, gu_ref, down_ref, own_gu, own_down, hid_s, dout_s, dgu_s
    )
    decay = decay_ref[head]
    mine = pl.multiple_of(me * part, part)

    @pl.when(jnp.logical_not(leading))
    def _():
        own_gu[pl.ds(mine, part), :] += decay * packs[0][width:, :].astype(F32)
        own_gu[pl.ds(width + mine, part), :] += decay * packs[1][width:, :].astype(F32)
        own_down[pl.ds(mine, part), :] += decay * packs[2][width:, :].astype(F32)

    round_out(own_gu, own_down, send_gate, send_up, send_down)


def updated(rate, old_ref, own_ref, recvs, first):
    width = own_ref.shape[1]
    at = pl.ds(first, width)
    moment = own_ref[at, :]
    for recv in recvs:
        moment = moment + recv[...].astype(F32)
    old = old_ref[at, :].astype(F32)
    moved = old - rate * moment
    old_norm = jnp.sqrt(jnp.mean(old * old, axis=1, keepdims=True) + 1e-06)
    new_norm = jnp.sqrt(jnp.mean(moved * moved, axis=1, keepdims=True) + 1e-06)
    return (moved * (old_norm / new_norm)).astype(BF16), moment


def update_one(n, head, m, tok_ref, rate_ref, old_ref, own_ref, *refs):
    recvs = refs[: n - 1]
    pack_ref, moment_s = refs[n - 1 :]
    width = own_ref.shape[1]
    part = width // n
    mine = pl.multiple_of(tok_ref[0] * part, part)
    first = width if m == 1 else 0
    new, moment = updated(rate_ref[head, m], old_ref, own_ref, recvs, first)
    pack_ref[:width, :] = new
    moment_s[...] = moment
    pack_ref[width:, :] = moment_s[pl.ds(mine, part), :].astype(BF16)


def update_two(n, head, m, tok_ref, rate_ref, old_ref, own_ref, *refs):
    recvs = refs[: n - 1]
    rest = refs[n - 1 :]
    width = own_ref.shape[1]
    part = width // n
    mine = pl.multiple_of(tok_ref[0] * part, part)
    first = width if m == 1 else 0
    new_s, moment_s, fast_s, mine_s, sems = rest[-5:]
    if m == 0:
        new_ref, fast_ref, moment_ref = rest[-8:-5]
    elif m == 1:
        q_ref, gate_ref = rest[:2]
        new_ref = new_s
        q_s, q_sems = rest[-7:-5]
        hq_ref, fast_ref, moment_ref = rest[-10:-7]
        load_q = fetch_rows(1, head, q_ref, q_s, q_sems, 0)
    else:
        hq_ref = rest[0]
        new_ref = new_s
        out_s, out_sems = rest[-7:-5]
        out_ref, fast_ref, moment_ref = rest[-10:-7]
    new, moment = updated(rate_ref[head, m], old_ref, own_ref, recvs, first)
    new_ref[...] = new
    moment_s[...] = moment
    fast_s[...] = new_ref[pl.ds(mine, part), :]
    mine_s[...] = moment_s[pl.ds(mine, part), :]
    stores = [
        pltpu.make_async_copy(fast_s, fast_ref.at[0, m, head], sems.at[0]),
        pltpu.make_async_copy(mine_s, moment_ref.at[0, m, head], sems.at[1]),
    ]
    for store in stores:
        store.start()
    if m == 1:
        for at, load in zip(row_chunks(q_s.shape[0]), load_q):
            load.wait()
            gate = mm(q_s[at, :], gate_ref[...], ((1,), (1,)))
            upper = mm(q_s[at, :], new_ref[...], ((1,), (1,)))
            hq_ref[at, :] = (jax.nn.silu(gate) * upper).astype(BF16)
    if m == 2:
        for i, at in enumerate(row_chunks(hq_ref.shape[0])):
            out_s[at, :] = mm(hq_ref[at, :], new_ref[...], ((1,), (1,))).astype(BF16)
            store = pltpu.make_async_copy(
                out_s.at[at, :],
                out_ref.at[1, at, pl.ds(head * width, width)],
                out_sems.at[0, i],
            )
            store.start()
            stores.append(store)
    for store in stores:
        store.wait()


def apply_one(head, q_ref, gate_ref, up_ref, down_ref, *refs):
    out_ref, q_s, out_s, sems = refs[-4:]
    rows, width = q_s.shape
    loads = fetch_rows(0, head, q_ref, q_s, sems, 0)
    stores = []
    for i, at in enumerate(row_chunks(rows)):
        loads[i].wait()
        gate = mm(q_s[at, :], gate_ref[:width, :], ((1,), (1,)))
        upper = mm(q_s[at, :], up_ref[:width, :], ((1,), (1,)))
        hq = (jax.nn.silu(gate) * upper).astype(BF16)
        out_s[at, :] = mm(hq, down_ref[:width, :], ((1,), (1,))).astype(BF16)
        store = pltpu.make_async_copy(
            out_s.at[at, :], out_ref.at[0, at, pl.ds(head * width, width)], sems.at[1, i]
        )
        store.start()
        stores.append(store)
    for store in stores:
        store.wait()


def on_device(keys, values, queries, fast_in, moment_in, initial_fast, rates, decays):
    n = lax.axis_size("tok")
    blocks = lax.axis_size("block")
    _, rows, features = keys.shape
    heads = rates.shape[1]
    width = features // heads
    part = width // n
    chunks = len(row_chunks(rows))
    divisor = float(rows * n)
    tok = lax.axis_index("tok").astype(jnp.int32).reshape(1)
    block = lax.axis_index("block").astype(jnp.int32).reshape(1)
    fast_t = jnp.swapaxes(fast_in, 3, 4)
    moment_t = jnp.swapaxes(moment_in, 3, 4)
    begin_t = jnp.swapaxes(initial_fast, 2, 3)
    rates = rates.T
    keys, values, queries, fast_t, moment_t, begin_t = (
        pltpu.with_memory_space_constraint(x, pltpu.HBM)
        for x in (keys, values, queries, fast_t, moment_t, begin_t)
    )

    def turned(x):
        return [lax.ppermute(x, "tok", [(i, (i + r) % n) for i in range(n)]) for r in range(1, n)]

    def forward(x):
        return lax.ppermute(x, "block", [(i, i + 1) for i in range(blocks - 1)])

    def shape(*dims, dtype=BF16):
        return jax.ShapeDtypeStruct(dims, dtype)

    matrix = shape(width, width)
    row_scratch = pltpu.VMEM((rows, width), BF16)
    grad_scratch = (
        row_scratch,
        row_scratch,
        None,
        row_scratch,
        row_scratch,
        pltpu.VMEM((rows, 2 * width), BF16),
        DMA((2, chunks)),
        DMA(()),
    )
    grad_out = (
        shape(2 * width, width),
        matrix,
        matrix,
        matrix,
        matrix,
        shape(2 * width, width, dtype=F32),
        shape(width, width, dtype=F32),
    )

    def grad_call(kernel, n_vmem, extra, hbm_at):
        scratch = tuple(pltpu.VMEM((3, part, width), extra) if s is None else s for s in grad_scratch)
        specs = [SMEM] * hbm_at + [HBM] * 3 + [VMEM] * n_vmem
        return call(kernel, grad_out, specs, (VMEM,) * 7, scratch)

    recv_fast, owned = [], []
    for h in range(heads):
        owned.append(
            call(functools.partial(take_head, h), shape(3, part, width), [HBM], VMEM)(fast_t)
        )
        recv_fast.append(turned(owned[h]))

    n_pieces = 3 * heads
    sources = [(2 * (p + 1)) % blocks for p in range(n_pieces)]
    piece = call(
        functools.partial(take_piece, sources), shape(part, width), [SMEM, HBM], VMEM
    )(block, begin_t)
    crossed = [
        lax.ppermute(
            piece,
            ("block", "tok"),
            [(s * n + i, s * n + (i + r) % n) for s in sorted(set(sources)) for i in range(n)],
        )
        for r in range(1, n)
    ]

    first = [
        grad_call(functools.partial(grads_one, n, h, divisor), n, F32, 2)(
            tok, decays, keys, values, moment_t, owned[h], *recv_fast[h]
        )
        for h in range(heads)
    ]

    def olds(state):
        gu, down, own_gu, own_down = state[0], state[1], state[5], state[6]
        return ((gu, own_gu), (gu, own_gu), (down, own_down))

    packs = []
    for h in range(heads):
        packs.append([])
        for m in range(3):
            recvs = turned(first[h][2 + m])
            old, own = olds(first[h])[m]
            packs[h].append(
                call(
                    functools.partial(update_one, n, h, m),
                    shape(width + part, width),
                    [SMEM, SMEM] + [VMEM] * (1 + n),
                    VMEM,
                    (pltpu.VMEM((width, width), F32),),
                )(tok, rates, old, own, *recvs)
            )

    begins = []
    for p in range(n_pieces):
        begins.append(
            [
                lax.ppermute(
                    x, ("block", "tok"), [(sources[p] * n + i, i) for i in range(n)]
                )
                for x in crossed
            ]
        )

    second = []
    for h in range(heads):
        arrived = [forward(packs[h][m]) for m in range(3)]
        pieces = [begins[m * heads + h][r] for r in range(n - 1) for m in range(3)]
        second.append(
            grad_call(
                functools.partial(grads_two, n, h, divisor), 3 * n, BF16, 3
            )(tok, block, decays, keys, values, begin_t, *arrived, *pieces)
        )

    out_shape = jax.ShapeDtypeStruct(keys.shape, BF16)
    outputs = None
    for h in range(heads):
        prior = [] if outputs is None else [outputs]
        outputs = call(
            functools.partial(apply_one, h),
            out_shape,
            [HBM] + [VMEM] * 3 + [HBM] * len(prior),
            HBM,
            (row_scratch, row_scratch, DMA((2, chunks))),
            aliases={4: 0} if prior else None,
        )(queries, *packs[h], *prior)

    fast_shape = jax.ShapeDtypeStruct(fast_t.shape, BF16)
    moment_shape = jax.ShapeDtypeStruct(moment_t.shape, F32)
    ends = []
    last_scratch = (
        pltpu.VMEM((width, width), BF16),
        pltpu.VMEM((width, width), F32),
        pltpu.VMEM((part, width), BF16),
        pltpu.VMEM((part, width), F32),
        DMA((2,)),
    )
    for h in range(heads):
        recvs = [turned(second[h][2 + m]) for m in range(3)]
        state = olds(second[h])
        at = 4 + (n - 1)
        specs = [SMEM, SMEM] + [VMEM] * (1 + n)
        rows_sems = (row_scratch, DMA((1, chunks)))
        gate, *ends = call(
            functools.partial(update_two, n, h, 0),
            (matrix, fast_shape, moment_shape),
            specs + [HBM] * len(ends),
            (VMEM, HBM, HBM),
            last_scratch,
            aliases={at: 1, at + 1: 2} if ends else None,
        )(tok, rates, *state[0], *recvs[0], *ends)
        hq, *ends = call(
            functools.partial(update_two, n, h, 1),
            (shape(rows, width), fast_shape, moment_shape),
            specs + [HBM, VMEM, HBM, HBM],
            (VMEM, HBM, HBM),
            rows_sems + last_scratch,
            aliases={at + 2: 1, at + 3: 2},
        )(tok, rates, *state[1], *recvs[1], queries, gate, *ends)
        outputs, *ends = call(
            functools.partial(update_two, n, h, 2),
            (out_shape, fast_shape, moment_shape),
            specs + [VMEM] + [HBM] * 3,
            (HBM,) * 3,
            rows_sems + last_scratch,
            aliases={at + 1: 0, at + 2: 1, at + 3: 2},
        )(tok, rates, *state[2], *recvs[2], hq, outputs, *ends)
    return (outputs, jnp.swapaxes(ends[0], 3, 4), jnp.swapaxes(ends[1], 3, 4))


def solution(mesh):
    placed = (
        P(None, ("block", "tok"), None),
        P(None, ("block", "tok"), None),
        P(None, ("block", "tok"), None),
        P("block", None, None, None, "tok"),
        P("block", None, None, None, "tok"),
        P(None, None, None, "tok"),
        P(),
        P(),
    )
    step = jax.shard_map(
        on_device,
        mesh=mesh,
        in_specs=placed,
        out_specs=(
            P(None, ("block", "tok"), None),
            P("block", None, None, None, "tok"),
            P("block", None, None, None, "tok"),
        ),
        check_vma=False,
    )

    def run(*args):
        with jax.sharding.use_abstract_mesh(mesh.abstract_mesh):
            return step(*args)

    return run
```

time: 125 us -> 125 us (level)
  waiting for transfers between devices: 52.8 us -> 28.2 us
  starting transfers between devices: 24.1 us -> 43.6 us
  Pallas kernels: 40.7 us -> 51.4 us
  local copies, waits for them, and re-layouts: 6.14 us -> 0.01 us
    ppermute x11 -> x21, waiting for transfers between devices: 52.8 us -> 28.1 us  [the longest x14 17.7 us: turned(): lax.ppermute(x, 'tok', [(i, (i + r) % n) for i in range(n)])]
    pallas_call x16 -> x21, Pallas kernels: 40.7 us -> 51.4 us  [the longest x2 11.9 us: on_device(): grad_call(functools.partial(grads_two, n, h, divisor), 3 * n, BF16, 3)]
    ppermute x11 -> x21, starting transfers between devices: 15.6 us -> 26 us  [the longest x14 17.7 us: turned(): lax.ppermute(x, 'tok', [(i, (i + r) % n) for i in range(n)])]
    ppermute x4 -> x6, starting transfers between devices: 8.53 us -> 17.6 us  [forward(): return lax.ppermute(x, 'block', [(i, i + 1) for i in range(blocks - 1)])]
    unnamed x18 -> x4, local copies, waits for them, and re-layouts: 6.14 us -> 0.01 us
  transfers between devices with their start and end apart: 15 -> 27, of which waited for: 7 -> 10; matrix products, arithmetic and copies ran while one was open for 0% -> 0% of each run, Pallas kernels for 31% -> 39%
where the time goes in v3:
time: 125 us; the launch traced here: 124 us
  Pallas kernels  51.4 us (41%)
  starting transfers between devices  43.6 us (35%)
  waiting for transfers between devices  28.2 us (23%)
    ppermute x14, waiting for transfers between devices, turned(): lax.ppermute(x, 'tok', [(i, (i + r) % n) for i in range(n)])  17.7 us
    ppermute x14, starting transfers between devices, turned(): lax.ppermute(x, 'tok', [(i, (i + r) % n) for i in range(n)])  17.7 us
    ppermute x6, starting transfers between devices, forward(): return lax.ppermute(x, 'block', [(i, i + 1) for i in range(blocks - 1)])  17.6 us
    pallas_call x2, Pallas kernels, on_device(): grad_call(functools.partial(grads_two, n, h, divisor), 3 * n, BF16, 3)  11.9 us
    pallas_call x2, Pallas kernels, on_device(): grad_call(functools.partial(grads_one, n, h, divisor), n, F32, 2)  10.5 us
    ppermute x6, waiting for transfers between devices, on_device(): lax.ppermute(x, ('block', 'tok'), [(sources[p] * n + i, i) for i in range...  10.4 us
    ppermute x6, starting transfers between devices, on_device(): lax.ppermute(x, ('block', 'tok'), [(sources[p] * n + i, i) for i in range...  7.71 us
    pallas_call x2, Pallas kernels, on_device(): call(functools.partial(apply_one, h), out_shape, [HBM] + [VMEM] * 3 + [HB...  7.34 us
  transfers between devices with their start and end apart: 27, of which 10 were waited for; matrix products, arithmetic and copies ran while one was open for 0% of the time, Pallas kernels for 39%

profile of v3, /device:TPU:0, one launch (start us, length us, event | category | flops | bytes accessed | tf_op | source)
XLA Modules:
  0.0 124.3 jit_solution(15990714696136227825)
XLA Ops:
  1.7 3.0 %collective-permute-start.14 = (bf16[3,192,384]{2,1,0:T(8,128)(2,1)S(1)}, bf16[3,192,384]{2,1,0:T(8,128)(2,1)S(1)}, u32[]{:S(2)}, u32[]{:S(2)}) collective-permute-start(bf16[3,192,384]{2,1,0:T(8,128)(2,1)S(1)} %shard_map.110.refs_0_), channel_id=1, source_target_pairs={{0,1},{1,0},{2,3},{3,2},{4,5},{5,4},{6,7},{7,6},{8,9},{9,8},{10,11... | collective-permute-start | bytes 1327112 | tf_op jit(solution)/shard_map/ppermute | solution.py:294
  7.2 8.4 %collective-permute-done.14.refs_1_ = bf16[3,192,384]{2,1,0:T(8,128)(2,1)S(1)} collective-permute-done((bf16[3,192,384]{2,1,0:T(8,128)(2,1)S(1)}, bf16[3,192,384]{2,1,0:T(8,128)(2,1)S(1)}, u32[]{:S(2)}, u32[]{:S(2)}) %collective-permute-start.14) | collective-permute-done | bytes 442400 | tf_op jit(solution)/shard_map/ppermute | solution.py:294
  15.6 5.3 %shard_map.111 = (bf16[768,384]{1,0:T(8,128)(2,1)S(1)}, bf16[384,384]{1,0:T(8,128)(2,1)S(1)}, bf16[384,384]{1,0:T(8,128)(2,1)S(1)}, bf16[384,384]{1,0:T(8,128)(2...) custom-call(s32[1]{0:T(128)} %bitcast.tok_ref, f32[2]{0:T(128)S(1)} %copy-done.1, ...), custom_call_target="tpu_custom_call" | custom-call | tf_op jit(solution)/shard_map/pallas_call | solution.py:351
  20.9 2.1 %collective-permute-start.15 = (bf16[384,384]{1,0:T(8,128)(2,1)S(1)}, bf16[384,384]{1,0:T(8,128)(2,1)S(1)}, u32[]{:S(2)}, u32[]{:S(2)}) collective-permute-start(bf16[384,384]{1,0:T(8,128)(2,1)S(1)} %get-tuple-element.65), channel_id=1, source_target_pairs={{0,1},{1,0},{2,3},{3,2},{4,5},{5,4},{6,7},{7,6},{8,9},{9,8},{10,11... | collective-permute-start | bytes 884744 | tf_op jit(solution)/shard_map/ppermute | solution.py:294
  23.1 1.9 %collective-permute-start.19 = (bf16[384,384]{1,0:T(8,128)(2,1)S(1)}, bf16[384,384]{1,0:T(8,128)(2,1)S(1)}, u32[]{:S(2)}, u32[]{:S(2)}) collective-permute-start(bf16[384,384]{1,0:T(8,128)(2,1)S(1)} %get-tuple-element.69), channel_id=1, source_target_pairs={{0,1},{1,0},{2,3},{3,2},{4,5},{5,4},{6,7},{7,6},{8,9},{9,8},{10,11... | collective-permute-start | bytes 884744 | tf_op jit(solution)/shard_map/ppermute | solution.py:294
  26.3 5.2 %shard_map.104 = (bf16[768,384]{1,0:T(8,128)(2,1)S(1)}, bf16[384,384]{1,0:T(8,128)(2,1)S(1)}, bf16[384,384]{1,0:T(8,128)(2,1)S(1)}, bf16[384,384]{1,0:T(8,128)(2...) custom-call(s32[1]{0:T(128)} %bitcast.tok_ref, f32[2]{0:T(128)S(1)} %copy-done.1, ...), custom_call_target="tpu_custom_call" | custom-call | tf_op jit(solution)/shard_map/pallas_call | solution.py:351
  32.4 2.3 %collective-permute-done.21.refs_3_ = bf16[192,384]{1,0:T(8,128)(2,1)S(1)} collective-permute-done((bf16[192,384]{1,0:T(8,128)(2,1)S(1)}, bf16[192,384]{1,0:T(8,128)(2,1)S(1)}, u32[]{:S(2)}, u32[]{:S(2)}) %collective-permute-start.21) | collective-permute-done | bytes 147488 | tf_op jit(solution)/shard_map/ppermute | solution.py:381
  40.7 3.4 %collective-permute-done.19.refs_0_ = bf16[384,384]{1,0:T(8,128)(2,1)S(1)} collective-permute-done((bf16[384,384]{1,0:T(8,128)(2,1)S(1)}, bf16[384,384]{1,0:T(8,128)(2,1)S(1)}, u32[]{:S(2)}, u32[]{:S(2)}) %collective-permute-start.19) | collective-permute-done | bytes 294944 | tf_op jit(solution)/shard_map/ppermute | solution.py:294
  44.1 3.7 %collective-permute-start.18 = (bf16[576,384]{1,0:T(8,128)(2,1)S(1)}, bf16[576,384]{1,0:T(8,128)(2,1)S(1)}, u32[]{:S(2)}, u32[]{:S(2)}) collective-permute-start(bf16[576,384]{1,0:T(8,128)(2,1)S(1)} %shard_map.113.up_ref), channel_id=1, source_target_pairs={{0,2},{2,4},{4,6},{6,8},{8,10},{10,12},{12,14},{14,16},{16,18},{18... | collective-permute-start | bytes 1327112 | tf_op jit(solution)/shard_map/ppermute | solution.py:297
  48.8 5.4 %collective-permute-start.20 = (bf16[576,384]{1,0:T(8,128)(2,1)S(1)}, bf16[576,384]{1,0:T(8,128)(2,1)S(1)}, u32[]{:S(2)}, u32[]{:S(2)}) collective-permute-start(bf16[576,384]{1,0:T(8,128)(2,1)S(1)} %shard_map.114.down_ref), channel_id=1, source_target_pairs={{0,2},{2,4},{4,6},{6,8},{8,10},{10,12},{12,14},{14,16},{16,18},{18... | collective-permute-start | bytes 1327112 | tf_op jit(solution)/shard_map/ppermute | solution.py:297
  59.0 4.2 %collective-permute-done.5.refs_0_ = bf16[384,384]{1,0:T(8,128)(2,1)S(1)} collective-permute-done((bf16[384,384]{1,0:T(8,128)(2,1)S(1)}, bf16[384,384]{1,0:T(8,128)(2,1)S(1)}, u32[]{:S(2)}, u32[]{:S(2)}) %collective-permute-start.5) | collective-permute-done | bytes 294944 | tf_op jit(solution)/shard_map/ppermute | solution.py:294
  66.5 3.9 %collective-permute-start.2 = (bf16[576,384]{1,0:T(8,128)(2,1)S(1)}, bf16[576,384]{1,0:T(8,128)(2,1)S(1)}, u32[]{:S(2)}, u32[]{:S(2)}) collective-permute-start(bf16[576,384]{1,0:T(8,128)(2,1)S(1)} %shard_map.105.gate_ref), channel_id=1, source_target_pairs={{0,2},{2,4},{4,6},{6,8},{8,10},{10,12},{12,14},{14,16},{16,18},{18... | collective-permute-start | bytes 1327112 | tf_op jit(solution)/shard_map/ppermute | solution.py:297
  70.4 1.9 %collective-permute-start.6 = (bf16[576,384]{1,0:T(8,128)(2,1)S(1)}, bf16[576,384]{1,0:T(8,128)(2,1)S(1)}, u32[]{:S(2)}, u32[]{:S(2)}) collective-permute-start(bf16[576,384]{1,0:T(8,128)(2,1)S(1)} %shard_map.107.down_ref), channel_id=1, source_target_pairs={{0,2},{2,4},{4,6},{6,8},{8,10},{10,12},{12,14},{14,16},{16,18},{18... | collective-permute-start | bytes 1327112 | tf_op jit(solution)/shard_map/ppermute | solution.py:297
  75.0 5.9 %shard_map.115 = (bf16[768,384]{1,0:T(8,128)(2,1)S(1)}, bf16[384,384]{1,0:T(8,128)(2,1)S(1)}, bf16[384,384]{1,0:T(8,128)(2,1)S(1)}, bf16[384,384]{1,0:T(8,128)(2...) custom-call(s32[1]{0:T(128)} %bitcast.tok_ref, s32[1]{0:T(128)} %bitcast.2.block_ref, ...), custom_call_target="tpu_custom_call" | custom-call | tf_op jit(solution)/shard_map/pallas_call | solution.py:393
  84.1 6.6 %collective-permute-done.9.refs_4_ = bf16[192,384]{1,0:T(8,128)(2,1)S(1)} collective-permute-done((bf16[192,384]{1,0:T(8,128)(2,1)S(1)}, bf16[192,384]{1,0:T(8,128)(2,1)S(1)}, u32[]{:S(2)}, u32[]{:S(2)}) %collective-permute-start.9) | collective-permute-done | bytes 147488 | tf_op jit(solution)/shard_map/ppermute | solution.py:381
  92.8 6.0 %shard_map.109 = (bf16[768,384]{1,0:T(8,128)(2,1)S(1)}, bf16[384,384]{1,0:T(8,128)(2,1)S(1)}, bf16[384,384]{1,0:T(8,128)(2,1)S(1)}, bf16[384,384]{1,0:T(8,128)(2...) custom-call(s32[1]{0:T(128)} %bitcast.tok_ref, s32[1]{0:T(128)} %bitcast.2.block_ref, ...), custom_call_target="tpu_custom_call" | custom-call | tf_op jit(solution)/shard_map/pallas_call | solution.py:393
  101.8 3.7 %shard_map.118.refs_0_ = bf16[2,768,768]{2,1,0:T(8,128)(2,1)} custom-call(bf16[2,768,768]{2,1,0:T(8,128)(2,1)} %refs_1_.3, bf16[576,384]{1,0:T(8,128)(2,1)S(1)} %shard_map.112.gate_ref, bf16[576,384]{1,0:T(8,128)(2,1)S(1)} %shard_map.113.up_ref, bf16[576,384]{1,0:T(8,128)(2,1)S(1)} %shard_map.114.down_ref), custom_call_target="tpu_custom_call" | custom-call | tf_op jit(solution)/shard_map/pallas_call | solution.py:402
  105.5 3.7 %shard_map.119.refs_2_ = bf16[2,768,768]{2,1,0:T(8,128)(2,1)} custom-call(bf16[2,768,768]{2,1,0:T(8,128)(2,1)} %refs_1_.3, bf16[576,384]{1,0:T(8,128)(2,1)S(1)} %shard_map.105.gate_ref, bf16[576,384]{1,0:T(8,128)(2,1)S(1)} %shard_map.106.up_ref, bf16[576,384]{1,0:T(8,128)(2,1)S(1)} %shard_map.107.down_ref, ...), custom_call_target="tpu_custom_call", output_to_operand_aliasing={{}: (4, {})} | custom-call | tf_op jit(solution)/shard_map/pallas_call | solution.py:402
  109.2 1.7 %shard_map.116 = (bf16[384,384]{1,0:T(8,128)(2,1)S(1)}, bf16[1,3,2,192,384]{4,3,2,1,0:T(8,128)(2,1)}, f32[1,3,2,192,384]{4,3,2,1,0:T(8,128)}) custom-call(s32[1]{0:T(128)} %bitcast.tok_ref, f32[2,3]{1,0:T(2,128)S(1)} %bitcast.14, bf16[768,384]{1,0:T(8,128)(2,1)S(1)} %get-tuple-element.73.old_ref, f32[768,384]{1,0:T(8,128)S(1)} %get-tuple-element.74.own_ref, ...), custom_call_target="tpu_custom_call" | custom-call | tf_op jit(solution)/shard_map/pallas_call | solution.py:427
  110.9 2.8 %shard_map.117 = (bf16[768,384]{1,0:T(8,128)(2,1)S(1)}, bf16[1,3,2,192,384]{4,3,2,1,0:T(8,128)(2,1)}, f32[1,3,2,192,384]{4,3,2,1,0:T(8,128)}) custom-call(s32[1]{0:T(128)} %bitcast.tok_ref, f32[2,3]{1,0:T(2,128)S(1)} %bitcast.15, bf16[768,384]{1,0:T(8,128)(2,1)S(1)} %get-tuple-element.73.old_ref, ...), custom_call_target="tpu_custom_call", output_to_operand_aliasing={{1}: (7, {}), {2}: (8, {})} | custom-call | tf_op jit(solution)/shard_map/pallas_call | solution.py:435
  113.7 2.2 %shard_map.120 = (bf16[2,768,768]{2,1,0:T(8,128)(2,1)}, bf16[1,3,2,192,384]{4,3,2,1,0:T(8,128)(2,1)}, f32[1,3,2,192,384]{4,3,2,1,0:T(8,128)}) custom-call(s32[1]{0:T(128)} %bitcast.tok_ref, f32[2,3]{1,0:T(2,128)S(1)} %bitcast.16, bf16[384,384]{1,0:T(8,128)(2,1)S(1)} %get-tuple-element.70.old_ref, ...), custom_call_target="tpu_custom_call", output_to_operand_aliasing={{0}: (6, {}), {1}: (7, {}), {2}: (8, {})} | custom-call | tf_op jit(solution)/shard_map/pallas_call | solution.py:443
  115.9 1.7 %shard_map.121 = (bf16[384,384]{1,0:T(8,128)(2,1)S(1)}, bf16[1,3,2,192,384]{4,3,2,1,0:T(8,128)(2,1)}, f32[1,3,2,192,384]{4,3,2,1,0:T(8,128)}) custom-call(s32[1]{0:T(128)} %bitcast.tok_ref, f32[2,3]{1,0:T(2,128)S(1)} %bitcast.17, bf16[768,384]{1,0:T(8,128)(2,1)S(1)} %get-tuple-element.59.old_ref, ...), custom_call_target="tpu_custom_call", output_to_operand_aliasing={{1}: (5, {}), {2}: (6, {})} | custom-call | tf_op jit(solution)/shard_map/pallas_call | solution.py:427
  118.8 2.8 %shard_map.122 = (bf16[768,384]{1,0:T(8,128)(2,1)S(1)}, bf16[1,3,2,192,384]{4,3,2,1,0:T(8,128)(2,1)}, f32[1,3,2,192,384]{4,3,2,1,0:T(8,128)}) custom-call(s32[1]{0:T(128)} %bitcast.tok_ref, f32[2,3]{1,0:T(2,128)S(1)} %bitcast.18, bf16[768,384]{1,0:T(8,128)(2,1)S(1)} %get-tuple-element.59.old_ref, ...), custom_call_target="tpu_custom_call", output_to_operand_aliasing={{1}: (7, {}), {2}: (8, {})} | custom-call | tf_op jit(solution)/shard_map/pallas_call | solution.py:435
  122.0 2.2 %shard_map.123 = (bf16[2,768,768]{2,1,0:T(8,128)(2,1)}, bf16[1,3,2,192,384]{4,3,2,1,0:T(8,128)(2,1)}, f32[1,3,2,192,384]{4,3,2,1,0:T(8,128)}) custom-call(s32[1]{0:T(128)} %bitcast.tok_ref, f32[2,3]{1,0:T(2,128)S(1)} %bitcast.19, bf16[384,384]{1,0:T(8,128)(2,1)S(1)} %get-tuple-element.56.old_ref, ...), custom_call_target="tpu_custom_call", output_to_operand_aliasing={{0}: (6, {}), {1}: (7, {}), {2}: (8, {})} | custom-call | tf_op jit(solution)/shard_map/pallas_call | solution.py:443
  (55 shorter events, 33.2 us)
Async XLA Ops:
  1.7 14.0 %collective-permute-start.14 = (bf16[3,192,384]{2,1,0:T(8,128)(2,1)S(1)}, bf16[3,192,384]{2,1,0:T(8,128)(2,1)S(1)}, u32[]{:S(2)}, u32[]{:S(2)}) collective-permute-start(bf16[3,192,384]{2,1,0:T(8,128)(2,1)S(1)} %shard_map.110.refs_0_), channel_id=1, source_target_pairs={{0,1},{1,0},{2,3},{3,2},{4,5},{5,4},{6,7},{7,6},{8,9},{9,8},{10,11... | collective-permute-start | bytes 1327112 | tf_op jit(solution)/shard_map/ppermute | solution.py:294
  5.6 20.7 %collective-permute-start = (bf16[3,192,384]{2,1,0:T(8,128)(2,1)S(1)}, bf16[3,192,384]{2,1,0:T(8,128)(2,1)S(1)}, u32[]{:S(2)}, u32[]{:S(2)}) collective-permute-start(bf16[3,192,384]{2,1,0:T(8,128)(2,1)S(1)} %shard_map.103.refs_0_), channel_id=1, source_target_pairs={{0,1},{1,0},{2,3},{3,2},{4,5},{5,4},{6,7},{7,6},{8,9},{9,8},{10,11... | collective-permute-start | bytes 1327112 | tf_op jit(solution)/shard_map/ppermute | solution.py:294
  6.6 18.5 %collective-permute-start.7 = (bf16[192,384]{1,0:T(8,128)(2,1)S(1)}, bf16[192,384]{1,0:T(8,128)(2,1)S(1)}, u32[]{:S(2)}, u32[]{:S(2)}) collective-permute-start(bf16[192,384]{1,0:T(8,128)(2,1)S(1)} %shard_map.108), channel_id=1, source_target_pairs={{4,5},{5,4},{8,9},{9,8},{12,13},{13,12},{16,17},{17,16},{20,21},{2... | collective-permute-start | bytes 442376 | tf_op jit(solution)/shard_map/ppermute | solution.py:342
  20.9 15.1 %collective-permute-start.15 = (bf16[384,384]{1,0:T(8,128)(2,1)S(1)}, bf16[384,384]{1,0:T(8,128)(2,1)S(1)}, u32[]{:S(2)}, u32[]{:S(2)}) collective-permute-start(bf16[384,384]{1,0:T(8,128)(2,1)S(1)} %get-tuple-element.65), channel_id=1, source_target_pairs={{0,1},{1,0},{2,3},{3,2},{4,5},{5,4},{6,7},{7,6},{8,9},{9,8},{10,11... | collective-permute-start | bytes 884744 | tf_op jit(solution)/shard_map/ppermute | solution.py:294
  23.0 15.5 %collective-permute-start.17 = (bf16[384,384]{1,0:T(8,128)(2,1)S(1)}, bf16[384,384]{1,0:T(8,128)(2,1)S(1)}, u32[]{:S(2)}, u32[]{:S(2)}) collective-permute-start(bf16[384,384]{1,0:T(8,128)(2,1)S(1)} %get-tuple-element.66), channel_id=1, source_target_pairs={{0,1},{1,0},{2,3},{3,2},{4,5},{5,4},{6,7},{7,6},{8,9},{9,8},{10,11... | collective-permute-start | bytes 884744 | tf_op jit(solution)/shard_map/ppermute | solution.py:294
  23.1 21.0 %collective-permute-start.19 = (bf16[384,384]{1,0:T(8,128)(2,1)S(1)}, bf16[384,384]{1,0:T(8,128)(2,1)S(1)}, u32[]{:S(2)}, u32[]{:S(2)}) collective-permute-start(bf16[384,384]{1,0:T(8,128)(2,1)S(1)} %get-tuple-element.69), channel_id=1, source_target_pairs={{0,1},{1,0},{2,3},{3,2},{4,5},{5,4},{6,7},{7,6},{8,9},{9,8},{10,11... | collective-permute-start | bytes 884744 | tf_op jit(solution)/shard_map/ppermute | solution.py:294
  25.0 9.7 %collective-permute-start.21 = (bf16[192,384]{1,0:T(8,128)(2,1)S(1)}, bf16[192,384]{1,0:T(8,128)(2,1)S(1)}, u32[]{:S(2)}, u32[]{:S(2)}) collective-permute-start(bf16[192,384]{1,0:T(8,128)(2,1)S(1)} %collective-permute-done.7), channel_id=1, source_target_pairs={{4,0},{5,1}} | collective-permute-start | bytes 442376 | tf_op jit(solution)/shard_map/ppermute | solution.py:381
  31.6 22.6 %collective-permute-start.3 = (bf16[384,384]{1,0:T(8,128)(2,1)S(1)}, bf16[384,384]{1,0:T(8,128)(2,1)S(1)}, u32[]{:S(2)}, u32[]{:S(2)}) collective-permute-start(bf16[384,384]{1,0:T(8,128)(2,1)S(1)} %get-tuple-element.52), channel_id=1, source_target_pairs={{0,1},{1,0},{2,3},{3,2},{4,5},{5,4},{6,7},{7,6},{8,9},{9,8},{10,11... | collective-permute-start | bytes 884744 | tf_op jit(solution)/shard_map/ppermute | solution.py:294
  34.7 14.0 %collective-permute-start.22 = (bf16[192,384]{1,0:T(8,128)(2,1)S(1)}, bf16[192,384]{1,0:T(8,128)(2,1)S(1)}, u32[]{:S(2)}, u32[]{:S(2)}) collective-permute-start(bf16[192,384]{1,0:T(8,128)(2,1)S(1)} %collective-permute-done.7), channel_id=1, source_target_pairs={{12,0},{13,1}} | collective-permute-start | bytes 442376 | tf_op jit(solution)/shard_map/ppermute | solution.py:381
  36.0 19.9 %collective-permute-start.1 = (bf16[384,384]{1,0:T(8,128)(2,1)S(1)}, bf16[384,384]{1,0:T(8,128)(2,1)S(1)}, u32[]{:S(2)}, u32[]{:S(2)}) collective-permute-start(bf16[384,384]{1,0:T(8,128)(2,1)S(1)} %get-tuple-element.51), channel_id=1, source_target_pairs={{0,1},{1,0},{2,3},{3,2},{4,5},{5,4},{6,7},{7,6},{8,9},{9,8},{10,11... | collective-permute-start | bytes 884744 | tf_op jit(solution)/shard_map/ppermute | solution.py:294
  38.5 31.9 %collective-permute-start.16 = (bf16[576,384]{1,0:T(8,128)(2,1)S(1)}, bf16[576,384]{1,0:T(8,128)(2,1)S(1)}, u32[]{:S(2)}, u32[]{:S(2)}) collective-permute-start(bf16[576,384]{1,0:T(8,128)(2,1)S(1)} %shard_map.112.gate_ref), channel_id=1, source_target_pairs={{0,2},{2,4},{4,6},{6,8},{8,10},{10,12},{12,14},{14,16},{16,18},{18... | collective-permute-start | bytes 1327112 | tf_op jit(solution)/shard_map/ppermute | solution.py:297
  44.1 28.3 %collective-permute-start.18 = (bf16[576,384]{1,0:T(8,128)(2,1)S(1)}, bf16[576,384]{1,0:T(8,128)(2,1)S(1)}, u32[]{:S(2)}, u32[]{:S(2)}) collective-permute-start(bf16[576,384]{1,0:T(8,128)(2,1)S(1)} %shard_map.113.up_ref), channel_id=1, source_target_pairs={{0,2},{2,4},{4,6},{6,8},{8,10},{10,12},{12,14},{14,16},{16,18},{18... | collective-permute-start | bytes 1327112 | tf_op jit(solution)/shard_map/ppermute | solution.py:297
  48.8 24.9 %collective-permute-start.20 = (bf16[576,384]{1,0:T(8,128)(2,1)S(1)}, bf16[576,384]{1,0:T(8,128)(2,1)S(1)}, u32[]{:S(2)}, u32[]{:S(2)}) collective-permute-start(bf16[576,384]{1,0:T(8,128)(2,1)S(1)} %shard_map.114.down_ref), channel_id=1, source_target_pairs={{0,2},{2,4},{4,6},{6,8},{8,10},{10,12},{12,14},{14,16},{16,18},{18... | collective-permute-start | bytes 1327112 | tf_op jit(solution)/shard_map/ppermute | solution.py:297
  55.9 10.6 %collective-permute-start.23 = (bf16[192,384]{1,0:T(8,128)(2,1)S(1)}, bf16[192,384]{1,0:T(8,128)(2,1)S(1)}, u32[]{:S(2)}, u32[]{:S(2)}) collective-permute-start(bf16[192,384]{1,0:T(8,128)(2,1)S(1)} %collective-permute-done.7), channel_id=1, source_target_pairs={{20,0},{21,1}} | collective-permute-start | bytes 442376 | tf_op jit(solution)/shard_map/ppermute | solution.py:381
  63.1 28.6 %collective-permute-start.4 = (bf16[576,384]{1,0:T(8,128)(2,1)S(1)}, bf16[576,384]{1,0:T(8,128)(2,1)S(1)}, u32[]{:S(2)}, u32[]{:S(2)}) collective-permute-start(bf16[576,384]{1,0:T(8,128)(2,1)S(1)} %shard_map.106.up_ref), channel_id=1, source_target_pairs={{0,2},{2,4},{4,6},{6,8},{8,10},{10,12},{12,14},{14,16},{16,18},{18... | collective-permute-start | bytes 1327112 | tf_op jit(solution)/shard_map/ppermute | solution.py:297
  66.5 26.2 %collective-permute-start.2 = (bf16[576,384]{1,0:T(8,128)(2,1)S(1)}, bf16[576,384]{1,0:T(8,128)(2,1)S(1)}, u32[]{:S(2)}, u32[]{:S(2)}) collective-permute-start(bf16[576,384]{1,0:T(8,128)(2,1)S(1)} %shard_map.105.gate_ref), channel_id=1, source_target_pairs={{0,2},{2,4},{4,6},{6,8},{8,10},{10,12},{12,14},{14,16},{16,18},{18... | collective-permute-start | bytes 1327112 | tf_op jit(solution)/shard_map/ppermute | solution.py:297
  70.4 22.3 %collective-permute-start.6 = (bf16[576,384]{1,0:T(8,128)(2,1)S(1)}, bf16[576,384]{1,0:T(8,128)(2,1)S(1)}, u32[]{:S(2)}, u32[]{:S(2)}) collective-permute-start(bf16[576,384]{1,0:T(8,128)(2,1)S(1)} %shard_map.107.down_ref), channel_id=1, source_target_pairs={{0,2},{2,4},{4,6},{6,8},{8,10},{10,12},{12,14},{14,16},{16,18},{18... | collective-permute-start | bytes 1327112 | tf_op jit(solution)/shard_map/ppermute | solution.py:297
  73.7 9.1 %collective-permute-start.8 = (bf16[192,384]{1,0:T(8,128)(2,1)S(1)}, bf16[192,384]{1,0:T(8,128)(2,1)S(1)}, u32[]{:S(2)}, u32[]{:S(2)}) collective-permute-start(bf16[192,384]{1,0:T(8,128)(2,1)S(1)} %collective-permute-done.7), channel_id=1, source_target_pairs={{8,0},{9,1}} | collective-permute-start | bytes 442376 | tf_op jit(solution)/shard_map/ppermute | solution.py:381
  81.3 19.5 %collective-permute-start.26 = (bf16[384,384]{1,0:T(8,128)(2,1)S(1)}, bf16[384,384]{1,0:T(8,128)(2,1)S(1)}, u32[]{:S(2)}, u32[]{:S(2)}) collective-permute-start(bf16[384,384]{1,0:T(8,128)(2,1)S(1)} %get-tuple-element.76), channel_id=1, source_target_pairs={{0,1},{1,0},{2,3},{3,2},{4,5},{5,4},{6,7},{7,6},{8,9},{9,8},{10,11... | collective-permute-start | bytes 884744 | tf_op jit(solution)/shard_map/ppermute | solution.py:294
  90.7 20.1 %collective-permute-start.25 = (bf16[384,384]{1,0:T(8,128)(2,1)S(1)}, bf16[384,384]{1,0:T(8,128)(2,1)S(1)}, u32[]{:S(2)}, u32[]{:S(2)}) collective-permute-start(bf16[384,384]{1,0:T(8,128)(2,1)S(1)} %get-tuple-element.75), channel_id=1, source_target_pairs={{0,1},{1,0},{2,3},{3,2},{4,5},{5,4},{6,7},{7,6},{8,9},{9,8},{10,11... | collective-permute-start | bytes 884744 | tf_op jit(solution)/shard_map/ppermute | solution.py:294
  91.7 22.0 %collective-permute-start.24 = (bf16[384,384]{1,0:T(8,128)(2,1)S(1)}, bf16[384,384]{1,0:T(8,128)(2,1)S(1)}, u32[]{:S(2)}, u32[]{:S(2)}) collective-permute-start(bf16[384,384]{1,0:T(8,128)(2,1)S(1)} %get-tuple-element.72), channel_id=1, source_target_pairs={{0,1},{1,0},{2,3},{3,2},{4,5},{5,4},{6,7},{7,6},{8,9},{9,8},{10,11... | collective-permute-start | bytes 884744 | tf_op jit(solution)/shard_map/ppermute | solution.py:294
  98.7 17.2 %collective-permute-start.13 = (bf16[384,384]{1,0:T(8,128)(2,1)S(1)}, bf16[384,384]{1,0:T(8,128)(2,1)S(1)}, u32[]{:S(2)}, u32[]{:S(2)}) collective-permute-start(bf16[384,384]{1,0:T(8,128)(2,1)S(1)} %get-tuple-element.62), channel_id=1, source_target_pairs={{0,1},{1,0},{2,3},{3,2},{4,5},{5,4},{6,7},{7,6},{8,9},{9,8},{10,11... | collective-permute-start | bytes 884744 | tf_op jit(solution)/shard_map/ppermute | solution.py:294
  99.8 19.0 %collective-permute-start.12 = (bf16[384,384]{1,0:T(8,128)(2,1)S(1)}, bf16[384,384]{1,0:T(8,128)(2,1)S(1)}, u32[]{:S(2)}, u32[]{:S(2)}) collective-permute-start(bf16[384,384]{1,0:T(8,128)(2,1)S(1)} %get-tuple-element.61), channel_id=1, source_target_pairs={{0,1},{1,0},{2,3},{3,2},{4,5},{5,4},{6,7},{7,6},{8,9},{9,8},{10,11... | collective-permute-start | bytes 884744 | tf_op jit(solution)/shard_map/ppermute | solution.py:294
  100.8 21.2 %collective-permute-start.11 = (bf16[384,384]{1,0:T(8,128)(2,1)S(1)}, bf16[384,384]{1,0:T(8,128)(2,1)S(1)}, u32[]{:S(2)}, u32[]{:S(2)}) collective-permute-start(bf16[384,384]{1,0:T(8,128)(2,1)S(1)} %get-tuple-element.58), channel_id=1, source_target_pairs={{0,1},{1,0},{2,3},{3,2},{4,5},{5,4},{6,7},{7,6},{8,9},{9,8},{10,11... | collective-permute-start | bytes 884744 | tf_op jit(solution)/shard_map/ppermute | solution.py:294
  (5 other events, 55.3 us)

commit v4 on v2

v4 whole, which is shorter than its diff:
```python
import functools

import jax
import jax.numpy as jnp
from jax import lax
from jax.experimental import pallas as pl
from jax.experimental.pallas import tpu as pltpu
from jax.sharding import PartitionSpec as P


F32 = jnp.float32
BF16 = jnp.bfloat16
VMEM = pl.BlockSpec(memory_space=pltpu.VMEM)
SMEM = pl.BlockSpec(memory_space=pltpu.SMEM)
HBM = pl.BlockSpec(memory_space=pltpu.HBM)
DMA = pltpu.SemaphoreType.DMA


def mm(a, b, dims):
    return lax.dot_general(a, b, (dims, ((), ())), preferred_element_type=F32)


def call(kernel, out, in_specs, out_specs, scratch=(), aliases=None):
    return pl.pallas_call(
        kernel,
        out_shape=out,
        in_specs=in_specs,
        out_specs=out_specs,
        scratch_shapes=list(scratch),
        input_output_aliases=aliases or {},
        compiler_params=pltpu.CompilerParams(vmem_limit_bytes=12 << 20),
    )


def row_chunks(rows):
    for size in (256, 384, 128):
        if rows % size == 0:
            return [pl.ds(first, size) for first in range(0, rows, size)]
    return [pl.ds(0, rows)]


def assemble(me, shards, gu_ref, down_ref):
    n = len(shards)
    width = down_ref.shape[0]
    part = width // n
    for r, shard in enumerate(shards):
        at = pl.multiple_of(lax.rem(me - r + n, n) * part, part)
        gu_ref[pl.ds(at, part), :] = shard(0)
        gu_ref[pl.ds(width + at, part), :] = shard(1)
        down_ref[pl.ds(at, part), :] = shard(2)


def grads_core(divisor, k_ref, v_ref, gu_ref, down_ref, own_gu, own_down, hid_s, dout_s, dgu_s):
    rows, width = k_ref.shape
    for at in row_chunks(rows):
        both = mm(k_ref[at, :], gu_ref[...], ((1,), (1,)))
        gate, upper = both[:, :width], both[:, width:]
        dout = (-v_ref[at, :].astype(F32) / divisor).astype(BF16)
        dhid = mm(dout, down_ref[...], ((1,), (0,)))
        sigma = jax.nn.sigmoid(gate)
        silu = gate * sigma
        hid_s[at, :] = (silu * upper).astype(BF16)
        dout_s[at, :] = dout
        dgu_s[at, :width] = (dhid * upper * sigma * (1.0 + gate * (1.0 - sigma))).astype(BF16)
        dgu_s[at, width:] = (dhid * silu).astype(BF16)
    own_gu[...] = mm(dgu_s[...], k_ref[...], ((0,), (0,)))
    own_down[...] = mm(dout_s[...], hid_s[...], ((0,), (0,)))


def take_head(head, fast_ref, own_ref):
    pltpu.sync_copy(fast_ref.at[0, :, head], own_ref)


def take_piece(sources, block_ref, begin_ref, piece_ref):
    block = block_ref[0]
    piece = jnp.int32(0)
    for p, source in enumerate(sources):
        piece = jnp.where(block == source, jnp.int32(p), piece)
    pltpu.sync_copy(begin_ref.at[piece], piece_ref)


def load_all(steps, heads, k_ref, v_ref, q_ref, m_ref, begin_ref, *refs):
    sems = refs[-1]
    copies = []

    def add(source, target):
        copies.append(pltpu.make_async_copy(source, target, sems.at[len(copies)]))
        copies[-1].start()

    targets = list(refs[:-1])
    for step in range(steps):
        for head in range(heads):
            for ref in (k_ref, v_ref, q_ref):
                target = targets.pop(0)
                width = target.shape[1]
                add(ref.at[step, :, pl.ds(head * width, width)], target)
    for head in range(heads):
        add(m_ref.at[0, :, head], targets.pop(0))
    for head in range(heads):
        add(begin_ref.at[:, head], targets.pop(0))
    for copy in copies:
        copy.wait()


def grads_one(n, head, divisor, tok_ref, decay_ref, k_ref, v_ref, m_ref, *refs):
    shards = refs[:n]
    gu_ref, down_ref, send_gu, send_down, own_gu, own_down, hid_s, dout_s, dgu_s = refs[n:]
    width = down_ref.shape[0]
    part = width // n
    me = tok_ref[0]
    assemble(me, [lambda m, ref=ref: ref[m] for ref in shards], gu_ref, down_ref)
    grads_core(divisor, k_ref, v_ref, gu_ref, down_ref, own_gu, own_down, hid_s, dout_s, dgu_s)
    decay = decay_ref[head]
    mine = pl.multiple_of(me * part, part)
    own_gu[pl.ds(mine, part), :] += decay * m_ref[0]
    own_gu[pl.ds(width + mine, part), :] += decay * m_ref[1]
    own_down[pl.ds(mine, part), :] += decay * m_ref[2]
    send_gu[...] = own_gu[...].astype(BF16)
    send_down[...] = own_down[...].astype(BF16)


def grads_two(n, head, divisor, tok_ref, block_ref, decay_ref, k_ref, v_ref, begin_ref, *refs):
    (pgu_ref, pdown_ref), pieces = refs[:2], refs[2 : 2 + 3 * (n - 1)]
    gu_ref, down_ref, send_gu, send_down, own_gu, own_down, hid_s, dout_s, dgu_s = refs[-9:]
    width = down_ref.shape[0]
    part = width // n
    me = tok_ref[0]
    leading = block_ref[0] == 0

    @pl.when(leading)
    def _():
        shards = [lambda m: begin_ref[m]]
        for r in range(n - 1):
            shards.append(lambda m, r=r: pieces[3 * r + m][head])
        assemble(me, shards, gu_ref, down_ref)

    @pl.when(jnp.logical_not(leading))
    def _():
        gu_ref[...] = pgu_ref[: 2 * width, :]
        down_ref[...] = pdown_ref[:width, :]

    grads_core(divisor, k_ref, v_ref, gu_ref, down_ref, own_gu, own_down, hid_s, dout_s, dgu_s)
    decay = decay_ref[head]
    mine = pl.multiple_of(me * part, part)

    @pl.when(jnp.logical_not(leading))
    def _():
        for m in range(2):
            old = pgu_ref[2 * width + m * part : 2 * width + (m + 1) * part, :]
            own_gu[pl.ds(m * width + mine, part), :] += decay * old.astype(F32)
        own_down[pl.ds(mine, part), :] += decay * pdown_ref[width:, :].astype(F32)

    send_gu[...] = own_gu[...].astype(BF16)
    send_down[...] = own_down[...].astype(BF16)


def updated(rate, old_ref, own_ref, recvs, first):
    width = own_ref.shape[1]
    at = pl.ds(first, width)
    moment = own_ref[at, :]
    for recv in recvs:
        moment = moment + recv[at, :].astype(F32)
    old = old_ref[at, :].astype(F32)
    moved = old - rate * moment
    old_norm = jnp.sqrt(jnp.mean(old * old, axis=1, keepdims=True) + 1e-06)
    new_norm = jnp.sqrt(jnp.mean(moved * moved, axis=1, keepdims=True) + 1e-06)
    return (moved * (old_norm / new_norm)).astype(BF16), moment


def update_one(n, head, mats, tok_ref, rate_ref, old_ref, own_ref, *refs):
    recvs = refs[: n - 1]
    pack_ref, moment_s = refs[n - 1 :]
    width = own_ref.shape[1]
    part = width // n
    total = len(mats) * width
    mine = pl.multiple_of(tok_ref[0] * part, part)
    for i, m in enumerate(mats):
        new, moment = updated(rate_ref[head, m], old_ref, own_ref, recvs, i * width)
        pack_ref[i * width : (i + 1) * width, :] = new
        moment_s[...] = moment
        held = slice(total + i * part, total + (i + 1) * part)
        pack_ref[held, :] = moment_s[pl.ds(mine, part), :].astype(BF16)


def store_mine(n, m, head, me, new_s, moment_s, fast_s, mine_s, fast_ref, moment_ref, sems):
    width = moment_s.shape[1]
    part = width // n
    mine = pl.multiple_of(me * part, part)
    fast_s[...] = new_s[pl.ds(mine, part), :]
    mine_s[...] = moment_s[pl.ds(mine, part), :]
    stores = [
        pltpu.make_async_copy(fast_s, fast_ref.at[0, m, head], sems.at[0]),
        pltpu.make_async_copy(mine_s, moment_ref.at[0, m, head], sems.at[1]),
    ]
    for store in stores:
        store.start()
    return stores


def update_two_gu(n, head, tok_ref, rate_ref, old_ref, own_ref, q_ref, *refs):
    recvs = refs[: n - 1]
    hq_ref, fast_ref, moment_ref, gu_s, moment_s, fast_s, mine_s, sems = refs[-8:]
    width = own_ref.shape[1]
    stores = []
    for m in range(2):
        new, moment = updated(rate_ref[head, m], old_ref, own_ref, recvs, m * width)
        new_s = gu_s.at[pl.ds(m * width, width), :]
        new_s[...] = new
        moment_s[...] = moment
        stores += store_mine(
            n,
            m,
            head,
            tok_ref[0],
            new_s,
            moment_s,
            fast_s.at[m],
            mine_s.at[m],
            fast_ref,
            moment_ref,
            sems.at[m],
        )
    for at in row_chunks(q_ref.shape[0]):
        both = mm(q_ref[at, :], gu_s[...], ((1,), (1,)))
        hq_ref[at, :] = (jax.nn.silu(both[:, :width]) * both[:, width:]).astype(BF16)
    for store in stores:
        store.wait()


def update_two_down(n, head, tok_ref, rate_ref, old_ref, own_ref, hq_ref, *refs):
    recvs = refs[: n - 1]
    out_ref, fast_ref, moment_ref, out_s, down_s, moment_s, fast_s, mine_s, out_sems, sems = refs[-10:]
    width = own_ref.shape[1]
    new, moment = updated(rate_ref[head, 2], old_ref, own_ref, recvs, 0)
    down_s[...] = new
    moment_s[...] = moment
    stores = store_mine(
        n, 2, head, tok_ref[0], down_s, moment_s, fast_s, mine_s, fast_ref, moment_ref, sems
    )
    for i, at in enumerate(row_chunks(hq_ref.shape[0])):
        out_s[at, :] = mm(hq_ref[at, :], down_s[...], ((1,), (1,))).astype(BF16)
        stores.append(
            pltpu.make_async_copy(
                out_s.at[at, :], out_ref.at[1, at, pl.ds(head * width, width)], out_sems.at[i]
            )
        )
        stores[-1].start()
    for store in stores:
        store.wait()


def apply_one(head, q_ref, pgu_ref, pdown_ref, *refs):
    out_ref, out_s, sems = refs[-3:]
    rows, width = q_ref.shape
    stores = []
    for i, at in enumerate(row_chunks(rows)):
        both = mm(q_ref[at, :], pgu_ref[: 2 * width, :], ((1,), (1,)))
        hq = (jax.nn.silu(both[:, :width]) * both[:, width:]).astype(BF16)
        out_s[at, :] = mm(hq, pdown_ref[:width, :], ((1,), (1,))).astype(BF16)
        stores.append(
            pltpu.make_async_copy(
                out_s.at[at, :], out_ref.at[0, at, pl.ds(head * width, width)], sems.at[i]
            )
        )
        stores[-1].start()
    for store in stores:
        store.wait()


def on_device(keys, values, queries, fast_in, moment_in, initial_fast, rates, decays):
    n = lax.axis_size("tok")
    blocks = lax.axis_size("block")
    steps, rows, features = keys.shape
    heads = rates.shape[1]
    width = features // heads
    part = width // n
    chunks = len(row_chunks(rows))
    divisor = float(rows * n)
    tok = lax.axis_index("tok").astype(jnp.int32).reshape(1)
    block = lax.axis_index("block").astype(jnp.int32).reshape(1)
    fast_t = jnp.swapaxes(fast_in, 3, 4)
    moment_t = jnp.swapaxes(moment_in, 3, 4)
    begin_t = jnp.swapaxes(initial_fast, 2, 3)
    rates = rates.T
    keys, values, queries, fast_t, moment_t, begin_t = (
        pltpu.with_memory_space_constraint(x, pltpu.HBM)
        for x in (keys, values, queries, fast_t, moment_t, begin_t)
    )

    def turned(x):
        return [lax.ppermute(x, "tok", [(i, (i + r) % n) for i in range(n)]) for r in range(1, n)]

    def forward(x):
        return lax.ppermute(x, "block", [(i, i + 1) for i in range(blocks - 1)])

    def shape(*dims, dtype=BF16):
        return jax.ShapeDtypeStruct(dims, dtype)

    row_scratch = pltpu.VMEM((rows, width), BF16)
    grad_scratch = (row_scratch, row_scratch, pltpu.VMEM((rows, 2 * width), BF16))
    grad_out = (
        shape(2 * width, width),
        shape(width, width),
        shape(2 * width, width),
        shape(width, width),
        shape(2 * width, width, dtype=F32),
        shape(width, width, dtype=F32),
    )

    recv_fast, owned = [], []
    for h in range(heads):
        owned.append(
            call(functools.partial(take_head, h), shape(3, part, width), [HBM], VMEM)(fast_t)
        )
        recv_fast.append(turned(owned[h]))

    sources = [(2 * (m + 1)) % blocks for m in range(3)]
    piece = call(
        functools.partial(take_piece, sources), shape(heads, part, width), [SMEM, HBM], VMEM
    )(block, begin_t)
    crossed = [
        lax.ppermute(
            piece,
            ("block", "tok"),
            [(s * n + i, s * n + (i + r) % n) for s in sorted(set(sources)) for i in range(n)],
        )
        for r in range(1, n)
    ]

    loaded = list(
        call(
            functools.partial(load_all, steps, heads),
            (shape(rows, width),) * (3 * steps * heads)
            + (shape(3, part, width, dtype=F32),) * heads
            + (shape(3, part, width),) * heads,
            [HBM] * 5,
            (VMEM,) * (3 * steps * heads + 2 * heads),
            (DMA((3 * steps * heads + 2 * heads,)),),
        )(keys, values, queries, moment_t, begin_t)
    )
    kvq = [[[loaded.pop(0) for _ in range(3)] for _ in range(heads)] for _ in range(steps)]
    m_own, begin_own = loaded[:heads], loaded[heads:]

    first = [
        call(
            functools.partial(grads_one, n, h, divisor),
            grad_out,
            [SMEM, SMEM] + [VMEM] * (3 + n),
            (VMEM,) * 6,
            grad_scratch,
        )(tok, decays, *kvq[0][h][:2], m_own[h], owned[h], *recv_fast[h])
        for h in range(heads)
    ]

    packs = []
    for h in range(heads):
        gu, down, send_gu, send_down, own_gu, own_down = first[h]
        recv_gu, recv_down = turned(send_gu), turned(send_down)
        packs.append(
            [
                call(
                    functools.partial(update_one, n, h, mats),
                    shape(len(mats) * (width + part), width),
                    [SMEM, SMEM] + [VMEM] * (1 + n),
                    VMEM,
                    (pltpu.VMEM((width, width), F32),),
                )(tok, rates, old, own, *recvs)
                for mats, old, own, recvs in (
                    ((0, 1), gu, own_gu, recv_gu), ((2,), down, own_down, recv_down)
                )
            ]
        )

    begins = []
    for m in range(3):
        begins.append(
            [
                lax.ppermute(
                    x, ("block", "tok"), [(sources[m] * n + i, i) for i in range(n)]
                )
                for x in crossed
            ]
        )

    second = []
    for h in range(heads):
        arrived = [forward(packs[h][0]), forward(packs[h][1])]
        pieces = [begins[m][r] for r in range(n - 1) for m in range(3)]
        second.append(
            call(
                functools.partial(grads_two, n, h, divisor),
                grad_out,
                [SMEM] * 3 + [VMEM] * (5 + 3 * (n - 1)),
                (VMEM,) * 6,
                grad_scratch,
            )(tok, block, decays, *kvq[1][h][:2], begin_own[h], *arrived, *pieces)
        )

    out_shape = jax.ShapeDtypeStruct(keys.shape, BF16)
    outputs = None
    for h in range(heads):
        prior = [] if outputs is None else [outputs]
        outputs = call(
            functools.partial(apply_one, h),
            out_shape,
            [VMEM] * 3 + [HBM] * len(prior),
            HBM,
            (row_scratch, DMA((chunks,))),
            aliases={3: 0} if prior else None,
        )(kvq[0][h][2], *packs[h], *prior)

    fast_shape = jax.ShapeDtypeStruct(fast_t.shape, BF16)
    moment_shape = jax.ShapeDtypeStruct(moment_t.shape, F32)
    ends = []
    for h in range(heads):
        gu, down, send_gu, send_down, own_gu, own_down = second[h]
        recv_gu, recv_down = turned(send_gu), turned(send_down)
        at = 4 + n
        hq, *ends = call(
            functools.partial(update_two_gu, n, h),
            (shape(rows, width), fast_shape, moment_shape),
            [SMEM, SMEM] + [VMEM] * (2 + n) + [HBM] * len(ends),
            (VMEM, HBM, HBM),
            (
                pltpu.VMEM((2 * width, width), BF16),
                pltpu.VMEM((width, width), F32),
                pltpu.VMEM((2, part, width), BF16),
                pltpu.VMEM((2, part, width), F32),
                DMA((2, 2)),
            ),
            aliases={at: 1, at + 1: 2} if ends else None,
        )(tok, rates, gu, own_gu, kvq[1][h][2], *recv_gu, *ends)
        outputs, *ends = call(
            functools.partial(update_two_down, n, h),
            (out_shape, fast_shape, moment_shape),
            [SMEM, SMEM] + [VMEM] * (2 + n) + [HBM] * 3,
            (HBM,) * 3,
            (
                row_scratch,
                pltpu.VMEM((width, width), BF16),
                pltpu.VMEM((width, width), F32),
                pltpu.VMEM((part, width), BF16),
                pltpu.VMEM((part, width), F32),
                DMA((chunks,)),
                DMA((2,)),
            ),
            aliases={at: 0, at + 1: 1, at + 2: 2},
        )(tok, rates, down, own_down, hq, *recv_down, outputs, *ends)
    return (outputs, jnp.swapaxes(ends[0], 3, 4), jnp.swapaxes(ends[1], 3, 4))


def solution(mesh):
    placed = (
        P(None, ("block", "tok"), None),
        P(None, ("block", "tok"), None),
        P(None, ("block", "tok"), None),
        P("block", None, None, None, "tok"),
        P("block", None, None, None, "tok"),
        P(None, None, None, "tok"),
        P(),
        P(),
    )
    step = jax.shard_map(
        on_device,
        mesh=mesh,
        in_specs=placed,
        out_specs=(
            P(None, ("block", "tok"), None),
            P("block", None, None, None, "tok"),
            P("block", None, None, None, "tok"),
        ),
        check_vma=False,
    )

    def run(*args):
        with jax.sharding.use_abstract_mesh(mesh.abstract_mesh):
            return step(*args)

    return run
```

time: 125 us -> 123 us (0.984)
  waiting for transfers between devices: 52.8 us -> 39.7 us
  starting transfers between devices: 24.1 us -> 30.5 us
  local copies, waits for them, and re-layouts: 6.14 us -> 11 us
    ppermute x11 -> x14, waiting for transfers between devices: 52.8 us -> 39.6 us  [the longest x10 32.3 us: turned(): lax.ppermute(x, 'tok', [(i, (i + r) % n) for i in range(n)])]
    unnamed x18 -> x70, local copies, waits for them, and re-layouts: 6.14 us -> 11 us
    ppermute x4, starting transfers between devices: 8.53 us -> 12.6 us  [forward(): return lax.ppermute(x, 'block', [(i, i + 1) for i in range(blocks - 1)])]
    ppermute x11 -> x14, starting transfers between devices: 15.6 us -> 17.9 us  [the longest x10 13.4 us: turned(): lax.ppermute(x, 'tok', [(i, (i + r) % n) for i in range(n)])]
    pallas_call x4, Pallas kernels: 6.73 us -> 4.83 us  [on_device(): call(functools.partial(update_one, n, h, mats), shape(len(mats) * (width...]
    pallas_call x6 -> x8, Pallas kernels: 16.2 us -> 18 us  [the longest x2 6.48 us: on_device(): call(functools.partial(grads_two, n, h, divisor), grad_out, [SMEM] * 3 +...]
  transfers between devices with their start and end apart: 15 -> 18, of which waited for: 7 -> 8; matrix products, arithmetic and copies ran while one was open for 0% -> 0% of each run, Pallas kernels for 31% -> 30%
where the time goes in v4:
time: 123 us; the launch traced here: 122 us
  Pallas kernels  40.1 us (33%)
  waiting for transfers between devices  39.7 us (32%)
  starting transfers between devices  30.5 us (25%)
  local copies, waits for them, and re-layouts  11 us (9%)
    ppermute x10, waiting for transfers between devices, turned(): lax.ppermute(x, 'tok', [(i, (i + r) % n) for i in range(n)])  32.3 us
    ppermute x10, starting transfers between devices, turned(): lax.ppermute(x, 'tok', [(i, (i + r) % n) for i in range(n)])  13.4 us
    ppermute x4, starting transfers between devices, forward(): return lax.ppermute(x, 'block', [(i, i + 1) for i in range(blocks - 1)])  12.6 us
    unnamed x70, local copies, waits for them, and re-layouts  11 us
    pallas_call x2, Pallas kernels, on_device(): call(functools.partial(grads_one, n, h, divisor), grad_out, [SMEM, SMEM]...  7.36 us
    ppermute x3, waiting for transfers between devices, on_device(): lax.ppermute(x, ('block', 'tok'), [(sources[m] * n + i, i) for i in range...  7.32 us
    pallas_call x2, Pallas kernels, on_device(): call(functools.partial(grads_two, n, h, divisor), grad_out, [SMEM] * 3 +...  6.48 us
    pallas_call x2, Pallas kernels, on_device(): call(functools.partial(update_two_gu, n, h), (shape(rows, width), fast_sh...  5.62 us
  transfers between devices with their start and end apart: 18, of which 8 were waited for; matrix products, arithmetic and copies ran while one was open for 0% of the time, Pallas kernels for 30%

profile of v4, /device:TPU:0, one launch (start us, length us, event | category | flops | bytes accessed | tf_op | source)
XLA Modules:
  0.0 122.5 jit_solution(16695456668282951071)
XLA Ops:
  1.6 3.0 %collective-permute-start.10 = (bf16[3,192,384]{2,1,0:T(8,128)(2,1)S(1)}, bf16[3,192,384]{2,1,0:T(8,128)(2,1)S(1)}, u32[]{:S(2)}, u32[]{:S(2)}) collective-permute-start(bf16[3,192,384]{2,1,0:T(8,128)(2,1)S(1)} %shard_map.110.refs_0_), channel_id=1, source_target_pairs={{0,1},{1,0},{2,3},{3,2},{4,5},{5,4},{6,7},{7,6},{8,9},{9,8},{10,11... | collective-permute-start | bytes 1327112 | tf_op jit(solution)/shard_map/ppermute | solution.py:291
  5.6 3.9 %shard_map.103 = (bf16[768,384]{1,0:T(8,128)(2,1)S(1)}, bf16[768,384]{1,0:T(8,128)(2,1)S(1)}, bf16[768,384]{1,0:T(8,128)(2,1)S(1)}, bf16[768,384]{1,0:T(8,128)(2...) custom-call(bf16[2,768,768]{2,1,0:T(8,128)(2,1)} %k_ref.1, ...), custom_call_target="tpu_custom_call" | custom-call | tf_op jit(solution)/shard_map/pallas_call | solution.py:331
  15.6 3.7 %shard_map.111 = (bf16[768,384]{1,0:T(8,128)(2,1)S(1)}, bf16[384,384]{1,0:T(8,128)(2,1)S(1)}, bf16[768,384]{1,0:T(8,128)(2,1)}, bf16[384,384]{1,0:T(8,128)(2,1)S...) custom-call(s32[1]{0:T(128)} %bitcast.tok_ref, f32[2]{0:T(128)S(1)} %copy-done.31, ...), custom_call_target="tpu_custom_call" | custom-call | tf_op jit(solution)/shard_map/pallas_call | solution.py:345
  20.1 2.0 %collective-permute-start.11 = (bf16[768,384]{1,0:T(8,128)(2,1)}, bf16[768,384]{1,0:T(8,128)(2,1)}, u32[]{:S(2)}, u32[]{:S(2)}) collective-permute-start(bf16[768,384]{1,0:T(8,128)(2,1)} %get-tuple-element.81), channel_id=1, source_target_pairs={{0,1},{1,0},{2,3},{3,2},{4,5},{5,4},{6,7},{7,6},{8,9},{9,8},{10,11... | collective-permute-start | bytes 1769480 | tf_op jit(solution)/shard_map/ppermute | solution.py:291
  22.2 2.9 %collective-permute-done.refs_1_ = bf16[3,192,384]{2,1,0:T(8,128)(2,1)S(1)} collective-permute-done((bf16[3,192,384]{2,1,0:T(8,128)(2,1)S(1)}, bf16[3,192,384]{2,1,0:T(8,128)(2,1)S(1)}, u32[]{:S(2)}, u32[]{:S(2)}) %collective-permute-start) | collective-permute-done | bytes 442400 | tf_op jit(solution)/shard_map/ppermute | solution.py:291
  26.9 3.7 %shard_map.105 = (bf16[768,384]{1,0:T(8,128)(2,1)S(1)}, bf16[384,384]{1,0:T(8,128)(2,1)S(1)}, bf16[768,384]{1,0:T(8,128)(2,1)}, bf16[384,384]{1,0:T(8,128)(2,1)S...) custom-call(s32[1]{0:T(128)} %bitcast.tok_ref, f32[2]{0:T(128)S(1)} %copy-done.31, ...), custom_call_target="tpu_custom_call" | custom-call | tf_op jit(solution)/shard_map/pallas_call | solution.py:345
  33.0 2.0 %collective-permute-start.1 = (bf16[768,384]{1,0:T(8,128)(2,1)}, bf16[768,384]{1,0:T(8,128)(2,1)S(1)}, u32[]{:S(2)}, u32[]{:S(2)}) collective-permute-start(bf16[768,384]{1,0:T(8,128)(2,1)} %get-tuple-element.63), channel_id=1, source_target_pairs={{0,1},{1,0},{2,3},{3,2},{4,5},{5,4},{6,7},{7,6},{8,9},{9,8},{10,11... | collective-permute-start | bytes 1769480 | tf_op jit(solution)/shard_map/ppermute | solution.py:291
  38.9 1.8 %shard_map.112.pgu_ref = bf16[1152,384]{1,0:T(8,128)(2,1)S(1)} custom-call(s32[1]{0:T(128)} %bitcast.tok_ref, f32[2,3]{1,0:T(2,128)S(1)} %bitcast.8, bf16[768,384]{1,0:T(8,128)(2,1)S(1)} %copy-done.5, f32[768,384]{1,0:T(8,128)S(1)} %get-tuple-element.80.own_ref, bf16[768,384]{1,0:T(8,128)(2,1)} %collective-permute-done.11.refs_0_), custom_call_target="tpu_custom_call" | custom-call | tf_op jit(solution)/shard_map/pallas_call | solution.py:361
  42.2 8.2 %collective-permute-done.1.refs_0_ = bf16[768,384]{1,0:T(8,128)(2,1)S(1)} collective-permute-done((bf16[768,384]{1,0:T(8,128)(2,1)}, bf16[768,384]{1,0:T(8,128)(2,1)S(1)}, u32[]{:S(2)}, u32[]{:S(2)}) %collective-permute-start.1) | collective-permute-done | bytes 589856 | tf_op jit(solution)/shard_map/ppermute | solution.py:291
  53.2 2.1 %collective-permute-start.3 = (bf16[384,384]{1,0:T(8,128)(2,1)S(1)}, bf16[384,384]{1,0:T(8,128)(2,1)S(1)}, u32[]{:S(2)}, u32[]{:S(2)}) collective-permute-start(bf16[384,384]{1,0:T(8,128)(2,1)S(1)} %copy-done.34), channel_id=1, source_target_pairs={{0,1},{1,0},{2,3},{3,2},{4,5},{5,4},{6,7},{7,6},{8,9},{9,8},{10,11... | collective-permute-start | bytes 884744 | tf_op jit(solution)/shard_map/ppermute | solution.py:291
  58.8 2.7 %collective-permute-done.3.refs_0_ = bf16[384,384]{1,0:T(8,128)(2,1)S(1)} collective-permute-done((bf16[384,384]{1,0:T(8,128)(2,1)S(1)}, bf16[384,384]{1,0:T(8,128)(2,1)S(1)}, u32[]{:S(2)}, u32[]{:S(2)}) %collective-permute-start.3) | collective-permute-done | bytes 294944 | tf_op jit(solution)/shard_map/ppermute | solution.py:291
  61.4 3.7 %collective-permute-start.14 = (bf16[576,384]{1,0:T(8,128)(2,1)S(1)}, bf16[576,384]{1,0:T(8,128)(2,1)S(1)}, u32[]{:S(2)}, u32[]{:S(2)}) collective-permute-start(bf16[576,384]{1,0:T(8,128)(2,1)S(1)} %shard_map.113.pdown_ref), channel_id=1, source_target_pairs={{0,2},{2,4},{4,6},{6,8},{8,10},{10,12},{12,14},{14,16},{16,18},{18... | collective-permute-start | bytes 1327112 | tf_op jit(solution)/shard_map/ppermute | solution.py:294
  66.1 5.9 %collective-permute-start.4 = (bf16[576,384]{1,0:T(8,128)(2,1)S(1)}, bf16[576,384]{1,0:T(8,128)(2,1)S(1)}, u32[]{:S(2)}, u32[]{:S(2)}) collective-permute-start(bf16[576,384]{1,0:T(8,128)(2,1)S(1)} %shard_map.107.pdown_ref), channel_id=1, source_target_pairs={{0,2},{2,4},{4,6},{6,8},{8,10},{10,12},{12,14},{14,16},{16,18},{18... | collective-permute-start | bytes 1327112 | tf_op jit(solution)/shard_map/ppermute | solution.py:294
  73.3 7.3 %collective-permute-done.6.refs_2_ = bf16[2,192,384]{2,1,0:T(8,128)(2,1)S(1)} collective-permute-done((bf16[2,192,384]{2,1,0:T(8,128)(2,1)S(1)}, bf16[2,192,384]{2,1,0:T(8,128)(2,1)S(1)}, u32[]{:S(2)}, u32[]{:S(2)}) %collective-permute-start.6) | collective-permute-done | bytes 294944 | tf_op jit(solution)/shard_map/ppermute | solution.py:378
  80.7 3.1 %shard_map.114 = (bf16[768,384]{1,0:T(8,128)(2,1)S(1)}, bf16[384,384]{1,0:T(8,128)(2,1)S(1)}, bf16[768,384]{1,0:T(8,128)(2,1)S(1)}, bf16[384,384]{1,0:T(8,128)(2...) custom-call(s32[1]{0:T(128)} %bitcast.tok_ref, s32[1]{0:T(128)} %bitcast.2.block_ref, f32[2]{0:T(128)S(1)} %copy-done.31, ...), custom_call_target="tpu_custom_call" | custom-call | tf_op jit(solution)/shard_map/pallas_call | solution.py:390
  85.4 3.3 %shard_map.109 = (bf16[768,384]{1,0:T(8,128)(2,1)S(1)}, bf16[384,384]{1,0:T(8,128)(2,1)S(1)}, bf16[768,384]{1,0:T(8,128)(2,1)S(1)}, bf16[384,384]{1,0:T(8,128)(2...) custom-call(s32[1]{0:T(128)} %bitcast.tok_ref, s32[1]{0:T(128)} %bitcast.2.block_ref, f32[2]{0:T(128)S(1)} %copy-done.31, ...), custom_call_target="tpu_custom_call" | custom-call | tf_op jit(solution)/shard_map/pallas_call | solution.py:390
  91.4 2.3 %shard_map.116.refs_0_ = bf16[2,768,768]{2,1,0:T(8,128)(2,1)} custom-call(bf16[768,384]{1,0:T(8,128)(2,1)S(1)} %copy-done.15, bf16[1152,384]{1,0:T(8,128)(2,1)S(1)} %shard_map.112.pgu_ref, bf16[576,384]{1,0:T(8,128)(2,1)S(1)} %shard_map.113.pdown_ref), custom_call_target="tpu_custom_call" | custom-call | tf_op jit(solution)/shard_map/pallas_call | solution.py:403
  93.7 2.3 %shard_map.117.refs_1_ = bf16[2,768,768]{2,1,0:T(8,128)(2,1)} custom-call(bf16[768,384]{1,0:T(8,128)(2,1)S(1)} %copy-done.3, bf16[1152,384]{1,0:T(8,128)(2,1)S(1)} %shard_map.106.pgu_ref, bf16[576,384]{1,0:T(8,128)(2,1)S(1)} %shard_map.107.pdown_ref, bf16[2,768,768]{2,1,0:T(8,128)(2,1)} %shard_map.116.refs_0_), custom_call_target="tpu_custom_call", output_to_operand_aliasing={{}: (3, {})} | custom-call | tf_op jit(solution)/shard_map/pallas_call | solution.py:403
  96.0 4.1 %collective-permute-done.15.refs_0_ = bf16[768,384]{1,0:T(8,128)(2,1)S(1)} collective-permute-done((bf16[768,384]{1,0:T(8,128)(2,1)S(1)}, bf16[768,384]{1,0:T(8,128)(2,1)S(1)}, u32[]{:S(2)}, u32[]{:S(2)}) %collective-permute-start.15) | collective-permute-done | bytes 589856 | tf_op jit(solution)/shard_map/ppermute | solution.py:291
  100.1 2.8 %shard_map.115 = (bf16[768,384]{1,0:T(8,128)(2,1)S(1)}, bf16[1,3,2,192,384]{4,3,2,1,0:T(8,128)(2,1)}, f32[1,3,2,192,384]{4,3,2,1,0:T(8,128)}) custom-call(s32[1]{0:T(128)} %bitcast.tok_ref, f32[2,3]{1,0:T(2,128)S(1)} %bitcast.12, bf16[768,384]{1,0:T(8,128)(2,1)S(1)} %get-tuple-element.87.old_ref, f32[768,384]{1,0:T(8,128)S(1)} %get-tuple-element.88.own_ref, ...), custom_call_target="tpu_custom_call" | custom-call | tf_op jit(solution)/shard_map/pallas_call | solution.py:419
  102.9 12.2 %collective-permute-done.16.refs_0_ = bf16[384,384]{1,0:T(8,128)(2,1)S(1)} collective-permute-done((bf16[384,384]{1,0:T(8,128)(2,1)S(1)}, bf16[384,384]{1,0:T(8,128)(2,1)S(1)}, u32[]{:S(2)}, u32[]{:S(2)}) %collective-permute-start.16) | collective-permute-done | bytes 294944 | tf_op jit(solution)/shard_map/ppermute | solution.py:291
  115.1 2.2 %shard_map.118 = (bf16[2,768,768]{2,1,0:T(8,128)(2,1)}, bf16[1,3,2,192,384]{4,3,2,1,0:T(8,128)(2,1)}, f32[1,3,2,192,384]{4,3,2,1,0:T(8,128)}) custom-call(s32[1]{0:T(128)} %bitcast.tok_ref, f32[2,3]{1,0:T(2,128)S(1)} %bitcast.13, bf16[384,384]{1,0:T(8,128)(2,1)S(1)} %get-tuple-element.85.old_ref, ...), custom_call_target="tpu_custom_call", output_to_operand_aliasing={{0}: (6, {}), {1}: (7, {}), {2}: (8, {})} | custom-call | tf_op jit(solution)/shard_map/pallas_call | solution.py:433
  117.3 2.8 %shard_map.119 = (bf16[768,384]{1,0:T(8,128)(2,1)S(1)}, bf16[1,3,2,192,384]{4,3,2,1,0:T(8,128)(2,1)}, f32[1,3,2,192,384]{4,3,2,1,0:T(8,128)}) custom-call(s32[1]{0:T(128)} %bitcast.tok_ref, f32[2,3]{1,0:T(2,128)S(1)} %bitcast.14, bf16[768,384]{1,0:T(8,128)(2,1)S(1)} %get-tuple-element.69.old_ref, ...), custom_call_target="tpu_custom_call", output_to_operand_aliasing={{1}: (6, {}), {2}: (7, {})} | custom-call | tf_op jit(solution)/shard_map/pallas_call | solution.py:419
  120.1 2.2 %shard_map.120 = (bf16[2,768,768]{2,1,0:T(8,128)(2,1)}, bf16[1,3,2,192,384]{4,3,2,1,0:T(8,128)(2,1)}, f32[1,3,2,192,384]{4,3,2,1,0:T(8,128)}) custom-call(s32[1]{0:T(128)} %bitcast.tok_ref, f32[2,3]{1,0:T(2,128)S(1)} %bitcast.15, bf16[384,384]{1,0:T(8,128)(2,1)S(1)} %get-tuple-element.67.old_ref, ...), custom_call_target="tpu_custom_call", output_to_operand_aliasing={{0}: (6, {}), {1}: (7, {}), {2}: (8, {})} | custom-call | tf_op jit(solution)/shard_map/pallas_call | solution.py:433
  (100 shorter events, 31.1 us)
Async XLA Ops:
  1.6 14.0 %collective-permute-start.10 = (bf16[3,192,384]{2,1,0:T(8,128)(2,1)S(1)}, bf16[3,192,384]{2,1,0:T(8,128)(2,1)S(1)}, u32[]{:S(2)}, u32[]{:S(2)}) collective-permute-start(bf16[3,192,384]{2,1,0:T(8,128)(2,1)S(1)} %shard_map.110.refs_0_), channel_id=1, source_target_pairs={{0,1},{1,0},{2,3},{3,2},{4,5},{5,4},{6,7},{7,6},{8,9},{9,8},{10,11... | collective-permute-start | bytes 1327112 | tf_op jit(solution)/shard_map/ppermute | solution.py:291
  5.6 19.5 %collective-permute-start = (bf16[3,192,384]{2,1,0:T(8,128)(2,1)S(1)}, bf16[3,192,384]{2,1,0:T(8,128)(2,1)S(1)}, u32[]{:S(2)}, u32[]{:S(2)}) collective-permute-start(bf16[3,192,384]{2,1,0:T(8,128)(2,1)S(1)} %shard_map.104.refs_0_), channel_id=1, source_target_pairs={{0,1},{1,0},{2,3},{3,2},{4,5},{5,4},{6,7},{7,6},{8,9},{9,8},{10,11... | collective-permute-start | bytes 1327112 | tf_op jit(solution)/shard_map/ppermute | solution.py:291
  14.5 16.1 %copy-start.24 = (bf16[3,192,384]{2,1,0:T(8,128)(2,1)}, bf16[3,192,384]{2,1,0:T(8,128)(2,1)S(1)}, u32[]{:S(2)}) copy-start(bf16[3,192,384]{2,1,0:T(8,128)(2,1)S(1)} %get-tuple-element.57.begin_ref) | copy-start | bytes 1327108
  14.5 16.1 %copy-start.26 = (bf16[3,192,384]{2,1,0:T(8,128)(2,1)}, bf16[3,192,384]{2,1,0:T(8,128)(2,1)S(1)}, u32[]{:S(2)}) copy-start(bf16[3,192,384]{2,1,0:T(8,128)(2,1)S(1)} %get-tuple-element.75.begin_ref) | copy-start | bytes 1327108
  20.1 17.7 %collective-permute-start.11 = (bf16[768,384]{1,0:T(8,128)(2,1)}, bf16[768,384]{1,0:T(8,128)(2,1)}, u32[]{:S(2)}, u32[]{:S(2)}) collective-permute-start(bf16[768,384]{1,0:T(8,128)(2,1)} %get-tuple-element.81), channel_id=1, source_target_pairs={{0,1},{1,0},{2,3},{3,2},{4,5},{5,4},{6,7},{7,6},{8,9},{9,8},{10,11... | collective-permute-start | bytes 1769480 | tf_op jit(solution)/shard_map/ppermute | solution.py:291
  33.0 17.4 %collective-permute-start.1 = (bf16[768,384]{1,0:T(8,128)(2,1)}, bf16[768,384]{1,0:T(8,128)(2,1)S(1)}, u32[]{:S(2)}, u32[]{:S(2)}) collective-permute-start(bf16[768,384]{1,0:T(8,128)(2,1)} %get-tuple-element.63), channel_id=1, source_target_pairs={{0,1},{1,0},{2,3},{3,2},{4,5},{5,4},{6,7},{7,6},{8,9},{9,8},{10,11... | collective-permute-start | bytes 1769480 | tf_op jit(solution)/shard_map/ppermute | solution.py:291
  36.0 19.2 %collective-permute-start.5 = (bf16[2,192,384]{2,1,0:T(8,128)(2,1)S(1)}, bf16[2,192,384]{2,1,0:T(8,128)(2,1)S(1)}, u32[]{:S(2)}, u32[]{:S(2)}) collective-permute-start(bf16[2,192,384]{2,1,0:T(8,128)(2,1)S(1)} %shard_map.108), channel_id=1, source_target_pairs={{4,5},{5,4},{8,9},{9,8},{12,13},{13,12}} | collective-permute-start | bytes 884744 | tf_op jit(solution)/shard_map/ppermute | solution.py:322
  36.7 19.8 %collective-permute-start.13 = (bf16[384,384]{1,0:T(8,128)(2,1)}, bf16[384,384]{1,0:T(8,128)(2,1)S(1)}, u32[]{:S(2)}, u32[]{:S(2)}) collective-permute-start(bf16[384,384]{1,0:T(8,128)(2,1)} %copy-done.32), channel_id=1, source_target_pairs={{0,1},{1,0},{2,3},{3,2},{4,5},{5,4},{6,7},{7,6},{8,9},{9,8},{10,11... | collective-permute-start | bytes 884744 | tf_op jit(solution)/shard_map/ppermute | solution.py:291
  40.7 17.2 %copy-start.9 = (f32[384,384]{1,0:T(8,128)S(1)}, f32[384,384]{1,0:T(8,128)}, u32[]{:S(2)}) copy-start(f32[384,384]{1,0:T(8,128)} %copy-done.8) | copy-start | bytes 1769476
  40.7 39.9 %collective-permute-start.12 = (bf16[1152,384]{1,0:T(8,128)(2,1)S(1)}, bf16[1152,384]{1,0:T(8,128)(2,1)S(1)}, u32[]{:S(2)}, u32[]{:S(2)}) collective-permute-start(bf16[1152,384]{1,0:T(8,128)(2,1)S(1)} %shard_map.112.pgu_ref), channel_id=1, source_target_pairs={{0,2},{2,4},{4,6},{6,8},{8,10},{10,12},{12,14},{14,16},{16,18},{18... | collective-permute-start | bytes 2654216 | tf_op jit(solution)/shard_map/ppermute | solution.py:294
  51.7 29.0 %copy-start.21 = (bf16[768,384]{1,0:T(8,128)(2,1)S(1)}, bf16[768,384]{1,0:T(8,128)(2,1)}, u32[]{:S(2)}) copy-start(bf16[768,384]{1,0:T(8,128)(2,1)} %copy-done.20) | copy-start | bytes 1769476
  51.7 29.0 %copy-start.23 = (bf16[768,384]{1,0:T(8,128)(2,1)S(1)}, bf16[768,384]{1,0:T(8,128)(2,1)}, u32[]{:S(2)}) copy-start(bf16[768,384]{1,0:T(8,128)(2,1)} %copy-done.22) | copy-start | bytes 1769476
  51.7 29.0 %copy-start.27 = (bf16[3,192,384]{2,1,0:T(8,128)(2,1)S(1)}, bf16[3,192,384]{2,1,0:T(8,128)(2,1)}, u32[]{:S(2)}) copy-start(bf16[3,192,384]{2,1,0:T(8,128)(2,1)} %copy-done.26) | copy-start | bytes 1327108
  51.7 33.7 %collective-permute-start.2 = (bf16[1152,384]{1,0:T(8,128)(2,1)S(1)}, bf16[1152,384]{1,0:T(8,128)(2,1)S(1)}, u32[]{:S(2)}, u32[]{:S(2)}) collective-permute-start(bf16[1152,384]{1,0:T(8,128)(2,1)S(1)} %shard_map.106.pgu_ref), channel_id=1, source_target_pairs={{0,2},{2,4},{4,6},{6,8},{8,10},{10,12},{12,14},{14,16},{16,18},{18... | collective-permute-start | bytes 2654216 | tf_op jit(solution)/shard_map/ppermute | solution.py:294
  53.2 8.3 %collective-permute-start.3 = (bf16[384,384]{1,0:T(8,128)(2,1)S(1)}, bf16[384,384]{1,0:T(8,128)(2,1)S(1)}, u32[]{:S(2)}, u32[]{:S(2)}) collective-permute-start(bf16[384,384]{1,0:T(8,128)(2,1)S(1)} %copy-done.34), channel_id=1, source_target_pairs={{0,1},{1,0},{2,3},{3,2},{4,5},{5,4},{6,7},{7,6},{8,9},{9,8},{10,11... | collective-permute-start | bytes 884744 | tf_op jit(solution)/shard_map/ppermute | solution.py:291
  55.3 10.8 %collective-permute-start.8 = (bf16[2,192,384]{2,1,0:T(8,128)(2,1)S(1)}, bf16[2,192,384]{2,1,0:T(8,128)(2,1)S(1)}, u32[]{:S(2)}, u32[]{:S(2)}) collective-permute-start(bf16[2,192,384]{2,1,0:T(8,128)(2,1)S(1)} %collective-permute-done.5), channel_id=1, source_target_pairs={{12,0},{13,1}} | collective-permute-start | bytes 884744 | tf_op jit(solution)/shard_map/ppermute | solution.py:378
  56.6 15.4 %collective-permute-start.7 = (bf16[2,192,384]{2,1,0:T(8,128)(2,1)S(1)}, bf16[2,192,384]{2,1,0:T(8,128)(2,1)S(1)}, u32[]{:S(2)}, u32[]{:S(2)}) collective-permute-start(bf16[2,192,384]{2,1,0:T(8,128)(2,1)S(1)} %collective-permute-done.5), channel_id=1, source_target_pairs={{8,0},{9,1}} | collective-permute-start | bytes 884744 | tf_op jit(solution)/shard_map/ppermute | solution.py:378
  61.4 19.2 %collective-permute-start.14 = (bf16[576,384]{1,0:T(8,128)(2,1)S(1)}, bf16[576,384]{1,0:T(8,128)(2,1)S(1)}, u32[]{:S(2)}, u32[]{:S(2)}) collective-permute-start(bf16[576,384]{1,0:T(8,128)(2,1)S(1)} %shard_map.113.pdown_ref), channel_id=1, source_target_pairs={{0,2},{2,4},{4,6},{6,8},{8,10},{10,12},{12,14},{14,16},{16,18},{18... | collective-permute-start | bytes 1327112 | tf_op jit(solution)/shard_map/ppermute | solution.py:294
  66.1 19.3 %collective-permute-start.4 = (bf16[576,384]{1,0:T(8,128)(2,1)S(1)}, bf16[576,384]{1,0:T(8,128)(2,1)S(1)}, u32[]{:S(2)}, u32[]{:S(2)}) collective-permute-start(bf16[576,384]{1,0:T(8,128)(2,1)S(1)} %shard_map.107.pdown_ref), channel_id=1, source_target_pairs={{0,2},{2,4},{4,6},{6,8},{8,10},{10,12},{12,14},{14,16},{16,18},{18... | collective-permute-start | bytes 1327112 | tf_op jit(solution)/shard_map/ppermute | solution.py:294
  72.0 8.6 %collective-permute-start.6 = (bf16[2,192,384]{2,1,0:T(8,128)(2,1)S(1)}, bf16[2,192,384]{2,1,0:T(8,128)(2,1)S(1)}, u32[]{:S(2)}, u32[]{:S(2)}) collective-permute-start(bf16[2,192,384]{2,1,0:T(8,128)(2,1)S(1)} %collective-permute-done.5), channel_id=1, source_target_pairs={{4,0},{5,1}} | collective-permute-start | bytes 884744 | tf_op jit(solution)/shard_map/ppermute | solution.py:378
  83.8 16.3 %collective-permute-start.15 = (bf16[768,384]{1,0:T(8,128)(2,1)S(1)}, bf16[768,384]{1,0:T(8,128)(2,1)S(1)}, u32[]{:S(2)}, u32[]{:S(2)}) collective-permute-start(bf16[768,384]{1,0:T(8,128)(2,1)S(1)} %get-tuple-element.90), channel_id=1, source_target_pairs={{0,1},{1,0},{2,3},{3,2},{4,5},{5,4},{6,7},{7,6},{8,9},{9,8},{10,11... | collective-permute-start | bytes 1769480 | tf_op jit(solution)/shard_map/ppermute | solution.py:291
  88.8 28.5 %collective-permute-start.9 = (bf16[768,384]{1,0:T(8,128)(2,1)S(1)}, bf16[768,384]{1,0:T(8,128)(2,1)S(1)}, u32[]{:S(2)}, u32[]{:S(2)}) collective-permute-start(bf16[768,384]{1,0:T(8,128)(2,1)S(1)} %get-tuple-element.72), channel_id=1, source_target_pairs={{0,1},{1,0},{2,3},{3,2},{4,5},{5,4},{6,7},{7,6},{8,9},{9,8},{10,11... | collective-permute-start | bytes 1769480 | tf_op jit(solution)/shard_map/ppermute | solution.py:291
  89.4 25.7 %collective-permute-start.16 = (bf16[384,384]{1,0:T(8,128)(2,1)S(1)}, bf16[384,384]{1,0:T(8,128)(2,1)S(1)}, u32[]{:S(2)}, u32[]{:S(2)}) collective-permute-start(bf16[384,384]{1,0:T(8,128)(2,1)S(1)} %get-tuple-element.92), channel_id=1, source_target_pairs={{0,1},{1,0},{2,3},{3,2},{4,5},{5,4},{6,7},{7,6},{8,9},{9,8},{10,11... | collective-permute-start | bytes 884744 | tf_op jit(solution)/shard_map/ppermute | solution.py:291
  90.9 29.3 %collective-permute-start.17 = (bf16[384,384]{1,0:T(8,128)(2,1)S(1)}, bf16[384,384]{1,0:T(8,128)(2,1)S(1)}, u32[]{:S(2)}, u32[]{:S(2)}) collective-permute-start(bf16[384,384]{1,0:T(8,128)(2,1)S(1)} %get-tuple-element.100), channel_id=1, source_target_pairs={{0,1},{1,0},{2,3},{3,2},{4,5},{5,4},{6,7},{7,6},{8,9},{9,8},{10,11... | collective-permute-start | bytes 884744 | tf_op jit(solution)/shard_map/ppermute | solution.py:291
  (29 other events, 154.1 us)

commit v5 on v4

--- a/solution.py
+++ b/solution.py
@@ -71,12 +71,12 @@
     pltpu.sync_copy(fast_ref.at[0, :, head], own_ref)
 
 
-def take_piece(sources, block_ref, begin_ref, piece_ref):
-    block = block_ref[0]
+def take_piece(sources, begin_ref, piece_ref):
+    block = lax.axis_index("block")
     piece = jnp.int32(0)
     for p, source in enumerate(sources):
         piece = jnp.where(block == source, jnp.int32(p), piece)
-    pltpu.sync_copy(begin_ref.at[piece], piece_ref)
+    pltpu.sync_copy(begin_ref.at[lax.rem(piece, 3), piece // 3], piece_ref)
 
 
 def load_all(steps, heads, k_ref, v_ref, q_ref, m_ref, begin_ref, *refs):
@@ -102,12 +102,12 @@
         copy.wait()
 
 
-def grads_one(n, head, divisor, tok_ref, decay_ref, k_ref, v_ref, m_ref, *refs):
+def grads_one(n, head, divisor, decay_ref, k_ref, v_ref, m_ref, *refs):
     shards = refs[:n]
     gu_ref, down_ref, send_gu, send_down, own_gu, own_down, hid_s, dout_s, dgu_s = refs[n:]
     width = down_ref.shape[0]
     part = width // n
-    me = tok_ref[0]
+    me = lax.axis_index("tok")
     assemble(me, [lambda m, ref=ref: ref[m] for ref in shards], gu_ref, down_ref)
     grads_core(divisor, k_ref, v_ref, gu_ref, down_ref, own_gu, own_down, hid_s, dout_s, dgu_s)
     decay = decay_ref[head]
@@ -119,47 +119,32 @@
     send_down[...] = own_down[...].astype(BF16)
 
 
-def grads_two(n, head, divisor, tok_ref, block_ref, decay_ref, k_ref, v_ref, begin_ref, *refs):
+def grads_two(n, divisor, k_ref, v_ref, begin_ref, *refs):
     (pgu_ref, pdown_ref), pieces = refs[:2], refs[2 : 2 + 3 * (n - 1)]
     gu_ref, down_ref, send_gu, send_down, own_gu, own_down, hid_s, dout_s, dgu_s = refs[-9:]
-    width = down_ref.shape[0]
-    part = width // n
-    me = tok_ref[0]
-    leading = block_ref[0] == 0
+    leading = lax.axis_index("block") == 0
 
     @pl.when(leading)
     def _():
         shards = [lambda m: begin_ref[m]]
         for r in range(n - 1):
-            shards.append(lambda m, r=r: pieces[3 * r + m][head])
-        assemble(me, shards, gu_ref, down_ref)
+            shards.append(lambda m, r=r: pieces[3 * r + m][...])
+        assemble(lax.axis_index("tok"), shards, gu_ref, down_ref)
 
     @pl.when(jnp.logical_not(leading))
     def _():
-        gu_ref[...] = pgu_ref[: 2 * width, :]
-        down_ref[...] = pdown_ref[:width, :]
+        gu_ref[...] = pgu_ref[...]
+        down_ref[...] = pdown_ref[...]
 
     grads_core(divisor, k_ref, v_ref, gu_ref, down_ref, own_gu, own_down, hid_s, dout_s, dgu_s)
-    decay = decay_ref[head]
-    mine = pl.multiple_of(me * part, part)
-
-    @pl.when(jnp.logical_not(leading))
-    def _():
-        for m in range(2):
-            old = pgu_ref[2 * width + m * part : 2 * width + (m + 1) * part, :]
-            own_gu[pl.ds(m * width + mine, part), :] += decay * old.astype(F32)
-        own_down[pl.ds(mine, part), :] += decay * pdown_ref[width:, :].astype(F32)
-
     send_gu[...] = own_gu[...].astype(BF16)
     send_down[...] = own_down[...].astype(BF16)
 
 
-def updated(rate, old_ref, own_ref, recvs, first):
-    width = own_ref.shape[1]
+def updated(rate, old_ref, moments, first):
+    width = old_ref.shape[1]
     at = pl.ds(first, width)
-    moment = own_ref[at, :]
-    for recv in recvs:
-        moment = moment + recv[at, :].astype(F32)
+    moment = moments(at)
     old = old_ref[at, :].astype(F32)
     moved = old - rate * moment
     old_norm = jnp.sqrt(jnp.mean(old * old, axis=1, keepdims=True) + 1e-06)
@@ -167,19 +152,34 @@
     return (moved * (old_norm / new_norm)).astype(BF16), moment
 
 
-def update_one(n, head, mats, tok_ref, rate_ref, old_ref, own_ref, *refs):
+def summed(own_ref, recvs, at):
+    total = own_ref[at, :]
+    for recv in recvs:
+        total = total + recv[at, :].astype(F32)
+    return total
+
+
+def update_one(n, head, mats, rate_ref, old_ref, own_ref, *refs):
     recvs = refs[: n - 1]
-    pack_ref, moment_s = refs[n - 1 :]
+    new_ref, moment_ref = refs[-2:]
     width = own_ref.shape[1]
-    part = width // n
-    total = len(mats) * width
-    mine = pl.multiple_of(tok_ref[0] * part, part)
     for i, m in enumerate(mats):
-        new, moment = updated(rate_ref[head, m], old_ref, own_ref, recvs, i * width)
-        pack_ref[i * width : (i + 1) * width, :] = new
-        moment_s[...] = moment
-        held = slice(total + i * part, total + (i + 1) * part)
-        pack_ref[held, :] = moment_s[pl.ds(mine, part), :].astype(BF16)
+        at = slice(i * width, (i + 1) * width)
+        new, moment = updated(
+            rate_ref[head, m], old_ref, lambda at: summed(own_ref, recvs, at), i * width
+        )
+        new_ref[at, :] = new
+        moment_ref[m * width : (m + 1) * width, :] = moment.astype(BF16)
+
+
+def later_moment(decay, m, earlier_ref, own_ref, recvs):
+    width = earlier_ref.shape[1]
+
+    def moment(at):
+        earlier = earlier_ref[m * width : (m + 1) * width, :].astype(F32)
+        return decay * earlier + summed(own_ref, recvs, at)
+
+    return moment
 
 
 def store_mine(n, m, head, me, new_s, moment_s, fast_s, mine_s, fast_ref, moment_ref, sems):
@@ -197,13 +197,14 @@
     return stores
 
 
-def update_two_gu(n, head, tok_ref, rate_ref, old_ref, own_ref, q_ref, *refs):
+def update_two_gu(n, head, rate_ref, decay_ref, old_ref, own_ref, earlier_ref, q_ref, *refs):
     recvs = refs[: n - 1]
     hq_ref, fast_ref, moment_ref, gu_s, moment_s, fast_s, mine_s, sems = refs[-8:]
     width = own_ref.shape[1]
     stores = []
     for m in range(2):
-        new, moment = updated(rate_ref[head, m], old_ref, own_ref, recvs, m * width)
+        moments = later_moment(decay_ref[head], m, earlier_ref, own_ref, recvs)
+        new, moment = updated(rate_ref[head, m], old_ref, moments, m * width)
         new_s = gu_s.at[pl.ds(m * width, width), :]
         new_s[...] = new
         moment_s[...] = moment
@@ -211,7 +212,7 @@
             n,
             m,
             head,
-            tok_ref[0],
+            lax.axis_index("tok"),
             new_s,
             moment_s,
             fast_s.at[m],
@@ -227,15 +228,16 @@
         store.wait()
 
 
-def update_two_down(n, head, tok_ref, rate_ref, old_ref, own_ref, hq_ref, *refs):
+def update_two_down(n, head, rate_ref, decay_ref, old_ref, own_ref, earlier_ref, hq_ref, *refs):
     recvs = refs[: n - 1]
     out_ref, fast_ref, moment_ref, out_s, down_s, moment_s, fast_s, mine_s, out_sems, sems = refs[-10:]
     width = own_ref.shape[1]
-    new, moment = updated(rate_ref[head, 2], old_ref, own_ref, recvs, 0)
+    moments = later_moment(decay_ref[head], 2, earlier_ref, own_ref, recvs)
+    new, moment = updated(rate_ref[head, 2], old_ref, moments, 0)
     down_s[...] = new
     moment_s[...] = moment
     stores = store_mine(
-        n, 2, head, tok_ref[0], down_s, moment_s, fast_s, mine_s, fast_ref, moment_ref, sems
+        n, 2, head, lax.axis_index("tok"), down_s, moment_s, fast_s, mine_s, fast_ref, moment_ref, sems
     )
     for i, at in enumerate(row_chunks(hq_ref.shape[0])):
         out_s[at, :] = mm(hq_ref[at, :], down_s[...], ((1,), (1,))).astype(BF16)
@@ -254,9 +256,9 @@
     rows, width = q_ref.shape
     stores = []
     for i, at in enumerate(row_chunks(rows)):
-        both = mm(q_ref[at, :], pgu_ref[: 2 * width, :], ((1,), (1,)))
+        both = mm(q_ref[at, :], pgu_ref[...], ((1,), (1,)))
         hq = (jax.nn.silu(both[:, :width]) * both[:, width:]).astype(BF16)
-        out_s[at, :] = mm(hq, pdown_ref[:width, :], ((1,), (1,))).astype(BF16)
+        out_s[at, :] = mm(hq, pdown_ref[...], ((1,), (1,))).astype(BF16)
         stores.append(
             pltpu.make_async_copy(
                 out_s.at[at, :], out_ref.at[0, at, pl.ds(head * width, width)], sems.at[i]
@@ -276,8 +278,6 @@
     part = width // n
     chunks = len(row_chunks(rows))
     divisor = float(rows * n)
-    tok = lax.axis_index("tok").astype(jnp.int32).reshape(1)
-    block = lax.axis_index("block").astype(jnp.int32).reshape(1)
     fast_t = jnp.swapaxes(fast_in, 3, 4)
     moment_t = jnp.swapaxes(moment_in, 3, 4)
     begin_t = jnp.swapaxes(initial_fast, 2, 3)
@@ -314,10 +314,8 @@
         )
         recv_fast.append(turned(owned[h]))
 
-    sources = [(2 * (m + 1)) % blocks for m in range(3)]
-    piece = call(
-        functools.partial(take_piece, sources), shape(heads, part, width), [SMEM, HBM], VMEM
-    )(block, begin_t)
+    sources = [(2 * (p + 1)) % blocks for p in range(3 * heads)]
+    piece = call(functools.partial(take_piece, sources), shape(part, width), [HBM], VMEM)(begin_t)
     crossed = [
         lax.ppermute(
             piece,
@@ -345,38 +343,38 @@
         call(
             functools.partial(grads_one, n, h, divisor),
             grad_out,
-            [SMEM, SMEM] + [VMEM] * (3 + n),
+            [SMEM] + [VMEM] * (3 + n),
             (VMEM,) * 6,
             grad_scratch,
-        )(tok, decays, *kvq[0][h][:2], m_own[h], owned[h], *recv_fast[h])
+        )(decays, *kvq[0][h][:2], m_own[h], owned[h], *recv_fast[h])
         for h in range(heads)
     ]
 
-    packs = []
+    packs, moments = [], []
     for h in range(heads):
         gu, down, send_gu, send_down, own_gu, own_down = first[h]
         recv_gu, recv_down = turned(send_gu), turned(send_down)
-        packs.append(
-            [
-                call(
-                    functools.partial(update_one, n, h, mats),
-                    shape(len(mats) * (width + part), width),
-                    [SMEM, SMEM] + [VMEM] * (1 + n),
-                    VMEM,
-                    (pltpu.VMEM((width, width), F32),),
-                )(tok, rates, old, own, *recvs)
-                for mats, old, own, recvs in (
-                    ((0, 1), gu, own_gu, recv_gu), ((2,), down, own_down, recv_down)
-                )
-            ]
-        )
+        pack, moment = [], []
+        for mats, old, own, recvs in (
+            ((0, 1), gu, own_gu, recv_gu), ((2,), down, own_down, recv_down)
+        ):
+            new, *moment = call(
+                functools.partial(update_one, n, h, mats),
+                (shape(len(mats) * width, width), shape(3 * width, width)),
+                [SMEM] + [VMEM] * (1 + n + len(moment)),
+                (VMEM, VMEM),
+                aliases={2 + n: 1} if moment else None,
+            )(rates, old, own, *recvs, *moment)
+            pack.append(new)
+        packs.append(pack)
+        moments.append(forward(moment[0]))
 
     begins = []
-    for m in range(3):
+    for p in range(3 * heads):
         begins.append(
             [
                 lax.ppermute(
-                    x, ("block", "tok"), [(sources[m] * n + i, i) for i in range(n)]
+                    x, ("block", "tok"), [(sources[p] * n + i, i) for i in range(n)]
                 )
                 for x in crossed
             ]
@@ -385,15 +383,15 @@
     second = []
     for h in range(heads):
         arrived = [forward(packs[h][0]), forward(packs[h][1])]
-        pieces = [begins[m][r] for r in range(n - 1) for m in range(3)]
+        pieces = [begins[3 * h + m][r] for r in range(n - 1) for m in range(3)]
         second.append(
             call(
-                functools.partial(grads_two, n, h, divisor),
+                functools.partial(grads_two, n, divisor),
                 grad_out,
-                [SMEM] * 3 + [VMEM] * (5 + 3 * (n - 1)),
+                [VMEM] * (5 + 3 * (n - 1)),
                 (VMEM,) * 6,
                 grad_scratch,
-            )(tok, block, decays, *kvq[1][h][:2], begin_own[h], *arrived, *pieces)
+            )(*kvq[1][h][:2], begin_own[h], *arrived, *pieces)
         )
 
     out_shape = jax.ShapeDtypeStruct(keys.shape, BF16)
@@ -415,11 +413,11 @@
     for h in range(heads):
         gu, down, send_gu, send_down, own_gu, own_down = second[h]
         recv_gu, recv_down = turned(send_gu), turned(send_down)
-        at = 4 + n
+        at = 5 + n
         hq, *ends = call(
             functools.partial(update_two_gu, n, h),
             (shape(rows, width), fast_shape, moment_shape),
-            [SMEM, SMEM] + [VMEM] * (2 + n) + [HBM] * len(ends),
+            [SMEM] * 2 + [VMEM] * (3 + n) + [HBM] * len(ends),
             (VMEM, HBM, HBM),
             (
                 pltpu.VMEM((2 * width, width), BF16),
@@ -429,11 +427,11 @@
                 DMA((2, 2)),
             ),
             aliases={at: 1, at + 1: 2} if ends else None,
-        )(tok, rates, gu, own_gu, kvq[1][h][2], *recv_gu, *ends)
+        )(rates, decays, gu, own_gu, moments[h], kvq[1][h][2], *recv_gu, *ends)
         outputs, *ends = call(
             functools.partial(update_two_down, n, h),
             (out_shape, fast_shape, moment_shape),
-            [SMEM, SMEM] + [VMEM] * (2 + n) + [HBM] * 3,
+            [SMEM] * 2 + [VMEM] * (3 + n) + [HBM] * 3,
             (HBM,) * 3,
             (
                 row_scratch,
@@ -445,7 +443,7 @@
                 DMA((2,)),
             ),
             aliases={at: 0, at + 1: 1, at + 2: 2},
-        )(tok, rates, down, own_down, hq, *recv_down, outputs, *ends)
+        )(rates, decays, down, own_down, moments[h], hq, *recv_down, outputs, *ends)
     return (outputs, jnp.swapaxes(ends[0], 3, 4), jnp.swapaxes(ends[1], 3, 4))
 
 

time: 123 us -> 132 us (1.073)
  waiting for transfers between devices: 39.7 us -> 62.9 us
  local copies, waits for them, and re-layouts: 11 us -> 0.01 us
  Pallas kernels: 40.1 us -> 37.2 us
    ppermute x3 -> x6, waiting for transfers between devices: 7.32 us -> 31.2 us  [on_device(): lax.ppermute(x, ('block', 'tok'), [(sources[p] * n + i, i) for i in range...]
    unnamed x70 -> x4, local copies, waits for them, and re-layouts: 11 us -> 0.01 us
    ppermute x4 -> x6, starting transfers between devices: 12.6 us -> 8.52 us  [forward(): return lax.ppermute(x, 'block', [(i, i + 1) for i in range(blocks - 1)])]
    ppermute x3 -> x6, starting transfers between devices: 3.87 us -> 7.73 us  [on_device(): lax.ppermute(x, ('block', 'tok'), [(sources[p] * n + i, i) for i in range...]
    pallas_call x9, Pallas kernels: 19.7 us -> 16.8 us  [the longest x2 6.63 us: on_device(): call(functools.partial(grads_one, n, h, divisor), grad_out, [SMEM] + [VME...]
  transfers between devices with their start and end apart: 18 -> 23, of which waited for: 8 -> 10; matrix products, arithmetic and copies ran while one was open for 0% -> 0% of each run, Pallas kernels for 30% -> 26%
where the time goes in v5:
time: 132 us
  waiting for transfers between devices  62.9 us (48%)
  Pallas kernels  37.2 us (28%)
  starting transfers between devices  30.4 us (23%)
    ppermute x10, waiting for transfers between devices, turned(): lax.ppermute(x, 'tok', [(i, (i + r) % n) for i in range(n)])  31.6 us
    ppermute x6, waiting for transfers between devices, on_device(): lax.ppermute(x, ('block', 'tok'), [(sources[p] * n + i, i) for i in range...  31.2 us
    ppermute x10, starting transfers between devices, turned(): lax.ppermute(x, 'tok', [(i, (i + r) % n) for i in range(n)])  13.4 us
    ppermute x6, starting transfers between devices, forward(): return lax.ppermute(x, 'block', [(i, i + 1) for i in range(blocks - 1)])  8.52 us
    ppermute x6, starting transfers between devices, on_device(): lax.ppermute(x, ('block', 'tok'), [(sources[p] * n + i, i) for i in range...  7.73 us
    pallas_call x2, Pallas kernels, on_device(): call(functools.partial(grads_one, n, h, divisor), grad_out, [SMEM] + [VME...  6.63 us
    pallas_call x2, Pallas kernels, on_device(): call(functools.partial(update_two_gu, n, h), (shape(rows, width), fast_sh...  5.62 us
    pallas_call x2, Pallas kernels, on_device(): call(functools.partial(grads_two, n, divisor), grad_out, [VMEM] * (5 + 3...  4.99 us
  transfers between devices with their start and end apart: 23, of which 10 were waited for; matrix products, arithmetic and copies ran while one was open for 0% of the time, Pallas kernels for 26%

profile of v5, /device:TPU:0, one launch (start us, length us, event | category | flops | bytes accessed | tf_op | source)
XLA Modules:
  0.0 131.5 jit_solution(13508972139345900291)
XLA Ops:
  1.6 3.0 %collective-permute-start.11 = (bf16[3,192,384]{2,1,0:T(8,128)(2,1)S(1)}, bf16[3,192,384]{2,1,0:T(8,128)(2,1)S(1)}, u32[]{:S(2)}, u32[]{:S(2)}) collective-permute-start(bf16[3,192,384]{2,1,0:T(8,128)(2,1)S(1)} %shard_map.110.refs_0_), channel_id=1, source_target_pairs={{0,1},{1,0},{2,3},{3,2},{4,5},{5,4},{6,7},{7,6},{8,9},{9,8},{10,11... | collective-permute-start | bytes 1327112 | tf_op jit(solution)/shard_map/ppermute | solution.py:291
  5.6 3.9 %shard_map.103 = (bf16[768,384]{1,0:T(8,128)(2,1)S(1)}, bf16[768,384]{1,0:T(8,128)(2,1)S(1)}, bf16[768,384]{1,0:T(8,128)(2,1)S(1)}, bf16[768,384]{1,0:T(8,128)(2...) custom-call(bf16[2,768,768]{2,1,0:T(8,128)(2,1)} %k_ref.1, ...), custom_call_target="tpu_custom_call" | custom-call | tf_op jit(solution)/shard_map/pallas_call | solution.py:329
  9.5 6.1 %collective-permute-done.11.refs_1_ = bf16[3,192,384]{2,1,0:T(8,128)(2,1)S(1)} collective-permute-done((bf16[3,192,384]{2,1,0:T(8,128)(2,1)S(1)}, bf16[3,192,384]{2,1,0:T(8,128)(2,1)S(1)}, u32[]{:S(2)}, u32[]{:S(2)}) %collective-permute-start.11) | collective-permute-done | bytes 442400 | tf_op jit(solution)/shard_map/ppermute | solution.py:291
  15.6 3.3 %shard_map.111 = (bf16[768,384]{1,0:T(8,128)(2,1)S(1)}, bf16[384,384]{1,0:T(8,128)(2,1)S(1)}, bf16[768,384]{1,0:T(8,128)(2,1)S(1)}, bf16[384,384]{1,0:T(8,128)(2...) custom-call(f32[2]{0:T(128)S(1)} %copy-done.1, bf16[768,384]{1,0:T(8,128)(2,1)S(1)} %get-tuple-element.88.k_ref, ...), custom_call_target="tpu_custom_call" | custom-call | tf_op jit(solution)/shard_map/pallas_call | solution.py:343
  18.9 2.1 %collective-permute-start.12 = (bf16[768,384]{1,0:T(8,128)(2,1)S(1)}, bf16[768,384]{1,0:T(8,128)(2,1)S(1)}, u32[]{:S(2)}, u32[]{:S(2)}) collective-permute-start(bf16[768,384]{1,0:T(8,128)(2,1)S(1)} %get-tuple-element.93), channel_id=1, source_target_pairs={{0,1},{1,0},{2,3},{3,2},{4,5},{5,4},{6,7},{7,6},{8,9},{9,8},{10,11... | collective-permute-start | bytes 1769480 | tf_op jit(solution)/shard_map/ppermute | solution.py:291
  21.0 4.1 %collective-permute-done.refs_1_ = bf16[3,192,384]{2,1,0:T(8,128)(2,1)S(1)} collective-permute-done((bf16[3,192,384]{2,1,0:T(8,128)(2,1)S(1)}, bf16[3,192,384]{2,1,0:T(8,128)(2,1)S(1)}, u32[]{:S(2)}, u32[]{:S(2)}) %collective-permute-start) | collective-permute-done | bytes 442400 | tf_op jit(solution)/shard_map/ppermute | solution.py:291
  25.1 3.3 %shard_map.105 = (bf16[768,384]{1,0:T(8,128)(2,1)S(1)}, bf16[384,384]{1,0:T(8,128)(2,1)S(1)}, bf16[768,384]{1,0:T(8,128)(2,1)S(1)}, bf16[384,384]{1,0:T(8,128)(2...) custom-call(f32[2]{0:T(128)S(1)} %copy-done.1, bf16[768,384]{1,0:T(8,128)(2,1)S(1)} %get-tuple-element.66.k_ref, ...), custom_call_target="tpu_custom_call" | custom-call | tf_op jit(solution)/shard_map/pallas_call | solution.py:343
  28.5 2.1 %collective-permute-start.1 = (bf16[768,384]{1,0:T(8,128)(2,1)S(1)}, bf16[768,384]{1,0:T(8,128)(2,1)S(1)}, u32[]{:S(2)}, u32[]{:S(2)}) collective-permute-start(bf16[768,384]{1,0:T(8,128)(2,1)S(1)} %get-tuple-element.71), channel_id=1, source_target_pairs={{0,1},{1,0},{2,3},{3,2},{4,5},{5,4},{6,7},{7,6},{8,9},{9,8},{10,11... | collective-permute-start | bytes 1769480 | tf_op jit(solution)/shard_map/ppermute | solution.py:291
  33.5 4.2 %collective-permute-done.12.refs_0_ = bf16[768,384]{1,0:T(8,128)(2,1)S(1)} collective-permute-done((bf16[768,384]{1,0:T(8,128)(2,1)S(1)}, bf16[768,384]{1,0:T(8,128)(2,1)S(1)}, u32[]{:S(2)}, u32[]{:S(2)}) %collective-permute-start.12) | collective-permute-done | bytes 589856 | tf_op jit(solution)/shard_map/ppermute | solution.py:291
  40.3 2.1 %collective-permute-start.3 = (bf16[384,384]{1,0:T(8,128)(2,1)S(1)}, bf16[384,384]{1,0:T(8,128)(2,1)S(1)}, u32[]{:S(2)}, u32[]{:S(2)}) collective-permute-start(bf16[384,384]{1,0:T(8,128)(2,1)S(1)} %get-tuple-element.75), channel_id=1, source_target_pairs={{0,1},{1,0},{2,3},{3,2},{4,5},{5,4},{6,7},{7,6},{8,9},{9,8},{10,11... | collective-permute-start | bytes 884744 | tf_op jit(solution)/shard_map/ppermute | solution.py:291
  42.4 17.6 %collective-permute-done.16.refs_2_ = bf16[192,384]{1,0:T(8,128)(2,1)S(1)} collective-permute-done((bf16[192,384]{1,0:T(8,128)(2,1)S(1)}, bf16[192,384]{1,0:T(8,128)(2,1)S(1)}, u32[]{:S(2)}, u32[]{:S(2)}) %collective-permute-start.16) | collective-permute-done | bytes 147488 | tf_op jit(solution)/shard_map/ppermute | solution.py:376
  70.5 1.9 %collective-permute-start.19 = (bf16[1152,384]{1,0:T(8,128)(2,1)S(1)}, bf16[1152,384]{1,0:T(8,128)(2,1)S(1)}, u32[]{:S(2)}, u32[]{:S(2)}) collective-permute-start(bf16[1152,384]{1,0:T(8,128)(2,1)S(1)} %get-tuple-element.102), channel_id=1, source_target_pairs={{0,2},{2,4},{4,6},{6,8},{8,10},{10,12},{12,14},{14,16},{16,18},{18... | collective-permute-start | bytes 2654216 | tf_op jit(solution)/shard_map/ppermute | solution.py:294
  74.7 6.6 %collective-permute-done.7.refs_3_ = bf16[192,384]{1,0:T(8,128)(2,1)S(1)} collective-permute-done((bf16[192,384]{1,0:T(8,128)(2,1)S(1)}, bf16[192,384]{1,0:T(8,128)(2,1)S(1)}, u32[]{:S(2)}, u32[]{:S(2)}) %collective-permute-start.7) | collective-permute-done | bytes 147488 | tf_op jit(solution)/shard_map/ppermute | solution.py:376
  85.3 2.4 %shard_map.114 = (bf16[768,384]{1,0:T(8,128)(2,1)S(1)}, bf16[384,384]{1,0:T(8,128)(2,1)S(1)}, bf16[768,384]{1,0:T(8,128)(2,1)S(1)}, bf16[384,384]{1,0:T(8,128)(2...) custom-call(bf16[768,384]{1,0:T(8,128)(2,1)S(1)} %get-tuple-element.85.k_ref, ...), custom_call_target="tpu_custom_call" | custom-call | tf_op jit(solution)/shard_map/pallas_call | solution.py:388
  87.7 5.1 %collective-permute-done.8.refs_4_ = bf16[192,384]{1,0:T(8,128)(2,1)S(1)} collective-permute-done((bf16[192,384]{1,0:T(8,128)(2,1)S(1)}, bf16[192,384]{1,0:T(8,128)(2,1)S(1)}, u32[]{:S(2)}, u32[]{:S(2)}) %collective-permute-start.8) | collective-permute-done | bytes 147488 | tf_op jit(solution)/shard_map/ppermute | solution.py:376
  93.7 2.6 %shard_map.109 = (bf16[768,384]{1,0:T(8,128)(2,1)S(1)}, bf16[384,384]{1,0:T(8,128)(2,1)S(1)}, bf16[768,384]{1,0:T(8,128)(2,1)S(1)}, bf16[384,384]{1,0:T(8,128)(2...) custom-call(bf16[768,384]{1,0:T(8,128)(2,1)S(1)} %get-tuple-element.63.k_ref, ...), custom_call_target="tpu_custom_call" | custom-call | tf_op jit(solution)/shard_map/pallas_call | solution.py:388
  99.6 2.3 %shard_map.116.refs_0_ = bf16[2,768,768]{2,1,0:T(8,128)(2,1)} custom-call(bf16[768,384]{1,0:T(8,128)(2,1)S(1)} %get-tuple-element.110.q_ref, bf16[768,384]{1,0:T(8,128)(2,1)S(1)} %get-tuple-element.94.pgu_ref, bf16[384,384]{1,0:T(8,128)(2,1)S(1)} %get-tuple-element.99.pdown_ref), custom_call_target="tpu_custom_call" | custom-call | tf_op jit(solution)/shard_map/pallas_call | solution.py:401
  101.8 2.3 %shard_map.117.refs_1_ = bf16[2,768,768]{2,1,0:T(8,128)(2,1)} custom-call(bf16[768,384]{1,0:T(8,128)(2,1)S(1)} %get-tuple-element.109.q_ref, bf16[768,384]{1,0:T(8,128)(2,1)S(1)} %get-tuple-element.72.pgu_ref, bf16[384,384]{1,0:T(8,128)(2,1)S(1)} %get-tuple-element.77.pdown_ref, bf16[2,768,768]{2,1,0:T(8,128)(2,1)} %shard_map.116.refs_0_), custom_call_target="tpu_custom_call", output_to_operand_aliasing={{}: (3, {})} | custom-call | tf_op jit(solution)/shard_map/pallas_call | solution.py:401
  104.1 4.9 %collective-permute-done.20.refs_0_ = bf16[768,384]{1,0:T(8,128)(2,1)S(1)} collective-permute-done((bf16[768,384]{1,0:T(8,128)(2,1)S(1)}, bf16[768,384]{1,0:T(8,128)(2,1)S(1)}, u32[]{:S(2)}, u32[]{:S(2)}) %collective-permute-start.20) | collective-permute-done | bytes 589856 | tf_op jit(solution)/shard_map/ppermute | solution.py:291
  109.0 2.8 %shard_map.115 = (bf16[768,384]{1,0:T(8,128)(2,1)S(1)}, bf16[1,3,2,192,384]{4,3,2,1,0:T(8,128)(2,1)}, f32[1,3,2,192,384]{4,3,2,1,0:T(8,128)}) custom-call(f32[2,3]{1,0:T(2,128)S(1)} %bitcast.10, f32[2]{0:T(128)S(1)} %copy-done.1, bf16[768,384]{1,0:T(8,128)(2,1)S(1)} %get-tuple-element.103.old_ref, f32[768,384]{1,0:T(8,128)S(1)} %get-tuple-element.104.own_ref, ...), custom_call_target="tpu_custom_call" | custom-call | tf_op jit(solution)/shard_map/pallas_call | solution.py:417
  111.9 12.3 %collective-permute-done.21.refs_0_ = bf16[384,384]{1,0:T(8,128)(2,1)S(1)} collective-permute-done((bf16[384,384]{1,0:T(8,128)(2,1)S(1)}, bf16[384,384]{1,0:T(8,128)(2,1)S(1)}, u32[]{:S(2)}, u32[]{:S(2)}) %collective-permute-start.21) | collective-permute-done | bytes 294944 | tf_op jit(solution)/shard_map/ppermute | solution.py:291
  124.1 2.2 %shard_map.118 = (bf16[2,768,768]{2,1,0:T(8,128)(2,1)}, bf16[1,3,2,192,384]{4,3,2,1,0:T(8,128)(2,1)}, f32[1,3,2,192,384]{4,3,2,1,0:T(8,128)}) custom-call(f32[2,3]{1,0:T(2,128)S(1)} %bitcast.11, f32[2]{0:T(128)S(1)} %copy-done.1, bf16[384,384]{1,0:T(8,128)(2,1)S(1)} %get-tuple-element.100.old_ref, ...), custom_call_target="tpu_custom_call", output_to_operand_aliasing={{0}: (7, {}), {1}: (8, {}), {2}: (9, {})} | custom-call | tf_op jit(solution)/shard_map/pallas_call | solution.py:431
  126.4 2.8 %shard_map.119 = (bf16[768,384]{1,0:T(8,128)(2,1)S(1)}, bf16[1,3,2,192,384]{4,3,2,1,0:T(8,128)(2,1)}, f32[1,3,2,192,384]{4,3,2,1,0:T(8,128)}) custom-call(f32[2,3]{1,0:T(2,128)S(1)} %bitcast.12, f32[2]{0:T(128)S(1)} %copy-done.1, bf16[768,384]{1,0:T(8,128)(2,1)S(1)} %get-tuple-element.81.old_ref, ...), custom_call_target="tpu_custom_call", output_to_operand_aliasing={{1}: (7, {}), {2}: (8, {})} | custom-call | tf_op jit(solution)/shard_map/pallas_call | solution.py:417
  129.2 2.2 %shard_map.120 = (bf16[2,768,768]{2,1,0:T(8,128)(2,1)}, bf16[1,3,2,192,384]{4,3,2,1,0:T(8,128)(2,1)}, f32[1,3,2,192,384]{4,3,2,1,0:T(8,128)}) custom-call(f32[2,3]{1,0:T(2,128)S(1)} %bitcast.13, f32[2]{0:T(128)S(1)} %copy-done.1, bf16[384,384]{1,0:T(8,128)(2,1)S(1)} %get-tuple-element.78.old_ref, ...), custom_call_target="tpu_custom_call", output_to_operand_aliasing={{0}: (7, {}), {1}: (8, {}), {2}: (9, {})} | custom-call | tf_op jit(solution)/shard_map/pallas_call | solution.py:431
  (44 shorter events, 28.3 us)
Async XLA Ops:
  1.6 14.0 %collective-permute-start.11 = (bf16[3,192,384]{2,1,0:T(8,128)(2,1)S(1)}, bf16[3,192,384]{2,1,0:T(8,128)(2,1)S(1)}, u32[]{:S(2)}, u32[]{:S(2)}) collective-permute-start(bf16[3,192,384]{2,1,0:T(8,128)(2,1)S(1)} %shard_map.110.refs_0_), channel_id=1, source_target_pairs={{0,1},{1,0},{2,3},{3,2},{4,5},{5,4},{6,7},{7,6},{8,9},{9,8},{10,11... | collective-permute-start | bytes 1327112 | tf_op jit(solution)/shard_map/ppermute | solution.py:291
  5.6 19.5 %collective-permute-start = (bf16[3,192,384]{2,1,0:T(8,128)(2,1)S(1)}, bf16[3,192,384]{2,1,0:T(8,128)(2,1)S(1)}, u32[]{:S(2)}, u32[]{:S(2)}) collective-permute-start(bf16[3,192,384]{2,1,0:T(8,128)(2,1)S(1)} %shard_map.104.refs_0_), channel_id=1, source_target_pairs={{0,1},{1,0},{2,3},{3,2},{4,5},{5,4},{6,7},{7,6},{8,9},{9,8},{10,11... | collective-permute-start | bytes 1327112 | tf_op jit(solution)/shard_map/ppermute | solution.py:291
  18.9 18.8 %collective-permute-start.12 = (bf16[768,384]{1,0:T(8,128)(2,1)S(1)}, bf16[768,384]{1,0:T(8,128)(2,1)S(1)}, u32[]{:S(2)}, u32[]{:S(2)}) collective-permute-start(bf16[768,384]{1,0:T(8,128)(2,1)S(1)} %get-tuple-element.93), channel_id=1, source_target_pairs={{0,1},{1,0},{2,3},{3,2},{4,5},{5,4},{6,7},{7,6},{8,9},{9,8},{10,11... | collective-permute-start | bytes 1769480 | tf_op jit(solution)/shard_map/ppermute | solution.py:291
  25.1 12.6 %copy-start = (f32[3,2]{0,1:T(2,128)S(1)}, f32[3,2]{0,1:T(2,128)}, u32[]{:S(2)}) copy-start(f32[3,2]{0,1:T(2,128)} %param.14) | copy-start | bytes 76
  28.5 34.1 %collective-permute-start.1 = (bf16[768,384]{1,0:T(8,128)(2,1)S(1)}, bf16[768,384]{1,0:T(8,128)(2,1)S(1)}, u32[]{:S(2)}, u32[]{:S(2)}) collective-permute-start(bf16[768,384]{1,0:T(8,128)(2,1)S(1)} %get-tuple-element.71), channel_id=1, source_target_pairs={{0,1},{1,0},{2,3},{3,2},{4,5},{5,4},{6,7},{7,6},{8,9},{9,8},{10,11... | collective-permute-start | bytes 1769480 | tf_op jit(solution)/shard_map/ppermute | solution.py:291
  31.4 0.8 collective-permute-start.5
  32.1 29.2 %collective-permute-start.14 = (bf16[384,384]{1,0:T(8,128)(2,1)S(1)}, bf16[384,384]{1,0:T(8,128)(2,1)S(1)}, u32[]{:S(2)}, u32[]{:S(2)}) collective-permute-start(bf16[384,384]{1,0:T(8,128)(2,1)S(1)} %get-tuple-element.97), channel_id=1, source_target_pairs={{0,1},{1,0},{2,3},{3,2},{4,5},{5,4},{6,7},{7,6},{8,9},{9,8},{10,11... | collective-permute-start | bytes 884744 | tf_op jit(solution)/shard_map/ppermute | solution.py:291
  32.2 27.8 %collective-permute-start.16 = (bf16[192,384]{1,0:T(8,128)(2,1)S(1)}, bf16[192,384]{1,0:T(8,128)(2,1)S(1)}, u32[]{:S(2)}, u32[]{:S(2)}) collective-permute-start(bf16[192,384]{1,0:T(8,128)(2,1)S(1)} %collective-permute-done.5), channel_id=1, source_target_pairs={{4,0},{5,1}} | collective-permute-start | bytes 442376 | tf_op jit(solution)/shard_map/ppermute | solution.py:376
  39.0 45.0 %collective-permute-start.13 = (bf16[768,384]{1,0:T(8,128)(2,1)S(1)}, bf16[768,384]{1,0:T(8,128)(2,1)S(1)}, u32[]{:S(2)}, u32[]{:S(2)}) collective-permute-start(bf16[768,384]{1,0:T(8,128)(2,1)S(1)} %get-tuple-element.94.pgu_ref), channel_id=1, source_target_pairs={{0,2},{2,4},{4,6},{6,8},{8,10},{10,12},{12,14},{14,16},{16,18},{18... | collective-permute-start | bytes 1769480 | tf_op jit(solution)/shard_map/ppermute | solution.py:294
  40.3 32.2 %collective-permute-start.3 = (bf16[384,384]{1,0:T(8,128)(2,1)S(1)}, bf16[384,384]{1,0:T(8,128)(2,1)S(1)}, u32[]{:S(2)}, u32[]{:S(2)}) collective-permute-start(bf16[384,384]{1,0:T(8,128)(2,1)S(1)} %get-tuple-element.75), channel_id=1, source_target_pairs={{0,1},{1,0},{2,3},{3,2},{4,5},{5,4},{6,7},{7,6},{8,9},{9,8},{10,11... | collective-permute-start | bytes 884744 | tf_op jit(solution)/shard_map/ppermute | solution.py:291
  60.0 7.0 %collective-permute-start.17 = (bf16[192,384]{1,0:T(8,128)(2,1)S(1)}, bf16[192,384]{1,0:T(8,128)(2,1)S(1)}, u32[]{:S(2)}, u32[]{:S(2)}) collective-permute-start(bf16[192,384]{1,0:T(8,128)(2,1)S(1)} %collective-permute-done.5), channel_id=1, source_target_pairs={{8,0},{9,1}} | collective-permute-start | bytes 442376 | tf_op jit(solution)/shard_map/ppermute | solution.py:376
  61.3 7.9 %collective-permute-start.18 = (bf16[192,384]{1,0:T(8,128)(2,1)S(1)}, bf16[192,384]{1,0:T(8,128)(2,1)S(1)}, u32[]{:S(2)}, u32[]{:S(2)}) collective-permute-start(bf16[192,384]{1,0:T(8,128)(2,1)S(1)} %collective-permute-done.5), channel_id=1, source_target_pairs={{12,0},{13,1}} | collective-permute-start | bytes 442376 | tf_op jit(solution)/shard_map/ppermute | solution.py:376
  62.6 7.9 %collective-permute-start.6 = (bf16[192,384]{1,0:T(8,128)(2,1)S(1)}, bf16[192,384]{1,0:T(8,128)(2,1)S(1)}, u32[]{:S(2)}, u32[]{:S(2)}) collective-permute-start(bf16[192,384]{1,0:T(8,128)(2,1)S(1)} %collective-permute-done.5), channel_id=1, source_target_pairs={{16,0},{17,1}} | collective-permute-start | bytes 442376 | tf_op jit(solution)/shard_map/ppermute | solution.py:376
  67.0 26.7 %collective-permute-start.2 = (bf16[768,384]{1,0:T(8,128)(2,1)S(1)}, bf16[768,384]{1,0:T(8,128)(2,1)S(1)}, u32[]{:S(2)}, u32[]{:S(2)}) collective-permute-start(bf16[768,384]{1,0:T(8,128)(2,1)S(1)} %get-tuple-element.72.pgu_ref), channel_id=1, source_target_pairs={{0,2},{2,4},{4,6},{6,8},{8,10},{10,12},{12,14},{14,16},{16,18},{18... | collective-permute-start | bytes 1769480 | tf_op jit(solution)/shard_map/ppermute | solution.py:294
  69.2 13.4 %collective-permute-start.15 = (bf16[384,384]{1,0:T(8,128)(2,1)S(1)}, bf16[384,384]{1,0:T(8,128)(2,1)S(1)}, u32[]{:S(2)}, u32[]{:S(2)}) collective-permute-start(bf16[384,384]{1,0:T(8,128)(2,1)S(1)} %get-tuple-element.99.pdown_ref), channel_id=1, source_target_pairs={{0,2},{2,4},{4,6},{6,8},{8,10},{10,12},{12,14},{14,16},{16,18},{18... | collective-permute-start | bytes 884744 | tf_op jit(solution)/shard_map/ppermute | solution.py:294
  70.5 27.9 %collective-permute-start.19 = (bf16[1152,384]{1,0:T(8,128)(2,1)S(1)}, bf16[1152,384]{1,0:T(8,128)(2,1)S(1)}, u32[]{:S(2)}, u32[]{:S(2)}) collective-permute-start(bf16[1152,384]{1,0:T(8,128)(2,1)S(1)} %get-tuple-element.102), channel_id=1, source_target_pairs={{0,2},{2,4},{4,6},{6,8},{8,10},{10,12},{12,14},{14,16},{16,18},{18... | collective-permute-start | bytes 2654216 | tf_op jit(solution)/shard_map/ppermute | solution.py:294
  72.5 8.8 %collective-permute-start.7 = (bf16[192,384]{1,0:T(8,128)(2,1)S(1)}, bf16[192,384]{1,0:T(8,128)(2,1)S(1)}, u32[]{:S(2)}, u32[]{:S(2)}) collective-permute-start(bf16[192,384]{1,0:T(8,128)(2,1)S(1)} %collective-permute-done.5), channel_id=1, source_target_pairs={{20,0},{21,1}} | collective-permute-start | bytes 442376 | tf_op jit(solution)/shard_map/ppermute | solution.py:376
  81.3 12.4 %collective-permute-start.4 = (bf16[384,384]{1,0:T(8,128)(2,1)S(1)}, bf16[384,384]{1,0:T(8,128)(2,1)S(1)}, u32[]{:S(2)}, u32[]{:S(2)}) collective-permute-start(bf16[384,384]{1,0:T(8,128)(2,1)S(1)} %get-tuple-element.77.pdown_ref), channel_id=1, source_target_pairs={{0,2},{2,4},{4,6},{6,8},{8,10},{10,12},{12,14},{14,16},{16,18},{18... | collective-permute-start | bytes 884744 | tf_op jit(solution)/shard_map/ppermute | solution.py:294
  82.6 43.7 %collective-permute-start.9 = (bf16[1152,384]{1,0:T(8,128)(2,1)S(1)}, bf16[1152,384]{1,0:T(8,128)(2,1)S(1)}, u32[]{:S(2)}, u32[]{:S(2)}) collective-permute-start(bf16[1152,384]{1,0:T(8,128)(2,1)S(1)} %get-tuple-element.80), channel_id=1, source_target_pairs={{0,2},{2,4},{4,6},{6,8},{8,10},{10,12},{12,14},{14,16},{16,18},{18... | collective-permute-start | bytes 2654216 | tf_op jit(solution)/shard_map/ppermute | solution.py:294
  84.0 8.8 %collective-permute-start.8 = (bf16[192,384]{1,0:T(8,128)(2,1)S(1)}, bf16[192,384]{1,0:T(8,128)(2,1)S(1)}, u32[]{:S(2)}, u32[]{:S(2)}) collective-permute-start(bf16[192,384]{1,0:T(8,128)(2,1)S(1)} %collective-permute-done.5), channel_id=1, source_target_pairs={{24,0},{25,1}} | collective-permute-start | bytes 442376 | tf_op jit(solution)/shard_map/ppermute | solution.py:376
  92.8 16.2 %collective-permute-start.20 = (bf16[768,384]{1,0:T(8,128)(2,1)S(1)}, bf16[768,384]{1,0:T(8,128)(2,1)S(1)}, u32[]{:S(2)}, u32[]{:S(2)}) collective-permute-start(bf16[768,384]{1,0:T(8,128)(2,1)S(1)} %get-tuple-element.106), channel_id=1, source_target_pairs={{0,1},{1,0},{2,3},{3,2},{4,5},{5,4},{6,7},{7,6},{8,9},{9,8},{10,11... | collective-permute-start | bytes 1769480 | tf_op jit(solution)/shard_map/ppermute | solution.py:291
  96.3 30.0 %collective-permute-start.10 = (bf16[768,384]{1,0:T(8,128)(2,1)S(1)}, bf16[768,384]{1,0:T(8,128)(2,1)S(1)}, u32[]{:S(2)}, u32[]{:S(2)}) collective-permute-start(bf16[768,384]{1,0:T(8,128)(2,1)S(1)} %get-tuple-element.84), channel_id=1, source_target_pairs={{0,1},{1,0},{2,3},{3,2},{4,5},{5,4},{6,7},{7,6},{8,9},{9,8},{10,11... | collective-permute-start | bytes 1769480 | tf_op jit(solution)/shard_map/ppermute | solution.py:291
  97.5 26.6 %collective-permute-start.21 = (bf16[384,384]{1,0:T(8,128)(2,1)S(1)}, bf16[384,384]{1,0:T(8,128)(2,1)S(1)}, u32[]{:S(2)}, u32[]{:S(2)}) collective-permute-start(bf16[384,384]{1,0:T(8,128)(2,1)S(1)} %get-tuple-element.108), channel_id=1, source_target_pairs={{0,1},{1,0},{2,3},{3,2},{4,5},{5,4},{6,7},{7,6},{8,9},{9,8},{10,11... | collective-permute-start | bytes 884744 | tf_op jit(solution)/shard_map/ppermute | solution.py:291
  98.4 30.8 %collective-permute-start.22 = (bf16[384,384]{1,0:T(8,128)(2,1)S(1)}, bf16[384,384]{1,0:T(8,128)(2,1)S(1)}, u32[]{:S(2)}, u32[]{:S(2)}) collective-permute-start(bf16[384,384]{1,0:T(8,128)(2,1)S(1)} %get-tuple-element.116), channel_id=1, source_target_pairs={{0,1},{1,0},{2,3},{3,2},{4,5},{5,4},{6,7},{7,6},{8,9},{9,8},{10,11... | collective-permute-start | bytes 884744 | tf_op jit(solution)/shard_map/ppermute | solution.py:291
  (1 other events, 10.0 us)

commit v6 on v5

--- a/solution.py
+++ b/solution.py
@@ -121,7 +121,8 @@
 
 def grads_two(n, divisor, k_ref, v_ref, begin_ref, *refs):
     (pgu_ref, pdown_ref), pieces = refs[:2], refs[2 : 2 + 3 * (n - 1)]
-    gu_ref, down_ref, send_gu, send_down, own_gu, own_down, hid_s, dout_s, dgu_s = refs[-9:]
+    gu_ref, down_ref, own_gu, own_down, send_gu, *sends = refs[2 + 3 * (n - 1) : -3]
+    hid_s, dout_s, dgu_s = refs[-3:]
     leading = lax.axis_index("block") == 0
 
     @pl.when(leading)
@@ -138,24 +139,24 @@
 
     grads_core(divisor, k_ref, v_ref, gu_ref, down_ref, own_gu, own_down, hid_s, dout_s, dgu_s)
     send_gu[...] = own_gu[...].astype(BF16)
-    send_down[...] = own_down[...].astype(BF16)
-
-
-def updated(rate, old_ref, moments, first):
-    width = old_ref.shape[1]
-    at = pl.ds(first, width)
-    moment = moments(at)
+    first = 0
+    for send in sends:
+        send[...] = own_down[pl.ds(first, send.shape[0]), :].astype(BF16)
+        first += send.shape[0]
+
+
+def updated(rate, old_ref, at, moment):
     old = old_ref[at, :].astype(F32)
     moved = old - rate * moment
     old_norm = jnp.sqrt(jnp.mean(old * old, axis=1, keepdims=True) + 1e-06)
     new_norm = jnp.sqrt(jnp.mean(moved * moved, axis=1, keepdims=True) + 1e-06)
-    return (moved * (old_norm / new_norm)).astype(BF16), moment
-
-
-def summed(own_ref, recvs, at):
-    total = own_ref[at, :]
+    return (moved * (old_norm / new_norm)).astype(BF16)
+
+
+def summed(own_ref, recvs, first, size, sent_from=0):
+    total = own_ref[pl.ds(first, size), :]
     for recv in recvs:
-        total = total + recv[at, :].astype(F32)
+        total = total + recv[pl.ds(first - sent_from, size), :].astype(F32)
     return total
 
 
@@ -164,22 +165,10 @@
     new_ref, moment_ref = refs[-2:]
     width = own_ref.shape[1]
     for i, m in enumerate(mats):
-        at = slice(i * width, (i + 1) * width)
-        new, moment = updated(
-            rate_ref[head, m], old_ref, lambda at: summed(own_ref, recvs, at), i * width
-        )
-        new_ref[at, :] = new
+        at = pl.ds(i * width, width)
+        moment = summed(own_ref, recvs, i * width, width)
+        new_ref[at, :] = updated(rate_ref[head, m], old_ref, at, moment)
         moment_ref[m * width : (m + 1) * width, :] = moment.astype(BF16)
-
-
-def later_moment(decay, m, earlier_ref, own_ref, recvs):
-    width = earlier_ref.shape[1]
-
-    def moment(at):
-        earlier = earlier_ref[m * width : (m + 1) * width, :].astype(F32)
-        return decay * earlier + summed(own_ref, recvs, at)
-
-    return moment
 
 
 def store_mine(n, m, head, me, new_s, moment_s, fast_s, mine_s, fast_ref, moment_ref, sems):
@@ -203,10 +192,11 @@
     width = own_ref.shape[1]
     stores = []
     for m in range(2):
-        moments = later_moment(decay_ref[head], m, earlier_ref, own_ref, recvs)
-        new, moment = updated(rate_ref[head, m], old_ref, moments, m * width)
-        new_s = gu_s.at[pl.ds(m * width, width), :]
-        new_s[...] = new
+        at = pl.ds(m * width, width)
+        moment = decay_ref[head] * earlier_ref[at, :].astype(F32)
+        moment = moment + summed(own_ref, recvs, m * width, width)
+        new_s = gu_s.at[at, :]
+        new_s[...] = updated(rate_ref[head, m], old_ref, at, moment)
         moment_s[...] = moment
         stores += store_mine(
             n,
@@ -228,23 +218,35 @@
         store.wait()
 
 
-def update_two_down(n, head, rate_ref, decay_ref, old_ref, own_ref, earlier_ref, hq_ref, *refs):
+def update_two_down(n, head, first, rate_ref, decay_ref, old_ref, own_ref, earlier_ref, hq_ref, *refs):
     recvs = refs[: n - 1]
-    out_ref, fast_ref, moment_ref, out_s, down_s, moment_s, fast_s, mine_s, out_sems, sems = refs[-10:]
-    width = own_ref.shape[1]
-    moments = later_moment(decay_ref[head], 2, earlier_ref, own_ref, recvs)
-    new, moment = updated(rate_ref[head, 2], old_ref, moments, 0)
-    down_s[...] = new
-    moment_s[...] = moment
-    stores = store_mine(
-        n, 2, head, lax.axis_index("tok"), down_s, moment_s, fast_s, mine_s, fast_ref, moment_ref, sems
-    )
-    for i, at in enumerate(row_chunks(hq_ref.shape[0])):
-        out_s[at, :] = mm(hq_ref[at, :], down_s[...], ((1,), (1,))).astype(BF16)
+    width = old_ref.shape[1]
+    size = recvs[0].shape[0]
+    last = first + size == width
+    if last:
+        out_ref, fast_ref, moment_ref, new_s, kept_s, out_s, fast_s, mine_s, out_sems, sems = refs[-10:]
+    else:
+        out_ref, new_s, kept_s, out_s, out_sems = refs[-5:]
+    if first and last:
+        before_new, before_kept = refs[n - 1 : n + 1]
+        new_s[:first, :] = before_new[:first, :]
+        kept_s[:first, :] = before_kept[:first, :]
+    at = pl.ds(first, size)
+    moment = decay_ref[head] * earlier_ref[pl.ds(2 * width + first, size), :].astype(F32)
+    moment = moment + summed(own_ref, recvs, first, size, first)
+    new_s[at, :] = updated(rate_ref[head, 2], old_ref, at, moment)
+    kept_s[at, :] = moment
+    stores = []
+    if last:
+        me = lax.axis_index("tok")
+        stores = store_mine(
+            n, 2, head, me, new_s, kept_s, fast_s, mine_s, fast_ref, moment_ref, sems
+        )
+    cols = pl.ds(head * width + first, size)
+    for i, rows in enumerate(row_chunks(hq_ref.shape[0])):
+        out_s[rows, :] = mm(hq_ref[rows, :], new_s[at, :], ((1,), (1,))).astype(BF16)
         stores.append(
-            pltpu.make_async_copy(
-                out_s.at[at, :], out_ref.at[1, at, pl.ds(head * width, width)], out_sems.at[i]
-            )
+            pltpu.make_async_copy(out_s.at[rows, :], out_ref.at[1, rows, cols], out_sems.at[i])
         )
         stores[-1].start()
     for store in stores:
@@ -384,12 +386,20 @@
     for h in range(heads):
         arrived = [forward(packs[h][0]), forward(packs[h][1])]
         pieces = [begins[3 * h + m][r] for r in range(n - 1) for m in range(3)]
+        cuts = [width - 128, 128] if h == heads - 1 and width % 128 == 0 else [width]
         second.append(
             call(
                 functools.partial(grads_two, n, divisor),
-                grad_out,
+                (
+                    shape(2 * width, width),
+                    shape(width, width),
+                    shape(2 * width, width, dtype=F32),
+                    shape(width, width, dtype=F32),
+                    shape(2 * width, width),
+                )
+                + tuple(shape(size, width) for size in cuts),
                 [VMEM] * (5 + 3 * (n - 1)),
-                (VMEM,) * 6,
+                (VMEM,) * (5 + len(cuts)),
                 grad_scratch,
             )(*kvq[1][h][:2], begin_own[h], *arrived, *pieces)
         )
@@ -411,8 +421,9 @@
     moment_shape = jax.ShapeDtypeStruct(moment_t.shape, F32)
     ends = []
     for h in range(heads):
-        gu, down, send_gu, send_down, own_gu, own_down = second[h]
-        recv_gu, recv_down = turned(send_gu), turned(send_down)
+        gu, down, own_gu, own_down, send_gu, *sends = second[h]
+        recv_gu = turned(send_gu)
+        recv_down = [turned(x) for x in sends]
         at = 5 + n
         hq, *ends = call(
             functools.partial(update_two_gu, n, h),
@@ -428,22 +439,37 @@
             ),
             aliases={at: 1, at + 1: 2} if ends else None,
         )(rates, decays, gu, own_gu, moments[h], kvq[1][h][2], *recv_gu, *ends)
-        outputs, *ends = call(
-            functools.partial(update_two_down, n, h),
-            (out_shape, fast_shape, moment_shape),
-            [SMEM] * 2 + [VMEM] * (3 + n) + [HBM] * 3,
-            (HBM,) * 3,
-            (
-                row_scratch,
-                pltpu.VMEM((width, width), BF16),
-                pltpu.VMEM((width, width), F32),
-                pltpu.VMEM((part, width), BF16),
-                pltpu.VMEM((part, width), F32),
-                DMA((chunks,)),
-                DMA((2,)),
-            ),
-            aliases={at: 0, at + 1: 1, at + 2: 2},
-        )(rates, decays, down, own_down, moments[h], hq, *recv_down, outputs, *ends)
+        kept, first_row = [], 0
+        for recvs in recv_down:
+            size = recvs[0].shape[0]
+            last = first_row + size == width
+            if last:
+                outs = (out_shape, fast_shape, moment_shape)
+                aliases = {at + len(kept) + j: j for j in range(3)}
+                extra = [*kept, outputs, *ends]
+            else:
+                outs = (out_shape, shape(width, width), shape(width, width, dtype=F32))
+                aliases = {at: 0}
+                extra = [outputs]
+            buffers = (pltpu.VMEM((width, width), BF16), pltpu.VMEM((width, width), F32))
+            mine = (pltpu.VMEM((part, width), BF16), pltpu.VMEM((part, width), F32))
+            outputs, *rest = call(
+                functools.partial(update_two_down, n, h, first_row),
+                outs,
+                [SMEM] * 2 + [VMEM] * (3 + n + len(kept)) + [HBM] * (len(extra) - len(kept)),
+                (HBM,) * 3 if last else (HBM, VMEM, VMEM),
+                (buffers if last else ())
+                + (pltpu.VMEM((rows, size), BF16),)
+                + (mine if last else ())
+                + (DMA((chunks,)),)
+                + ((DMA((2,)),) if last else ()),
+                aliases=aliases,
+            )(rates, decays, down, own_down, moments[h], hq, *recvs, *extra)
+            if last:
+                ends = rest
+            else:
+                kept = rest
+            first_row += size
     return (outputs, jnp.swapaxes(ends[0], 3, 4), jnp.swapaxes(ends[1], 3, 4))
 
 

time: 132 us -> 134 us (1.015)
  Pallas kernels: 37.2 us -> 38.8 us
    pallas_call x4 -> x5, Pallas kernels: 9.36 us -> 10.9 us  [the longest x3 5.93 us: on_device(): call(functools.partial(update_two_down, n, h, first_row), outs, [SMEM] *...]
    ppermute x10 -> x11, starting transfers between devices: 13.4 us -> 14.3 us  [turned(): lax.ppermute(x, 'tok', [(i, (i + r) % n) for i in range(n)])]
    ppermute x10 -> x11, waiting for transfers between devices: 31.6 us -> 30.8 us  [turned(): lax.ppermute(x, 'tok', [(i, (i + r) % n) for i in range(n)])]
  transfers between devices with their start and end apart: 23 -> 24, of which waited for: 10 -> 10; matrix products, arithmetic and copies ran while one was open for 0% -> 0% of each run, Pallas kernels for 26% -> 27%
where the time goes in v6:
time: 134 us; the launch traced here: 133 us
  waiting for transfers between devices  62 us (46%)
  Pallas kernels  38.8 us (29%)
  starting transfers between devices  31.3 us (23%)
    ppermute x6, waiting for transfers between devices, on_device(): lax.ppermute(x, ('block', 'tok'), [(sources[p] * n + i, i) for i in range...  31.2 us
    ppermute x11, waiting for transfers between devices, turned(): lax.ppermute(x, 'tok', [(i, (i + r) % n) for i in range(n)])  30.8 us
    ppermute x11, starting transfers between devices, turned(): lax.ppermute(x, 'tok', [(i, (i + r) % n) for i in range(n)])  14.3 us
    ppermute x6, starting transfers between devices, forward(): return lax.ppermute(x, 'block', [(i, i + 1) for i in range(blocks - 1)])  8.52 us
    ppermute x6, starting transfers between devices, on_device(): lax.ppermute(x, ('block', 'tok'), [(sources[p] * n + i, i) for i in range...  7.73 us
    pallas_call x2, Pallas kernels, on_device(): call(functools.partial(grads_one, n, h, divisor), grad_out, [SMEM] + [VME...  6.62 us
    pallas_call x3, Pallas kernels, on_device(): call(functools.partial(update_two_down, n, h, first_row), outs, [SMEM] *...  5.93 us
    pallas_call x2, Pallas kernels, on_device(): call(functools.partial(update_two_gu, n, h), (shape(rows, width), fast_sh...  5.61 us
  transfers between devices with their start and end apart: 24, of which 10 were waited for; matrix products, arithmetic and copies ran while one was open for 0% of the time, Pallas kernels for 27%

profile of v6, /device:TPU:0, one launch (start us, length us, event | category | flops | bytes accessed | tf_op | source)
XLA Modules:
  0.0 133.1 jit_solution(14719034421536152626)
XLA Ops:
  1.6 3.0 %collective-permute-start.11 = (bf16[3,192,384]{2,1,0:T(8,128)(2,1)S(1)}, bf16[3,192,384]{2,1,0:T(8,128)(2,1)S(1)}, u32[]{:S(2)}, u32[]{:S(2)}) collective-permute-start(bf16[3,192,384]{2,1,0:T(8,128)(2,1)S(1)} %shard_map.110.refs_0_), channel_id=1, source_target_pairs={{0,1},{1,0},{2,3},{3,2},{4,5},{5,4},{6,7},{7,6},{8,9},{9,8},{10,11... | collective-permute-start | bytes 1327112 | tf_op jit(solution)/shard_map/ppermute | solution.py:293
  5.6 3.9 %shard_map.103 = (bf16[768,384]{1,0:T(8,128)(2,1)S(1)}, bf16[768,384]{1,0:T(8,128)(2,1)S(1)}, bf16[768,384]{1,0:T(8,128)(2,1)S(1)}, bf16[768,384]{1,0:T(8,128)(2...) custom-call(bf16[2,768,768]{2,1,0:T(8,128)(2,1)} %k_ref.1, ...), custom_call_target="tpu_custom_call" | custom-call | tf_op jit(solution)/shard_map/pallas_call | solution.py:331
  9.5 6.1 %collective-permute-done.11.refs_1_ = bf16[3,192,384]{2,1,0:T(8,128)(2,1)S(1)} collective-permute-done((bf16[3,192,384]{2,1,0:T(8,128)(2,1)S(1)}, bf16[3,192,384]{2,1,0:T(8,128)(2,1)S(1)}, u32[]{:S(2)}, u32[]{:S(2)}) %collective-permute-start.11) | collective-permute-done | bytes 442400 | tf_op jit(solution)/shard_map/ppermute | solution.py:293
  15.6 3.3 %shard_map.111 = (bf16[768,384]{1,0:T(8,128)(2,1)S(1)}, bf16[384,384]{1,0:T(8,128)(2,1)S(1)}, bf16[768,384]{1,0:T(8,128)(2,1)S(1)}, bf16[384,384]{1,0:T(8,128)(2...) custom-call(f32[2]{0:T(128)S(1)} %copy-done.1, bf16[768,384]{1,0:T(8,128)(2,1)S(1)} %get-tuple-element.92.k_ref, ...), custom_call_target="tpu_custom_call" | custom-call | tf_op jit(solution)/shard_map/pallas_call | solution.py:345
  18.9 2.1 %collective-permute-start.12 = (bf16[768,384]{1,0:T(8,128)(2,1)S(1)}, bf16[768,384]{1,0:T(8,128)(2,1)S(1)}, u32[]{:S(2)}, u32[]{:S(2)}) collective-permute-start(bf16[768,384]{1,0:T(8,128)(2,1)S(1)} %get-tuple-element.97), channel_id=1, source_target_pairs={{0,1},{1,0},{2,3},{3,2},{4,5},{5,4},{6,7},{7,6},{8,9},{9,8},{10,11... | collective-permute-start | bytes 1769480 | tf_op jit(solution)/shard_map/ppermute | solution.py:293
  21.0 4.1 %collective-permute-done.refs_1_ = bf16[3,192,384]{2,1,0:T(8,128)(2,1)S(1)} collective-permute-done((bf16[3,192,384]{2,1,0:T(8,128)(2,1)S(1)}, bf16[3,192,384]{2,1,0:T(8,128)(2,1)S(1)}, u32[]{:S(2)}, u32[]{:S(2)}) %collective-permute-start) | collective-permute-done | bytes 442400 | tf_op jit(solution)/shard_map/ppermute | solution.py:293
  25.1 3.3 %shard_map.105 = (bf16[768,384]{1,0:T(8,128)(2,1)S(1)}, bf16[384,384]{1,0:T(8,128)(2,1)S(1)}, bf16[768,384]{1,0:T(8,128)(2,1)S(1)}, bf16[384,384]{1,0:T(8,128)(2...) custom-call(f32[2]{0:T(128)S(1)} %copy-done.1, bf16[768,384]{1,0:T(8,128)(2,1)S(1)} %get-tuple-element.70.k_ref, ...), custom_call_target="tpu_custom_call" | custom-call | tf_op jit(solution)/shard_map/pallas_call | solution.py:345
  28.4 2.1 %collective-permute-start.1 = (bf16[768,384]{1,0:T(8,128)(2,1)S(1)}, bf16[768,384]{1,0:T(8,128)(2,1)S(1)}, u32[]{:S(2)}, u32[]{:S(2)}) collective-permute-start(bf16[768,384]{1,0:T(8,128)(2,1)S(1)} %get-tuple-element.75), channel_id=1, source_target_pairs={{0,1},{1,0},{2,3},{3,2},{4,5},{5,4},{6,7},{7,6},{8,9},{9,8},{10,11... | collective-permute-start | bytes 1769480 | tf_op jit(solution)/shard_map/ppermute | solution.py:293
  33.5 4.2 %collective-permute-done.12.refs_0_ = bf16[768,384]{1,0:T(8,128)(2,1)S(1)} collective-permute-done((bf16[768,384]{1,0:T(8,128)(2,1)S(1)}, bf16[768,384]{1,0:T(8,128)(2,1)S(1)}, u32[]{:S(2)}, u32[]{:S(2)}) %collective-permute-start.12) | collective-permute-done | bytes 589856 | tf_op jit(solution)/shard_map/ppermute | solution.py:293
  40.3 2.1 %collective-permute-start.3 = (bf16[384,384]{1,0:T(8,128)(2,1)S(1)}, bf16[384,384]{1,0:T(8,128)(2,1)S(1)}, u32[]{:S(2)}, u32[]{:S(2)}) collective-permute-start(bf16[384,384]{1,0:T(8,128)(2,1)S(1)} %get-tuple-element.79), channel_id=1, source_target_pairs={{0,1},{1,0},{2,3},{3,2},{4,5},{5,4},{6,7},{7,6},{8,9},{9,8},{10,11... | collective-permute-start | bytes 884744 | tf_op jit(solution)/shard_map/ppermute | solution.py:293
  42.4 17.6 %collective-permute-done.16.refs_2_ = bf16[192,384]{1,0:T(8,128)(2,1)S(1)} collective-permute-done((bf16[192,384]{1,0:T(8,128)(2,1)S(1)}, bf16[192,384]{1,0:T(8,128)(2,1)S(1)}, u32[]{:S(2)}, u32[]{:S(2)}) %collective-permute-start.16) | collective-permute-done | bytes 147488 | tf_op jit(solution)/shard_map/ppermute | solution.py:378
  70.5 1.9 %collective-permute-start.19 = (bf16[1152,384]{1,0:T(8,128)(2,1)S(1)}, bf16[1152,384]{1,0:T(8,128)(2,1)S(1)}, u32[]{:S(2)}, u32[]{:S(2)}) collective-permute-start(bf16[1152,384]{1,0:T(8,128)(2,1)S(1)} %get-tuple-element.106), channel_id=1, source_target_pairs={{0,2},{2,4},{4,6},{6,8},{8,10},{10,12},{12,14},{14,16},{16,18},{18... | collective-permute-start | bytes 2654216 | tf_op jit(solution)/shard_map/ppermute | solution.py:296
  74.7 6.6 %collective-permute-done.7.refs_3_ = bf16[192,384]{1,0:T(8,128)(2,1)S(1)} collective-permute-done((bf16[192,384]{1,0:T(8,128)(2,1)S(1)}, bf16[192,384]{1,0:T(8,128)(2,1)S(1)}, u32[]{:S(2)}, u32[]{:S(2)}) %collective-permute-start.7) | collective-permute-done | bytes 147488 | tf_op jit(solution)/shard_map/ppermute | solution.py:378
  85.3 2.4 %shard_map.114 = (bf16[768,384]{1,0:T(8,128)(2,1)S(1)}, bf16[384,384]{1,0:T(8,128)(2,1)S(1)}, f32[768,384]{1,0:T(8,128)S(1)}, f32[384,384]{1,0:T(8,128)S(1)}, bf...) custom-call(bf16[768,384]{1,0:T(8,128)(2,1)S(1)} %get-tuple-element.89.k_ref, ...), custom_call_target="tpu_custom_call" | custom-call | tf_op jit(solution)/shard_map/pallas_call | solution.py:391
  87.7 5.1 %collective-permute-done.8.refs_4_ = bf16[192,384]{1,0:T(8,128)(2,1)S(1)} collective-permute-done((bf16[192,384]{1,0:T(8,128)(2,1)S(1)}, bf16[192,384]{1,0:T(8,128)(2,1)S(1)}, u32[]{:S(2)}, u32[]{:S(2)}) %collective-permute-start.8) | collective-permute-done | bytes 147488 | tf_op jit(solution)/shard_map/ppermute | solution.py:378
  93.7 2.6 %shard_map.109 = (bf16[768,384]{1,0:T(8,128)(2,1)S(1)}, bf16[384,384]{1,0:T(8,128)(2,1)S(1)}, f32[768,384]{1,0:T(8,128)S(1)}, f32[384,384]{1,0:T(8,128)S(1)}, bf...) custom-call(bf16[768,384]{1,0:T(8,128)(2,1)S(1)} %get-tuple-element.67.k_ref, ...), custom_call_target="tpu_custom_call" | custom-call | tf_op jit(solution)/shard_map/pallas_call | solution.py:391
  99.6 9.5 %collective-permute-done.20.refs_0_ = bf16[768,384]{1,0:T(8,128)(2,1)S(1)} collective-permute-done((bf16[768,384]{1,0:T(8,128)(2,1)S(1)}, bf16[768,384]{1,0:T(8,128)(2,1)S(1)}, u32[]{:S(2)}, u32[]{:S(2)}) %collective-permute-start.20) | collective-permute-done | bytes 589856 | tf_op jit(solution)/shard_map/ppermute | solution.py:293
  109.9 2.3 %shard_map.116.refs_0_ = bf16[2,768,768]{2,1,0:T(8,128)(2,1)} custom-call(bf16[768,384]{1,0:T(8,128)(2,1)S(1)} %get-tuple-element.114.q_ref, bf16[768,384]{1,0:T(8,128)(2,1)S(1)} %get-tuple-element.98.pgu_ref, bf16[384,384]{1,0:T(8,128)(2,1)S(1)} %get-tuple-element.103.pdown_ref), custom_call_target="tpu_custom_call" | custom-call | tf_op jit(solution)/shard_map/pallas_call | solution.py:411
  112.2 2.3 %shard_map.117.refs_1_ = bf16[2,768,768]{2,1,0:T(8,128)(2,1)} custom-call(bf16[768,384]{1,0:T(8,128)(2,1)S(1)} %get-tuple-element.113.q_ref, bf16[768,384]{1,0:T(8,128)(2,1)S(1)} %get-tuple-element.76.pgu_ref, bf16[384,384]{1,0:T(8,128)(2,1)S(1)} %get-tuple-element.81.pdown_ref, bf16[2,768,768]{2,1,0:T(8,128)(2,1)} %shard_map.116.refs_0_), custom_call_target="tpu_custom_call", output_to_operand_aliasing={{}: (3, {})} | custom-call | tf_op jit(solution)/shard_map/pallas_call | solution.py:411
  114.5 2.8 %shard_map.115 = (bf16[768,384]{1,0:T(8,128)(2,1)S(1)}, bf16[1,3,2,192,384]{4,3,2,1,0:T(8,128)(2,1)}, f32[1,3,2,192,384]{4,3,2,1,0:T(8,128)}) custom-call(f32[2,3]{1,0:T(2,128)S(1)} %bitcast.10, f32[2]{0:T(128)S(1)} %copy-done.1, bf16[768,384]{1,0:T(8,128)(2,1)S(1)} %get-tuple-element.107.old_ref, f32[768,384]{1,0:T(8,128)S(1)} %get-tuple-element.108.own_ref, ...), custom_call_target="tpu_custom_call" | custom-call | tf_op jit(solution)/shard_map/pallas_call | solution.py:428
  117.3 6.8 %collective-permute-done.21.refs_0_ = bf16[384,384]{1,0:T(8,128)(2,1)S(1)} collective-permute-done((bf16[384,384]{1,0:T(8,128)(2,1)S(1)}, bf16[384,384]{1,0:T(8,128)(2,1)S(1)}, u32[]{:S(2)}, u32[]{:S(2)}) %collective-permute-start.21) | collective-permute-done | bytes 294944 | tf_op jit(solution)/shard_map/ppermute | solution.py:293
  124.1 2.2 %shard_map.118 = (bf16[2,768,768]{2,1,0:T(8,128)(2,1)}, bf16[1,3,2,192,384]{4,3,2,1,0:T(8,128)(2,1)}, f32[1,3,2,192,384]{4,3,2,1,0:T(8,128)}) custom-call(f32[2,3]{1,0:T(2,128)S(1)} %bitcast.11, f32[2]{0:T(128)S(1)} %copy-done.1, bf16[384,384]{1,0:T(8,128)(2,1)S(1)} %get-tuple-element.104.old_ref, ...), custom_call_target="tpu_custom_call", output_to_operand_aliasing={{0}: (7, {}), {1}: (8, {}), {2}: (9, {})} | custom-call | tf_op jit(solution)/shard_map/pallas_call | solution.py:456
  126.4 2.8 %shard_map.119 = (bf16[768,384]{1,0:T(8,128)(2,1)S(1)}, bf16[1,3,2,192,384]{4,3,2,1,0:T(8,128)(2,1)}, f32[1,3,2,192,384]{4,3,2,1,0:T(8,128)}) custom-call(f32[2,3]{1,0:T(2,128)S(1)} %bitcast.12, f32[2]{0:T(128)S(1)} %copy-done.1, bf16[768,384]{1,0:T(8,128)(2,1)S(1)} %get-tuple-element.85.old_ref, ...), custom_call_target="tpu_custom_call", output_to_operand_aliasing={{1}: (7, {}), {2}: (8, {})} | custom-call | tf_op jit(solution)/shard_map/pallas_call | solution.py:428
  129.2 1.9 %shard_map.120 = (bf16[2,768,768]{2,1,0:T(8,128)(2,1)}, bf16[384,384]{1,0:T(8,128)(2,1)S(1)}, f32[384,384]{1,0:T(8,128)S(1)}) custom-call(f32[2,3]{1,0:T(2,128)S(1)} %bitcast.13, f32[2]{0:T(128)S(1)} %copy-done.1, bf16[384,384]{1,0:T(8,128)(2,1)S(1)} %get-tuple-element.82.old_ref, ...), custom_call_target="tpu_custom_call", output_to_operand_aliasing={{0}: (7, {})} | custom-call | tf_op jit(solution)/shard_map/pallas_call | solution.py:456
  (47 shorter events, 31.0 us)
Async XLA Ops:
  1.6 14.0 %collective-permute-start.11 = (bf16[3,192,384]{2,1,0:T(8,128)(2,1)S(1)}, bf16[3,192,384]{2,1,0:T(8,128)(2,1)S(1)}, u32[]{:S(2)}, u32[]{:S(2)}) collective-permute-start(bf16[3,192,384]{2,1,0:T(8,128)(2,1)S(1)} %shard_map.110.refs_0_), channel_id=1, source_target_pairs={{0,1},{1,0},{2,3},{3,2},{4,5},{5,4},{6,7},{7,6},{8,9},{9,8},{10,11... | collective-permute-start | bytes 1327112 | tf_op jit(solution)/shard_map/ppermute | solution.py:293
  5.6 19.5 %collective-permute-start = (bf16[3,192,384]{2,1,0:T(8,128)(2,1)S(1)}, bf16[3,192,384]{2,1,0:T(8,128)(2,1)S(1)}, u32[]{:S(2)}, u32[]{:S(2)}) collective-permute-start(bf16[3,192,384]{2,1,0:T(8,128)(2,1)S(1)} %shard_map.104.refs_0_), channel_id=1, source_target_pairs={{0,1},{1,0},{2,3},{3,2},{4,5},{5,4},{6,7},{7,6},{8,9},{9,8},{10,11... | collective-permute-start | bytes 1327112 | tf_op jit(solution)/shard_map/ppermute | solution.py:293
  18.9 18.8 %collective-permute-start.12 = (bf16[768,384]{1,0:T(8,128)(2,1)S(1)}, bf16[768,384]{1,0:T(8,128)(2,1)S(1)}, u32[]{:S(2)}, u32[]{:S(2)}) collective-permute-start(bf16[768,384]{1,0:T(8,128)(2,1)S(1)} %get-tuple-element.97), channel_id=1, source_target_pairs={{0,1},{1,0},{2,3},{3,2},{4,5},{5,4},{6,7},{7,6},{8,9},{9,8},{10,11... | collective-permute-start | bytes 1769480 | tf_op jit(solution)/shard_map/ppermute | solution.py:293
  28.4 34.1 %collective-permute-start.1 = (bf16[768,384]{1,0:T(8,128)(2,1)S(1)}, bf16[768,384]{1,0:T(8,128)(2,1)S(1)}, u32[]{:S(2)}, u32[]{:S(2)}) collective-permute-start(bf16[768,384]{1,0:T(8,128)(2,1)S(1)} %get-tuple-element.75), channel_id=1, source_target_pairs={{0,1},{1,0},{2,3},{3,2},{4,5},{5,4},{6,7},{7,6},{8,9},{9,8},{10,11... | collective-permute-start | bytes 1769480 | tf_op jit(solution)/shard_map/ppermute | solution.py:293
  31.4 0.8 collective-permute-start.5
  32.1 29.2 %collective-permute-start.14 = (bf16[384,384]{1,0:T(8,128)(2,1)S(1)}, bf16[384,384]{1,0:T(8,128)(2,1)S(1)}, u32[]{:S(2)}, u32[]{:S(2)}) collective-permute-start(bf16[384,384]{1,0:T(8,128)(2,1)S(1)} %get-tuple-element.101), channel_id=1, source_target_pairs={{0,1},{1,0},{2,3},{3,2},{4,5},{5,4},{6,7},{7,6},{8,9},{9,8},{10,11... | collective-permute-start | bytes 884744 | tf_op jit(solution)/shard_map/ppermute | solution.py:293
  32.2 27.8 %collective-permute-start.16 = (bf16[192,384]{1,0:T(8,128)(2,1)S(1)}, bf16[192,384]{1,0:T(8,128)(2,1)S(1)}, u32[]{:S(2)}, u32[]{:S(2)}) collective-permute-start(bf16[192,384]{1,0:T(8,128)(2,1)S(1)} %collective-permute-done.5), channel_id=1, source_target_pairs={{4,0},{5,1}} | collective-permute-start | bytes 442376 | tf_op jit(solution)/shard_map/ppermute | solution.py:378
  39.0 45.0 %collective-permute-start.13 = (bf16[768,384]{1,0:T(8,128)(2,1)S(1)}, bf16[768,384]{1,0:T(8,128)(2,1)S(1)}, u32[]{:S(2)}, u32[]{:S(2)}) collective-permute-start(bf16[768,384]{1,0:T(8,128)(2,1)S(1)} %get-tuple-element.98.pgu_ref), channel_id=1, source_target_pairs={{0,2},{2,4},{4,6},{6,8},{8,10},{10,12},{12,14},{14,16},{16,18},{18... | collective-permute-start | bytes 1769480 | tf_op jit(solution)/shard_map/ppermute | solution.py:296
  40.3 32.2 %collective-permute-start.3 = (bf16[384,384]{1,0:T(8,128)(2,1)S(1)}, bf16[384,384]{1,0:T(8,128)(2,1)S(1)}, u32[]{:S(2)}, u32[]{:S(2)}) collective-permute-start(bf16[384,384]{1,0:T(8,128)(2,1)S(1)} %get-tuple-element.79), channel_id=1, source_target_pairs={{0,1},{1,0},{2,3},{3,2},{4,5},{5,4},{6,7},{7,6},{8,9},{9,8},{10,11... | collective-permute-start | bytes 884744 | tf_op jit(solution)/shard_map/ppermute | solution.py:293
  60.0 7.0 %collective-permute-start.17 = (bf16[192,384]{1,0:T(8,128)(2,1)S(1)}, bf16[192,384]{1,0:T(8,128)(2,1)S(1)}, u32[]{:S(2)}, u32[]{:S(2)}) collective-permute-start(bf16[192,384]{1,0:T(8,128)(2,1)S(1)} %collective-permute-done.5), channel_id=1, source_target_pairs={{8,0},{9,1}} | collective-permute-start | bytes 442376 | tf_op jit(solution)/shard_map/ppermute | solution.py:378
  61.3 7.9 %collective-permute-start.18 = (bf16[192,384]{1,0:T(8,128)(2,1)S(1)}, bf16[192,384]{1,0:T(8,128)(2,1)S(1)}, u32[]{:S(2)}, u32[]{:S(2)}) collective-permute-start(bf16[192,384]{1,0:T(8,128)(2,1)S(1)} %collective-permute-done.5), channel_id=1, source_target_pairs={{12,0},{13,1}} | collective-permute-start | bytes 442376 | tf_op jit(solution)/shard_map/ppermute | solution.py:378
  62.6 7.9 %collective-permute-start.6 = (bf16[192,384]{1,0:T(8,128)(2,1)S(1)}, bf16[192,384]{1,0:T(8,128)(2,1)S(1)}, u32[]{:S(2)}, u32[]{:S(2)}) collective-permute-start(bf16[192,384]{1,0:T(8,128)(2,1)S(1)} %collective-permute-done.5), channel_id=1, source_target_pairs={{16,0},{17,1}} | collective-permute-start | bytes 442376 | tf_op jit(solution)/shard_map/ppermute | solution.py:378
  67.0 26.7 %collective-permute-start.2 = (bf16[768,384]{1,0:T(8,128)(2,1)S(1)}, bf16[768,384]{1,0:T(8,128)(2,1)S(1)}, u32[]{:S(2)}, u32[]{:S(2)}) collective-permute-start(bf16[768,384]{1,0:T(8,128)(2,1)S(1)} %get-tuple-element.76.pgu_ref), channel_id=1, source_target_pairs={{0,2},{2,4},{4,6},{6,8},{8,10},{10,12},{12,14},{14,16},{16,18},{18... | collective-permute-start | bytes 1769480 | tf_op jit(solution)/shard_map/ppermute | solution.py:296
  69.2 13.4 %collective-permute-start.15 = (bf16[384,384]{1,0:T(8,128)(2,1)S(1)}, bf16[384,384]{1,0:T(8,128)(2,1)S(1)}, u32[]{:S(2)}, u32[]{:S(2)}) collective-permute-start(bf16[384,384]{1,0:T(8,128)(2,1)S(1)} %get-tuple-element.103.pdown_ref), channel_id=1, source_target_pairs={{0,2},{2,4},{4,6},{6,8},{8,10},{10,12},{12,14},{14,16},{16,18},{18... | collective-permute-start | bytes 884744 | tf_op jit(solution)/shard_map/ppermute | solution.py:296
  70.5 27.9 %collective-permute-start.19 = (bf16[1152,384]{1,0:T(8,128)(2,1)S(1)}, bf16[1152,384]{1,0:T(8,128)(2,1)S(1)}, u32[]{:S(2)}, u32[]{:S(2)}) collective-permute-start(bf16[1152,384]{1,0:T(8,128)(2,1)S(1)} %get-tuple-element.106), channel_id=1, source_target_pairs={{0,2},{2,4},{4,6},{6,8},{8,10},{10,12},{12,14},{14,16},{16,18},{18... | collective-permute-start | bytes 2654216 | tf_op jit(solution)/shard_map/ppermute | solution.py:296
  72.5 8.8 %collective-permute-start.7 = (bf16[192,384]{1,0:T(8,128)(2,1)S(1)}, bf16[192,384]{1,0:T(8,128)(2,1)S(1)}, u32[]{:S(2)}, u32[]{:S(2)}) collective-permute-start(bf16[192,384]{1,0:T(8,128)(2,1)S(1)} %collective-permute-done.5), channel_id=1, source_target_pairs={{20,0},{21,1}} | collective-permute-start | bytes 442376 | tf_op jit(solution)/shard_map/ppermute | solution.py:378
  81.3 12.4 %collective-permute-start.4 = (bf16[384,384]{1,0:T(8,128)(2,1)S(1)}, bf16[384,384]{1,0:T(8,128)(2,1)S(1)}, u32[]{:S(2)}, u32[]{:S(2)}) collective-permute-start(bf16[384,384]{1,0:T(8,128)(2,1)S(1)} %get-tuple-element.81.pdown_ref), channel_id=1, source_target_pairs={{0,2},{2,4},{4,6},{6,8},{8,10},{10,12},{12,14},{14,16},{16,18},{18... | collective-permute-start | bytes 884744 | tf_op jit(solution)/shard_map/ppermute | solution.py:296
  82.6 43.7 %collective-permute-start.9 = (bf16[1152,384]{1,0:T(8,128)(2,1)S(1)}, bf16[1152,384]{1,0:T(8,128)(2,1)S(1)}, u32[]{:S(2)}, u32[]{:S(2)}) collective-permute-start(bf16[1152,384]{1,0:T(8,128)(2,1)S(1)} %get-tuple-element.84), channel_id=1, source_target_pairs={{0,2},{2,4},{4,6},{6,8},{8,10},{10,12},{12,14},{14,16},{16,18},{18... | collective-permute-start | bytes 2654216 | tf_op jit(solution)/shard_map/ppermute | solution.py:296
  84.0 8.8 %collective-permute-start.8 = (bf16[192,384]{1,0:T(8,128)(2,1)S(1)}, bf16[192,384]{1,0:T(8,128)(2,1)S(1)}, u32[]{:S(2)}, u32[]{:S(2)}) collective-permute-start(bf16[192,384]{1,0:T(8,128)(2,1)S(1)} %collective-permute-done.5), channel_id=1, source_target_pairs={{24,0},{25,1}} | collective-permute-start | bytes 442376 | tf_op jit(solution)/shard_map/ppermute | solution.py:378
  92.8 16.2 %collective-permute-start.20 = (bf16[768,384]{1,0:T(8,128)(2,1)S(1)}, bf16[768,384]{1,0:T(8,128)(2,1)S(1)}, u32[]{:S(2)}, u32[]{:S(2)}) collective-permute-start(bf16[768,384]{1,0:T(8,128)(2,1)S(1)} %get-tuple-element.110), channel_id=1, source_target_pairs={{0,1},{1,0},{2,3},{3,2},{4,5},{5,4},{6,7},{7,6},{8,9},{9,8},{10,11... | collective-permute-start | bytes 1769480 | tf_op jit(solution)/shard_map/ppermute | solution.py:293
  96.3 30.0 %collective-permute-start.10 = (bf16[768,384]{1,0:T(8,128)(2,1)S(1)}, bf16[768,384]{1,0:T(8,128)(2,1)S(1)}, u32[]{:S(2)}, u32[]{:S(2)}) collective-permute-start(bf16[768,384]{1,0:T(8,128)(2,1)S(1)} %get-tuple-element.88), channel_id=1, source_target_pairs={{0,1},{1,0},{2,3},{3,2},{4,5},{5,4},{6,7},{7,6},{8,9},{9,8},{10,11... | collective-permute-start | bytes 1769480 | tf_op jit(solution)/shard_map/ppermute | solution.py:293
  97.5 26.6 %collective-permute-start.21 = (bf16[384,384]{1,0:T(8,128)(2,1)S(1)}, bf16[384,384]{1,0:T(8,128)(2,1)S(1)}, u32[]{:S(2)}, u32[]{:S(2)}) collective-permute-start(bf16[384,384]{1,0:T(8,128)(2,1)S(1)} %get-tuple-element.112), channel_id=1, source_target_pairs={{0,1},{1,0},{2,3},{3,2},{4,5},{5,4},{6,7},{7,6},{8,9},{9,8},{10,11... | collective-permute-start | bytes 884744 | tf_op jit(solution)/shard_map/ppermute | solution.py:293
  98.4 30.7 %collective-permute-start.23 = (bf16[256,384]{1,0:T(8,128)(2,1)S(1)}, bf16[256,384]{1,0:T(8,128)(2,1)S(1)}, u32[]{:S(2)}, u32[]{:S(2)}) collective-permute-start(bf16[256,384]{1,0:T(8,128)(2,1)S(1)} %get-tuple-element.121), channel_id=1, source_target_pairs={{0,1},{1,0},{2,3},{3,2},{4,5},{5,4},{6,7},{7,6},{8,9},{9,8},{10,11... | collective-permute-start | bytes 589832 | tf_op jit(solution)/shard_map/ppermute | solution.py:293
  109.0 22.0 %collective-permute-start.22 = (bf16[128,384]{1,0:T(8,128)(2,1)S(1)}, bf16[128,384]{1,0:T(8,128)(2,1)S(1)}, u32[]{:S(2)}, u32[]{:S(2)}) collective-permute-start(bf16[128,384]{1,0:T(8,128)(2,1)S(1)} %get-tuple-element.120), channel_id=1, source_target_pairs={{0,1},{1,0},{2,3},{3,2},{4,5},{5,4},{6,7},{7,6},{8,9},{9,8},{10,11... | collective-permute-start | bytes 294920 | tf_op jit(solution)/shard_map/ppermute | solution.py:293
  (2 other events, 22.6 us)

commit v7 on v6

--- a/solution.py
+++ b/solution.py
@@ -11,7 +11,6 @@
 F32 = jnp.float32
 BF16 = jnp.bfloat16
 VMEM = pl.BlockSpec(memory_space=pltpu.VMEM)
-SMEM = pl.BlockSpec(memory_space=pltpu.SMEM)
 HBM = pl.BlockSpec(memory_space=pltpu.HBM)
 DMA = pltpu.SemaphoreType.DMA
 
@@ -110,7 +109,7 @@
     me = lax.axis_index("tok")
     assemble(me, [lambda m, ref=ref: ref[m] for ref in shards], gu_ref, down_ref)
     grads_core(divisor, k_ref, v_ref, gu_ref, down_ref, own_gu, own_down, hid_s, dout_s, dgu_s)
-    decay = decay_ref[head]
+    decay = decay_ref[:, head : head + 1]
     mine = pl.multiple_of(me * part, part)
     own_gu[pl.ds(mine, part), :] += decay * m_ref[0]
     own_gu[pl.ds(width + mine, part), :] += decay * m_ref[1]
@@ -167,7 +166,7 @@
     for i, m in enumerate(mats):
         at = pl.ds(i * width, width)
         moment = summed(own_ref, recvs, i * width, width)
-        new_ref[at, :] = updated(rate_ref[head, m], old_ref, at, moment)
+        new_ref[at, :] = updated(rate_ref[head : head + 1, m : m + 1], old_ref, at, moment)
         moment_ref[m * width : (m + 1) * width, :] = moment.astype(BF16)
 
 
@@ -193,10 +192,10 @@
     stores = []
     for m in range(2):
         at = pl.ds(m * width, width)
-        moment = decay_ref[head] * earlier_ref[at, :].astype(F32)
+        moment = decay_ref[:, head : head + 1] * earlier_ref[at, :].astype(F32)
         moment = moment + summed(own_ref, recvs, m * width, width)
         new_s = gu_s.at[at, :]
-        new_s[...] = updated(rate_ref[head, m], old_ref, at, moment)
+        new_s[...] = updated(rate_ref[head : head + 1, m : m + 1], old_ref, at, moment)
         moment_s[...] = moment
         stores += store_mine(
             n,
@@ -232,9 +231,9 @@
         new_s[:first, :] = before_new[:first, :]
         kept_s[:first, :] = before_kept[:first, :]
     at = pl.ds(first, size)
-    moment = decay_ref[head] * earlier_ref[pl.ds(2 * width + first, size), :].astype(F32)
+    moment = decay_ref[:, head : head + 1] * earlier_ref[pl.ds(2 * width + first, size), :].astype(F32)
     moment = moment + summed(own_ref, recvs, first, size, first)
-    new_s[at, :] = updated(rate_ref[head, 2], old_ref, at, moment)
+    new_s[at, :] = updated(rate_ref[head : head + 1, 2:], old_ref, at, moment)
     kept_s[at, :] = moment
     stores = []
     if last:
@@ -284,6 +283,7 @@
     moment_t = jnp.swapaxes(moment_in, 3, 4)
     begin_t = jnp.swapaxes(initial_fast, 2, 3)
     rates = rates.T
+    decays = decays.reshape(1, heads)
     keys, values, queries, fast_t, moment_t, begin_t = (
         pltpu.with_memory_space_constraint(x, pltpu.HBM)
         for x in (keys, values, queries, fast_t, moment_t, begin_t)
@@ -345,7 +345,7 @@
         call(
             functools.partial(grads_one, n, h, divisor),
             grad_out,
-            [SMEM] + [VMEM] * (3 + n),
+            [VMEM] * (4 + n),
             (VMEM,) * 6,
             grad_scratch,
         )(decays, *kvq[0][h][:2], m_own[h], owned[h], *recv_fast[h])
@@ -363,7 +363,7 @@
             new, *moment = call(
                 functools.partial(update_one, n, h, mats),
                 (shape(len(mats) * width, width), shape(3 * width, width)),
-                [SMEM] + [VMEM] * (1 + n + len(moment)),
+                [VMEM] * (2 + n + len(moment)),
                 (VMEM, VMEM),
                 aliases={2 + n: 1} if moment else None,
             )(rates, old, own, *recvs, *moment)
@@ -428,7 +428,7 @@
         hq, *ends = call(
             functools.partial(update_two_gu, n, h),
             (shape(rows, width), fast_shape, moment_shape),
-            [SMEM] * 2 + [VMEM] * (3 + n) + [HBM] * len(ends),
+            [VMEM] * (5 + n) + [HBM] * len(ends),
             (VMEM, HBM, HBM),
             (
                 pltpu.VMEM((2 * width, width), BF16),
@@ -456,7 +456,7 @@
             outputs, *rest = call(
                 functools.partial(update_two_down, n, h, first_row),
                 outs,
-                [SMEM] * 2 + [VMEM] * (3 + n + len(kept)) + [HBM] * (len(extra) - len(kept)),
+                [VMEM] * (5 + n + len(kept)) + [HBM] * (len(extra) - len(kept)),
                 (HBM,) * 3 if last else (HBM, VMEM, VMEM),
                 (buffers if last else ())
                 + (pltpu.VMEM((rows, size), BF16),)

time: 134 us -> 129 us (0.963)
  Pallas kernels: 38.8 us -> 32.1 us
  waiting for transfers between devices: 62 us -> 64.6 us
    pallas_call x5, Pallas kernels: 12.6 us -> 10.1 us  [the longest x2 5.61 us: on_device(): call(functools.partial(grads_one, n, h, divisor), grad_out, [VMEM] * (4 +...]
    pallas_call x2, Pallas kernels: 5.61 us -> 3.44 us  [on_device(): call(functools.partial(update_two_gu, n, h), (shape(rows, width), fast_sh...]
    pallas_call x4, Pallas kernels: 4.25 us -> 2.14 us  [on_device(): call(functools.partial(update_one, n, h, mats), (shape(len(mats) * width,...]
    ppermute x6, waiting for transfers between devices: 31.2 us -> 33.3 us  [on_device(): lax.ppermute(x, ('block', 'tok'), [(sources[p] * n + i, i) for i in range...]
  transfers between devices with their start and end apart: 24 -> 24, of which waited for: 10 -> 10; matrix products, arithmetic and copies ran while one was open for 0% -> 0% of each run, Pallas kernels for 27% -> 23%
where the time goes in v7:
time: 129 us
  waiting for transfers between devices  64.6 us (50%)
  Pallas kernels  32.1 us (25%)
  starting transfers between devices  31.2 us (24%)
    ppermute x6, waiting for transfers between devices, on_device(): lax.ppermute(x, ('block', 'tok'), [(sources[p] * n + i, i) for i in range...  33.3 us
    ppermute x11, waiting for transfers between devices, turned(): lax.ppermute(x, 'tok', [(i, (i + r) % n) for i in range(n)])  31.3 us
    ppermute x11, starting transfers between devices, turned(): lax.ppermute(x, 'tok', [(i, (i + r) % n) for i in range(n)])  14.9 us
    ppermute x6, starting transfers between devices, forward(): return lax.ppermute(x, 'block', [(i, i + 1) for i in range(blocks - 1)])  7.93 us
    ppermute x6, starting transfers between devices, on_device(): lax.ppermute(x, ('block', 'tok'), [(sources[p] * n + i, i) for i in range...  7.73 us
    pallas_call x2, Pallas kernels, on_device(): call(functools.partial(grads_one, n, h, divisor), grad_out, [VMEM] * (4 +...  5.61 us
    pallas_call x2, Pallas kernels, on_device(): call(functools.partial(grads_two, n, divisor), (shape(2 * width, width),...  4.99 us
    pallas_call x2, Pallas kernels, on_device(): call(functools.partial(apply_one, h), out_shape, [VMEM] * 3 + [HBM] * len...  4.54 us
  transfers between devices with their start and end apart: 24, of which 10 were waited for; matrix products, arithmetic and copies ran while one was open for 0% of the time, Pallas kernels for 23%

profile of v7, /device:TPU:0, one launch (start us, length us, event | category | flops | bytes accessed | tf_op | source)
XLA Modules:
  0.0 129.0 jit_solution(18113493089493605721)
XLA Ops:
  1.6 3.0 %collective-permute-start.11 = (bf16[3,192,384]{2,1,0:T(8,128)(2,1)S(1)}, bf16[3,192,384]{2,1,0:T(8,128)(2,1)S(1)}, u32[]{:S(2)}, u32[]{:S(2)}) collective-permute-start(bf16[3,192,384]{2,1,0:T(8,128)(2,1)S(1)} %shard_map.110.refs_0_), channel_id=1, source_target_pairs={{0,1},{1,0},{2,3},{3,2},{4,5},{5,4},{6,7},{7,6},{8,9},{9,8},{10,11... | collective-permute-start | bytes 1327112 | tf_op jit(solution)/shard_map/ppermute | solution.py:293
  5.6 3.9 %shard_map.103 = (bf16[768,384]{1,0:T(8,128)(2,1)S(1)}, bf16[768,384]{1,0:T(8,128)(2,1)S(1)}, bf16[768,384]{1,0:T(8,128)(2,1)S(1)}, bf16[768,384]{1,0:T(8,128)(2...) custom-call(bf16[2,768,768]{2,1,0:T(8,128)(2,1)} %k_ref.1, ...), custom_call_target="tpu_custom_call" | custom-call | tf_op jit(solution)/shard_map/pallas_call | solution.py:331
  9.5 6.1 %collective-permute-done.11.refs_1_ = bf16[3,192,384]{2,1,0:T(8,128)(2,1)S(1)} collective-permute-done((bf16[3,192,384]{2,1,0:T(8,128)(2,1)S(1)}, bf16[3,192,384]{2,1,0:T(8,128)(2,1)S(1)}, u32[]{:S(2)}, u32[]{:S(2)}) %collective-permute-start.11) | collective-permute-done | bytes 442400 | tf_op jit(solution)/shard_map/ppermute | solution.py:293
  15.6 2.8 %shard_map.111 = (bf16[768,384]{1,0:T(8,128)(2,1)S(1)}, bf16[384,384]{1,0:T(8,128)(2,1)S(1)}, bf16[768,384]{1,0:T(8,128)(2,1)S(1)}, bf16[384,384]{1,0:T(8,128)(2...) custom-call(f32[1,2]{1,0:T(1,128)S(1)} %bitcast.16, bf16[768,384]{1,0:T(8,128)(2,1)S(1)} %get-tuple-element.92.k_ref, ...), custom_call_target="tpu_custom_call" | custom-call | tf_op jit(solution)/shard_map/pallas_call | solution.py:345
  18.4 2.1 %collective-permute-start.12 = (bf16[768,384]{1,0:T(8,128)(2,1)S(1)}, bf16[768,384]{1,0:T(8,128)(2,1)S(1)}, u32[]{:S(2)}, u32[]{:S(2)}) collective-permute-start(bf16[768,384]{1,0:T(8,128)(2,1)S(1)} %get-tuple-element.97), channel_id=1, source_target_pairs={{0,1},{1,0},{2,3},{3,2},{4,5},{5,4},{6,7},{7,6},{8,9},{9,8},{10,11... | collective-permute-start | bytes 1769480 | tf_op jit(solution)/shard_map/ppermute | solution.py:293
  20.5 4.6 %collective-permute-done.refs_1_ = bf16[3,192,384]{2,1,0:T(8,128)(2,1)S(1)} collective-permute-done((bf16[3,192,384]{2,1,0:T(8,128)(2,1)S(1)}, bf16[3,192,384]{2,1,0:T(8,128)(2,1)S(1)}, u32[]{:S(2)}, u32[]{:S(2)}) %collective-permute-start) | collective-permute-done | bytes 442400 | tf_op jit(solution)/shard_map/ppermute | solution.py:293
  25.1 2.8 %shard_map.105 = (bf16[768,384]{1,0:T(8,128)(2,1)S(1)}, bf16[384,384]{1,0:T(8,128)(2,1)S(1)}, bf16[768,384]{1,0:T(8,128)(2,1)S(1)}, bf16[384,384]{1,0:T(8,128)(2...) custom-call(f32[1,2]{1,0:T(1,128)S(1)} %bitcast.17, bf16[768,384]{1,0:T(8,128)(2,1)S(1)} %get-tuple-element.70.k_ref, ...), custom_call_target="tpu_custom_call" | custom-call | tf_op jit(solution)/shard_map/pallas_call | solution.py:345
  27.9 2.1 %collective-permute-start.1 = (bf16[768,384]{1,0:T(8,128)(2,1)S(1)}, bf16[768,384]{1,0:T(8,128)(2,1)S(1)}, u32[]{:S(2)}, u32[]{:S(2)}) collective-permute-start(bf16[768,384]{1,0:T(8,128)(2,1)S(1)} %get-tuple-element.75), channel_id=1, source_target_pairs={{0,1},{1,0},{2,3},{3,2},{4,5},{5,4},{6,7},{7,6},{8,9},{9,8},{10,11... | collective-permute-start | bytes 1769480 | tf_op jit(solution)/shard_map/ppermute | solution.py:293
  33.0 4.8 %collective-permute-done.12.refs_0_ = bf16[768,384]{1,0:T(8,128)(2,1)S(1)} collective-permute-done((bf16[768,384]{1,0:T(8,128)(2,1)S(1)}, bf16[768,384]{1,0:T(8,128)(2,1)S(1)}, u32[]{:S(2)}, u32[]{:S(2)}) %collective-permute-start.12) | collective-permute-done | bytes 589856 | tf_op jit(solution)/shard_map/ppermute | solution.py:293
  39.8 2.1 %collective-permute-start.3 = (bf16[384,384]{1,0:T(8,128)(2,1)S(1)}, bf16[384,384]{1,0:T(8,128)(2,1)S(1)}, u32[]{:S(2)}, u32[]{:S(2)}) collective-permute-start(bf16[384,384]{1,0:T(8,128)(2,1)S(1)} %get-tuple-element.79), channel_id=1, source_target_pairs={{0,1},{1,0},{2,3},{3,2},{4,5},{5,4},{6,7},{7,6},{8,9},{9,8},{10,11... | collective-permute-start | bytes 884744 | tf_op jit(solution)/shard_map/ppermute | solution.py:293
  41.9 18.1 %collective-permute-done.16.refs_2_ = bf16[192,384]{1,0:T(8,128)(2,1)S(1)} collective-permute-done((bf16[192,384]{1,0:T(8,128)(2,1)S(1)}, bf16[192,384]{1,0:T(8,128)(2,1)S(1)}, u32[]{:S(2)}, u32[]{:S(2)}) %collective-permute-start.16) | collective-permute-done | bytes 147488 | tf_op jit(solution)/shard_map/ppermute | solution.py:378
  65.0 2.0 %collective-permute-done.17.refs_3_ = bf16[192,384]{1,0:T(8,128)(2,1)S(1)} collective-permute-done((bf16[192,384]{1,0:T(8,128)(2,1)S(1)}, bf16[192,384]{1,0:T(8,128)(2,1)S(1)}, u32[]{:S(2)}, u32[]{:S(2)}) %collective-permute-start.17) | collective-permute-done | bytes 147488 | tf_op jit(solution)/shard_map/ppermute | solution.py:378
  73.6 7.2 %collective-permute-done.7.refs_3_ = bf16[192,384]{1,0:T(8,128)(2,1)S(1)} collective-permute-done((bf16[192,384]{1,0:T(8,128)(2,1)S(1)}, bf16[192,384]{1,0:T(8,128)(2,1)S(1)}, u32[]{:S(2)}, u32[]{:S(2)}) %collective-permute-start.7) | collective-permute-done | bytes 147488 | tf_op jit(solution)/shard_map/ppermute | solution.py:378
  84.7 2.4 %shard_map.114 = (bf16[768,384]{1,0:T(8,128)(2,1)S(1)}, bf16[384,384]{1,0:T(8,128)(2,1)S(1)}, f32[768,384]{1,0:T(8,128)S(1)}, f32[384,384]{1,0:T(8,128)S(1)}, bf...) custom-call(bf16[768,384]{1,0:T(8,128)(2,1)S(1)} %get-tuple-element.89.k_ref, ...), custom_call_target="tpu_custom_call" | custom-call | tf_op jit(solution)/shard_map/pallas_call | solution.py:391
  87.1 5.1 %collective-permute-done.8.refs_4_ = bf16[192,384]{1,0:T(8,128)(2,1)S(1)} collective-permute-done((bf16[192,384]{1,0:T(8,128)(2,1)S(1)}, bf16[192,384]{1,0:T(8,128)(2,1)S(1)}, u32[]{:S(2)}, u32[]{:S(2)}) %collective-permute-start.8) | collective-permute-done | bytes 147488 | tf_op jit(solution)/shard_map/ppermute | solution.py:378
  93.7 2.6 %shard_map.109 = (bf16[768,384]{1,0:T(8,128)(2,1)S(1)}, bf16[384,384]{1,0:T(8,128)(2,1)S(1)}, f32[768,384]{1,0:T(8,128)S(1)}, f32[384,384]{1,0:T(8,128)S(1)}, bf...) custom-call(bf16[768,384]{1,0:T(8,128)(2,1)S(1)} %get-tuple-element.67.k_ref, ...), custom_call_target="tpu_custom_call" | custom-call | tf_op jit(solution)/shard_map/pallas_call | solution.py:391
  96.9 1.5 %collective-permute-start.21 = (bf16[384,384]{1,0:T(8,128)(2,1)S(1)}, bf16[384,384]{1,0:T(8,128)(2,1)S(1)}, u32[]{:S(2)}, u32[]{:S(2)}) collective-permute-start(bf16[384,384]{1,0:T(8,128)(2,1)S(1)} %get-tuple-element.112), channel_id=1, source_target_pairs={{0,1},{1,0},{2,3},{3,2},{4,5},{5,4},{6,7},{7,6},{8,9},{9,8},{10,11... | collective-permute-start | bytes 884744 | tf_op jit(solution)/shard_map/ppermute | solution.py:293
  99.0 9.5 %collective-permute-done.20.refs_0_ = bf16[768,384]{1,0:T(8,128)(2,1)S(1)} collective-permute-done((bf16[768,384]{1,0:T(8,128)(2,1)S(1)}, bf16[768,384]{1,0:T(8,128)(2,1)S(1)}, u32[]{:S(2)}, u32[]{:S(2)}) %collective-permute-start.20) | collective-permute-done | bytes 589856 | tf_op jit(solution)/shard_map/ppermute | solution.py:293
  109.9 2.3 %shard_map.116.refs_0_ = bf16[2,768,768]{2,1,0:T(8,128)(2,1)} custom-call(bf16[768,384]{1,0:T(8,128)(2,1)S(1)} %get-tuple-element.114.q_ref, bf16[768,384]{1,0:T(8,128)(2,1)S(1)} %get-tuple-element.98.pgu_ref, bf16[384,384]{1,0:T(8,128)(2,1)S(1)} %get-tuple-element.103.pdown_ref), custom_call_target="tpu_custom_call" | custom-call | tf_op jit(solution)/shard_map/pallas_call | solution.py:411
  112.2 2.3 %shard_map.117.refs_1_ = bf16[2,768,768]{2,1,0:T(8,128)(2,1)} custom-call(bf16[768,384]{1,0:T(8,128)(2,1)S(1)} %get-tuple-element.113.q_ref, bf16[768,384]{1,0:T(8,128)(2,1)S(1)} %get-tuple-element.76.pgu_ref, bf16[384,384]{1,0:T(8,128)(2,1)S(1)} %get-tuple-element.81.pdown_ref, bf16[2,768,768]{2,1,0:T(8,128)(2,1)} %shard_map.116.refs_0_), custom_call_target="tpu_custom_call", output_to_operand_aliasing={{}: (3, {})} | custom-call | tf_op jit(solution)/shard_map/pallas_call | solution.py:411
  114.5 1.7 %shard_map.115 = (bf16[768,384]{1,0:T(8,128)(2,1)S(1)}, bf16[1,3,2,192,384]{4,3,2,1,0:T(8,128)(2,1)}, f32[1,3,2,192,384]{4,3,2,1,0:T(8,128)}) custom-call(f32[2,3]{1,0:T(2,128)S(1)} %bitcast.11, f32[1,2]{1,0:T(1,128)S(1)} %bitcast.18, bf16[768,384]{1,0:T(8,128)(2,1)S(1)} %get-tuple-element.107.old_ref, f32[768,384]{1,0:T(8,128)S(1)} %get-tuple-element.108.own_ref, ...), custom_call_target="tpu_custom_call" | custom-call | tf_op jit(solution)/shard_map/pallas_call | solution.py:428
  116.2 6.3 %collective-permute-done.21.refs_0_ = bf16[384,384]{1,0:T(8,128)(2,1)S(1)} collective-permute-done((bf16[384,384]{1,0:T(8,128)(2,1)S(1)}, bf16[384,384]{1,0:T(8,128)(2,1)S(1)}, u32[]{:S(2)}, u32[]{:S(2)}) %collective-permute-start.21) | collective-permute-done | bytes 294944 | tf_op jit(solution)/shard_map/ppermute | solution.py:293
  122.6 1.7 %shard_map.118 = (bf16[2,768,768]{2,1,0:T(8,128)(2,1)}, bf16[1,3,2,192,384]{4,3,2,1,0:T(8,128)(2,1)}, f32[1,3,2,192,384]{4,3,2,1,0:T(8,128)}) custom-call(f32[2,3]{1,0:T(2,128)S(1)} %bitcast.12, f32[1,2]{1,0:T(1,128)S(1)} %bitcast.19, bf16[384,384]{1,0:T(8,128)(2,1)S(1)} %get-tuple-element.104.old_ref, ...), custom_call_target="tpu_custom_call", output_to_operand_aliasing={{0}: (7, {}), {1}: (8, {}), {2}: (9, {})} | custom-call | tf_op jit(solution)/shard_map/pallas_call | solution.py:456
  124.3 1.7 %shard_map.119 = (bf16[768,384]{1,0:T(8,128)(2,1)S(1)}, bf16[1,3,2,192,384]{4,3,2,1,0:T(8,128)(2,1)}, f32[1,3,2,192,384]{4,3,2,1,0:T(8,128)}) custom-call(f32[2,3]{1,0:T(2,128)S(1)} %bitcast.13, f32[1,2]{1,0:T(1,128)S(1)} %bitcast.20, bf16[768,384]{1,0:T(8,128)(2,1)S(1)} %get-tuple-element.85.old_ref, ...), custom_call_target="tpu_custom_call", output_to_operand_aliasing={{1}: (7, {}), {2}: (8, {})} | custom-call | tf_op jit(solution)/shard_map/pallas_call | solution.py:428
  (47 shorter events, 29.3 us)
Async XLA Ops:
  1.6 14.0 %collective-permute-start.11 = (bf16[3,192,384]{2,1,0:T(8,128)(2,1)S(1)}, bf16[3,192,384]{2,1,0:T(8,128)(2,1)S(1)}, u32[]{:S(2)}, u32[]{:S(2)}) collective-permute-start(bf16[3,192,384]{2,1,0:T(8,128)(2,1)S(1)} %shard_map.110.refs_0_), channel_id=1, source_target_pairs={{0,1},{1,0},{2,3},{3,2},{4,5},{5,4},{6,7},{7,6},{8,9},{9,8},{10,11... | collective-permute-start | bytes 1327112 | tf_op jit(solution)/shard_map/ppermute | solution.py:293
  5.6 19.5 %collective-permute-start = (bf16[3,192,384]{2,1,0:T(8,128)(2,1)S(1)}, bf16[3,192,384]{2,1,0:T(8,128)(2,1)S(1)}, u32[]{:S(2)}, u32[]{:S(2)}) collective-permute-start(bf16[3,192,384]{2,1,0:T(8,128)(2,1)S(1)} %shard_map.104.refs_0_), channel_id=1, source_target_pairs={{0,1},{1,0},{2,3},{3,2},{4,5},{5,4},{6,7},{7,6},{8,9},{9,8},{10,11... | collective-permute-start | bytes 1327112 | tf_op jit(solution)/shard_map/ppermute | solution.py:293
  18.4 19.3 %collective-permute-start.12 = (bf16[768,384]{1,0:T(8,128)(2,1)S(1)}, bf16[768,384]{1,0:T(8,128)(2,1)S(1)}, u32[]{:S(2)}, u32[]{:S(2)}) collective-permute-start(bf16[768,384]{1,0:T(8,128)(2,1)S(1)} %get-tuple-element.97), channel_id=1, source_target_pairs={{0,1},{1,0},{2,3},{3,2},{4,5},{5,4},{6,7},{7,6},{8,9},{9,8},{10,11... | collective-permute-start | bytes 1769480 | tf_op jit(solution)/shard_map/ppermute | solution.py:293
  27.9 34.6 %collective-permute-start.1 = (bf16[768,384]{1,0:T(8,128)(2,1)S(1)}, bf16[768,384]{1,0:T(8,128)(2,1)S(1)}, u32[]{:S(2)}, u32[]{:S(2)}) collective-permute-start(bf16[768,384]{1,0:T(8,128)(2,1)S(1)} %get-tuple-element.75), channel_id=1, source_target_pairs={{0,1},{1,0},{2,3},{3,2},{4,5},{5,4},{6,7},{7,6},{8,9},{9,8},{10,11... | collective-permute-start | bytes 1769480 | tf_op jit(solution)/shard_map/ppermute | solution.py:293
  30.9 0.8 collective-permute-start.5
  31.6 29.7 %collective-permute-start.14 = (bf16[384,384]{1,0:T(8,128)(2,1)S(1)}, bf16[384,384]{1,0:T(8,128)(2,1)S(1)}, u32[]{:S(2)}, u32[]{:S(2)}) collective-permute-start(bf16[384,384]{1,0:T(8,128)(2,1)S(1)} %get-tuple-element.101), channel_id=1, source_target_pairs={{0,1},{1,0},{2,3},{3,2},{4,5},{5,4},{6,7},{7,6},{8,9},{9,8},{10,11... | collective-permute-start | bytes 884744 | tf_op jit(solution)/shard_map/ppermute | solution.py:293
  31.7 28.3 %collective-permute-start.16 = (bf16[192,384]{1,0:T(8,128)(2,1)S(1)}, bf16[192,384]{1,0:T(8,128)(2,1)S(1)}, u32[]{:S(2)}, u32[]{:S(2)}) collective-permute-start(bf16[192,384]{1,0:T(8,128)(2,1)S(1)} %collective-permute-done.5), channel_id=1, source_target_pairs={{4,0},{5,1}} | collective-permute-start | bytes 442376 | tf_op jit(solution)/shard_map/ppermute | solution.py:378
  38.5 45.0 %collective-permute-start.13 = (bf16[768,384]{1,0:T(8,128)(2,1)S(1)}, bf16[768,384]{1,0:T(8,128)(2,1)S(1)}, u32[]{:S(2)}, u32[]{:S(2)}) collective-permute-start(bf16[768,384]{1,0:T(8,128)(2,1)S(1)} %get-tuple-element.98.pgu_ref), channel_id=1, source_target_pairs={{0,2},{2,4},{4,6},{6,8},{8,10},{10,12},{12,14},{14,16},{16,18},{18... | collective-permute-start | bytes 1769480 | tf_op jit(solution)/shard_map/ppermute | solution.py:296
  39.8 32.1 %collective-permute-start.3 = (bf16[384,384]{1,0:T(8,128)(2,1)S(1)}, bf16[384,384]{1,0:T(8,128)(2,1)S(1)}, u32[]{:S(2)}, u32[]{:S(2)}) collective-permute-start(bf16[384,384]{1,0:T(8,128)(2,1)S(1)} %get-tuple-element.79), channel_id=1, source_target_pairs={{0,1},{1,0},{2,3},{3,2},{4,5},{5,4},{6,7},{7,6},{8,9},{9,8},{10,11... | collective-permute-start | bytes 884744 | tf_op jit(solution)/shard_map/ppermute | solution.py:293
  60.0 7.0 %collective-permute-start.17 = (bf16[192,384]{1,0:T(8,128)(2,1)S(1)}, bf16[192,384]{1,0:T(8,128)(2,1)S(1)}, u32[]{:S(2)}, u32[]{:S(2)}) collective-permute-start(bf16[192,384]{1,0:T(8,128)(2,1)S(1)} %collective-permute-done.5), channel_id=1, source_target_pairs={{8,0},{9,1}} | collective-permute-start | bytes 442376 | tf_op jit(solution)/shard_map/ppermute | solution.py:378
  61.3 7.9 %collective-permute-start.18 = (bf16[192,384]{1,0:T(8,128)(2,1)S(1)}, bf16[192,384]{1,0:T(8,128)(2,1)S(1)}, u32[]{:S(2)}, u32[]{:S(2)}) collective-permute-start(bf16[192,384]{1,0:T(8,128)(2,1)S(1)} %collective-permute-done.5), channel_id=1, source_target_pairs={{12,0},{13,1}} | collective-permute-start | bytes 442376 | tf_op jit(solution)/shard_map/ppermute | solution.py:378
  62.6 7.9 %collective-permute-start.6 = (bf16[192,384]{1,0:T(8,128)(2,1)S(1)}, bf16[192,384]{1,0:T(8,128)(2,1)S(1)}, u32[]{:S(2)}, u32[]{:S(2)}) collective-permute-start(bf16[192,384]{1,0:T(8,128)(2,1)S(1)} %collective-permute-done.5), channel_id=1, source_target_pairs={{16,0},{17,1}} | collective-permute-start | bytes 442376 | tf_op jit(solution)/shard_map/ppermute | solution.py:378
  67.0 26.7 %collective-permute-start.2 = (bf16[768,384]{1,0:T(8,128)(2,1)S(1)}, bf16[768,384]{1,0:T(8,128)(2,1)S(1)}, u32[]{:S(2)}, u32[]{:S(2)}) collective-permute-start(bf16[768,384]{1,0:T(8,128)(2,1)S(1)} %get-tuple-element.76.pgu_ref), channel_id=1, source_target_pairs={{0,2},{2,4},{4,6},{6,8},{8,10},{10,12},{12,14},{14,16},{16,18},{18... | collective-permute-start | bytes 1769480 | tf_op jit(solution)/shard_map/ppermute | solution.py:296
  69.2 12.8 %collective-permute-start.15 = (bf16[384,384]{1,0:T(8,128)(2,1)S(1)}, bf16[384,384]{1,0:T(8,128)(2,1)S(1)}, u32[]{:S(2)}, u32[]{:S(2)}) collective-permute-start(bf16[384,384]{1,0:T(8,128)(2,1)S(1)} %get-tuple-element.103.pdown_ref), channel_id=1, source_target_pairs={{0,2},{2,4},{4,6},{6,8},{8,10},{10,12},{12,14},{14,16},{16,18},{18... | collective-permute-start | bytes 884744 | tf_op jit(solution)/shard_map/ppermute | solution.py:296
  70.5 27.9 %collective-permute-start.19 = (bf16[1152,384]{1,0:T(8,128)(2,1)S(1)}, bf16[1152,384]{1,0:T(8,128)(2,1)S(1)}, u32[]{:S(2)}, u32[]{:S(2)}) collective-permute-start(bf16[1152,384]{1,0:T(8,128)(2,1)S(1)} %get-tuple-element.106), channel_id=1, source_target_pairs={{0,2},{2,4},{4,6},{6,8},{8,10},{10,12},{12,14},{14,16},{16,18},{18... | collective-permute-start | bytes 2654216 | tf_op jit(solution)/shard_map/ppermute | solution.py:296
  71.9 8.8 %collective-permute-start.7 = (bf16[192,384]{1,0:T(8,128)(2,1)S(1)}, bf16[192,384]{1,0:T(8,128)(2,1)S(1)}, u32[]{:S(2)}, u32[]{:S(2)}) collective-permute-start(bf16[192,384]{1,0:T(8,128)(2,1)S(1)} %collective-permute-done.5), channel_id=1, source_target_pairs={{20,0},{21,1}} | collective-permute-start | bytes 442376 | tf_op jit(solution)/shard_map/ppermute | solution.py:378
  80.7 13.0 %collective-permute-start.4 = (bf16[384,384]{1,0:T(8,128)(2,1)S(1)}, bf16[384,384]{1,0:T(8,128)(2,1)S(1)}, u32[]{:S(2)}, u32[]{:S(2)}) collective-permute-start(bf16[384,384]{1,0:T(8,128)(2,1)S(1)} %get-tuple-element.81.pdown_ref), channel_id=1, source_target_pairs={{0,2},{2,4},{4,6},{6,8},{8,10},{10,12},{12,14},{14,16},{16,18},{18... | collective-permute-start | bytes 884744 | tf_op jit(solution)/shard_map/ppermute | solution.py:296
  82.0 42.2 %collective-permute-start.9 = (bf16[1152,384]{1,0:T(8,128)(2,1)S(1)}, bf16[1152,384]{1,0:T(8,128)(2,1)S(1)}, u32[]{:S(2)}, u32[]{:S(2)}) collective-permute-start(bf16[1152,384]{1,0:T(8,128)(2,1)S(1)} %get-tuple-element.84), channel_id=1, source_target_pairs={{0,2},{2,4},{4,6},{6,8},{8,10},{10,12},{12,14},{14,16},{16,18},{18... | collective-permute-start | bytes 2654216 | tf_op jit(solution)/shard_map/ppermute | solution.py:296
  83.4 8.8 %collective-permute-start.8 = (bf16[192,384]{1,0:T(8,128)(2,1)S(1)}, bf16[192,384]{1,0:T(8,128)(2,1)S(1)}, u32[]{:S(2)}, u32[]{:S(2)}) collective-permute-start(bf16[192,384]{1,0:T(8,128)(2,1)S(1)} %collective-permute-done.5), channel_id=1, source_target_pairs={{24,0},{25,1}} | collective-permute-start | bytes 442376 | tf_op jit(solution)/shard_map/ppermute | solution.py:378
  92.2 16.2 %collective-permute-start.20 = (bf16[768,384]{1,0:T(8,128)(2,1)S(1)}, bf16[768,384]{1,0:T(8,128)(2,1)S(1)}, u32[]{:S(2)}, u32[]{:S(2)}) collective-permute-start(bf16[768,384]{1,0:T(8,128)(2,1)S(1)} %get-tuple-element.110), channel_id=1, source_target_pairs={{0,1},{1,0},{2,3},{3,2},{4,5},{5,4},{6,7},{7,6},{8,9},{9,8},{10,11... | collective-permute-start | bytes 1769480 | tf_op jit(solution)/shard_map/ppermute | solution.py:293
  96.3 27.9 %collective-permute-start.10 = (bf16[768,384]{1,0:T(8,128)(2,1)S(1)}, bf16[768,384]{1,0:T(8,128)(2,1)S(1)}, u32[]{:S(2)}, u32[]{:S(2)}) collective-permute-start(bf16[768,384]{1,0:T(8,128)(2,1)S(1)} %get-tuple-element.88), channel_id=1, source_target_pairs={{0,1},{1,0},{2,3},{3,2},{4,5},{5,4},{6,7},{7,6},{8,9},{9,8},{10,11... | collective-permute-start | bytes 1769480 | tf_op jit(solution)/shard_map/ppermute | solution.py:293
  96.9 25.6 %collective-permute-start.21 = (bf16[384,384]{1,0:T(8,128)(2,1)S(1)}, bf16[384,384]{1,0:T(8,128)(2,1)S(1)}, u32[]{:S(2)}, u32[]{:S(2)}) collective-permute-start(bf16[384,384]{1,0:T(8,128)(2,1)S(1)} %get-tuple-element.112), channel_id=1, source_target_pairs={{0,1},{1,0},{2,3},{3,2},{4,5},{5,4},{6,7},{7,6},{8,9},{9,8},{10,11... | collective-permute-start | bytes 884744 | tf_op jit(solution)/shard_map/ppermute | solution.py:293
  98.4 27.6 %collective-permute-start.23 = (bf16[256,384]{1,0:T(8,128)(2,1)S(1)}, bf16[256,384]{1,0:T(8,128)(2,1)S(1)}, u32[]{:S(2)}, u32[]{:S(2)}) collective-permute-start(bf16[256,384]{1,0:T(8,128)(2,1)S(1)} %get-tuple-element.121), channel_id=1, source_target_pairs={{0,1},{1,0},{2,3},{3,2},{4,5},{5,4},{6,7},{7,6},{8,9},{9,8},{10,11... | collective-permute-start | bytes 589832 | tf_op jit(solution)/shard_map/ppermute | solution.py:293
  108.4 19.0 %collective-permute-start.22 = (bf16[128,384]{1,0:T(8,128)(2,1)S(1)}, bf16[128,384]{1,0:T(8,128)(2,1)S(1)}, u32[]{:S(2)}, u32[]{:S(2)}) collective-permute-start(bf16[128,384]{1,0:T(8,128)(2,1)S(1)} %get-tuple-element.120), channel_id=1, source_target_pairs={{0,1},{1,0},{2,3},{3,2},{4,5},{5,4},{6,7},{7,6},{8,9},{9,8},{10,11... | collective-permute-start | bytes 294920 | tf_op jit(solution)/shard_map/ppermute | solution.py:293
  (2 other events, 22.6 us)

commit v8 on v7

--- a/solution.py
+++ b/solution.py
@@ -66,8 +66,15 @@
     own_down[...] = mm(dout_s[...], hid_s[...], ((0,), (0,)))
 
 
-def take_head(head, fast_ref, own_ref):
-    pltpu.sync_copy(fast_ref.at[0, :, head], own_ref)
+def take_head(head, fast_ref, own_ref, sems):
+    copies = [
+        pltpu.make_async_copy(fast_ref.at[0, m, head], own_ref.at[m], sems.at[m])
+        for m in range(own_ref.shape[0])
+    ]
+    for copy in copies:
+        copy.start()
+    for copy in copies:
+        copy.wait()
 
 
 def take_piece(sources, begin_ref, piece_ref):
@@ -163,6 +170,9 @@
     recvs = refs[: n - 1]
     new_ref, moment_ref = refs[-2:]
     width = own_ref.shape[1]
+    if mats[0]:
+        before = refs[n - 1]
+        moment_ref[: mats[0] * width, :] = before[...]
     for i, m in enumerate(mats):
         at = pl.ds(i * width, width)
         moment = summed(own_ref, recvs, i * width, width)
@@ -312,11 +322,14 @@
     recv_fast, owned = [], []
     for h in range(heads):
         owned.append(
-            call(functools.partial(take_head, h), shape(3, part, width), [HBM], VMEM)(fast_t)
+            call(
+                functools.partial(take_head, h), shape(3, part, width), [HBM], VMEM, (DMA((3,)),)
+            )(fast_t)
         )
         recv_fast.append(turned(owned[h]))
 
-    sources = [(2 * (p + 1)) % blocks for p in range(3 * heads)]
+    apart = max(blocks // (3 * heads + 2), 1)
+    sources = [apart * (p + 1) % blocks for p in range(3 * heads)]
     piece = call(functools.partial(take_piece, sources), shape(part, width), [HBM], VMEM)(begin_t)
     crossed = [
         lax.ppermute(
@@ -362,10 +375,9 @@
         ):
             new, *moment = call(
                 functools.partial(update_one, n, h, mats),
-                (shape(len(mats) * width, width), shape(3 * width, width)),
+                (shape(len(mats) * width, width), shape((mats[-1] + 1) * width, width)),
                 [VMEM] * (2 + n + len(moment)),
                 (VMEM, VMEM),
-                aliases={2 + n: 1} if moment else None,
             )(rates, old, own, *recvs, *moment)
             pack.append(new)
         packs.append(pack)
@@ -386,7 +398,7 @@
     for h in range(heads):
         arrived = [forward(packs[h][0]), forward(packs[h][1])]
         pieces = [begins[3 * h + m][r] for r in range(n - 1) for m in range(3)]
-        cuts = [width - 128, 128] if h == heads - 1 and width % 128 == 0 else [width]
+        cuts = [128, width - 128] if h == heads - 1 and width % 128 == 0 else [width]
         second.append(
             call(
                 functools.partial(grads_two, n, divisor),

time: 129 us -> 130 us (level)
  no operation moved by 1% of the time
where the time goes in v8:
time: 130 us; the launch traced here: 129 us
  waiting for transfers between devices  64.3 us (49%)
  Pallas kernels  32.3 us (25%)
  starting transfers between devices  31.4 us (24%)
    ppermute x6, waiting for transfers between devices, on_device(): lax.ppermute(x, ('block', 'tok'), [(sources[p] * n + i, i) for i in range...  33.2 us
    ppermute x11, waiting for transfers between devices, turned(): lax.ppermute(x, 'tok', [(i, (i + r) % n) for i in range(n)])  31.1 us
    ppermute x11, starting transfers between devices, turned(): lax.ppermute(x, 'tok', [(i, (i + r) % n) for i in range(n)])  15.1 us
    ppermute x6, starting transfers between devices, forward(): return lax.ppermute(x, 'block', [(i, i + 1) for i in range(blocks - 1)])  7.93 us
    ppermute x6, starting transfers between devices, on_device(): lax.ppermute(x, ('block', 'tok'), [(sources[p] * n + i, i) for i in range...  7.73 us
    pallas_call x2, Pallas kernels, on_device(): call(functools.partial(grads_one, n, h, divisor), grad_out, [VMEM] * (4 +...  5.65 us
    pallas_call x2, Pallas kernels, on_device(): call(functools.partial(grads_two, n, divisor), (shape(2 * width, width),...  4.99 us
    pallas_call x2, Pallas kernels, on_device(): call(functools.partial(apply_one, h), out_shape, [VMEM] * 3 + [HBM] * len...  4.55 us
  transfers between devices with their start and end apart: 24, of which 10 were waited for; matrix products, arithmetic and copies ran while one was open for 0% of the time, Pallas kernels for 23%

profile of v8, /device:TPU:0, one launch (start us, length us, event | category | flops | bytes accessed | tf_op | source)
XLA Modules:
  0.0 129.1 jit_solution(11943603507321662419)
XLA Ops:
  1.7 3.0 %collective-permute-start.11 = (bf16[3,192,384]{2,1,0:T(8,128)(2,1)S(1)}, bf16[3,192,384]{2,1,0:T(8,128)(2,1)S(1)}, u32[]{:S(2)}, u32[]{:S(2)}) collective-permute-start(bf16[3,192,384]{2,1,0:T(8,128)(2,1)S(1)} %shard_map.110.refs_0_), channel_id=1, source_target_pairs={{0,1},{1,0},{2,3},{3,2},{4,5},{5,4},{6,7},{7,6},{8,9},{9,8},{10,11... | collective-permute-start | bytes 1327112 | tf_op jit(solution)/shard_map/ppermute | solution.py:303
  5.9 3.9 %shard_map.103 = (bf16[768,384]{1,0:T(8,128)(2,1)S(1)}, bf16[768,384]{1,0:T(8,128)(2,1)S(1)}, bf16[768,384]{1,0:T(8,128)(2,1)S(1)}, bf16[768,384]{1,0:T(8,128)(2...) custom-call(bf16[2,768,768]{2,1,0:T(8,128)(2,1)} %k_ref.1, ...), custom_call_target="tpu_custom_call" | custom-call | tf_op jit(solution)/shard_map/pallas_call | solution.py:344
  9.8 5.9 %collective-permute-done.11.refs_1_ = bf16[3,192,384]{2,1,0:T(8,128)(2,1)S(1)} collective-permute-done((bf16[3,192,384]{2,1,0:T(8,128)(2,1)S(1)}, bf16[3,192,384]{2,1,0:T(8,128)(2,1)S(1)}, u32[]{:S(2)}, u32[]{:S(2)}) %collective-permute-start.11) | collective-permute-done | bytes 442400 | tf_op jit(solution)/shard_map/ppermute | solution.py:303
  15.8 2.8 %shard_map.111 = (bf16[768,384]{1,0:T(8,128)(2,1)S(1)}, bf16[384,384]{1,0:T(8,128)(2,1)S(1)}, bf16[768,384]{1,0:T(8,128)(2,1)S(1)}, bf16[384,384]{1,0:T(8,128)(2...) custom-call(f32[1,2]{1,0:T(1,128)S(1)} %bitcast.16, bf16[768,384]{1,0:T(8,128)(2,1)S(1)} %get-tuple-element.92.k_ref, ...), custom_call_target="tpu_custom_call" | custom-call | tf_op jit(solution)/shard_map/pallas_call | solution.py:358
  18.6 2.1 %collective-permute-start.12 = (bf16[768,384]{1,0:T(8,128)(2,1)S(1)}, bf16[768,384]{1,0:T(8,128)(2,1)S(1)}, u32[]{:S(2)}, u32[]{:S(2)}) collective-permute-start(bf16[768,384]{1,0:T(8,128)(2,1)S(1)} %get-tuple-element.97), channel_id=1, source_target_pairs={{0,1},{1,0},{2,3},{3,2},{4,5},{5,4},{6,7},{7,6},{8,9},{9,8},{10,11... | collective-permute-start | bytes 1769480 | tf_op jit(solution)/shard_map/ppermute | solution.py:303
  20.7 4.6 %collective-permute-done.refs_1_ = bf16[3,192,384]{2,1,0:T(8,128)(2,1)S(1)} collective-permute-done((bf16[3,192,384]{2,1,0:T(8,128)(2,1)S(1)}, bf16[3,192,384]{2,1,0:T(8,128)(2,1)S(1)}, u32[]{:S(2)}, u32[]{:S(2)}) %collective-permute-start) | collective-permute-done | bytes 442400 | tf_op jit(solution)/shard_map/ppermute | solution.py:303
  25.3 2.8 %shard_map.105 = (bf16[768,384]{1,0:T(8,128)(2,1)S(1)}, bf16[384,384]{1,0:T(8,128)(2,1)S(1)}, bf16[768,384]{1,0:T(8,128)(2,1)S(1)}, bf16[384,384]{1,0:T(8,128)(2...) custom-call(f32[1,2]{1,0:T(1,128)S(1)} %bitcast.17, bf16[768,384]{1,0:T(8,128)(2,1)S(1)} %get-tuple-element.70.k_ref, ...), custom_call_target="tpu_custom_call" | custom-call | tf_op jit(solution)/shard_map/pallas_call | solution.py:358
  28.1 2.1 %collective-permute-start.1 = (bf16[768,384]{1,0:T(8,128)(2,1)S(1)}, bf16[768,384]{1,0:T(8,128)(2,1)S(1)}, u32[]{:S(2)}, u32[]{:S(2)}) collective-permute-start(bf16[768,384]{1,0:T(8,128)(2,1)S(1)} %get-tuple-element.75), channel_id=1, source_target_pairs={{0,1},{1,0},{2,3},{3,2},{4,5},{5,4},{6,7},{7,6},{8,9},{9,8},{10,11... | collective-permute-start | bytes 1769480 | tf_op jit(solution)/shard_map/ppermute | solution.py:303
  33.1 4.8 %collective-permute-done.12.refs_0_ = bf16[768,384]{1,0:T(8,128)(2,1)S(1)} collective-permute-done((bf16[768,384]{1,0:T(8,128)(2,1)S(1)}, bf16[768,384]{1,0:T(8,128)(2,1)S(1)}, u32[]{:S(2)}, u32[]{:S(2)}) %collective-permute-start.12) | collective-permute-done | bytes 589856 | tf_op jit(solution)/shard_map/ppermute | solution.py:303
  39.9 2.1 %collective-permute-start.3 = (bf16[384,384]{1,0:T(8,128)(2,1)S(1)}, bf16[384,384]{1,0:T(8,128)(2,1)S(1)}, u32[]{:S(2)}, u32[]{:S(2)}) collective-permute-start(bf16[384,384]{1,0:T(8,128)(2,1)S(1)} %get-tuple-element.79), channel_id=1, source_target_pairs={{0,1},{1,0},{2,3},{3,2},{4,5},{5,4},{6,7},{7,6},{8,9},{9,8},{10,11... | collective-permute-start | bytes 884744 | tf_op jit(solution)/shard_map/ppermute | solution.py:303
  42.0 18.1 %collective-permute-done.16.refs_2_ = bf16[192,384]{1,0:T(8,128)(2,1)S(1)} collective-permute-done((bf16[192,384]{1,0:T(8,128)(2,1)S(1)}, bf16[192,384]{1,0:T(8,128)(2,1)S(1)}, u32[]{:S(2)}, u32[]{:S(2)}) %collective-permute-start.16) | collective-permute-done | bytes 147488 | tf_op jit(solution)/shard_map/ppermute | solution.py:390
  65.2 2.0 %collective-permute-done.17.refs_3_ = bf16[192,384]{1,0:T(8,128)(2,1)S(1)} collective-permute-done((bf16[192,384]{1,0:T(8,128)(2,1)S(1)}, bf16[192,384]{1,0:T(8,128)(2,1)S(1)}, u32[]{:S(2)}, u32[]{:S(2)}) %collective-permute-start.17) | collective-permute-done | bytes 147488 | tf_op jit(solution)/shard_map/ppermute | solution.py:390
  73.8 7.1 %collective-permute-done.7.refs_3_ = bf16[192,384]{1,0:T(8,128)(2,1)S(1)} collective-permute-done((bf16[192,384]{1,0:T(8,128)(2,1)S(1)}, bf16[192,384]{1,0:T(8,128)(2,1)S(1)}, u32[]{:S(2)}, u32[]{:S(2)}) %collective-permute-start.7) | collective-permute-done | bytes 147488 | tf_op jit(solution)/shard_map/ppermute | solution.py:390
  84.9 2.4 %shard_map.114 = (bf16[768,384]{1,0:T(8,128)(2,1)S(1)}, bf16[384,384]{1,0:T(8,128)(2,1)S(1)}, f32[768,384]{1,0:T(8,128)S(1)}, f32[384,384]{1,0:T(8,128)S(1)}, bf...) custom-call(bf16[768,384]{1,0:T(8,128)(2,1)S(1)} %get-tuple-element.89.k_ref, ...), custom_call_target="tpu_custom_call" | custom-call | tf_op jit(solution)/shard_map/pallas_call | solution.py:403
  87.3 5.1 %collective-permute-done.8.refs_4_ = bf16[192,384]{1,0:T(8,128)(2,1)S(1)} collective-permute-done((bf16[192,384]{1,0:T(8,128)(2,1)S(1)}, bf16[192,384]{1,0:T(8,128)(2,1)S(1)}, u32[]{:S(2)}, u32[]{:S(2)}) %collective-permute-start.8) | collective-permute-done | bytes 147488 | tf_op jit(solution)/shard_map/ppermute | solution.py:390
  93.9 2.6 %shard_map.109 = (bf16[768,384]{1,0:T(8,128)(2,1)S(1)}, bf16[384,384]{1,0:T(8,128)(2,1)S(1)}, f32[768,384]{1,0:T(8,128)S(1)}, f32[384,384]{1,0:T(8,128)S(1)}, bf...) custom-call(bf16[768,384]{1,0:T(8,128)(2,1)S(1)} %get-tuple-element.67.k_ref, ...), custom_call_target="tpu_custom_call" | custom-call | tf_op jit(solution)/shard_map/pallas_call | solution.py:403
  99.1 9.5 %collective-permute-done.20.refs_0_ = bf16[768,384]{1,0:T(8,128)(2,1)S(1)} collective-permute-done((bf16[768,384]{1,0:T(8,128)(2,1)S(1)}, bf16[768,384]{1,0:T(8,128)(2,1)S(1)}, u32[]{:S(2)}, u32[]{:S(2)}) %collective-permute-start.20) | collective-permute-done | bytes 589856 | tf_op jit(solution)/shard_map/ppermute | solution.py:303
  110.1 2.3 %shard_map.116.refs_0_ = bf16[2,768,768]{2,1,0:T(8,128)(2,1)} custom-call(bf16[768,384]{1,0:T(8,128)(2,1)S(1)} %get-tuple-element.114.q_ref, bf16[768,384]{1,0:T(8,128)(2,1)S(1)} %get-tuple-element.98.pgu_ref, bf16[384,384]{1,0:T(8,128)(2,1)S(1)} %get-tuple-element.103.pdown_ref), custom_call_target="tpu_custom_call" | custom-call | tf_op jit(solution)/shard_map/pallas_call | solution.py:423
  112.4 2.3 %shard_map.117.refs_1_ = bf16[2,768,768]{2,1,0:T(8,128)(2,1)} custom-call(bf16[768,384]{1,0:T(8,128)(2,1)S(1)} %get-tuple-element.113.q_ref, bf16[768,384]{1,0:T(8,128)(2,1)S(1)} %get-tuple-element.76.pgu_ref, bf16[384,384]{1,0:T(8,128)(2,1)S(1)} %get-tuple-element.81.pdown_ref, bf16[2,768,768]{2,1,0:T(8,128)(2,1)} %shard_map.116.refs_0_), custom_call_target="tpu_custom_call", output_to_operand_aliasing={{}: (3, {})} | custom-call | tf_op jit(solution)/shard_map/pallas_call | solution.py:423
  114.6 1.7 %shard_map.115 = (bf16[768,384]{1,0:T(8,128)(2,1)S(1)}, bf16[1,3,2,192,384]{4,3,2,1,0:T(8,128)(2,1)}, f32[1,3,2,192,384]{4,3,2,1,0:T(8,128)}) custom-call(f32[2,3]{1,0:T(2,128)S(1)} %bitcast.11, f32[1,2]{1,0:T(1,128)S(1)} %bitcast.18, bf16[768,384]{1,0:T(8,128)(2,1)S(1)} %get-tuple-element.107.old_ref, f32[768,384]{1,0:T(8,128)S(1)} %get-tuple-element.108.own_ref, ...), custom_call_target="tpu_custom_call" | custom-call | tf_op jit(solution)/shard_map/pallas_call | solution.py:440
  116.4 6.4 %collective-permute-done.21.refs_0_ = bf16[384,384]{1,0:T(8,128)(2,1)S(1)} collective-permute-done((bf16[384,384]{1,0:T(8,128)(2,1)S(1)}, bf16[384,384]{1,0:T(8,128)(2,1)S(1)}, u32[]{:S(2)}, u32[]{:S(2)}) %collective-permute-start.21) | collective-permute-done | bytes 294944 | tf_op jit(solution)/shard_map/ppermute | solution.py:303
  122.7 1.7 %shard_map.118 = (bf16[2,768,768]{2,1,0:T(8,128)(2,1)}, bf16[1,3,2,192,384]{4,3,2,1,0:T(8,128)(2,1)}, f32[1,3,2,192,384]{4,3,2,1,0:T(8,128)}) custom-call(f32[2,3]{1,0:T(2,128)S(1)} %bitcast.12, f32[1,2]{1,0:T(1,128)S(1)} %bitcast.19, bf16[384,384]{1,0:T(8,128)(2,1)S(1)} %get-tuple-element.104.old_ref, ...), custom_call_target="tpu_custom_call", output_to_operand_aliasing={{0}: (7, {}), {1}: (8, {}), {2}: (9, {})} | custom-call | tf_op jit(solution)/shard_map/pallas_call | solution.py:468
  124.5 1.7 %shard_map.119 = (bf16[768,384]{1,0:T(8,128)(2,1)S(1)}, bf16[1,3,2,192,384]{4,3,2,1,0:T(8,128)(2,1)}, f32[1,3,2,192,384]{4,3,2,1,0:T(8,128)}) custom-call(f32[2,3]{1,0:T(2,128)S(1)} %bitcast.13, f32[1,2]{1,0:T(1,128)S(1)} %bitcast.20, bf16[768,384]{1,0:T(8,128)(2,1)S(1)} %get-tuple-element.85.old_ref, ...), custom_call_target="tpu_custom_call", output_to_operand_aliasing={{1}: (7, {}), {2}: (8, {})} | custom-call | tf_op jit(solution)/shard_map/pallas_call | solution.py:440
  127.5 1.5 %shard_map.121 = (bf16[2,768,768]{2,1,0:T(8,128)(2,1)}, bf16[1,3,2,192,384]{4,3,2,1,0:T(8,128)(2,1)}, f32[1,3,2,192,384]{4,3,2,1,0:T(8,128)}) custom-call(f32[2,3]{1,0:T(2,128)S(1)} %bitcast.15, f32[1,2]{1,0:T(1,128)S(1)} %bitcast.22, bf16[384,384]{1,0:T(8,128)(2,1)S(1)} %get-tuple-element.82.old_ref, ...), custom_call_target="tpu_custom_call", output_to_operand_aliasing={{0}: (9, {}), {1}: (10, {}), {2}: (11, {})} | custom-call | tf_op jit(solution)/shard_map/pallas_call | solution.py:468
  (47 shorter events, 29.6 us)
Async XLA Ops:
  1.7 14.1 %collective-permute-start.11 = (bf16[3,192,384]{2,1,0:T(8,128)(2,1)S(1)}, bf16[3,192,384]{2,1,0:T(8,128)(2,1)S(1)}, u32[]{:S(2)}, u32[]{:S(2)}) collective-permute-start(bf16[3,192,384]{2,1,0:T(8,128)(2,1)S(1)} %shard_map.110.refs_0_), channel_id=1, source_target_pairs={{0,1},{1,0},{2,3},{3,2},{4,5},{5,4},{6,7},{7,6},{8,9},{9,8},{10,11... | collective-permute-start | bytes 1327112 | tf_op jit(solution)/shard_map/ppermute | solution.py:303
  5.8 19.4 %collective-permute-start = (bf16[3,192,384]{2,1,0:T(8,128)(2,1)S(1)}, bf16[3,192,384]{2,1,0:T(8,128)(2,1)S(1)}, u32[]{:S(2)}, u32[]{:S(2)}) collective-permute-start(bf16[3,192,384]{2,1,0:T(8,128)(2,1)S(1)} %shard_map.104.refs_0_), channel_id=1, source_target_pairs={{0,1},{1,0},{2,3},{3,2},{4,5},{5,4},{6,7},{7,6},{8,9},{9,8},{10,11... | collective-permute-start | bytes 1327112 | tf_op jit(solution)/shard_map/ppermute | solution.py:303
  18.6 19.3 %collective-permute-start.12 = (bf16[768,384]{1,0:T(8,128)(2,1)S(1)}, bf16[768,384]{1,0:T(8,128)(2,1)S(1)}, u32[]{:S(2)}, u32[]{:S(2)}) collective-permute-start(bf16[768,384]{1,0:T(8,128)(2,1)S(1)} %get-tuple-element.97), channel_id=1, source_target_pairs={{0,1},{1,0},{2,3},{3,2},{4,5},{5,4},{6,7},{7,6},{8,9},{9,8},{10,11... | collective-permute-start | bytes 1769480 | tf_op jit(solution)/shard_map/ppermute | solution.py:303
  28.1 34.6 %collective-permute-start.1 = (bf16[768,384]{1,0:T(8,128)(2,1)S(1)}, bf16[768,384]{1,0:T(8,128)(2,1)S(1)}, u32[]{:S(2)}, u32[]{:S(2)}) collective-permute-start(bf16[768,384]{1,0:T(8,128)(2,1)S(1)} %get-tuple-element.75), channel_id=1, source_target_pairs={{0,1},{1,0},{2,3},{3,2},{4,5},{5,4},{6,7},{7,6},{8,9},{9,8},{10,11... | collective-permute-start | bytes 1769480 | tf_op jit(solution)/shard_map/ppermute | solution.py:303
  31.1 0.8 collective-permute-start.5
  31.7 29.7 %collective-permute-start.14 = (bf16[384,384]{1,0:T(8,128)(2,1)S(1)}, bf16[384,384]{1,0:T(8,128)(2,1)S(1)}, u32[]{:S(2)}, u32[]{:S(2)}) collective-permute-start(bf16[384,384]{1,0:T(8,128)(2,1)S(1)} %get-tuple-element.101), channel_id=1, source_target_pairs={{0,1},{1,0},{2,3},{3,2},{4,5},{5,4},{6,7},{7,6},{8,9},{9,8},{10,11... | collective-permute-start | bytes 884744 | tf_op jit(solution)/shard_map/ppermute | solution.py:303
  31.8 28.3 %collective-permute-start.16 = (bf16[192,384]{1,0:T(8,128)(2,1)S(1)}, bf16[192,384]{1,0:T(8,128)(2,1)S(1)}, u32[]{:S(2)}, u32[]{:S(2)}) collective-permute-start(bf16[192,384]{1,0:T(8,128)(2,1)S(1)} %collective-permute-done.5), channel_id=1, source_target_pairs={{4,0},{5,1}} | collective-permute-start | bytes 442376 | tf_op jit(solution)/shard_map/ppermute | solution.py:390
  38.6 44.9 %collective-permute-start.13 = (bf16[768,384]{1,0:T(8,128)(2,1)S(1)}, bf16[768,384]{1,0:T(8,128)(2,1)S(1)}, u32[]{:S(2)}, u32[]{:S(2)}) collective-permute-start(bf16[768,384]{1,0:T(8,128)(2,1)S(1)} %get-tuple-element.98.pgu_ref), channel_id=1, source_target_pairs={{0,2},{2,4},{4,6},{6,8},{8,10},{10,12},{12,14},{14,16},{16,18},{18... | collective-permute-start | bytes 1769480 | tf_op jit(solution)/shard_map/ppermute | solution.py:306
  39.9 32.1 %collective-permute-start.3 = (bf16[384,384]{1,0:T(8,128)(2,1)S(1)}, bf16[384,384]{1,0:T(8,128)(2,1)S(1)}, u32[]{:S(2)}, u32[]{:S(2)}) collective-permute-start(bf16[384,384]{1,0:T(8,128)(2,1)S(1)} %get-tuple-element.79), channel_id=1, source_target_pairs={{0,1},{1,0},{2,3},{3,2},{4,5},{5,4},{6,7},{7,6},{8,9},{9,8},{10,11... | collective-permute-start | bytes 884744 | tf_op jit(solution)/shard_map/ppermute | solution.py:303
  60.1 7.0 %collective-permute-start.17 = (bf16[192,384]{1,0:T(8,128)(2,1)S(1)}, bf16[192,384]{1,0:T(8,128)(2,1)S(1)}, u32[]{:S(2)}, u32[]{:S(2)}) collective-permute-start(bf16[192,384]{1,0:T(8,128)(2,1)S(1)} %collective-permute-done.5), channel_id=1, source_target_pairs={{8,0},{9,1}} | collective-permute-start | bytes 442376 | tf_op jit(solution)/shard_map/ppermute | solution.py:390
  61.4 7.9 %collective-permute-start.18 = (bf16[192,384]{1,0:T(8,128)(2,1)S(1)}, bf16[192,384]{1,0:T(8,128)(2,1)S(1)}, u32[]{:S(2)}, u32[]{:S(2)}) collective-permute-start(bf16[192,384]{1,0:T(8,128)(2,1)S(1)} %collective-permute-done.5), channel_id=1, source_target_pairs={{12,0},{13,1}} | collective-permute-start | bytes 442376 | tf_op jit(solution)/shard_map/ppermute | solution.py:390
  62.7 7.9 %collective-permute-start.6 = (bf16[192,384]{1,0:T(8,128)(2,1)S(1)}, bf16[192,384]{1,0:T(8,128)(2,1)S(1)}, u32[]{:S(2)}, u32[]{:S(2)}) collective-permute-start(bf16[192,384]{1,0:T(8,128)(2,1)S(1)} %collective-permute-done.5), channel_id=1, source_target_pairs={{16,0},{17,1}} | collective-permute-start | bytes 442376 | tf_op jit(solution)/shard_map/ppermute | solution.py:390
  67.1 26.7 %collective-permute-start.2 = (bf16[768,384]{1,0:T(8,128)(2,1)S(1)}, bf16[768,384]{1,0:T(8,128)(2,1)S(1)}, u32[]{:S(2)}, u32[]{:S(2)}) collective-permute-start(bf16[768,384]{1,0:T(8,128)(2,1)S(1)} %get-tuple-element.76.pgu_ref), channel_id=1, source_target_pairs={{0,2},{2,4},{4,6},{6,8},{8,10},{10,12},{12,14},{14,16},{16,18},{18... | collective-permute-start | bytes 1769480 | tf_op jit(solution)/shard_map/ppermute | solution.py:306
  69.4 12.8 %collective-permute-start.15 = (bf16[384,384]{1,0:T(8,128)(2,1)S(1)}, bf16[384,384]{1,0:T(8,128)(2,1)S(1)}, u32[]{:S(2)}, u32[]{:S(2)}) collective-permute-start(bf16[384,384]{1,0:T(8,128)(2,1)S(1)} %get-tuple-element.103.pdown_ref), channel_id=1, source_target_pairs={{0,2},{2,4},{4,6},{6,8},{8,10},{10,12},{12,14},{14,16},{16,18},{18... | collective-permute-start | bytes 884744 | tf_op jit(solution)/shard_map/ppermute | solution.py:306
  70.7 27.9 %collective-permute-start.19 = (bf16[1152,384]{1,0:T(8,128)(2,1)S(1)}, bf16[1152,384]{1,0:T(8,128)(2,1)S(1)}, u32[]{:S(2)}, u32[]{:S(2)}) collective-permute-start(bf16[1152,384]{1,0:T(8,128)(2,1)S(1)} %get-tuple-element.106), channel_id=1, source_target_pairs={{0,2},{2,4},{4,6},{6,8},{8,10},{10,12},{12,14},{14,16},{16,18},{18... | collective-permute-start | bytes 2654216 | tf_op jit(solution)/shard_map/ppermute | solution.py:306
  72.0 8.8 %collective-permute-start.7 = (bf16[192,384]{1,0:T(8,128)(2,1)S(1)}, bf16[192,384]{1,0:T(8,128)(2,1)S(1)}, u32[]{:S(2)}, u32[]{:S(2)}) collective-permute-start(bf16[192,384]{1,0:T(8,128)(2,1)S(1)} %collective-permute-done.5), channel_id=1, source_target_pairs={{20,0},{21,1}} | collective-permute-start | bytes 442376 | tf_op jit(solution)/shard_map/ppermute | solution.py:390
  80.9 13.0 %collective-permute-start.4 = (bf16[384,384]{1,0:T(8,128)(2,1)S(1)}, bf16[384,384]{1,0:T(8,128)(2,1)S(1)}, u32[]{:S(2)}, u32[]{:S(2)}) collective-permute-start(bf16[384,384]{1,0:T(8,128)(2,1)S(1)} %get-tuple-element.81.pdown_ref), channel_id=1, source_target_pairs={{0,2},{2,4},{4,6},{6,8},{8,10},{10,12},{12,14},{14,16},{16,18},{18... | collective-permute-start | bytes 884744 | tf_op jit(solution)/shard_map/ppermute | solution.py:306
  82.2 42.3 %collective-permute-start.9 = (bf16[1152,384]{1,0:T(8,128)(2,1)S(1)}, bf16[1152,384]{1,0:T(8,128)(2,1)S(1)}, u32[]{:S(2)}, u32[]{:S(2)}) collective-permute-start(bf16[1152,384]{1,0:T(8,128)(2,1)S(1)} %get-tuple-element.84), channel_id=1, source_target_pairs={{0,2},{2,4},{4,6},{6,8},{8,10},{10,12},{12,14},{14,16},{16,18},{18... | collective-permute-start | bytes 2654216 | tf_op jit(solution)/shard_map/ppermute | solution.py:306
  83.6 8.8 %collective-permute-start.8 = (bf16[192,384]{1,0:T(8,128)(2,1)S(1)}, bf16[192,384]{1,0:T(8,128)(2,1)S(1)}, u32[]{:S(2)}, u32[]{:S(2)}) collective-permute-start(bf16[192,384]{1,0:T(8,128)(2,1)S(1)} %collective-permute-done.5), channel_id=1, source_target_pairs={{24,0},{25,1}} | collective-permute-start | bytes 442376 | tf_op jit(solution)/shard_map/ppermute | solution.py:390
  92.4 16.2 %collective-permute-start.20 = (bf16[768,384]{1,0:T(8,128)(2,1)S(1)}, bf16[768,384]{1,0:T(8,128)(2,1)S(1)}, u32[]{:S(2)}, u32[]{:S(2)}) collective-permute-start(bf16[768,384]{1,0:T(8,128)(2,1)S(1)} %get-tuple-element.110), channel_id=1, source_target_pairs={{0,1},{1,0},{2,3},{3,2},{4,5},{5,4},{6,7},{7,6},{8,9},{9,8},{10,11... | collective-permute-start | bytes 1769480 | tf_op jit(solution)/shard_map/ppermute | solution.py:303
  96.5 28.0 %collective-permute-start.10 = (bf16[768,384]{1,0:T(8,128)(2,1)S(1)}, bf16[768,384]{1,0:T(8,128)(2,1)S(1)}, u32[]{:S(2)}, u32[]{:S(2)}) collective-permute-start(bf16[768,384]{1,0:T(8,128)(2,1)S(1)} %get-tuple-element.88), channel_id=1, source_target_pairs={{0,1},{1,0},{2,3},{3,2},{4,5},{5,4},{6,7},{7,6},{8,9},{9,8},{10,11... | collective-permute-start | bytes 1769480 | tf_op jit(solution)/shard_map/ppermute | solution.py:303
  97.1 25.7 %collective-permute-start.21 = (bf16[384,384]{1,0:T(8,128)(2,1)S(1)}, bf16[384,384]{1,0:T(8,128)(2,1)S(1)}, u32[]{:S(2)}, u32[]{:S(2)}) collective-permute-start(bf16[384,384]{1,0:T(8,128)(2,1)S(1)} %get-tuple-element.112), channel_id=1, source_target_pairs={{0,1},{1,0},{2,3},{3,2},{4,5},{5,4},{6,7},{7,6},{8,9},{9,8},{10,11... | collective-permute-start | bytes 884744 | tf_op jit(solution)/shard_map/ppermute | solution.py:303
  98.6 28.9 %collective-permute-start.22 = (bf16[256,384]{1,0:T(8,128)(2,1)S(1)}, bf16[256,384]{1,0:T(8,128)(2,1)S(1)}, u32[]{:S(2)}, u32[]{:S(2)}) collective-permute-start(bf16[256,384]{1,0:T(8,128)(2,1)S(1)} %get-tuple-element.120), channel_id=1, source_target_pairs={{0,1},{1,0},{2,3},{3,2},{4,5},{5,4},{6,7},{7,6},{8,9},{9,8},{10,11... | collective-permute-start | bytes 589832 | tf_op jit(solution)/shard_map/ppermute | solution.py:303
  108.6 17.6 %collective-permute-start.23 = (bf16[128,384]{1,0:T(8,128)(2,1)S(1)}, bf16[128,384]{1,0:T(8,128)(2,1)S(1)}, u32[]{:S(2)}, u32[]{:S(2)}) collective-permute-start(bf16[128,384]{1,0:T(8,128)(2,1)S(1)} %get-tuple-element.121), channel_id=1, source_target_pairs={{0,1},{1,0},{2,3},{3,2},{4,5},{5,4},{6,7},{7,6},{8,9},{9,8},{10,11... | collective-permute-start | bytes 294920 | tf_op jit(solution)/shard_map/ppermute | solution.py:303
  (2 other events, 22.5 us)

commit v9 on v7

--- a/solution.py
+++ b/solution.py
@@ -1,4 +1,5 @@
 import functools
+import math
 
 import jax
 import jax.numpy as jnp
@@ -138,10 +139,19 @@
 
     grads_core(divisor, k_ref, v_ref, gu_ref, down_ref, own_gu, own_down, hid_s, dout_s, dgu_s)
     send_gu[...] = own_gu[...].astype(BF16)
-    first = 0
-    for send in sends:
-        send[...] = own_down[pl.ds(first, send.shape[0]), :].astype(BF16)
-        first += send.shape[0]
+    if len(sends) == 1:
+        sends[0][...] = own_down[...].astype(BF16)
+    else:
+        partner = 1 - lax.axis_index("tok")
+        for send, (first, size) in zip(sends, cut_rows(down_ref.shape[0], partner)):
+            send[...] = own_down[pl.ds(first, size), :].astype(BF16)
+
+
+def cut_rows(width, tok):
+    return (
+        (pl.multiple_of(tok * 128, 128), width - 128),
+        (pl.multiple_of((1 - tok) * (width - 128), 128), 128),
+    )
 
 
 def updated(rate, old_ref, at, moment):
@@ -152,10 +162,10 @@
     return (moved * (old_norm / new_norm)).astype(BF16)
 
 
-def summed(own_ref, recvs, first, size, sent_from=0):
+def summed(own_ref, recvs, first, size, recv_first):
     total = own_ref[pl.ds(first, size), :]
     for recv in recvs:
-        total = total + recv[pl.ds(first - sent_from, size), :].astype(F32)
+        total = total + recv[pl.ds(recv_first, size), :].astype(F32)
     return total
 
 
@@ -163,17 +173,18 @@
     recvs = refs[: n - 1]
     new_ref, moment_ref = refs[-2:]
     width = own_ref.shape[1]
+    if mats[0]:
+        before = refs[n - 1]
+        moment_ref[: mats[0] * width, :] = before[...]
     for i, m in enumerate(mats):
         at = pl.ds(i * width, width)
-        moment = summed(own_ref, recvs, i * width, width)
+        moment = summed(own_ref, recvs, i * width, width, i * width)
         new_ref[at, :] = updated(rate_ref[head : head + 1, m : m + 1], old_ref, at, moment)
         moment_ref[m * width : (m + 1) * width, :] = moment.astype(BF16)
 
 
-def store_mine(n, m, head, me, new_s, moment_s, fast_s, mine_s, fast_ref, moment_ref, sems):
-    width = moment_s.shape[1]
-    part = width // n
-    mine = pl.multiple_of(me * part, part)
+def store_mine(m, head, mine, new_s, moment_s, fast_s, mine_s, fast_ref, moment_ref, sems):
+    part = fast_s.shape[0]
     fast_s[...] = new_s[pl.ds(mine, part), :]
     mine_s[...] = moment_s[pl.ds(mine, part), :]
     stores = [
@@ -189,19 +200,20 @@
     recvs = refs[: n - 1]
     hq_ref, fast_ref, moment_ref, gu_s, moment_s, fast_s, mine_s, sems = refs[-8:]
     width = own_ref.shape[1]
+    part = width // n
+    mine = pl.multiple_of(lax.axis_index("tok") * part, part)
     stores = []
     for m in range(2):
         at = pl.ds(m * width, width)
         moment = decay_ref[:, head : head + 1] * earlier_ref[at, :].astype(F32)
-        moment = moment + summed(own_ref, recvs, m * width, width)
+        moment = moment + summed(own_ref, recvs, m * width, width, m * width)
         new_s = gu_s.at[at, :]
         new_s[...] = updated(rate_ref[head : head + 1, m : m + 1], old_ref, at, moment)
         moment_s[...] = moment
         stores += store_mine(
-            n,
             m,
             head,
-            lax.axis_index("tok"),
+            mine,
             new_s,
             moment_s,
             fast_s.at[m],
@@ -217,33 +229,34 @@
         store.wait()
 
 
-def update_two_down(n, head, first, rate_ref, decay_ref, old_ref, own_ref, earlier_ref, hq_ref, *refs):
+def update_two_down(n, head, cut, rate_ref, decay_ref, old_ref, own_ref, earlier_ref, hq_ref, *refs):
     recvs = refs[: n - 1]
     width = old_ref.shape[1]
-    size = recvs[0].shape[0]
-    last = first + size == width
-    if last:
-        out_ref, fast_ref, moment_ref, new_s, kept_s, out_s, fast_s, mine_s, out_sems, sems = refs[-10:]
+    part = width // n
+    me = lax.axis_index("tok")
+    if cut is None:
+        first, size, mine = 0, width, me * part
     else:
-        out_ref, new_s, kept_s, out_s, out_sems = refs[-5:]
-    if first and last:
-        before_new, before_kept = refs[n - 1 : n + 1]
-        new_s[:first, :] = before_new[:first, :]
-        kept_s[:first, :] = before_kept[:first, :]
+        first, size = cut_rows(width, me)[cut]
+        mine = me * part - first
     at = pl.ds(first, size)
+    if cut == 1:
+        out_ref, new_s, out_s, out_sems = refs[-4:]
+    else:
+        out_ref, fast_ref, moment_ref, new_s, out_s, out_sems, kept_s, fast_s, mine_s, sems = refs[-10:]
     moment = decay_ref[:, head : head + 1] * earlier_ref[pl.ds(2 * width + first, size), :].astype(F32)
-    moment = moment + summed(own_ref, recvs, first, size, first)
-    new_s[at, :] = updated(rate_ref[head : head + 1, 2:], old_ref, at, moment)
-    kept_s[at, :] = moment
+    moment = moment + summed(own_ref, recvs, first, size, 0)
+    new_s[...] = updated(rate_ref[head : head + 1, 2:], old_ref, at, moment)
     stores = []
-    if last:
-        me = lax.axis_index("tok")
+    if cut != 1:
+        kept_s[...] = moment
+        mine = pl.multiple_of(mine, math.gcd(part, 128))
         stores = store_mine(
-            n, 2, head, me, new_s, kept_s, fast_s, mine_s, fast_ref, moment_ref, sems
-        )
-    cols = pl.ds(head * width + first, size)
+            2, head, mine, new_s, kept_s, fast_s, mine_s, fast_ref, moment_ref, sems
+        )
+    cols = pl.ds(pl.multiple_of(head * width + first, 128), size)
     for i, rows in enumerate(row_chunks(hq_ref.shape[0])):
-        out_s[rows, :] = mm(hq_ref[rows, :], new_s[at, :], ((1,), (1,))).astype(BF16)
+        out_s[rows, :] = mm(hq_ref[rows, :], new_s[...], ((1,), (1,))).astype(BF16)
         stores.append(
             pltpu.make_async_copy(out_s.at[rows, :], out_ref.at[1, rows, cols], out_sems.at[i])
         )
@@ -316,7 +329,8 @@
         )
         recv_fast.append(turned(owned[h]))
 
-    sources = [(2 * (p + 1)) % blocks for p in range(3 * heads)]
+    apart = max(blocks // (3 * heads + 2), 1)
+    sources = [apart * (p + 1) % blocks for p in range(3 * heads)]
     piece = call(functools.partial(take_piece, sources), shape(part, width), [HBM], VMEM)(begin_t)
     crossed = [
         lax.ppermute(
@@ -362,10 +376,9 @@
         ):
             new, *moment = call(
                 functools.partial(update_one, n, h, mats),
-                (shape(len(mats) * width, width), shape(3 * width, width)),
+                (shape(len(mats) * width, width), shape((mats[-1] + 1) * width, width)),
                 [VMEM] * (2 + n + len(moment)),
                 (VMEM, VMEM),
-                aliases={2 + n: 1} if moment else None,
             )(rates, old, own, *recvs, *moment)
             pack.append(new)
         packs.append(pack)
@@ -386,7 +399,8 @@
     for h in range(heads):
         arrived = [forward(packs[h][0]), forward(packs[h][1])]
         pieces = [begins[3 * h + m][r] for r in range(n - 1) for m in range(3)]
-        cuts = [width - 128, 128] if h == heads - 1 and width % 128 == 0 else [width]
+        cuttable = n == 2 and width % 128 == 0 and part <= width - 128
+        cuts = [width - 128, 128] if cuttable and h == heads - 1 else [width]
         second.append(
             call(
                 functools.partial(grads_two, n, divisor),
@@ -439,37 +453,31 @@
             ),
             aliases={at: 1, at + 1: 2} if ends else None,
         )(rates, decays, gu, own_gu, moments[h], kvq[1][h][2], *recv_gu, *ends)
-        kept, first_row = [], 0
-        for recvs in recv_down:
+        for i, recvs in enumerate(recv_down):
             size = recvs[0].shape[0]
-            last = first_row + size == width
-            if last:
-                outs = (out_shape, fast_shape, moment_shape)
-                aliases = {at + len(kept) + j: j for j in range(3)}
-                extra = [*kept, outputs, *ends]
-            else:
-                outs = (out_shape, shape(width, width), shape(width, width, dtype=F32))
-                aliases = {at: 0}
-                extra = [outputs]
-            buffers = (pltpu.VMEM((width, width), BF16), pltpu.VMEM((width, width), F32))
-            mine = (pltpu.VMEM((part, width), BF16), pltpu.VMEM((part, width), F32))
+            outs = (out_shape, fast_shape, moment_shape)[: 1 if i else 3]
+            extra = [outputs, *ends][: len(outs)]
+            scratch = (
+                pltpu.VMEM((size, width), BF16),
+                pltpu.VMEM((rows, size), BF16),
+                DMA((chunks,)),
+            )
+            if not i:
+                scratch += (
+                    pltpu.VMEM((size, width), F32),
+                    pltpu.VMEM((part, width), BF16),
+                    pltpu.VMEM((part, width), F32),
+                    DMA((2,)),
+                )
             outputs, *rest = call(
-                functools.partial(update_two_down, n, h, first_row),
+                functools.partial(update_two_down, n, h, i if len(recv_down) > 1 else None),
                 outs,
-                [VMEM] * (5 + n + len(kept)) + [HBM] * (len(extra) - len(kept)),
-                (HBM,) * 3 if last else (HBM, VMEM, VMEM),
-                (buffers if last else ())
-                + (pltpu.VMEM((rows, size), BF16),)
-                + (mine if last else ())
-                + (DMA((chunks,)),)
-                + ((DMA((2,)),) if last else ()),
-                aliases=aliases,
+                [VMEM] * (5 + n) + [HBM] * len(extra),
+                (HBM,) * len(outs),
+                scratch,
+                aliases={at + j: j for j in range(len(outs))},
             )(rates, decays, down, own_down, moments[h], hq, *recvs, *extra)
-            if last:
-                ends = rest
-            else:
-                kept = rest
-            first_row += size
+            ends = rest or ends
     return (outputs, jnp.swapaxes(ends[0], 3, 4), jnp.swapaxes(ends[1], 3, 4))
 
 

time: 129 us -> 129 us (level)
  no operation moved by 1% of the time
where the time goes in v9:
time: 129 us
  waiting for transfers between devices  64.5 us (50%)
  Pallas kernels  32.1 us (25%)
  starting transfers between devices  31.3 us (24%)
    ppermute x6, waiting for transfers between devices, on_device(): lax.ppermute(x, ('block', 'tok'), [(sources[p] * n + i, i) for i in range...  33.2 us
    ppermute x11, waiting for transfers between devices, turned(): lax.ppermute(x, 'tok', [(i, (i + r) % n) for i in range(n)])  31.3 us
    ppermute x11, starting transfers between devices, turned(): lax.ppermute(x, 'tok', [(i, (i + r) % n) for i in range(n)])  15 us
    ppermute x6, starting transfers between devices, forward(): return lax.ppermute(x, 'block', [(i, i + 1) for i in range(blocks - 1)])  7.93 us
    ppermute x6, starting transfers between devices, on_device(): lax.ppermute(x, ('block', 'tok'), [(sources[p] * n + i, i) for i in range...  7.73 us
    pallas_call x2, Pallas kernels, on_device(): call(functools.partial(grads_one, n, h, divisor), grad_out, [VMEM] * (4 +...  5.59 us
    pallas_call x2, Pallas kernels, on_device(): call(functools.partial(grads_two, n, divisor), (shape(2 * width, width),...  5.09 us
    pallas_call x2, Pallas kernels, on_device(): call(functools.partial(apply_one, h), out_shape, [VMEM] * 3 + [HBM] * len...  4.55 us
  transfers between devices with their start and end apart: 24, of which 10 were waited for; matrix products, arithmetic and copies ran while one was open for 0% of the time, Pallas kernels for 23%

profile of v9, /device:TPU:0, one launch (start us, length us, event | category | flops | bytes accessed | tf_op | source)
XLA Modules:
  0.0 129.0 jit_solution(14149893862792861110)
XLA Ops:
  1.6 3.0 %collective-permute-start.11 = (bf16[3,192,384]{2,1,0:T(8,128)(2,1)S(1)}, bf16[3,192,384]{2,1,0:T(8,128)(2,1)S(1)}, u32[]{:S(2)}, u32[]{:S(2)}) collective-permute-start(bf16[3,192,384]{2,1,0:T(8,128)(2,1)S(1)} %shard_map.110.refs_0_), channel_id=1, source_target_pairs={{0,1},{1,0},{2,3},{3,2},{4,5},{5,4},{6,7},{7,6},{8,9},{9,8},{10,11... | collective-permute-start | bytes 1327112 | tf_op jit(solution)/shard_map/ppermute | solution.py:306
  5.6 3.9 %shard_map.103 = (bf16[768,384]{1,0:T(8,128)(2,1)S(1)}, bf16[768,384]{1,0:T(8,128)(2,1)S(1)}, bf16[768,384]{1,0:T(8,128)(2,1)S(1)}, bf16[768,384]{1,0:T(8,128)(2...) custom-call(bf16[2,768,768]{2,1,0:T(8,128)(2,1)} %k_ref.1, ...), custom_call_target="tpu_custom_call" | custom-call | tf_op jit(solution)/shard_map/pallas_call | solution.py:345
  9.5 6.1 %collective-permute-done.11.refs_1_ = bf16[3,192,384]{2,1,0:T(8,128)(2,1)S(1)} collective-permute-done((bf16[3,192,384]{2,1,0:T(8,128)(2,1)S(1)}, bf16[3,192,384]{2,1,0:T(8,128)(2,1)S(1)}, u32[]{:S(2)}, u32[]{:S(2)}) %collective-permute-start.11) | collective-permute-done | bytes 442400 | tf_op jit(solution)/shard_map/ppermute | solution.py:306
  15.6 2.8 %shard_map.111 = (bf16[768,384]{1,0:T(8,128)(2,1)S(1)}, bf16[384,384]{1,0:T(8,128)(2,1)S(1)}, bf16[768,384]{1,0:T(8,128)(2,1)S(1)}, bf16[384,384]{1,0:T(8,128)(2...) custom-call(f32[1,2]{1,0:T(1,128)S(1)} %bitcast.16, bf16[768,384]{1,0:T(8,128)(2,1)S(1)} %get-tuple-element.89.k_ref, ...), custom_call_target="tpu_custom_call" | custom-call | tf_op jit(solution)/shard_map/pallas_call | solution.py:359
  18.4 2.1 %collective-permute-start.12 = (bf16[768,384]{1,0:T(8,128)(2,1)S(1)}, bf16[768,384]{1,0:T(8,128)(2,1)S(1)}, u32[]{:S(2)}, u32[]{:S(2)}) collective-permute-start(bf16[768,384]{1,0:T(8,128)(2,1)S(1)} %get-tuple-element.94), channel_id=1, source_target_pairs={{0,1},{1,0},{2,3},{3,2},{4,5},{5,4},{6,7},{7,6},{8,9},{9,8},{10,11... | collective-permute-start | bytes 1769480 | tf_op jit(solution)/shard_map/ppermute | solution.py:306
  20.5 4.6 %collective-permute-done.refs_1_ = bf16[3,192,384]{2,1,0:T(8,128)(2,1)S(1)} collective-permute-done((bf16[3,192,384]{2,1,0:T(8,128)(2,1)S(1)}, bf16[3,192,384]{2,1,0:T(8,128)(2,1)S(1)}, u32[]{:S(2)}, u32[]{:S(2)}) %collective-permute-start) | collective-permute-done | bytes 442400 | tf_op jit(solution)/shard_map/ppermute | solution.py:306
  25.1 2.8 %shard_map.105 = (bf16[768,384]{1,0:T(8,128)(2,1)S(1)}, bf16[384,384]{1,0:T(8,128)(2,1)S(1)}, bf16[768,384]{1,0:T(8,128)(2,1)S(1)}, bf16[384,384]{1,0:T(8,128)(2...) custom-call(f32[1,2]{1,0:T(1,128)S(1)} %bitcast.17, bf16[768,384]{1,0:T(8,128)(2,1)S(1)} %get-tuple-element.67.k_ref, ...), custom_call_target="tpu_custom_call" | custom-call | tf_op jit(solution)/shard_map/pallas_call | solution.py:359
  27.9 2.1 %collective-permute-start.1 = (bf16[768,384]{1,0:T(8,128)(2,1)S(1)}, bf16[768,384]{1,0:T(8,128)(2,1)S(1)}, u32[]{:S(2)}, u32[]{:S(2)}) collective-permute-start(bf16[768,384]{1,0:T(8,128)(2,1)S(1)} %get-tuple-element.72), channel_id=1, source_target_pairs={{0,1},{1,0},{2,3},{3,2},{4,5},{5,4},{6,7},{7,6},{8,9},{9,8},{10,11... | collective-permute-start | bytes 1769480 | tf_op jit(solution)/shard_map/ppermute | solution.py:306
  33.0 4.8 %collective-permute-done.12.refs_0_ = bf16[768,384]{1,0:T(8,128)(2,1)S(1)} collective-permute-done((bf16[768,384]{1,0:T(8,128)(2,1)S(1)}, bf16[768,384]{1,0:T(8,128)(2,1)S(1)}, u32[]{:S(2)}, u32[]{:S(2)}) %collective-permute-start.12) | collective-permute-done | bytes 589856 | tf_op jit(solution)/shard_map/ppermute | solution.py:306
  39.8 2.1 %collective-permute-start.3 = (bf16[384,384]{1,0:T(8,128)(2,1)S(1)}, bf16[384,384]{1,0:T(8,128)(2,1)S(1)}, u32[]{:S(2)}, u32[]{:S(2)}) collective-permute-start(bf16[384,384]{1,0:T(8,128)(2,1)S(1)} %get-tuple-element.76), channel_id=1, source_target_pairs={{0,1},{1,0},{2,3},{3,2},{4,5},{5,4},{6,7},{7,6},{8,9},{9,8},{10,11... | collective-permute-start | bytes 884744 | tf_op jit(solution)/shard_map/ppermute | solution.py:306
  41.9 18.1 %collective-permute-done.16.refs_2_ = bf16[192,384]{1,0:T(8,128)(2,1)S(1)} collective-permute-done((bf16[192,384]{1,0:T(8,128)(2,1)S(1)}, bf16[192,384]{1,0:T(8,128)(2,1)S(1)}, u32[]{:S(2)}, u32[]{:S(2)}) %collective-permute-start.16) | collective-permute-done | bytes 147488 | tf_op jit(solution)/shard_map/ppermute | solution.py:391
  65.0 2.0 %collective-permute-done.17.refs_3_ = bf16[192,384]{1,0:T(8,128)(2,1)S(1)} collective-permute-done((bf16[192,384]{1,0:T(8,128)(2,1)S(1)}, bf16[192,384]{1,0:T(8,128)(2,1)S(1)}, u32[]{:S(2)}, u32[]{:S(2)}) %collective-permute-start.17) | collective-permute-done | bytes 147488 | tf_op jit(solution)/shard_map/ppermute | solution.py:391
  73.6 7.1 %collective-permute-done.7.refs_3_ = bf16[192,384]{1,0:T(8,128)(2,1)S(1)} collective-permute-done((bf16[192,384]{1,0:T(8,128)(2,1)S(1)}, bf16[192,384]{1,0:T(8,128)(2,1)S(1)}, u32[]{:S(2)}, u32[]{:S(2)}) %collective-permute-start.7) | collective-permute-done | bytes 147488 | tf_op jit(solution)/shard_map/ppermute | solution.py:391
  84.7 2.4 %shard_map.114 = (bf16[768,384]{1,0:T(8,128)(2,1)S(1)}, bf16[384,384]{1,0:T(8,128)(2,1)S(1)}, f32[768,384]{1,0:T(8,128)S(1)}, f32[384,384]{1,0:T(8,128)S(1)}, bf...) custom-call(bf16[768,384]{1,0:T(8,128)(2,1)S(1)} %get-tuple-element.86.k_ref, ...), custom_call_target="tpu_custom_call" | custom-call | tf_op jit(solution)/shard_map/pallas_call | solution.py:405
  87.1 5.1 %collective-permute-done.8.refs_4_ = bf16[192,384]{1,0:T(8,128)(2,1)S(1)} collective-permute-done((bf16[192,384]{1,0:T(8,128)(2,1)S(1)}, bf16[192,384]{1,0:T(8,128)(2,1)S(1)}, u32[]{:S(2)}, u32[]{:S(2)}) %collective-permute-start.8) | collective-permute-done | bytes 147488 | tf_op jit(solution)/shard_map/ppermute | solution.py:391
  93.7 2.7 %shard_map.109 = (bf16[768,384]{1,0:T(8,128)(2,1)S(1)}, bf16[384,384]{1,0:T(8,128)(2,1)S(1)}, f32[768,384]{1,0:T(8,128)S(1)}, f32[384,384]{1,0:T(8,128)S(1)}, bf...) custom-call(bf16[768,384]{1,0:T(8,128)(2,1)S(1)} %get-tuple-element.64.k_ref, ...), custom_call_target="tpu_custom_call" | custom-call | tf_op jit(solution)/shard_map/pallas_call | solution.py:405
  97.0 1.5 %collective-permute-start.21 = (bf16[384,384]{1,0:T(8,128)(2,1)S(1)}, bf16[384,384]{1,0:T(8,128)(2,1)S(1)}, u32[]{:S(2)}, u32[]{:S(2)}) collective-permute-start(bf16[384,384]{1,0:T(8,128)(2,1)S(1)} %get-tuple-element.109), channel_id=1, source_target_pairs={{0,1},{1,0},{2,3},{3,2},{4,5},{5,4},{6,7},{7,6},{8,9},{9,8},{10,11... | collective-permute-start | bytes 884744 | tf_op jit(solution)/shard_map/ppermute | solution.py:306
  99.1 9.4 %collective-permute-done.20.refs_0_ = bf16[768,384]{1,0:T(8,128)(2,1)S(1)} collective-permute-done((bf16[768,384]{1,0:T(8,128)(2,1)S(1)}, bf16[768,384]{1,0:T(8,128)(2,1)S(1)}, u32[]{:S(2)}, u32[]{:S(2)}) %collective-permute-start.20) | collective-permute-done | bytes 589856 | tf_op jit(solution)/shard_map/ppermute | solution.py:306
  109.9 2.3 %shard_map.116.refs_0_ = bf16[2,768,768]{2,1,0:T(8,128)(2,1)} custom-call(bf16[768,384]{1,0:T(8,128)(2,1)S(1)} %get-tuple-element.111.q_ref, bf16[768,384]{1,0:T(8,128)(2,1)S(1)} %get-tuple-element.95.pgu_ref, bf16[384,384]{1,0:T(8,128)(2,1)S(1)} %get-tuple-element.100.pdown_ref), custom_call_target="tpu_custom_call" | custom-call | tf_op jit(solution)/shard_map/pallas_call | solution.py:425
  112.2 2.3 %shard_map.117.refs_1_ = bf16[2,768,768]{2,1,0:T(8,128)(2,1)} custom-call(bf16[768,384]{1,0:T(8,128)(2,1)S(1)} %get-tuple-element.110.q_ref, bf16[768,384]{1,0:T(8,128)(2,1)S(1)} %get-tuple-element.73.pgu_ref, bf16[384,384]{1,0:T(8,128)(2,1)S(1)} %get-tuple-element.78.pdown_ref, bf16[2,768,768]{2,1,0:T(8,128)(2,1)} %shard_map.116.refs_0_), custom_call_target="tpu_custom_call", output_to_operand_aliasing={{}: (3, {})} | custom-call | tf_op jit(solution)/shard_map/pallas_call | solution.py:425
  114.5 1.7 %shard_map.115 = (bf16[768,384]{1,0:T(8,128)(2,1)S(1)}, bf16[1,3,2,192,384]{4,3,2,1,0:T(8,128)(2,1)}, f32[1,3,2,192,384]{4,3,2,1,0:T(8,128)}) custom-call(f32[2,3]{1,0:T(2,128)S(1)} %bitcast.11, f32[1,2]{1,0:T(1,128)S(1)} %bitcast.18, bf16[768,384]{1,0:T(8,128)(2,1)S(1)} %get-tuple-element.104.old_ref, f32[768,384]{1,0:T(8,128)S(1)} %get-tuple-element.105.own_ref, ...), custom_call_target="tpu_custom_call" | custom-call | tf_op jit(solution)/shard_map/pallas_call | solution.py:442
  116.2 6.5 %collective-permute-done.21.refs_0_ = bf16[384,384]{1,0:T(8,128)(2,1)S(1)} collective-permute-done((bf16[384,384]{1,0:T(8,128)(2,1)S(1)}, bf16[384,384]{1,0:T(8,128)(2,1)S(1)}, u32[]{:S(2)}, u32[]{:S(2)}) %collective-permute-start.21) | collective-permute-done | bytes 294944 | tf_op jit(solution)/shard_map/ppermute | solution.py:306
  122.7 1.7 %shard_map.118 = (bf16[2,768,768]{2,1,0:T(8,128)(2,1)}, bf16[1,3,2,192,384]{4,3,2,1,0:T(8,128)(2,1)}, f32[1,3,2,192,384]{4,3,2,1,0:T(8,128)}) custom-call(f32[2,3]{1,0:T(2,128)S(1)} %bitcast.12, f32[1,2]{1,0:T(1,128)S(1)} %bitcast.19, bf16[384,384]{1,0:T(8,128)(2,1)S(1)} %get-tuple-element.101.old_ref, ...), custom_call_target="tpu_custom_call", output_to_operand_aliasing={{0}: (7, {}), {1}: (8, {}), {2}: (9, {})} | custom-call | tf_op jit(solution)/shard_map/pallas_call | solution.py:472
  124.4 1.7 %shard_map.119 = (bf16[768,384]{1,0:T(8,128)(2,1)S(1)}, bf16[1,3,2,192,384]{4,3,2,1,0:T(8,128)(2,1)}, f32[1,3,2,192,384]{4,3,2,1,0:T(8,128)}) custom-call(f32[2,3]{1,0:T(2,128)S(1)} %bitcast.13, f32[1,2]{1,0:T(1,128)S(1)} %bitcast.20, bf16[768,384]{1,0:T(8,128)(2,1)S(1)} %get-tuple-element.82.old_ref, ...), custom_call_target="tpu_custom_call", output_to_operand_aliasing={{1}: (7, {}), {2}: (8, {})} | custom-call | tf_op jit(solution)/shard_map/pallas_call | solution.py:442
  (47 shorter events, 29.3 us)
Async XLA Ops:
  1.6 14.0 %collective-permute-start.11 = (bf16[3,192,384]{2,1,0:T(8,128)(2,1)S(1)}, bf16[3,192,384]{2,1,0:T(8,128)(2,1)S(1)}, u32[]{:S(2)}, u32[]{:S(2)}) collective-permute-start(bf16[3,192,384]{2,1,0:T(8,128)(2,1)S(1)} %shard_map.110.refs_0_), channel_id=1, source_target_pairs={{0,1},{1,0},{2,3},{3,2},{4,5},{5,4},{6,7},{7,6},{8,9},{9,8},{10,11... | collective-permute-start | bytes 1327112 | tf_op jit(solution)/shard_map/ppermute | solution.py:306
  5.6 19.5 %collective-permute-start = (bf16[3,192,384]{2,1,0:T(8,128)(2,1)S(1)}, bf16[3,192,384]{2,1,0:T(8,128)(2,1)S(1)}, u32[]{:S(2)}, u32[]{:S(2)}) collective-permute-start(bf16[3,192,384]{2,1,0:T(8,128)(2,1)S(1)} %shard_map.104.refs_0_), channel_id=1, source_target_pairs={{0,1},{1,0},{2,3},{3,2},{4,5},{5,4},{6,7},{7,6},{8,9},{9,8},{10,11... | collective-permute-start | bytes 1327112 | tf_op jit(solution)/shard_map/ppermute | solution.py:306
  18.4 19.3 %collective-permute-start.12 = (bf16[768,384]{1,0:T(8,128)(2,1)S(1)}, bf16[768,384]{1,0:T(8,128)(2,1)S(1)}, u32[]{:S(2)}, u32[]{:S(2)}) collective-permute-start(bf16[768,384]{1,0:T(8,128)(2,1)S(1)} %get-tuple-element.94), channel_id=1, source_target_pairs={{0,1},{1,0},{2,3},{3,2},{4,5},{5,4},{6,7},{7,6},{8,9},{9,8},{10,11... | collective-permute-start | bytes 1769480 | tf_op jit(solution)/shard_map/ppermute | solution.py:306
  27.9 34.7 %collective-permute-start.1 = (bf16[768,384]{1,0:T(8,128)(2,1)S(1)}, bf16[768,384]{1,0:T(8,128)(2,1)S(1)}, u32[]{:S(2)}, u32[]{:S(2)}) collective-permute-start(bf16[768,384]{1,0:T(8,128)(2,1)S(1)} %get-tuple-element.72), channel_id=1, source_target_pairs={{0,1},{1,0},{2,3},{3,2},{4,5},{5,4},{6,7},{7,6},{8,9},{9,8},{10,11... | collective-permute-start | bytes 1769480 | tf_op jit(solution)/shard_map/ppermute | solution.py:306
  30.9 0.8 collective-permute-start.5
  31.6 29.7 %collective-permute-start.14 = (bf16[384,384]{1,0:T(8,128)(2,1)S(1)}, bf16[384,384]{1,0:T(8,128)(2,1)S(1)}, u32[]{:S(2)}, u32[]{:S(2)}) collective-permute-start(bf16[384,384]{1,0:T(8,128)(2,1)S(1)} %get-tuple-element.98), channel_id=1, source_target_pairs={{0,1},{1,0},{2,3},{3,2},{4,5},{5,4},{6,7},{7,6},{8,9},{9,8},{10,11... | collective-permute-start | bytes 884744 | tf_op jit(solution)/shard_map/ppermute | solution.py:306
  31.7 28.3 %collective-permute-start.16 = (bf16[192,384]{1,0:T(8,128)(2,1)S(1)}, bf16[192,384]{1,0:T(8,128)(2,1)S(1)}, u32[]{:S(2)}, u32[]{:S(2)}) collective-permute-start(bf16[192,384]{1,0:T(8,128)(2,1)S(1)} %collective-permute-done.5), channel_id=1, source_target_pairs={{4,0},{5,1}} | collective-permute-start | bytes 442376 | tf_op jit(solution)/shard_map/ppermute | solution.py:391
  38.5 45.0 %collective-permute-start.13 = (bf16[768,384]{1,0:T(8,128)(2,1)S(1)}, bf16[768,384]{1,0:T(8,128)(2,1)S(1)}, u32[]{:S(2)}, u32[]{:S(2)}) collective-permute-start(bf16[768,384]{1,0:T(8,128)(2,1)S(1)} %get-tuple-element.95.pgu_ref), channel_id=1, source_target_pairs={{0,2},{2,4},{4,6},{6,8},{8,10},{10,12},{12,14},{14,16},{16,18},{18... | collective-permute-start | bytes 1769480 | tf_op jit(solution)/shard_map/ppermute | solution.py:309
  39.8 32.1 %collective-permute-start.3 = (bf16[384,384]{1,0:T(8,128)(2,1)S(1)}, bf16[384,384]{1,0:T(8,128)(2,1)S(1)}, u32[]{:S(2)}, u32[]{:S(2)}) collective-permute-start(bf16[384,384]{1,0:T(8,128)(2,1)S(1)} %get-tuple-element.76), channel_id=1, source_target_pairs={{0,1},{1,0},{2,3},{3,2},{4,5},{5,4},{6,7},{7,6},{8,9},{9,8},{10,11... | collective-permute-start | bytes 884744 | tf_op jit(solution)/shard_map/ppermute | solution.py:306
  60.0 7.0 %collective-permute-start.17 = (bf16[192,384]{1,0:T(8,128)(2,1)S(1)}, bf16[192,384]{1,0:T(8,128)(2,1)S(1)}, u32[]{:S(2)}, u32[]{:S(2)}) collective-permute-start(bf16[192,384]{1,0:T(8,128)(2,1)S(1)} %collective-permute-done.5), channel_id=1, source_target_pairs={{8,0},{9,1}} | collective-permute-start | bytes 442376 | tf_op jit(solution)/shard_map/ppermute | solution.py:391
  61.3 7.9 %collective-permute-start.18 = (bf16[192,384]{1,0:T(8,128)(2,1)S(1)}, bf16[192,384]{1,0:T(8,128)(2,1)S(1)}, u32[]{:S(2)}, u32[]{:S(2)}) collective-permute-start(bf16[192,384]{1,0:T(8,128)(2,1)S(1)} %collective-permute-done.5), channel_id=1, source_target_pairs={{12,0},{13,1}} | collective-permute-start | bytes 442376 | tf_op jit(solution)/shard_map/ppermute | solution.py:391
  62.6 7.9 %collective-permute-start.6 = (bf16[192,384]{1,0:T(8,128)(2,1)S(1)}, bf16[192,384]{1,0:T(8,128)(2,1)S(1)}, u32[]{:S(2)}, u32[]{:S(2)}) collective-permute-start(bf16[192,384]{1,0:T(8,128)(2,1)S(1)} %collective-permute-done.5), channel_id=1, source_target_pairs={{16,0},{17,1}} | collective-permute-start | bytes 442376 | tf_op jit(solution)/shard_map/ppermute | solution.py:391
  67.0 26.7 %collective-permute-start.2 = (bf16[768,384]{1,0:T(8,128)(2,1)S(1)}, bf16[768,384]{1,0:T(8,128)(2,1)S(1)}, u32[]{:S(2)}, u32[]{:S(2)}) collective-permute-start(bf16[768,384]{1,0:T(8,128)(2,1)S(1)} %get-tuple-element.73.pgu_ref), channel_id=1, source_target_pairs={{0,2},{2,4},{4,6},{6,8},{8,10},{10,12},{12,14},{14,16},{16,18},{18... | collective-permute-start | bytes 1769480 | tf_op jit(solution)/shard_map/ppermute | solution.py:309
  69.2 12.8 %collective-permute-start.15 = (bf16[384,384]{1,0:T(8,128)(2,1)S(1)}, bf16[384,384]{1,0:T(8,128)(2,1)S(1)}, u32[]{:S(2)}, u32[]{:S(2)}) collective-permute-start(bf16[384,384]{1,0:T(8,128)(2,1)S(1)} %get-tuple-element.100.pdown_ref), channel_id=1, source_target_pairs={{0,2},{2,4},{4,6},{6,8},{8,10},{10,12},{12,14},{14,16},{16,18},{18... | collective-permute-start | bytes 884744 | tf_op jit(solution)/shard_map/ppermute | solution.py:309
  70.5 28.0 %collective-permute-start.19 = (bf16[1152,384]{1,0:T(8,128)(2,1)S(1)}, bf16[1152,384]{1,0:T(8,128)(2,1)S(1)}, u32[]{:S(2)}, u32[]{:S(2)}) collective-permute-start(bf16[1152,384]{1,0:T(8,128)(2,1)S(1)} %get-tuple-element.103), channel_id=1, source_target_pairs={{0,2},{2,4},{4,6},{6,8},{8,10},{10,12},{12,14},{14,16},{16,18},{18... | collective-permute-start | bytes 2654216 | tf_op jit(solution)/shard_map/ppermute | solution.py:309
  71.9 8.8 %collective-permute-start.7 = (bf16[192,384]{1,0:T(8,128)(2,1)S(1)}, bf16[192,384]{1,0:T(8,128)(2,1)S(1)}, u32[]{:S(2)}, u32[]{:S(2)}) collective-permute-start(bf16[192,384]{1,0:T(8,128)(2,1)S(1)} %collective-permute-done.5), channel_id=1, source_target_pairs={{20,0},{21,1}} | collective-permute-start | bytes 442376 | tf_op jit(solution)/shard_map/ppermute | solution.py:391
  80.7 13.0 %collective-permute-start.4 = (bf16[384,384]{1,0:T(8,128)(2,1)S(1)}, bf16[384,384]{1,0:T(8,128)(2,1)S(1)}, u32[]{:S(2)}, u32[]{:S(2)}) collective-permute-start(bf16[384,384]{1,0:T(8,128)(2,1)S(1)} %get-tuple-element.78.pdown_ref), channel_id=1, source_target_pairs={{0,2},{2,4},{4,6},{6,8},{8,10},{10,12},{12,14},{14,16},{16,18},{18... | collective-permute-start | bytes 884744 | tf_op jit(solution)/shard_map/ppermute | solution.py:309
  82.0 42.3 %collective-permute-start.9 = (bf16[1152,384]{1,0:T(8,128)(2,1)S(1)}, bf16[1152,384]{1,0:T(8,128)(2,1)S(1)}, u32[]{:S(2)}, u32[]{:S(2)}) collective-permute-start(bf16[1152,384]{1,0:T(8,128)(2,1)S(1)} %get-tuple-element.81), channel_id=1, source_target_pairs={{0,2},{2,4},{4,6},{6,8},{8,10},{10,12},{12,14},{14,16},{16,18},{18... | collective-permute-start | bytes 2654216 | tf_op jit(solution)/shard_map/ppermute | solution.py:309
  83.4 8.8 %collective-permute-start.8 = (bf16[192,384]{1,0:T(8,128)(2,1)S(1)}, bf16[192,384]{1,0:T(8,128)(2,1)S(1)}, u32[]{:S(2)}, u32[]{:S(2)}) collective-permute-start(bf16[192,384]{1,0:T(8,128)(2,1)S(1)} %collective-permute-done.5), channel_id=1, source_target_pairs={{24,0},{25,1}} | collective-permute-start | bytes 442376 | tf_op jit(solution)/shard_map/ppermute | solution.py:391
  92.2 16.2 %collective-permute-start.20 = (bf16[768,384]{1,0:T(8,128)(2,1)S(1)}, bf16[768,384]{1,0:T(8,128)(2,1)S(1)}, u32[]{:S(2)}, u32[]{:S(2)}) collective-permute-start(bf16[768,384]{1,0:T(8,128)(2,1)S(1)} %get-tuple-element.107), channel_id=1, source_target_pairs={{0,1},{1,0},{2,3},{3,2},{4,5},{5,4},{6,7},{7,6},{8,9},{9,8},{10,11... | collective-permute-start | bytes 1769480 | tf_op jit(solution)/shard_map/ppermute | solution.py:306
  96.4 28.0 %collective-permute-start.10 = (bf16[768,384]{1,0:T(8,128)(2,1)S(1)}, bf16[768,384]{1,0:T(8,128)(2,1)S(1)}, u32[]{:S(2)}, u32[]{:S(2)}) collective-permute-start(bf16[768,384]{1,0:T(8,128)(2,1)S(1)} %get-tuple-element.85), channel_id=1, source_target_pairs={{0,1},{1,0},{2,3},{3,2},{4,5},{5,4},{6,7},{7,6},{8,9},{9,8},{10,11... | collective-permute-start | bytes 1769480 | tf_op jit(solution)/shard_map/ppermute | solution.py:306
  97.0 25.7 %collective-permute-start.21 = (bf16[384,384]{1,0:T(8,128)(2,1)S(1)}, bf16[384,384]{1,0:T(8,128)(2,1)S(1)}, u32[]{:S(2)}, u32[]{:S(2)}) collective-permute-start(bf16[384,384]{1,0:T(8,128)(2,1)S(1)} %get-tuple-element.109), channel_id=1, source_target_pairs={{0,1},{1,0},{2,3},{3,2},{4,5},{5,4},{6,7},{7,6},{8,9},{9,8},{10,11... | collective-permute-start | bytes 884744 | tf_op jit(solution)/shard_map/ppermute | solution.py:306
  98.5 27.6 %collective-permute-start.23 = (bf16[256,384]{1,0:T(8,128)(2,1)S(1)}, bf16[256,384]{1,0:T(8,128)(2,1)S(1)}, u32[]{:S(2)}, u32[]{:S(2)}) collective-permute-start(bf16[256,384]{1,0:T(8,128)(2,1)S(1)} %get-tuple-element.118), channel_id=1, source_target_pairs={{0,1},{1,0},{2,3},{3,2},{4,5},{5,4},{6,7},{7,6},{8,9},{9,8},{10,11... | collective-permute-start | bytes 589832 | tf_op jit(solution)/shard_map/ppermute | solution.py:306
  108.4 19.2 %collective-permute-start.22 = (bf16[128,384]{1,0:T(8,128)(2,1)S(1)}, bf16[128,384]{1,0:T(8,128)(2,1)S(1)}, u32[]{:S(2)}, u32[]{:S(2)}) collective-permute-start(bf16[128,384]{1,0:T(8,128)(2,1)S(1)} %get-tuple-element.117), channel_id=1, source_target_pairs={{0,1},{1,0},{2,3},{3,2},{4,5},{5,4},{6,7},{7,6},{8,9},{9,8},{10,11... | collective-permute-start | bytes 294920 | tf_op jit(solution)/shard_map/ppermute | solution.py:306
  (2 other events, 22.6 us)

commit v10 on v9

--- a/solution.py
+++ b/solution.py
@@ -230,39 +230,60 @@
 
 
 def update_two_down(n, head, cut, rate_ref, decay_ref, old_ref, own_ref, earlier_ref, hq_ref, *refs):
-    recvs = refs[: n - 1]
+    recvs, refs = refs[: n - 1], refs[n - 1 :]
     width = old_ref.shape[1]
     part = width // n
     me = lax.axis_index("tok")
-    if cut is None:
-        first, size, mine = 0, width, me * part
-    else:
-        first, size = cut_rows(width, me)[cut]
-        mine = me * part - first
+    parts = [(0, width)] if cut is None else cut_rows(width, me)
+    first, size = parts[cut or 0]
     at = pl.ds(first, size)
-    if cut == 1:
-        out_ref, new_s, out_s, out_sems = refs[-4:]
+    chunks = row_chunks(hq_ref.shape[0])
+
+    def columns(which):
+        first, size = parts[which]
+        return pl.ds(pl.multiple_of(head * width + first, 128), size)
+
+    if cut == 0:
+        out_s, fast_s, mine_s, new_s, kept_s = refs
+    elif cut == 1:
+        before = refs[:3]
+        out_ref, fast_ref, moment_ref, new_s, out_s, out_sems, sems = refs[-7:]
+        stores = [
+            pltpu.make_async_copy(before[0], out_ref.at[1, :, columns(0)], sems.at[0]),
+            pltpu.make_async_copy(before[1], fast_ref.at[0, 2, head], sems.at[1]),
+            pltpu.make_async_copy(before[2], moment_ref.at[0, 2, head], sems.at[2]),
+        ]
+        for store in stores:
+            store.start()
     else:
         out_ref, fast_ref, moment_ref, new_s, out_s, out_sems, kept_s, fast_s, mine_s, sems = refs[-10:]
     moment = decay_ref[:, head : head + 1] * earlier_ref[pl.ds(2 * width + first, size), :].astype(F32)
     moment = moment + summed(own_ref, recvs, first, size, 0)
     new_s[...] = updated(rate_ref[head : head + 1, 2:], old_ref, at, moment)
-    stores = []
     if cut != 1:
         kept_s[...] = moment
-        mine = pl.multiple_of(mine, math.gcd(part, 128))
-        stores = store_mine(
-            2, head, mine, new_s, kept_s, fast_s, mine_s, fast_ref, moment_ref, sems
-        )
-    cols = pl.ds(pl.multiple_of(head * width + first, 128), size)
-    for i, rows in enumerate(row_chunks(hq_ref.shape[0])):
+        mine = pl.ds(pl.multiple_of(me * part - first, math.gcd(part, 128)), part)
+        fast_s[...] = new_s[mine, :]
+        mine_s[...] = kept_s[mine, :]
+    if cut is None:
+        stores = [
+            pltpu.make_async_copy(fast_s, fast_ref.at[0, 2, head], sems.at[0]),
+            pltpu.make_async_copy(mine_s, moment_ref.at[0, 2, head], sems.at[1]),
+        ]
+        for store in stores:
+            store.start()
+    for i, rows in enumerate(chunks):
         out_s[rows, :] = mm(hq_ref[rows, :], new_s[...], ((1,), (1,))).astype(BF16)
-        stores.append(
-            pltpu.make_async_copy(out_s.at[rows, :], out_ref.at[1, rows, cols], out_sems.at[i])
-        )
-        stores[-1].start()
-    for store in stores:
-        store.wait()
+        if cut != 0:
+            stores.append(
+                pltpu.make_async_copy(
+                    out_s.at[rows, :], out_ref.at[1, rows, columns(cut or 0)], out_sems.at[i]
+                )
+            )
+            stores[-1].start()
+    if cut != 0:
+        for store in stores:
+            store.wait()
 
 
 def apply_one(head, q_ref, pgu_ref, pdown_ref, *refs):
@@ -453,31 +474,36 @@
             ),
             aliases={at: 1, at + 1: 2} if ends else None,
         )(rates, decays, gu, own_gu, moments[h], kvq[1][h][2], *recv_gu, *ends)
+        before = []
         for i, recvs in enumerate(recv_down):
+            cut = i if len(recv_down) > 1 else None
             size = recvs[0].shape[0]
-            outs = (out_shape, fast_shape, moment_shape)[: 1 if i else 3]
-            extra = [outputs, *ends][: len(outs)]
-            scratch = (
-                pltpu.VMEM((size, width), BF16),
-                pltpu.VMEM((rows, size), BF16),
-                DMA((chunks,)),
-            )
-            if not i:
-                scratch += (
-                    pltpu.VMEM((size, width), F32),
-                    pltpu.VMEM((part, width), BF16),
-                    pltpu.VMEM((part, width), F32),
-                    DMA((2,)),
-                )
-            outputs, *rest = call(
-                functools.partial(update_two_down, n, h, i if len(recv_down) > 1 else None),
+            new = pltpu.VMEM((size, width), BF16)
+            kept = pltpu.VMEM((size, width), F32)
+            if cut == 0:
+                outs = (shape(rows, size), shape(part, width), shape(part, width, dtype=F32))
+                extra, scratch, space = [], (new, kept), VMEM
+            else:
+                outs = (out_shape, fast_shape, moment_shape)
+                extra, space = [outputs, *ends], HBM
+                scratch = (new, pltpu.VMEM((rows, size), BF16), DMA((chunks,)))
+                if cut is None:
+                    scratch += (kept, pltpu.VMEM((part, width), BF16))
+                    scratch += (pltpu.VMEM((part, width), F32), DMA((2,)))
+                else:
+                    scratch += (DMA((3,)),)
+            results = call(
+                functools.partial(update_two_down, n, h, cut),
                 outs,
-                [VMEM] * (5 + n) + [HBM] * len(extra),
-                (HBM,) * len(outs),
+                [VMEM] * (5 + n + len(before)) + [HBM] * len(extra),
+                (space,) * 3,
                 scratch,
-                aliases={at + j: j for j in range(len(outs))},
-            )(rates, decays, down, own_down, moments[h], hq, *recvs, *extra)
-            ends = rest or ends
+                aliases={at + len(before) + j: j for j in range(len(extra))},
+            )(rates, decays, down, own_down, moments[h], hq, *recvs, *before, *extra)
+            if cut == 0:
+                before = results
+            else:
+                outputs, *ends = results
     return (outputs, jnp.swapaxes(ends[0], 3, 4), jnp.swapaxes(ends[1], 3, 4))
 
 

time: 129 us -> 129 us (level)
  no operation moved by 1% of the time
where the time goes in v10:
time: 129 us; the launch traced here: 128 us
  waiting for transfers between devices  64.5 us (50%)
  Pallas kernels  31.5 us (24%)
  starting transfers between devices  31.2 us (24%)
    ppermute x6, waiting for transfers between devices, on_device(): lax.ppermute(x, ('block', 'tok'), [(sources[p] * n + i, i) for i in range...  33.2 us
    ppermute x11, waiting for transfers between devices, turned(): lax.ppermute(x, 'tok', [(i, (i + r) % n) for i in range(n)])  31.3 us
    ppermute x11, starting transfers between devices, turned(): lax.ppermute(x, 'tok', [(i, (i + r) % n) for i in range(n)])  14.9 us
    ppermute x6, starting transfers between devices, forward(): return lax.ppermute(x, 'block', [(i, i + 1) for i in range(blocks - 1)])  7.93 us
    ppermute x6, starting transfers between devices, on_device(): lax.ppermute(x, ('block', 'tok'), [(sources[p] * n + i, i) for i in range...  7.73 us
    pallas_call x2, Pallas kernels, on_device(): call(functools.partial(grads_one, n, h, divisor), grad_out, [VMEM] * (4 +...  5.66 us
    pallas_call x2, Pallas kernels, on_device(): call(functools.partial(grads_two, n, divisor), (shape(2 * width, width),...  5.08 us
    pallas_call x2, Pallas kernels, on_device(): call(functools.partial(apply_one, h), out_shape, [VMEM] * 3 + [HBM] * len...  4.56 us
  transfers between devices with their start and end apart: 24, of which 10 were waited for; matrix products, arithmetic and copies ran while one was open for 0% of the time, Pallas kernels for 23%

profile of v10, /device:TPU:0, one launch (start us, length us, event | category | flops | bytes accessed | tf_op | source)
XLA Modules:
  0.0 128.3 jit_solution(16954962276131496090)
XLA Ops:
  1.6 3.0 %collective-permute-start.11 = (bf16[3,192,384]{2,1,0:T(8,128)(2,1)S(1)}, bf16[3,192,384]{2,1,0:T(8,128)(2,1)S(1)}, u32[]{:S(2)}, u32[]{:S(2)}) collective-permute-start(bf16[3,192,384]{2,1,0:T(8,128)(2,1)S(1)} %shard_map.110.refs_0_), channel_id=1, source_target_pairs={{0,1},{1,0},{2,3},{3,2},{4,5},{5,4},{6,7},{7,6},{8,9},{9,8},{10,11... | collective-permute-start | bytes 1327112 | tf_op jit(solution)/shard_map/ppermute | solution.py:327
  5.6 3.9 %shard_map.103 = (bf16[768,384]{1,0:T(8,128)(2,1)S(1)}, bf16[768,384]{1,0:T(8,128)(2,1)S(1)}, bf16[768,384]{1,0:T(8,128)(2,1)S(1)}, bf16[768,384]{1,0:T(8,128)(2...) custom-call(bf16[2,768,768]{2,1,0:T(8,128)(2,1)} %k_ref.1, ...), custom_call_target="tpu_custom_call" | custom-call | tf_op jit(solution)/shard_map/pallas_call | solution.py:366
  9.5 6.1 %collective-permute-done.11.refs_1_ = bf16[3,192,384]{2,1,0:T(8,128)(2,1)S(1)} collective-permute-done((bf16[3,192,384]{2,1,0:T(8,128)(2,1)S(1)}, bf16[3,192,384]{2,1,0:T(8,128)(2,1)S(1)}, u32[]{:S(2)}, u32[]{:S(2)}) %collective-permute-start.11) | collective-permute-done | bytes 442400 | tf_op jit(solution)/shard_map/ppermute | solution.py:327
  15.6 2.8 %shard_map.111 = (bf16[768,384]{1,0:T(8,128)(2,1)S(1)}, bf16[384,384]{1,0:T(8,128)(2,1)S(1)}, bf16[768,384]{1,0:T(8,128)(2,1)S(1)}, bf16[384,384]{1,0:T(8,128)(2...) custom-call(f32[1,2]{1,0:T(1,128)S(1)} %bitcast.16, bf16[768,384]{1,0:T(8,128)(2,1)S(1)} %get-tuple-element.92.k_ref, ...), custom_call_target="tpu_custom_call" | custom-call | tf_op jit(solution)/shard_map/pallas_call | solution.py:380
  18.5 2.1 %collective-permute-start.12 = (bf16[768,384]{1,0:T(8,128)(2,1)S(1)}, bf16[768,384]{1,0:T(8,128)(2,1)S(1)}, u32[]{:S(2)}, u32[]{:S(2)}) collective-permute-start(bf16[768,384]{1,0:T(8,128)(2,1)S(1)} %get-tuple-element.97), channel_id=1, source_target_pairs={{0,1},{1,0},{2,3},{3,2},{4,5},{5,4},{6,7},{7,6},{8,9},{9,8},{10,11... | collective-permute-start | bytes 1769480 | tf_op jit(solution)/shard_map/ppermute | solution.py:327
  20.6 4.6 %collective-permute-done.refs_1_ = bf16[3,192,384]{2,1,0:T(8,128)(2,1)S(1)} collective-permute-done((bf16[3,192,384]{2,1,0:T(8,128)(2,1)S(1)}, bf16[3,192,384]{2,1,0:T(8,128)(2,1)S(1)}, u32[]{:S(2)}, u32[]{:S(2)}) %collective-permute-start) | collective-permute-done | bytes 442400 | tf_op jit(solution)/shard_map/ppermute | solution.py:327
  25.1 2.8 %shard_map.105 = (bf16[768,384]{1,0:T(8,128)(2,1)S(1)}, bf16[384,384]{1,0:T(8,128)(2,1)S(1)}, bf16[768,384]{1,0:T(8,128)(2,1)S(1)}, bf16[384,384]{1,0:T(8,128)(2...) custom-call(f32[1,2]{1,0:T(1,128)S(1)} %bitcast.17, bf16[768,384]{1,0:T(8,128)(2,1)S(1)} %get-tuple-element.70.k_ref, ...), custom_call_target="tpu_custom_call" | custom-call | tf_op jit(solution)/shard_map/pallas_call | solution.py:380
  27.9 2.1 %collective-permute-start.1 = (bf16[768,384]{1,0:T(8,128)(2,1)S(1)}, bf16[768,384]{1,0:T(8,128)(2,1)S(1)}, u32[]{:S(2)}, u32[]{:S(2)}) collective-permute-start(bf16[768,384]{1,0:T(8,128)(2,1)S(1)} %get-tuple-element.75), channel_id=1, source_target_pairs={{0,1},{1,0},{2,3},{3,2},{4,5},{5,4},{6,7},{7,6},{8,9},{9,8},{10,11... | collective-permute-start | bytes 1769480 | tf_op jit(solution)/shard_map/ppermute | solution.py:327
  33.0 4.8 %collective-permute-done.12.refs_0_ = bf16[768,384]{1,0:T(8,128)(2,1)S(1)} collective-permute-done((bf16[768,384]{1,0:T(8,128)(2,1)S(1)}, bf16[768,384]{1,0:T(8,128)(2,1)S(1)}, u32[]{:S(2)}, u32[]{:S(2)}) %collective-permute-start.12) | collective-permute-done | bytes 589856 | tf_op jit(solution)/shard_map/ppermute | solution.py:327
  39.8 2.1 %collective-permute-start.3 = (bf16[384,384]{1,0:T(8,128)(2,1)S(1)}, bf16[384,384]{1,0:T(8,128)(2,1)S(1)}, u32[]{:S(2)}, u32[]{:S(2)}) collective-permute-start(bf16[384,384]{1,0:T(8,128)(2,1)S(1)} %get-tuple-element.79), channel_id=1, source_target_pairs={{0,1},{1,0},{2,3},{3,2},{4,5},{5,4},{6,7},{7,6},{8,9},{9,8},{10,11... | collective-permute-start | bytes 884744 | tf_op jit(solution)/shard_map/ppermute | solution.py:327
  41.9 18.1 %collective-permute-done.16.refs_2_ = bf16[192,384]{1,0:T(8,128)(2,1)S(1)} collective-permute-done((bf16[192,384]{1,0:T(8,128)(2,1)S(1)}, bf16[192,384]{1,0:T(8,128)(2,1)S(1)}, u32[]{:S(2)}, u32[]{:S(2)}) %collective-permute-start.16) | collective-permute-done | bytes 147488 | tf_op jit(solution)/shard_map/ppermute | solution.py:412
  65.0 2.0 %collective-permute-done.17.refs_3_ = bf16[192,384]{1,0:T(8,128)(2,1)S(1)} collective-permute-done((bf16[192,384]{1,0:T(8,128)(2,1)S(1)}, bf16[192,384]{1,0:T(8,128)(2,1)S(1)}, u32[]{:S(2)}, u32[]{:S(2)}) %collective-permute-start.17) | collective-permute-done | bytes 147488 | tf_op jit(solution)/shard_map/ppermute | solution.py:412
  73.6 7.1 %collective-permute-done.7.refs_3_ = bf16[192,384]{1,0:T(8,128)(2,1)S(1)} collective-permute-done((bf16[192,384]{1,0:T(8,128)(2,1)S(1)}, bf16[192,384]{1,0:T(8,128)(2,1)S(1)}, u32[]{:S(2)}, u32[]{:S(2)}) %collective-permute-start.7) | collective-permute-done | bytes 147488 | tf_op jit(solution)/shard_map/ppermute | solution.py:412
  84.7 2.4 %shard_map.114 = (bf16[768,384]{1,0:T(8,128)(2,1)S(1)}, bf16[384,384]{1,0:T(8,128)(2,1)S(1)}, f32[768,384]{1,0:T(8,128)S(1)}, f32[384,384]{1,0:T(8,128)S(1)}, bf...) custom-call(bf16[768,384]{1,0:T(8,128)(2,1)S(1)} %get-tuple-element.89.k_ref, ...), custom_call_target="tpu_custom_call" | custom-call | tf_op jit(solution)/shard_map/pallas_call | solution.py:426
  87.1 5.1 %collective-permute-done.8.refs_4_ = bf16[192,384]{1,0:T(8,128)(2,1)S(1)} collective-permute-done((bf16[192,384]{1,0:T(8,128)(2,1)S(1)}, bf16[192,384]{1,0:T(8,128)(2,1)S(1)}, u32[]{:S(2)}, u32[]{:S(2)}) %collective-permute-start.8) | collective-permute-done | bytes 147488 | tf_op jit(solution)/shard_map/ppermute | solution.py:412
  93.7 2.7 %shard_map.109 = (bf16[768,384]{1,0:T(8,128)(2,1)S(1)}, bf16[384,384]{1,0:T(8,128)(2,1)S(1)}, f32[768,384]{1,0:T(8,128)S(1)}, f32[384,384]{1,0:T(8,128)S(1)}, bf...) custom-call(bf16[768,384]{1,0:T(8,128)(2,1)S(1)} %get-tuple-element.67.k_ref, ...), custom_call_target="tpu_custom_call" | custom-call | tf_op jit(solution)/shard_map/pallas_call | solution.py:426
  97.0 1.5 %collective-permute-start.21 = (bf16[384,384]{1,0:T(8,128)(2,1)S(1)}, bf16[384,384]{1,0:T(8,128)(2,1)S(1)}, u32[]{:S(2)}, u32[]{:S(2)}) collective-permute-start(bf16[384,384]{1,0:T(8,128)(2,1)S(1)} %get-tuple-element.112), channel_id=1, source_target_pairs={{0,1},{1,0},{2,3},{3,2},{4,5},{5,4},{6,7},{7,6},{8,9},{9,8},{10,11... | collective-permute-start | bytes 884744 | tf_op jit(solution)/shard_map/ppermute | solution.py:327
  99.0 9.4 %collective-permute-done.20.refs_0_ = bf16[768,384]{1,0:T(8,128)(2,1)S(1)} collective-permute-done((bf16[768,384]{1,0:T(8,128)(2,1)S(1)}, bf16[768,384]{1,0:T(8,128)(2,1)S(1)}, u32[]{:S(2)}, u32[]{:S(2)}) %collective-permute-start.20) | collective-permute-done | bytes 589856 | tf_op jit(solution)/shard_map/ppermute | solution.py:327
  109.9 2.3 %shard_map.116.refs_0_ = bf16[2,768,768]{2,1,0:T(8,128)(2,1)} custom-call(bf16[768,384]{1,0:T(8,128)(2,1)S(1)} %get-tuple-element.114.q_ref, bf16[768,384]{1,0:T(8,128)(2,1)S(1)} %get-tuple-element.98.pgu_ref, bf16[384,384]{1,0:T(8,128)(2,1)S(1)} %get-tuple-element.103.pdown_ref), custom_call_target="tpu_custom_call" | custom-call | tf_op jit(solution)/shard_map/pallas_call | solution.py:446
  112.2 2.3 %shard_map.117.refs_1_ = bf16[2,768,768]{2,1,0:T(8,128)(2,1)} custom-call(bf16[768,384]{1,0:T(8,128)(2,1)S(1)} %get-tuple-element.113.q_ref, bf16[768,384]{1,0:T(8,128)(2,1)S(1)} %get-tuple-element.76.pgu_ref, bf16[384,384]{1,0:T(8,128)(2,1)S(1)} %get-tuple-element.81.pdown_ref, bf16[2,768,768]{2,1,0:T(8,128)(2,1)} %shard_map.116.refs_0_), custom_call_target="tpu_custom_call", output_to_operand_aliasing={{}: (3, {})} | custom-call | tf_op jit(solution)/shard_map/pallas_call | solution.py:446
  114.5 1.7 %shard_map.115 = (bf16[768,384]{1,0:T(8,128)(2,1)S(1)}, bf16[1,3,2,192,384]{4,3,2,1,0:T(8,128)(2,1)}, f32[1,3,2,192,384]{4,3,2,1,0:T(8,128)}) custom-call(f32[2,3]{1,0:T(2,128)S(1)} %bitcast.11, f32[1,2]{1,0:T(1,128)S(1)} %bitcast.18, bf16[768,384]{1,0:T(8,128)(2,1)S(1)} %get-tuple-element.107.old_ref, f32[768,384]{1,0:T(8,128)S(1)} %get-tuple-element.108.own_ref, ...), custom_call_target="tpu_custom_call" | custom-call | tf_op jit(solution)/shard_map/pallas_call | solution.py:463
  116.2 6.4 %collective-permute-done.21.refs_0_ = bf16[384,384]{1,0:T(8,128)(2,1)S(1)} collective-permute-done((bf16[384,384]{1,0:T(8,128)(2,1)S(1)}, bf16[384,384]{1,0:T(8,128)(2,1)S(1)}, u32[]{:S(2)}, u32[]{:S(2)}) %collective-permute-start.21) | collective-permute-done | bytes 294944 | tf_op jit(solution)/shard_map/ppermute | solution.py:327
  122.7 1.7 %shard_map.118 = (bf16[2,768,768]{2,1,0:T(8,128)(2,1)}, bf16[1,3,2,192,384]{4,3,2,1,0:T(8,128)(2,1)}, f32[1,3,2,192,384]{4,3,2,1,0:T(8,128)}) custom-call(f32[2,3]{1,0:T(2,128)S(1)} %bitcast.12, f32[1,2]{1,0:T(1,128)S(1)} %bitcast.19, bf16[384,384]{1,0:T(8,128)(2,1)S(1)} %get-tuple-element.104.old_ref, ...), custom_call_target="tpu_custom_call", output_to_operand_aliasing={{0}: (7, {}), {1}: (8, {}), {2}: (9, {})} | custom-call | tf_op jit(solution)/shard_map/pallas_call | solution.py:495
  124.4 1.7 %shard_map.119 = (bf16[768,384]{1,0:T(8,128)(2,1)S(1)}, bf16[1,3,2,192,384]{4,3,2,1,0:T(8,128)(2,1)}, f32[1,3,2,192,384]{4,3,2,1,0:T(8,128)}) custom-call(f32[2,3]{1,0:T(2,128)S(1)} %bitcast.13, f32[1,2]{1,0:T(1,128)S(1)} %bitcast.20, bf16[768,384]{1,0:T(8,128)(2,1)S(1)} %get-tuple-element.85.old_ref, ...), custom_call_target="tpu_custom_call", output_to_operand_aliasing={{1}: (7, {}), {2}: (8, {})} | custom-call | tf_op jit(solution)/shard_map/pallas_call | solution.py:463
  (47 shorter events, 28.6 us)
Async XLA Ops:
  1.6 14.0 %collective-permute-start.11 = (bf16[3,192,384]{2,1,0:T(8,128)(2,1)S(1)}, bf16[3,192,384]{2,1,0:T(8,128)(2,1)S(1)}, u32[]{:S(2)}, u32[]{:S(2)}) collective-permute-start(bf16[3,192,384]{2,1,0:T(8,128)(2,1)S(1)} %shard_map.110.refs_0_), channel_id=1, source_target_pairs={{0,1},{1,0},{2,3},{3,2},{4,5},{5,4},{6,7},{7,6},{8,9},{9,8},{10,11... | collective-permute-start | bytes 1327112 | tf_op jit(solution)/shard_map/ppermute | solution.py:327
  5.6 19.5 %collective-permute-start = (bf16[3,192,384]{2,1,0:T(8,128)(2,1)S(1)}, bf16[3,192,384]{2,1,0:T(8,128)(2,1)S(1)}, u32[]{:S(2)}, u32[]{:S(2)}) collective-permute-start(bf16[3,192,384]{2,1,0:T(8,128)(2,1)S(1)} %shard_map.104.refs_0_), channel_id=1, source_target_pairs={{0,1},{1,0},{2,3},{3,2},{4,5},{5,4},{6,7},{7,6},{8,9},{9,8},{10,11... | collective-permute-start | bytes 1327112 | tf_op jit(solution)/shard_map/ppermute | solution.py:327
  18.5 19.3 %collective-permute-start.12 = (bf16[768,384]{1,0:T(8,128)(2,1)S(1)}, bf16[768,384]{1,0:T(8,128)(2,1)S(1)}, u32[]{:S(2)}, u32[]{:S(2)}) collective-permute-start(bf16[768,384]{1,0:T(8,128)(2,1)S(1)} %get-tuple-element.97), channel_id=1, source_target_pairs={{0,1},{1,0},{2,3},{3,2},{4,5},{5,4},{6,7},{7,6},{8,9},{9,8},{10,11... | collective-permute-start | bytes 1769480 | tf_op jit(solution)/shard_map/ppermute | solution.py:327
  27.9 34.6 %collective-permute-start.1 = (bf16[768,384]{1,0:T(8,128)(2,1)S(1)}, bf16[768,384]{1,0:T(8,128)(2,1)S(1)}, u32[]{:S(2)}, u32[]{:S(2)}) collective-permute-start(bf16[768,384]{1,0:T(8,128)(2,1)S(1)} %get-tuple-element.75), channel_id=1, source_target_pairs={{0,1},{1,0},{2,3},{3,2},{4,5},{5,4},{6,7},{7,6},{8,9},{9,8},{10,11... | collective-permute-start | bytes 1769480 | tf_op jit(solution)/shard_map/ppermute | solution.py:327
  30.9 0.8 collective-permute-start.5
  31.6 29.7 %collective-permute-start.14 = (bf16[384,384]{1,0:T(8,128)(2,1)S(1)}, bf16[384,384]{1,0:T(8,128)(2,1)S(1)}, u32[]{:S(2)}, u32[]{:S(2)}) collective-permute-start(bf16[384,384]{1,0:T(8,128)(2,1)S(1)} %get-tuple-element.101), channel_id=1, source_target_pairs={{0,1},{1,0},{2,3},{3,2},{4,5},{5,4},{6,7},{7,6},{8,9},{9,8},{10,11... | collective-permute-start | bytes 884744 | tf_op jit(solution)/shard_map/ppermute | solution.py:327
  31.7 28.3 %collective-permute-start.16 = (bf16[192,384]{1,0:T(8,128)(2,1)S(1)}, bf16[192,384]{1,0:T(8,128)(2,1)S(1)}, u32[]{:S(2)}, u32[]{:S(2)}) collective-permute-start(bf16[192,384]{1,0:T(8,128)(2,1)S(1)} %collective-permute-done.5), channel_id=1, source_target_pairs={{4,0},{5,1}} | collective-permute-start | bytes 442376 | tf_op jit(solution)/shard_map/ppermute | solution.py:412
  38.5 45.0 %collective-permute-start.13 = (bf16[768,384]{1,0:T(8,128)(2,1)S(1)}, bf16[768,384]{1,0:T(8,128)(2,1)S(1)}, u32[]{:S(2)}, u32[]{:S(2)}) collective-permute-start(bf16[768,384]{1,0:T(8,128)(2,1)S(1)} %get-tuple-element.98.pgu_ref), channel_id=1, source_target_pairs={{0,2},{2,4},{4,6},{6,8},{8,10},{10,12},{12,14},{14,16},{16,18},{18... | collective-permute-start | bytes 1769480 | tf_op jit(solution)/shard_map/ppermute | solution.py:330
  39.8 32.1 %collective-permute-start.3 = (bf16[384,384]{1,0:T(8,128)(2,1)S(1)}, bf16[384,384]{1,0:T(8,128)(2,1)S(1)}, u32[]{:S(2)}, u32[]{:S(2)}) collective-permute-start(bf16[384,384]{1,0:T(8,128)(2,1)S(1)} %get-tuple-element.79), channel_id=1, source_target_pairs={{0,1},{1,0},{2,3},{3,2},{4,5},{5,4},{6,7},{7,6},{8,9},{9,8},{10,11... | collective-permute-start | bytes 884744 | tf_op jit(solution)/shard_map/ppermute | solution.py:327
  60.0 7.0 %collective-permute-start.17 = (bf16[192,384]{1,0:T(8,128)(2,1)S(1)}, bf16[192,384]{1,0:T(8,128)(2,1)S(1)}, u32[]{:S(2)}, u32[]{:S(2)}) collective-permute-start(bf16[192,384]{1,0:T(8,128)(2,1)S(1)} %collective-permute-done.5), channel_id=1, source_target_pairs={{8,0},{9,1}} | collective-permute-start | bytes 442376 | tf_op jit(solution)/shard_map/ppermute | solution.py:412
  61.3 7.9 %collective-permute-start.18 = (bf16[192,384]{1,0:T(8,128)(2,1)S(1)}, bf16[192,384]{1,0:T(8,128)(2,1)S(1)}, u32[]{:S(2)}, u32[]{:S(2)}) collective-permute-start(bf16[192,384]{1,0:T(8,128)(2,1)S(1)} %collective-permute-done.5), channel_id=1, source_target_pairs={{12,0},{13,1}} | collective-permute-start | bytes 442376 | tf_op jit(solution)/shard_map/ppermute | solution.py:412
  62.6 7.9 %collective-permute-start.6 = (bf16[192,384]{1,0:T(8,128)(2,1)S(1)}, bf16[192,384]{1,0:T(8,128)(2,1)S(1)}, u32[]{:S(2)}, u32[]{:S(2)}) collective-permute-start(bf16[192,384]{1,0:T(8,128)(2,1)S(1)} %collective-permute-done.5), channel_id=1, source_target_pairs={{16,0},{17,1}} | collective-permute-start | bytes 442376 | tf_op jit(solution)/shard_map/ppermute | solution.py:412
  67.0 26.7 %collective-permute-start.2 = (bf16[768,384]{1,0:T(8,128)(2,1)S(1)}, bf16[768,384]{1,0:T(8,128)(2,1)S(1)}, u32[]{:S(2)}, u32[]{:S(2)}) collective-permute-start(bf16[768,384]{1,0:T(8,128)(2,1)S(1)} %get-tuple-element.76.pgu_ref), channel_id=1, source_target_pairs={{0,2},{2,4},{4,6},{6,8},{8,10},{10,12},{12,14},{14,16},{16,18},{18... | collective-permute-start | bytes 1769480 | tf_op jit(solution)/shard_map/ppermute | solution.py:330
  69.2 12.8 %collective-permute-start.15 = (bf16[384,384]{1,0:T(8,128)(2,1)S(1)}, bf16[384,384]{1,0:T(8,128)(2,1)S(1)}, u32[]{:S(2)}, u32[]{:S(2)}) collective-permute-start(bf16[384,384]{1,0:T(8,128)(2,1)S(1)} %get-tuple-element.103.pdown_ref), channel_id=1, source_target_pairs={{0,2},{2,4},{4,6},{6,8},{8,10},{10,12},{12,14},{14,16},{16,18},{18... | collective-permute-start | bytes 884744 | tf_op jit(solution)/shard_map/ppermute | solution.py:330
  70.5 28.0 %collective-permute-start.19 = (bf16[1152,384]{1,0:T(8,128)(2,1)S(1)}, bf16[1152,384]{1,0:T(8,128)(2,1)S(1)}, u32[]{:S(2)}, u32[]{:S(2)}) collective-permute-start(bf16[1152,384]{1,0:T(8,128)(2,1)S(1)} %get-tuple-element.106), channel_id=1, source_target_pairs={{0,2},{2,4},{4,6},{6,8},{8,10},{10,12},{12,14},{14,16},{16,18},{18... | collective-permute-start | bytes 2654216 | tf_op jit(solution)/shard_map/ppermute | solution.py:330
  71.9 8.8 %collective-permute-start.7 = (bf16[192,384]{1,0:T(8,128)(2,1)S(1)}, bf16[192,384]{1,0:T(8,128)(2,1)S(1)}, u32[]{:S(2)}, u32[]{:S(2)}) collective-permute-start(bf16[192,384]{1,0:T(8,128)(2,1)S(1)} %collective-permute-done.5), channel_id=1, source_target_pairs={{20,0},{21,1}} | collective-permute-start | bytes 442376 | tf_op jit(solution)/shard_map/ppermute | solution.py:412
  80.7 13.0 %collective-permute-start.4 = (bf16[384,384]{1,0:T(8,128)(2,1)S(1)}, bf16[384,384]{1,0:T(8,128)(2,1)S(1)}, u32[]{:S(2)}, u32[]{:S(2)}) collective-permute-start(bf16[384,384]{1,0:T(8,128)(2,1)S(1)} %get-tuple-element.81.pdown_ref), channel_id=1, source_target_pairs={{0,2},{2,4},{4,6},{6,8},{8,10},{10,12},{12,14},{14,16},{16,18},{18... | collective-permute-start | bytes 884744 | tf_op jit(solution)/shard_map/ppermute | solution.py:330
  82.0 42.3 %collective-permute-start.9 = (bf16[1152,384]{1,0:T(8,128)(2,1)S(1)}, bf16[1152,384]{1,0:T(8,128)(2,1)S(1)}, u32[]{:S(2)}, u32[]{:S(2)}) collective-permute-start(bf16[1152,384]{1,0:T(8,128)(2,1)S(1)} %get-tuple-element.84), channel_id=1, source_target_pairs={{0,2},{2,4},{4,6},{6,8},{8,10},{10,12},{12,14},{14,16},{16,18},{18... | collective-permute-start | bytes 2654216 | tf_op jit(solution)/shard_map/ppermute | solution.py:330
  83.4 8.8 %collective-permute-start.8 = (bf16[192,384]{1,0:T(8,128)(2,1)S(1)}, bf16[192,384]{1,0:T(8,128)(2,1)S(1)}, u32[]{:S(2)}, u32[]{:S(2)}) collective-permute-start(bf16[192,384]{1,0:T(8,128)(2,1)S(1)} %collective-permute-done.5), channel_id=1, source_target_pairs={{24,0},{25,1}} | collective-permute-start | bytes 442376 | tf_op jit(solution)/shard_map/ppermute | solution.py:412
  92.2 16.2 %collective-permute-start.20 = (bf16[768,384]{1,0:T(8,128)(2,1)S(1)}, bf16[768,384]{1,0:T(8,128)(2,1)S(1)}, u32[]{:S(2)}, u32[]{:S(2)}) collective-permute-start(bf16[768,384]{1,0:T(8,128)(2,1)S(1)} %get-tuple-element.110), channel_id=1, source_target_pairs={{0,1},{1,0},{2,3},{3,2},{4,5},{5,4},{6,7},{7,6},{8,9},{9,8},{10,11... | collective-permute-start | bytes 1769480 | tf_op jit(solution)/shard_map/ppermute | solution.py:327
  96.4 28.0 %collective-permute-start.10 = (bf16[768,384]{1,0:T(8,128)(2,1)S(1)}, bf16[768,384]{1,0:T(8,128)(2,1)S(1)}, u32[]{:S(2)}, u32[]{:S(2)}) collective-permute-start(bf16[768,384]{1,0:T(8,128)(2,1)S(1)} %get-tuple-element.88), channel_id=1, source_target_pairs={{0,1},{1,0},{2,3},{3,2},{4,5},{5,4},{6,7},{7,6},{8,9},{9,8},{10,11... | collective-permute-start | bytes 1769480 | tf_op jit(solution)/shard_map/ppermute | solution.py:327
  97.0 25.7 %collective-permute-start.21 = (bf16[384,384]{1,0:T(8,128)(2,1)S(1)}, bf16[384,384]{1,0:T(8,128)(2,1)S(1)}, u32[]{:S(2)}, u32[]{:S(2)}) collective-permute-start(bf16[384,384]{1,0:T(8,128)(2,1)S(1)} %get-tuple-element.112), channel_id=1, source_target_pairs={{0,1},{1,0},{2,3},{3,2},{4,5},{5,4},{6,7},{7,6},{8,9},{9,8},{10,11... | collective-permute-start | bytes 884744 | tf_op jit(solution)/shard_map/ppermute | solution.py:327
  98.5 27.6 %collective-permute-start.23 = (bf16[256,384]{1,0:T(8,128)(2,1)S(1)}, bf16[256,384]{1,0:T(8,128)(2,1)S(1)}, u32[]{:S(2)}, u32[]{:S(2)}) collective-permute-start(bf16[256,384]{1,0:T(8,128)(2,1)S(1)} %get-tuple-element.121), channel_id=1, source_target_pairs={{0,1},{1,0},{2,3},{3,2},{4,5},{5,4},{6,7},{7,6},{8,9},{9,8},{10,11... | collective-permute-start | bytes 589832 | tf_op jit(solution)/shard_map/ppermute | solution.py:327
  108.5 18.4 %collective-permute-start.22 = (bf16[128,384]{1,0:T(8,128)(2,1)S(1)}, bf16[128,384]{1,0:T(8,128)(2,1)S(1)}, u32[]{:S(2)}, u32[]{:S(2)}) collective-permute-start(bf16[128,384]{1,0:T(8,128)(2,1)S(1)} %get-tuple-element.120), channel_id=1, source_target_pairs={{0,1},{1,0},{2,3},{3,2},{4,5},{5,4},{6,7},{7,6},{8,9},{9,8},{10,11... | collective-permute-start | bytes 294920 | tf_op jit(solution)/shard_map/ppermute | solution.py:327
  (2 other events, 22.6 us)

commit v11 on v10

--- a/solution.py
+++ b/solution.py
@@ -67,8 +67,8 @@
     own_down[...] = mm(dout_s[...], hid_s[...], ((0,), (0,)))
 
 
-def take_head(head, fast_ref, own_ref):
-    pltpu.sync_copy(fast_ref.at[0, :, head], own_ref)
+def take_head(head, first, fast_ref, own_ref):
+    pltpu.sync_copy(fast_ref.at[0, pl.ds(first, own_ref.shape[0]), head], own_ref)
 
 
 def take_piece(sources, begin_ref, piece_ref):
@@ -102,13 +102,20 @@
         copy.wait()
 
 
-def grads_one(n, head, divisor, decay_ref, k_ref, v_ref, m_ref, *refs):
-    shards = refs[:n]
-    gu_ref, down_ref, send_gu, send_down, own_gu, own_down, hid_s, dout_s, dgu_s = refs[n:]
+def grads_one(n, head, groups, divisor, decay_ref, k_ref, v_ref, m_ref, *refs):
+    count = len(groups)
+    shards, refs = refs[: n * count], refs[n * count :]
+
+    def block(r, m):
+        for ref, (first, end) in zip(shards[r * count :], groups):
+            if first <= m < end:
+                return ref[m - first]
+
+    gu_ref, down_ref, send_gu, send_down, own_gu, own_down, hid_s, dout_s, dgu_s = refs
     width = down_ref.shape[0]
     part = width // n
     me = lax.axis_index("tok")
-    assemble(me, [lambda m, ref=ref: ref[m] for ref in shards], gu_ref, down_ref)
+    assemble(me, [functools.partial(block, r) for r in range(n)], gu_ref, down_ref)
     grads_core(divisor, k_ref, v_ref, gu_ref, down_ref, own_gu, own_down, hid_s, dout_s, dgu_s)
     decay = decay_ref[:, head : head + 1]
     mine = pl.multiple_of(me * part, part)
@@ -343,12 +350,21 @@
         shape(width, width, dtype=F32),
     )
 
-    recv_fast, owned = [], []
+    groups = [[(0, 1), (1, 3)] if h == 0 else [(0, 3)] for h in range(heads)]
+    shards = []
     for h in range(heads):
-        owned.append(
-            call(functools.partial(take_head, h), shape(3, part, width), [HBM], VMEM)(fast_t)
-        )
-        recv_fast.append(turned(owned[h]))
+        owned, received = [], []
+        for begin, end in groups[h]:
+            owned.append(
+                call(
+                    functools.partial(take_head, h, begin),
+                    shape(end - begin, part, width),
+                    [HBM],
+                    VMEM,
+                )(fast_t)
+            )
+            received.append(turned(owned[-1]))
+        shards.append(owned + [group[r] for r in range(n - 1) for group in received])
 
     apart = max(blocks // (3 * heads + 2), 1)
     sources = [apart * (p + 1) % blocks for p in range(3 * heads)]
@@ -378,12 +394,12 @@
 
     first = [
         call(
-            functools.partial(grads_one, n, h, divisor),
+            functools.partial(grads_one, n, h, groups[h], divisor),
             grad_out,
-            [VMEM] * (4 + n),
+            [VMEM] * (4 + len(shards[h])),
             (VMEM,) * 6,
             grad_scratch,
-        )(decays, *kvq[0][h][:2], m_own[h], owned[h], *recv_fast[h])
+        )(decays, *kvq[0][h][:2], m_own[h], *shards[h])
         for h in range(heads)
     ]
 

time: 129 us -> 134 us (1.039)
  waiting for transfers between devices: 64.5 us -> 67.1 us
  starting transfers between devices: 31.2 us -> 32.7 us
    ppermute x11 -> x12, waiting for transfers between devices: 31.3 us -> 34.3 us  [turned(): lax.ppermute(x, 'tok', [(i, (i + r) % n) for i in range(n)])]
    ppermute x11 -> x12, starting transfers between devices: 14.9 us -> 16.4 us  [turned(): lax.ppermute(x, 'tok', [(i, (i + r) % n) for i in range(n)])]
    pallas_call x4 -> x5, Pallas kernels: 7.68 us -> 8.54 us  [the longest x2 5.65 us: on_device(): call(functools.partial(grads_one, n, h, groups[h], divisor), grad_out, [V...]
  transfers between devices with their start and end apart: 24 -> 25, of which waited for: 10 -> 9; matrix products, arithmetic and copies ran while one was open for 0% -> 0% of each run, Pallas kernels for 23% -> 23%
where the time goes in v11:
time: 134 us; the launch traced here: 133 us
  waiting for transfers between devices  67.1 us (50%)
  starting transfers between devices  32.7 us (24%)
  Pallas kernels  32.3 us (24%)
    ppermute x12, waiting for transfers between devices, turned(): lax.ppermute(x, 'tok', [(i, (i + r) % n) for i in range(n)])  34.3 us
    ppermute x6, waiting for transfers between devices, on_device(): lax.ppermute(x, ('block', 'tok'), [(sources[p] * n + i, i) for i in range...  32.8 us
    ppermute x12, starting transfers between devices, turned(): lax.ppermute(x, 'tok', [(i, (i + r) % n) for i in range(n)])  16.4 us
    ppermute x6, starting transfers between devices, forward(): return lax.ppermute(x, 'block', [(i, i + 1) for i in range(blocks - 1)])  7.93 us
    ppermute x6, starting transfers between devices, on_device(): lax.ppermute(x, ('block', 'tok'), [(sources[p] * n + i, i) for i in range...  7.73 us
    pallas_call x2, Pallas kernels, on_device(): call(functools.partial(grads_one, n, h, groups[h], divisor), grad_out, [V...  5.65 us
    pallas_call x2, Pallas kernels, on_device(): call(functools.partial(grads_two, n, divisor), (shape(2 * width, width),...  5.08 us
    pallas_call x2, Pallas kernels, on_device(): call(functools.partial(apply_one, h), out_shape, [VMEM] * 3 + [HBM] * len...  4.54 us
  transfers between devices with their start and end apart: 25, of which 9 were waited for; matrix products, arithmetic and copies ran while one was open for 0% of the time, Pallas kernels for 23%

profile of v11, /device:TPU:0, one launch (start us, length us, event | category | flops | bytes accessed | tf_op | source)
XLA Modules:
  0.0 133.2 jit_solution(10795560593168814042)
XLA Ops:
  1.6 3.0 %collective-permute-start.12 = (bf16[2,192,384]{2,1,0:T(8,128)(2,1)S(1)}, bf16[2,192,384]{2,1,0:T(8,128)(2,1)S(1)}, u32[]{:S(2)}, u32[]{:S(2)}) collective-permute-start(bf16[2,192,384]{2,1,0:T(8,128)(2,1)S(1)} %shard_map.111.refs_1_), channel_id=1, source_target_pairs={{0,1},{1,0},{2,3},{3,2},{4,5},{5,4},{6,7},{7,6},{8,9},{9,8},{10,11... | collective-permute-start | bytes 884744 | tf_op jit(solution)/shard_map/ppermute | solution.py:334
  6.5 2.0 %collective-permute-start.11 = (bf16[1,192,384]{2,1,0:T(8,128)(2,1)S(1)}, bf16[1,192,384]{2,1,0:T(8,128)(2,1)S(1)}, u32[]{:S(2)}, u32[]{:S(2)}) collective-permute-start(bf16[1,192,384]{2,1,0:T(8,128)(2,1)S(1)} %shard_map.110.refs_0_), channel_id=1, source_target_pairs={{0,1},{1,0},{2,3},{3,2},{4,5},{5,4},{6,7},{7,6},{8,9},{9,8},{10,11... | collective-permute-start | bytes 442376 | tf_op jit(solution)/shard_map/ppermute | solution.py:334
  8.5 3.9 %shard_map.103 = (bf16[768,384]{1,0:T(8,128)(2,1)S(1)}, bf16[768,384]{1,0:T(8,128)(2,1)S(1)}, bf16[768,384]{1,0:T(8,128)(2,1)S(1)}, bf16[768,384]{1,0:T(8,128)(2...) custom-call(bf16[2,768,768]{2,1,0:T(8,128)(2,1)} %k_ref.1, ...), custom_call_target="tpu_custom_call" | custom-call | tf_op jit(solution)/shard_map/pallas_call | solution.py:382
  12.4 11.8 %collective-permute-done.11.refs_2_ = bf16[1,192,384]{2,1,0:T(8,128)(2,1)S(1)} collective-permute-done((bf16[1,192,384]{2,1,0:T(8,128)(2,1)S(1)}, bf16[1,192,384]{2,1,0:T(8,128)(2,1)S(1)}, u32[]{:S(2)}, u32[]{:S(2)}) %collective-permute-start.11) | collective-permute-done | bytes 147488 | tf_op jit(solution)/shard_map/ppermute | solution.py:334
  24.2 2.8 %shard_map.112 = (bf16[768,384]{1,0:T(8,128)(2,1)S(1)}, bf16[384,384]{1,0:T(8,128)(2,1)S(1)}, bf16[768,384]{1,0:T(8,128)(2,1)S(1)}, bf16[384,384]{1,0:T(8,128)(2...) custom-call(f32[1,2]{1,0:T(1,128)S(1)} %bitcast.16, bf16[768,384]{1,0:T(8,128)(2,1)S(1)} %get-tuple-element.92.k_ref, ...), custom_call_target="tpu_custom_call" | custom-call | tf_op jit(solution)/shard_map/pallas_call | solution.py:396
  27.1 1.8 %collective-permute-start.13 = (bf16[768,384]{1,0:T(8,128)(2,1)S(1)}, bf16[768,384]{1,0:T(8,128)(2,1)S(1)}, u32[]{:S(2)}, u32[]{:S(2)}) collective-permute-start(bf16[768,384]{1,0:T(8,128)(2,1)S(1)} %get-tuple-element.97), channel_id=1, source_target_pairs={{0,1},{1,0},{2,3},{3,2},{4,5},{5,4},{6,7},{7,6},{8,9},{9,8},{10,11... | collective-permute-start | bytes 1769480 | tf_op jit(solution)/shard_map/ppermute | solution.py:334
  28.9 2.8 %shard_map.105 = (bf16[768,384]{1,0:T(8,128)(2,1)S(1)}, bf16[384,384]{1,0:T(8,128)(2,1)S(1)}, bf16[768,384]{1,0:T(8,128)(2,1)S(1)}, bf16[384,384]{1,0:T(8,128)(2...) custom-call(f32[1,2]{1,0:T(1,128)S(1)} %bitcast.17, bf16[768,384]{1,0:T(8,128)(2,1)S(1)} %get-tuple-element.70.k_ref, ...), custom_call_target="tpu_custom_call" | custom-call | tf_op jit(solution)/shard_map/pallas_call | solution.py:396
  33.6 1.8 %collective-permute-start.15 = (bf16[384,384]{1,0:T(8,128)(2,1)S(1)}, bf16[384,384]{1,0:T(8,128)(2,1)S(1)}, u32[]{:S(2)}, u32[]{:S(2)}) collective-permute-start(bf16[384,384]{1,0:T(8,128)(2,1)S(1)} %get-tuple-element.101), channel_id=1, source_target_pairs={{0,1},{1,0},{2,3},{3,2},{4,5},{5,4},{6,7},{7,6},{8,9},{9,8},{10,11... | collective-permute-start | bytes 884744 | tf_op jit(solution)/shard_map/ppermute | solution.py:334
  36.7 6.6 %collective-permute-done.13.refs_0_ = bf16[768,384]{1,0:T(8,128)(2,1)S(1)} collective-permute-done((bf16[768,384]{1,0:T(8,128)(2,1)S(1)}, bf16[768,384]{1,0:T(8,128)(2,1)S(1)}, u32[]{:S(2)}, u32[]{:S(2)}) %collective-permute-start.13) | collective-permute-done | bytes 589856 | tf_op jit(solution)/shard_map/ppermute | solution.py:334
  45.4 1.8 %collective-permute-start.3 = (bf16[384,384]{1,0:T(8,128)(2,1)S(1)}, bf16[384,384]{1,0:T(8,128)(2,1)S(1)}, u32[]{:S(2)}, u32[]{:S(2)}) collective-permute-start(bf16[384,384]{1,0:T(8,128)(2,1)S(1)} %get-tuple-element.79), channel_id=1, source_target_pairs={{0,1},{1,0},{2,3},{3,2},{4,5},{5,4},{6,7},{7,6},{8,9},{9,8},{10,11... | collective-permute-start | bytes 884744 | tf_op jit(solution)/shard_map/ppermute | solution.py:334
  47.2 17.7 %collective-permute-done.17.refs_2_ = bf16[192,384]{1,0:T(8,128)(2,1)S(1)} collective-permute-done((bf16[192,384]{1,0:T(8,128)(2,1)S(1)}, bf16[192,384]{1,0:T(8,128)(2,1)S(1)}, u32[]{:S(2)}, u32[]{:S(2)}) %collective-permute-start.17) | collective-permute-done | bytes 147488 | tf_op jit(solution)/shard_map/ppermute | solution.py:428
  69.9 2.0 %collective-permute-done.18.refs_3_ = bf16[192,384]{1,0:T(8,128)(2,1)S(1)} collective-permute-done((bf16[192,384]{1,0:T(8,128)(2,1)S(1)}, bf16[192,384]{1,0:T(8,128)(2,1)S(1)}, u32[]{:S(2)}, u32[]{:S(2)}) %collective-permute-start.18) | collective-permute-done | bytes 147488 | tf_op jit(solution)/shard_map/ppermute | solution.py:428
  78.5 7.1 %collective-permute-done.7.refs_3_ = bf16[192,384]{1,0:T(8,128)(2,1)S(1)} collective-permute-done((bf16[192,384]{1,0:T(8,128)(2,1)S(1)}, bf16[192,384]{1,0:T(8,128)(2,1)S(1)}, u32[]{:S(2)}, u32[]{:S(2)}) %collective-permute-start.7) | collective-permute-done | bytes 147488 | tf_op jit(solution)/shard_map/ppermute | solution.py:428
  89.6 2.4 %shard_map.115 = (bf16[768,384]{1,0:T(8,128)(2,1)S(1)}, bf16[384,384]{1,0:T(8,128)(2,1)S(1)}, f32[768,384]{1,0:T(8,128)S(1)}, f32[384,384]{1,0:T(8,128)S(1)}, bf...) custom-call(bf16[768,384]{1,0:T(8,128)(2,1)S(1)} %get-tuple-element.89.k_ref, ...), custom_call_target="tpu_custom_call" | custom-call | tf_op jit(solution)/shard_map/pallas_call | solution.py:442
  92.0 5.1 %collective-permute-done.8.refs_4_ = bf16[192,384]{1,0:T(8,128)(2,1)S(1)} collective-permute-done((bf16[192,384]{1,0:T(8,128)(2,1)S(1)}, bf16[192,384]{1,0:T(8,128)(2,1)S(1)}, u32[]{:S(2)}, u32[]{:S(2)}) %collective-permute-start.8) | collective-permute-done | bytes 147488 | tf_op jit(solution)/shard_map/ppermute | solution.py:428
  97.1 1.5 %collective-permute-start.21 = (bf16[768,384]{1,0:T(8,128)(2,1)S(1)}, bf16[768,384]{1,0:T(8,128)(2,1)S(1)}, u32[]{:S(2)}, u32[]{:S(2)}) collective-permute-start(bf16[768,384]{1,0:T(8,128)(2,1)S(1)} %get-tuple-element.110), channel_id=1, source_target_pairs={{0,1},{1,0},{2,3},{3,2},{4,5},{5,4},{6,7},{7,6},{8,9},{9,8},{10,11... | collective-permute-start | bytes 1769480 | tf_op jit(solution)/shard_map/ppermute | solution.py:334
  98.6 2.7 %shard_map.109 = (bf16[768,384]{1,0:T(8,128)(2,1)S(1)}, bf16[384,384]{1,0:T(8,128)(2,1)S(1)}, f32[768,384]{1,0:T(8,128)S(1)}, f32[384,384]{1,0:T(8,128)S(1)}, bf...) custom-call(bf16[768,384]{1,0:T(8,128)(2,1)S(1)} %get-tuple-element.67.k_ref, ...), custom_call_target="tpu_custom_call" | custom-call | tf_op jit(solution)/shard_map/pallas_call | solution.py:442
  103.9 9.4 %collective-permute-done.21.refs_0_ = bf16[768,384]{1,0:T(8,128)(2,1)S(1)} collective-permute-done((bf16[768,384]{1,0:T(8,128)(2,1)S(1)}, bf16[768,384]{1,0:T(8,128)(2,1)S(1)}, u32[]{:S(2)}, u32[]{:S(2)}) %collective-permute-start.21) | collective-permute-done | bytes 589856 | tf_op jit(solution)/shard_map/ppermute | solution.py:334
  114.8 2.3 %shard_map.117.refs_0_ = bf16[2,768,768]{2,1,0:T(8,128)(2,1)} custom-call(bf16[768,384]{1,0:T(8,128)(2,1)S(1)} %get-tuple-element.114.q_ref, bf16[768,384]{1,0:T(8,128)(2,1)S(1)} %get-tuple-element.98.pgu_ref, bf16[384,384]{1,0:T(8,128)(2,1)S(1)} %get-tuple-element.103.pdown_ref), custom_call_target="tpu_custom_call" | custom-call | tf_op jit(solution)/shard_map/pallas_call | solution.py:462
  117.1 2.3 %shard_map.118.refs_1_ = bf16[2,768,768]{2,1,0:T(8,128)(2,1)} custom-call(bf16[768,384]{1,0:T(8,128)(2,1)S(1)} %get-tuple-element.113.q_ref, bf16[768,384]{1,0:T(8,128)(2,1)S(1)} %get-tuple-element.76.pgu_ref, bf16[384,384]{1,0:T(8,128)(2,1)S(1)} %get-tuple-element.81.pdown_ref, bf16[2,768,768]{2,1,0:T(8,128)(2,1)} %shard_map.117.refs_0_), custom_call_target="tpu_custom_call", output_to_operand_aliasing={{}: (3, {})} | custom-call | tf_op jit(solution)/shard_map/pallas_call | solution.py:462
  119.4 1.7 %shard_map.116 = (bf16[768,384]{1,0:T(8,128)(2,1)S(1)}, bf16[1,3,2,192,384]{4,3,2,1,0:T(8,128)(2,1)}, f32[1,3,2,192,384]{4,3,2,1,0:T(8,128)}) custom-call(f32[2,3]{1,0:T(2,128)S(1)} %bitcast.11, f32[1,2]{1,0:T(1,128)S(1)} %bitcast.18, bf16[768,384]{1,0:T(8,128)(2,1)S(1)} %get-tuple-element.107.old_ref, f32[768,384]{1,0:T(8,128)S(1)} %get-tuple-element.108.own_ref, ...), custom_call_target="tpu_custom_call" | custom-call | tf_op jit(solution)/shard_map/pallas_call | solution.py:479
  121.1 6.5 %collective-permute-done.22.refs_0_ = bf16[384,384]{1,0:T(8,128)(2,1)S(1)} collective-permute-done((bf16[384,384]{1,0:T(8,128)(2,1)S(1)}, bf16[384,384]{1,0:T(8,128)(2,1)S(1)}, u32[]{:S(2)}, u32[]{:S(2)}) %collective-permute-start.22) | collective-permute-done | bytes 294944 | tf_op jit(solution)/shard_map/ppermute | solution.py:334
  127.6 1.7 %shard_map.119 = (bf16[2,768,768]{2,1,0:T(8,128)(2,1)}, bf16[1,3,2,192,384]{4,3,2,1,0:T(8,128)(2,1)}, f32[1,3,2,192,384]{4,3,2,1,0:T(8,128)}) custom-call(f32[2,3]{1,0:T(2,128)S(1)} %bitcast.12, f32[1,2]{1,0:T(1,128)S(1)} %bitcast.19, bf16[384,384]{1,0:T(8,128)(2,1)S(1)} %get-tuple-element.104.old_ref, ...), custom_call_target="tpu_custom_call", output_to_operand_aliasing={{0}: (7, {}), {1}: (8, {}), {2}: (9, {})} | custom-call | tf_op jit(solution)/shard_map/pallas_call | solution.py:511
  129.3 1.7 %shard_map.120 = (bf16[768,384]{1,0:T(8,128)(2,1)S(1)}, bf16[1,3,2,192,384]{4,3,2,1,0:T(8,128)(2,1)}, f32[1,3,2,192,384]{4,3,2,1,0:T(8,128)}) custom-call(f32[2,3]{1,0:T(2,128)S(1)} %bitcast.13, f32[1,2]{1,0:T(1,128)S(1)} %bitcast.20, bf16[768,384]{1,0:T(8,128)(2,1)S(1)} %get-tuple-element.85.old_ref, ...), custom_call_target="tpu_custom_call", output_to_operand_aliasing={{1}: (7, {}), {2}: (8, {})} | custom-call | tf_op jit(solution)/shard_map/pallas_call | solution.py:479
  (50 shorter events, 29.8 us)
Async XLA Ops:
  1.6 22.6 %collective-permute-start.12 = (bf16[2,192,384]{2,1,0:T(8,128)(2,1)S(1)}, bf16[2,192,384]{2,1,0:T(8,128)(2,1)S(1)}, u32[]{:S(2)}, u32[]{:S(2)}) collective-permute-start(bf16[2,192,384]{2,1,0:T(8,128)(2,1)S(1)} %shard_map.111.refs_1_), channel_id=1, source_target_pairs={{0,1},{1,0},{2,3},{3,2},{4,5},{5,4},{6,7},{7,6},{8,9},{9,8},{10,11... | collective-permute-start | bytes 884744 | tf_op jit(solution)/shard_map/ppermute | solution.py:334
  5.6 23.3 %collective-permute-start = (bf16[3,192,384]{2,1,0:T(8,128)(2,1)S(1)}, bf16[3,192,384]{2,1,0:T(8,128)(2,1)S(1)}, u32[]{:S(2)}, u32[]{:S(2)}) collective-permute-start(bf16[3,192,384]{2,1,0:T(8,128)(2,1)S(1)} %shard_map.104.refs_0_), channel_id=1, source_target_pairs={{0,1},{1,0},{2,3},{3,2},{4,5},{5,4},{6,7},{7,6},{8,9},{9,8},{10,11... | collective-permute-start | bytes 1327112 | tf_op jit(solution)/shard_map/ppermute | solution.py:334
  6.5 17.7 %collective-permute-start.11 = (bf16[1,192,384]{2,1,0:T(8,128)(2,1)S(1)}, bf16[1,192,384]{2,1,0:T(8,128)(2,1)S(1)}, u32[]{:S(2)}, u32[]{:S(2)}) collective-permute-start(bf16[1,192,384]{2,1,0:T(8,128)(2,1)S(1)} %shard_map.110.refs_0_), channel_id=1, source_target_pairs={{0,1},{1,0},{2,3},{3,2},{4,5},{5,4},{6,7},{7,6},{8,9},{9,8},{10,11... | collective-permute-start | bytes 442376 | tf_op jit(solution)/shard_map/ppermute | solution.py:334
  27.1 16.3 %collective-permute-start.13 = (bf16[768,384]{1,0:T(8,128)(2,1)S(1)}, bf16[768,384]{1,0:T(8,128)(2,1)S(1)}, u32[]{:S(2)}, u32[]{:S(2)}) collective-permute-start(bf16[768,384]{1,0:T(8,128)(2,1)S(1)} %get-tuple-element.97), channel_id=1, source_target_pairs={{0,1},{1,0},{2,3},{3,2},{4,5},{5,4},{6,7},{7,6},{8,9},{9,8},{10,11... | collective-permute-start | bytes 1769480 | tf_op jit(solution)/shard_map/ppermute | solution.py:334
  31.7 35.8 %collective-permute-start.1 = (bf16[768,384]{1,0:T(8,128)(2,1)S(1)}, bf16[768,384]{1,0:T(8,128)(2,1)S(1)}, u32[]{:S(2)}, u32[]{:S(2)}) collective-permute-start(bf16[768,384]{1,0:T(8,128)(2,1)S(1)} %get-tuple-element.75), channel_id=1, source_target_pairs={{0,1},{1,0},{2,3},{3,2},{4,5},{5,4},{6,7},{7,6},{8,9},{9,8},{10,11... | collective-permute-start | bytes 1769480 | tf_op jit(solution)/shard_map/ppermute | solution.py:334
  33.6 32.5 %collective-permute-start.15 = (bf16[384,384]{1,0:T(8,128)(2,1)S(1)}, bf16[384,384]{1,0:T(8,128)(2,1)S(1)}, u32[]{:S(2)}, u32[]{:S(2)}) collective-permute-start(bf16[384,384]{1,0:T(8,128)(2,1)S(1)} %get-tuple-element.101), channel_id=1, source_target_pairs={{0,1},{1,0},{2,3},{3,2},{4,5},{5,4},{6,7},{7,6},{8,9},{9,8},{10,11... | collective-permute-start | bytes 884744 | tf_op jit(solution)/shard_map/ppermute | solution.py:334
  35.4 29.4 %collective-permute-start.17 = (bf16[192,384]{1,0:T(8,128)(2,1)S(1)}, bf16[192,384]{1,0:T(8,128)(2,1)S(1)}, u32[]{:S(2)}, u32[]{:S(2)}) collective-permute-start(bf16[192,384]{1,0:T(8,128)(2,1)S(1)} %collective-permute-done.5), channel_id=1, source_target_pairs={{4,0},{5,1}} | collective-permute-start | bytes 442376 | tf_op jit(solution)/shard_map/ppermute | solution.py:428
  44.0 44.3 %collective-permute-start.14 = (bf16[768,384]{1,0:T(8,128)(2,1)S(1)}, bf16[768,384]{1,0:T(8,128)(2,1)S(1)}, u32[]{:S(2)}, u32[]{:S(2)}) collective-permute-start(bf16[768,384]{1,0:T(8,128)(2,1)S(1)} %get-tuple-element.98.pgu_ref), channel_id=1, source_target_pairs={{0,2},{2,4},{4,6},{6,8},{8,10},{10,12},{12,14},{14,16},{16,18},{18... | collective-permute-start | bytes 1769480 | tf_op jit(solution)/shard_map/ppermute | solution.py:337
  45.4 31.4 %collective-permute-start.3 = (bf16[384,384]{1,0:T(8,128)(2,1)S(1)}, bf16[384,384]{1,0:T(8,128)(2,1)S(1)}, u32[]{:S(2)}, u32[]{:S(2)}) collective-permute-start(bf16[384,384]{1,0:T(8,128)(2,1)S(1)} %get-tuple-element.79), channel_id=1, source_target_pairs={{0,1},{1,0},{2,3},{3,2},{4,5},{5,4},{6,7},{7,6},{8,9},{9,8},{10,11... | collective-permute-start | bytes 884744 | tf_op jit(solution)/shard_map/ppermute | solution.py:334
  64.9 7.0 %collective-permute-start.18 = (bf16[192,384]{1,0:T(8,128)(2,1)S(1)}, bf16[192,384]{1,0:T(8,128)(2,1)S(1)}, u32[]{:S(2)}, u32[]{:S(2)}) collective-permute-start(bf16[192,384]{1,0:T(8,128)(2,1)S(1)} %collective-permute-done.5), channel_id=1, source_target_pairs={{8,0},{9,1}} | collective-permute-start | bytes 442376 | tf_op jit(solution)/shard_map/ppermute | solution.py:428
  66.2 7.9 %collective-permute-start.19 = (bf16[192,384]{1,0:T(8,128)(2,1)S(1)}, bf16[192,384]{1,0:T(8,128)(2,1)S(1)}, u32[]{:S(2)}, u32[]{:S(2)}) collective-permute-start(bf16[192,384]{1,0:T(8,128)(2,1)S(1)} %collective-permute-done.5), channel_id=1, source_target_pairs={{12,0},{13,1}} | collective-permute-start | bytes 442376 | tf_op jit(solution)/shard_map/ppermute | solution.py:428
  67.5 7.9 %collective-permute-start.6 = (bf16[192,384]{1,0:T(8,128)(2,1)S(1)}, bf16[192,384]{1,0:T(8,128)(2,1)S(1)}, u32[]{:S(2)}, u32[]{:S(2)}) collective-permute-start(bf16[192,384]{1,0:T(8,128)(2,1)S(1)} %collective-permute-done.5), channel_id=1, source_target_pairs={{16,0},{17,1}} | collective-permute-start | bytes 442376 | tf_op jit(solution)/shard_map/ppermute | solution.py:428
  71.9 26.7 %collective-permute-start.2 = (bf16[768,384]{1,0:T(8,128)(2,1)S(1)}, bf16[768,384]{1,0:T(8,128)(2,1)S(1)}, u32[]{:S(2)}, u32[]{:S(2)}) collective-permute-start(bf16[768,384]{1,0:T(8,128)(2,1)S(1)} %get-tuple-element.76.pgu_ref), channel_id=1, source_target_pairs={{0,2},{2,4},{4,6},{6,8},{8,10},{10,12},{12,14},{14,16},{16,18},{18... | collective-permute-start | bytes 1769480 | tf_op jit(solution)/shard_map/ppermute | solution.py:337
  74.1 12.8 %collective-permute-start.16 = (bf16[384,384]{1,0:T(8,128)(2,1)S(1)}, bf16[384,384]{1,0:T(8,128)(2,1)S(1)}, u32[]{:S(2)}, u32[]{:S(2)}) collective-permute-start(bf16[384,384]{1,0:T(8,128)(2,1)S(1)} %get-tuple-element.103.pdown_ref), channel_id=1, source_target_pairs={{0,2},{2,4},{4,6},{6,8},{8,10},{10,12},{12,14},{14,16},{16,18},{18... | collective-permute-start | bytes 884744 | tf_op jit(solution)/shard_map/ppermute | solution.py:337
  75.4 28.0 %collective-permute-start.20 = (bf16[1152,384]{1,0:T(8,128)(2,1)S(1)}, bf16[1152,384]{1,0:T(8,128)(2,1)S(1)}, u32[]{:S(2)}, u32[]{:S(2)}) collective-permute-start(bf16[1152,384]{1,0:T(8,128)(2,1)S(1)} %get-tuple-element.106), channel_id=1, source_target_pairs={{0,2},{2,4},{4,6},{6,8},{8,10},{10,12},{12,14},{14,16},{16,18},{18... | collective-permute-start | bytes 2654216 | tf_op jit(solution)/shard_map/ppermute | solution.py:337
  76.8 8.8 %collective-permute-start.7 = (bf16[192,384]{1,0:T(8,128)(2,1)S(1)}, bf16[192,384]{1,0:T(8,128)(2,1)S(1)}, u32[]{:S(2)}, u32[]{:S(2)}) collective-permute-start(bf16[192,384]{1,0:T(8,128)(2,1)S(1)} %collective-permute-done.5), channel_id=1, source_target_pairs={{20,0},{21,1}} | collective-permute-start | bytes 442376 | tf_op jit(solution)/shard_map/ppermute | solution.py:428
  85.6 13.0 %collective-permute-start.4 = (bf16[384,384]{1,0:T(8,128)(2,1)S(1)}, bf16[384,384]{1,0:T(8,128)(2,1)S(1)}, u32[]{:S(2)}, u32[]{:S(2)}) collective-permute-start(bf16[384,384]{1,0:T(8,128)(2,1)S(1)} %get-tuple-element.81.pdown_ref), channel_id=1, source_target_pairs={{0,2},{2,4},{4,6},{6,8},{8,10},{10,12},{12,14},{14,16},{16,18},{18... | collective-permute-start | bytes 884744 | tf_op jit(solution)/shard_map/ppermute | solution.py:337
  86.9 42.3 %collective-permute-start.9 = (bf16[1152,384]{1,0:T(8,128)(2,1)S(1)}, bf16[1152,384]{1,0:T(8,128)(2,1)S(1)}, u32[]{:S(2)}, u32[]{:S(2)}) collective-permute-start(bf16[1152,384]{1,0:T(8,128)(2,1)S(1)} %get-tuple-element.84), channel_id=1, source_target_pairs={{0,2},{2,4},{4,6},{6,8},{8,10},{10,12},{12,14},{14,16},{16,18},{18... | collective-permute-start | bytes 2654216 | tf_op jit(solution)/shard_map/ppermute | solution.py:337
  88.3 8.8 %collective-permute-start.8 = (bf16[192,384]{1,0:T(8,128)(2,1)S(1)}, bf16[192,384]{1,0:T(8,128)(2,1)S(1)}, u32[]{:S(2)}, u32[]{:S(2)}) collective-permute-start(bf16[192,384]{1,0:T(8,128)(2,1)S(1)} %collective-permute-done.5), channel_id=1, source_target_pairs={{24,0},{25,1}} | collective-permute-start | bytes 442376 | tf_op jit(solution)/shard_map/ppermute | solution.py:428
  97.1 16.2 %collective-permute-start.21 = (bf16[768,384]{1,0:T(8,128)(2,1)S(1)}, bf16[768,384]{1,0:T(8,128)(2,1)S(1)}, u32[]{:S(2)}, u32[]{:S(2)}) collective-permute-start(bf16[768,384]{1,0:T(8,128)(2,1)S(1)} %get-tuple-element.110), channel_id=1, source_target_pairs={{0,1},{1,0},{2,3},{3,2},{4,5},{5,4},{6,7},{7,6},{8,9},{9,8},{10,11... | collective-permute-start | bytes 1769480 | tf_op jit(solution)/shard_map/ppermute | solution.py:334
  101.3 28.0 %collective-permute-start.10 = (bf16[768,384]{1,0:T(8,128)(2,1)S(1)}, bf16[768,384]{1,0:T(8,128)(2,1)S(1)}, u32[]{:S(2)}, u32[]{:S(2)}) collective-permute-start(bf16[768,384]{1,0:T(8,128)(2,1)S(1)} %get-tuple-element.88), channel_id=1, source_target_pairs={{0,1},{1,0},{2,3},{3,2},{4,5},{5,4},{6,7},{7,6},{8,9},{9,8},{10,11... | collective-permute-start | bytes 1769480 | tf_op jit(solution)/shard_map/ppermute | solution.py:334
  101.9 25.7 %collective-permute-start.22 = (bf16[384,384]{1,0:T(8,128)(2,1)S(1)}, bf16[384,384]{1,0:T(8,128)(2,1)S(1)}, u32[]{:S(2)}, u32[]{:S(2)}) collective-permute-start(bf16[384,384]{1,0:T(8,128)(2,1)S(1)} %get-tuple-element.112), channel_id=1, source_target_pairs={{0,1},{1,0},{2,3},{3,2},{4,5},{5,4},{6,7},{7,6},{8,9},{9,8},{10,11... | collective-permute-start | bytes 884744 | tf_op jit(solution)/shard_map/ppermute | solution.py:334
  103.4 27.6 %collective-permute-start.24 = (bf16[256,384]{1,0:T(8,128)(2,1)S(1)}, bf16[256,384]{1,0:T(8,128)(2,1)S(1)}, u32[]{:S(2)}, u32[]{:S(2)}) collective-permute-start(bf16[256,384]{1,0:T(8,128)(2,1)S(1)} %get-tuple-element.121), channel_id=1, source_target_pairs={{0,1},{1,0},{2,3},{3,2},{4,5},{5,4},{6,7},{7,6},{8,9},{9,8},{10,11... | collective-permute-start | bytes 589832 | tf_op jit(solution)/shard_map/ppermute | solution.py:334
  113.3 18.4 %collective-permute-start.23 = (bf16[128,384]{1,0:T(8,128)(2,1)S(1)}, bf16[128,384]{1,0:T(8,128)(2,1)S(1)}, u32[]{:S(2)}, u32[]{:S(2)}) collective-permute-start(bf16[128,384]{1,0:T(8,128)(2,1)S(1)} %get-tuple-element.120), channel_id=1, source_target_pairs={{0,1},{1,0},{2,3},{3,2},{4,5},{5,4},{6,7},{7,6},{8,9},{9,8},{10,11... | collective-permute-start | bytes 294920 | tf_op jit(solution)/shard_map/ppermute | solution.py:334
  (3 other events, 32.6 us)

commit v12 on v11

--- a/solution.py
+++ b/solution.py
@@ -251,17 +251,12 @@
         return pl.ds(pl.multiple_of(head * width + first, 128), size)
 
     if cut == 0:
-        out_s, fast_s, mine_s, new_s, kept_s = refs
+        out_s, fast_ref, moment_ref, new_s, kept_s, fast_s, mine_s, sems = refs[-8:]
     elif cut == 1:
-        before = refs[:3]
-        out_ref, fast_ref, moment_ref, new_s, out_s, out_sems, sems = refs[-7:]
-        stores = [
-            pltpu.make_async_copy(before[0], out_ref.at[1, :, columns(0)], sems.at[0]),
-            pltpu.make_async_copy(before[1], fast_ref.at[0, 2, head], sems.at[1]),
-            pltpu.make_async_copy(before[2], moment_ref.at[0, 2, head], sems.at[2]),
-        ]
-        for store in stores:
-            store.start()
+        before = refs[0]
+        out_ref, new_s, out_s, out_sems, sem = refs[-5:]
+        stores = [pltpu.make_async_copy(before, out_ref.at[1, :, columns(0)], sem)]
+        stores[0].start()
     else:
         out_ref, fast_ref, moment_ref, new_s, out_s, out_sems, kept_s, fast_s, mine_s, sems = refs[-10:]
     moment = decay_ref[:, head : head + 1] * earlier_ref[pl.ds(2 * width + first, size), :].astype(F32)
@@ -272,7 +267,6 @@
         mine = pl.ds(pl.multiple_of(me * part - first, math.gcd(part, 128)), part)
         fast_s[...] = new_s[mine, :]
         mine_s[...] = kept_s[mine, :]
-    if cut is None:
         stores = [
             pltpu.make_async_copy(fast_s, fast_ref.at[0, 2, head], sems.at[0]),
             pltpu.make_async_copy(mine_s, moment_ref.at[0, 2, head], sems.at[1]),
@@ -288,9 +282,8 @@
                 )
             )
             stores[-1].start()
-    if cut != 0:
-        for store in stores:
-            store.wait()
+    for store in stores:
+        store.wait()
 
 
 def apply_one(head, q_ref, pgu_ref, pdown_ref, *refs):
@@ -496,30 +489,32 @@
             size = recvs[0].shape[0]
             new = pltpu.VMEM((size, width), BF16)
             kept = pltpu.VMEM((size, width), F32)
+            mine = (pltpu.VMEM((part, width), BF16), pltpu.VMEM((part, width), F32), DMA((2,)))
+            product = (pltpu.VMEM((rows, size), BF16), DMA((chunks,)))
             if cut == 0:
-                outs = (shape(rows, size), shape(part, width), shape(part, width, dtype=F32))
-                extra, scratch, space = [], (new, kept), VMEM
+                outs = (shape(rows, size), fast_shape, moment_shape)
+                extra, scratch, spaces = [*ends], (new, kept) + mine, (VMEM, HBM, HBM)
+                aliases = {at: 1, at + 1: 2}
+            elif cut == 1:
+                outs, extra, spaces = (out_shape,), [outputs], (HBM,)
+                scratch, aliases = (new, *product, DMA(())), {at + 1: 0}
             else:
-                outs = (out_shape, fast_shape, moment_shape)
-                extra, space = [outputs, *ends], HBM
-                scratch = (new, pltpu.VMEM((rows, size), BF16), DMA((chunks,)))
-                if cut is None:
-                    scratch += (kept, pltpu.VMEM((part, width), BF16))
-                    scratch += (pltpu.VMEM((part, width), F32), DMA((2,)))
-                else:
-                    scratch += (DMA((3,)),)
+                outs, extra, spaces = (out_shape, fast_shape, moment_shape), [outputs, *ends], (HBM,) * 3
+                scratch, aliases = (new, *product, kept) + mine, {at + j: j for j in range(3)}
             results = call(
                 functools.partial(update_two_down, n, h, cut),
                 outs,
                 [VMEM] * (5 + n + len(before)) + [HBM] * len(extra),
-                (space,) * 3,
+                spaces,
                 scratch,
-                aliases={at + len(before) + j: j for j in range(len(extra))},
+                aliases=aliases,
             )(rates, decays, down, own_down, moments[h], hq, *recvs, *before, *extra)
             if cut == 0:
-                before = results
+                first_columns, *ends = results
+                before = [first_columns]
             else:
-                outputs, *ends = results
+                outputs, *rest = results
+                ends = rest or ends
     return (outputs, jnp.swapaxes(ends[0], 3, 4), jnp.swapaxes(ends[1], 3, 4))
 
 

time: 134 us -> 134 us (level)
  no operation moved by 1% of the time
where the time goes in v12:
time: 134 us
  waiting for transfers between devices  67.1 us (50%)
  Pallas kernels  32.9 us (25%)
  starting transfers between devices  32.7 us (24%)
    ppermute x12, waiting for transfers between devices, turned(): lax.ppermute(x, 'tok', [(i, (i + r) % n) for i in range(n)])  34.3 us
    ppermute x6, waiting for transfers between devices, on_device(): lax.ppermute(x, ('block', 'tok'), [(sources[p] * n + i, i) for i in range...  32.8 us
    ppermute x12, starting transfers between devices, turned(): lax.ppermute(x, 'tok', [(i, (i + r) % n) for i in range(n)])  16.4 us
    ppermute x6, starting transfers between devices, forward(): return lax.ppermute(x, 'block', [(i, i + 1) for i in range(blocks - 1)])  7.93 us
    ppermute x6, starting transfers between devices, on_device(): lax.ppermute(x, ('block', 'tok'), [(sources[p] * n + i, i) for i in range...  7.73 us
    pallas_call x2, Pallas kernels, on_device(): call(functools.partial(grads_one, n, h, groups[h], divisor), grad_out, [V...  5.65 us
    pallas_call x2, Pallas kernels, on_device(): call(functools.partial(grads_two, n, divisor), (shape(2 * width, width),...  5.08 us
    pallas_call x2, Pallas kernels, on_device(): call(functools.partial(apply_one, h), out_shape, [VMEM] * 3 + [HBM] * len...  4.54 us
  transfers between devices with their start and end apart: 25, of which 9 were waited for; matrix products, arithmetic and copies ran while one was open for 0% of the time, Pallas kernels for 23%

profile of v12, /device:TPU:0, one launch (start us, length us, event | category | flops | bytes accessed | tf_op | source)
XLA Modules:
  0.0 133.8 jit_solution(16455176736048076547)
XLA Ops:
  1.6 3.0 %collective-permute-start.12 = (bf16[2,192,384]{2,1,0:T(8,128)(2,1)S(1)}, bf16[2,192,384]{2,1,0:T(8,128)(2,1)S(1)}, u32[]{:S(2)}, u32[]{:S(2)}) collective-permute-start(bf16[2,192,384]{2,1,0:T(8,128)(2,1)S(1)} %shard_map.111.refs_1_), channel_id=1, source_target_pairs={{0,1},{1,0},{2,3},{3,2},{4,5},{5,4},{6,7},{7,6},{8,9},{9,8},{10,11... | collective-permute-start | bytes 884744 | tf_op jit(solution)/shard_map/ppermute | solution.py:327
  6.5 2.0 %collective-permute-start.11 = (bf16[1,192,384]{2,1,0:T(8,128)(2,1)S(1)}, bf16[1,192,384]{2,1,0:T(8,128)(2,1)S(1)}, u32[]{:S(2)}, u32[]{:S(2)}) collective-permute-start(bf16[1,192,384]{2,1,0:T(8,128)(2,1)S(1)} %shard_map.110.refs_0_), channel_id=1, source_target_pairs={{0,1},{1,0},{2,3},{3,2},{4,5},{5,4},{6,7},{7,6},{8,9},{9,8},{10,11... | collective-permute-start | bytes 442376 | tf_op jit(solution)/shard_map/ppermute | solution.py:327
  8.5 3.9 %shard_map.103 = (bf16[768,384]{1,0:T(8,128)(2,1)S(1)}, bf16[768,384]{1,0:T(8,128)(2,1)S(1)}, bf16[768,384]{1,0:T(8,128)(2,1)S(1)}, bf16[768,384]{1,0:T(8,128)(2...) custom-call(bf16[2,768,768]{2,1,0:T(8,128)(2,1)} %k_ref.1, ...), custom_call_target="tpu_custom_call" | custom-call | tf_op jit(solution)/shard_map/pallas_call | solution.py:375
  12.4 11.8 %collective-permute-done.11.refs_2_ = bf16[1,192,384]{2,1,0:T(8,128)(2,1)S(1)} collective-permute-done((bf16[1,192,384]{2,1,0:T(8,128)(2,1)S(1)}, bf16[1,192,384]{2,1,0:T(8,128)(2,1)S(1)}, u32[]{:S(2)}, u32[]{:S(2)}) %collective-permute-start.11) | collective-permute-done | bytes 147488 | tf_op jit(solution)/shard_map/ppermute | solution.py:327
  24.2 2.8 %shard_map.112 = (bf16[768,384]{1,0:T(8,128)(2,1)S(1)}, bf16[384,384]{1,0:T(8,128)(2,1)S(1)}, bf16[768,384]{1,0:T(8,128)(2,1)S(1)}, bf16[384,384]{1,0:T(8,128)(2...) custom-call(f32[1,2]{1,0:T(1,128)S(1)} %bitcast.16, bf16[768,384]{1,0:T(8,128)(2,1)S(1)} %get-tuple-element.89.k_ref, ...), custom_call_target="tpu_custom_call" | custom-call | tf_op jit(solution)/shard_map/pallas_call | solution.py:389
  27.1 1.8 %collective-permute-start.13 = (bf16[768,384]{1,0:T(8,128)(2,1)S(1)}, bf16[768,384]{1,0:T(8,128)(2,1)S(1)}, u32[]{:S(2)}, u32[]{:S(2)}) collective-permute-start(bf16[768,384]{1,0:T(8,128)(2,1)S(1)} %get-tuple-element.94), channel_id=1, source_target_pairs={{0,1},{1,0},{2,3},{3,2},{4,5},{5,4},{6,7},{7,6},{8,9},{9,8},{10,11... | collective-permute-start | bytes 1769480 | tf_op jit(solution)/shard_map/ppermute | solution.py:327
  28.9 2.8 %shard_map.105 = (bf16[768,384]{1,0:T(8,128)(2,1)S(1)}, bf16[384,384]{1,0:T(8,128)(2,1)S(1)}, bf16[768,384]{1,0:T(8,128)(2,1)S(1)}, bf16[384,384]{1,0:T(8,128)(2...) custom-call(f32[1,2]{1,0:T(1,128)S(1)} %bitcast.17, bf16[768,384]{1,0:T(8,128)(2,1)S(1)} %get-tuple-element.67.k_ref, ...), custom_call_target="tpu_custom_call" | custom-call | tf_op jit(solution)/shard_map/pallas_call | solution.py:389
  33.6 1.8 %collective-permute-start.15 = (bf16[384,384]{1,0:T(8,128)(2,1)S(1)}, bf16[384,384]{1,0:T(8,128)(2,1)S(1)}, u32[]{:S(2)}, u32[]{:S(2)}) collective-permute-start(bf16[384,384]{1,0:T(8,128)(2,1)S(1)} %get-tuple-element.98), channel_id=1, source_target_pairs={{0,1},{1,0},{2,3},{3,2},{4,5},{5,4},{6,7},{7,6},{8,9},{9,8},{10,11... | collective-permute-start | bytes 884744 | tf_op jit(solution)/shard_map/ppermute | solution.py:327
  36.7 6.6 %collective-permute-done.13.refs_0_ = bf16[768,384]{1,0:T(8,128)(2,1)S(1)} collective-permute-done((bf16[768,384]{1,0:T(8,128)(2,1)S(1)}, bf16[768,384]{1,0:T(8,128)(2,1)S(1)}, u32[]{:S(2)}, u32[]{:S(2)}) %collective-permute-start.13) | collective-permute-done | bytes 589856 | tf_op jit(solution)/shard_map/ppermute | solution.py:327
  45.4 1.8 %collective-permute-start.3 = (bf16[384,384]{1,0:T(8,128)(2,1)S(1)}, bf16[384,384]{1,0:T(8,128)(2,1)S(1)}, u32[]{:S(2)}, u32[]{:S(2)}) collective-permute-start(bf16[384,384]{1,0:T(8,128)(2,1)S(1)} %get-tuple-element.76), channel_id=1, source_target_pairs={{0,1},{1,0},{2,3},{3,2},{4,5},{5,4},{6,7},{7,6},{8,9},{9,8},{10,11... | collective-permute-start | bytes 884744 | tf_op jit(solution)/shard_map/ppermute | solution.py:327
  47.2 17.7 %collective-permute-done.17.refs_2_ = bf16[192,384]{1,0:T(8,128)(2,1)S(1)} collective-permute-done((bf16[192,384]{1,0:T(8,128)(2,1)S(1)}, bf16[192,384]{1,0:T(8,128)(2,1)S(1)}, u32[]{:S(2)}, u32[]{:S(2)}) %collective-permute-start.17) | collective-permute-done | bytes 147488 | tf_op jit(solution)/shard_map/ppermute | solution.py:421
  69.9 2.0 %collective-permute-done.18.refs_3_ = bf16[192,384]{1,0:T(8,128)(2,1)S(1)} collective-permute-done((bf16[192,384]{1,0:T(8,128)(2,1)S(1)}, bf16[192,384]{1,0:T(8,128)(2,1)S(1)}, u32[]{:S(2)}, u32[]{:S(2)}) %collective-permute-start.18) | collective-permute-done | bytes 147488 | tf_op jit(solution)/shard_map/ppermute | solution.py:421
  78.5 7.1 %collective-permute-done.7.refs_3_ = bf16[192,384]{1,0:T(8,128)(2,1)S(1)} collective-permute-done((bf16[192,384]{1,0:T(8,128)(2,1)S(1)}, bf16[192,384]{1,0:T(8,128)(2,1)S(1)}, u32[]{:S(2)}, u32[]{:S(2)}) %collective-permute-start.7) | collective-permute-done | bytes 147488 | tf_op jit(solution)/shard_map/ppermute | solution.py:421
  89.6 2.4 %shard_map.115 = (bf16[768,384]{1,0:T(8,128)(2,1)S(1)}, bf16[384,384]{1,0:T(8,128)(2,1)S(1)}, f32[768,384]{1,0:T(8,128)S(1)}, f32[384,384]{1,0:T(8,128)S(1)}, bf...) custom-call(bf16[768,384]{1,0:T(8,128)(2,1)S(1)} %get-tuple-element.86.k_ref, ...), custom_call_target="tpu_custom_call" | custom-call | tf_op jit(solution)/shard_map/pallas_call | solution.py:435
  92.0 5.1 %collective-permute-done.8.refs_4_ = bf16[192,384]{1,0:T(8,128)(2,1)S(1)} collective-permute-done((bf16[192,384]{1,0:T(8,128)(2,1)S(1)}, bf16[192,384]{1,0:T(8,128)(2,1)S(1)}, u32[]{:S(2)}, u32[]{:S(2)}) %collective-permute-start.8) | collective-permute-done | bytes 147488 | tf_op jit(solution)/shard_map/ppermute | solution.py:421
  97.1 1.5 %collective-permute-start.21 = (bf16[768,384]{1,0:T(8,128)(2,1)S(1)}, bf16[768,384]{1,0:T(8,128)(2,1)S(1)}, u32[]{:S(2)}, u32[]{:S(2)}) collective-permute-start(bf16[768,384]{1,0:T(8,128)(2,1)S(1)} %get-tuple-element.107), channel_id=1, source_target_pairs={{0,1},{1,0},{2,3},{3,2},{4,5},{5,4},{6,7},{7,6},{8,9},{9,8},{10,11... | collective-permute-start | bytes 1769480 | tf_op jit(solution)/shard_map/ppermute | solution.py:327
  98.6 2.7 %shard_map.109 = (bf16[768,384]{1,0:T(8,128)(2,1)S(1)}, bf16[384,384]{1,0:T(8,128)(2,1)S(1)}, f32[768,384]{1,0:T(8,128)S(1)}, f32[384,384]{1,0:T(8,128)S(1)}, bf...) custom-call(bf16[768,384]{1,0:T(8,128)(2,1)S(1)} %get-tuple-element.64.k_ref, ...), custom_call_target="tpu_custom_call" | custom-call | tf_op jit(solution)/shard_map/pallas_call | solution.py:435
  103.9 9.4 %collective-permute-done.21.refs_0_ = bf16[768,384]{1,0:T(8,128)(2,1)S(1)} collective-permute-done((bf16[768,384]{1,0:T(8,128)(2,1)S(1)}, bf16[768,384]{1,0:T(8,128)(2,1)S(1)}, u32[]{:S(2)}, u32[]{:S(2)}) %collective-permute-start.21) | collective-permute-done | bytes 589856 | tf_op jit(solution)/shard_map/ppermute | solution.py:327
  114.8 2.3 %shard_map.117.refs_0_ = bf16[2,768,768]{2,1,0:T(8,128)(2,1)} custom-call(bf16[768,384]{1,0:T(8,128)(2,1)S(1)} %get-tuple-element.111.q_ref, bf16[768,384]{1,0:T(8,128)(2,1)S(1)} %get-tuple-element.95.pgu_ref, bf16[384,384]{1,0:T(8,128)(2,1)S(1)} %get-tuple-element.100.pdown_ref), custom_call_target="tpu_custom_call" | custom-call | tf_op jit(solution)/shard_map/pallas_call | solution.py:455
  117.1 2.3 %shard_map.118.refs_1_ = bf16[2,768,768]{2,1,0:T(8,128)(2,1)} custom-call(bf16[768,384]{1,0:T(8,128)(2,1)S(1)} %get-tuple-element.110.q_ref, bf16[768,384]{1,0:T(8,128)(2,1)S(1)} %get-tuple-element.73.pgu_ref, bf16[384,384]{1,0:T(8,128)(2,1)S(1)} %get-tuple-element.78.pdown_ref, bf16[2,768,768]{2,1,0:T(8,128)(2,1)} %shard_map.117.refs_0_), custom_call_target="tpu_custom_call", output_to_operand_aliasing={{}: (3, {})} | custom-call | tf_op jit(solution)/shard_map/pallas_call | solution.py:455
  119.4 1.7 %shard_map.116 = (bf16[768,384]{1,0:T(8,128)(2,1)S(1)}, bf16[1,3,2,192,384]{4,3,2,1,0:T(8,128)(2,1)}, f32[1,3,2,192,384]{4,3,2,1,0:T(8,128)}) custom-call(f32[2,3]{1,0:T(2,128)S(1)} %bitcast.11, f32[1,2]{1,0:T(1,128)S(1)} %bitcast.18, bf16[768,384]{1,0:T(8,128)(2,1)S(1)} %get-tuple-element.104.old_ref, f32[768,384]{1,0:T(8,128)S(1)} %get-tuple-element.105.own_ref, ...), custom_call_target="tpu_custom_call" | custom-call | tf_op jit(solution)/shard_map/pallas_call | solution.py:472
  121.1 6.5 %collective-permute-done.22.refs_0_ = bf16[384,384]{1,0:T(8,128)(2,1)S(1)} collective-permute-done((bf16[384,384]{1,0:T(8,128)(2,1)S(1)}, bf16[384,384]{1,0:T(8,128)(2,1)S(1)}, u32[]{:S(2)}, u32[]{:S(2)}) %collective-permute-start.22) | collective-permute-done | bytes 294944 | tf_op jit(solution)/shard_map/ppermute | solution.py:327
  127.6 1.7 %shard_map.119 = (bf16[2,768,768]{2,1,0:T(8,128)(2,1)}, bf16[1,3,2,192,384]{4,3,2,1,0:T(8,128)(2,1)}, f32[1,3,2,192,384]{4,3,2,1,0:T(8,128)}) custom-call(f32[2,3]{1,0:T(2,128)S(1)} %bitcast.12, f32[1,2]{1,0:T(1,128)S(1)} %bitcast.19, bf16[384,384]{1,0:T(8,128)(2,1)S(1)} %get-tuple-element.101.old_ref, ...), custom_call_target="tpu_custom_call", output_to_operand_aliasing={{0}: (7, {}), {1}: (8, {}), {2}: (9, {})} | custom-call | tf_op jit(solution)/shard_map/pallas_call | solution.py:504
  129.3 1.7 %shard_map.120 = (bf16[768,384]{1,0:T(8,128)(2,1)S(1)}, bf16[1,3,2,192,384]{4,3,2,1,0:T(8,128)(2,1)}, f32[1,3,2,192,384]{4,3,2,1,0:T(8,128)}) custom-call(f32[2,3]{1,0:T(2,128)S(1)} %bitcast.13, f32[1,2]{1,0:T(1,128)S(1)} %bitcast.20, bf16[768,384]{1,0:T(8,128)(2,1)S(1)} %get-tuple-element.82.old_ref, ...), custom_call_target="tpu_custom_call", output_to_operand_aliasing={{1}: (7, {}), {2}: (8, {})} | custom-call | tf_op jit(solution)/shard_map/pallas_call | solution.py:472
  (50 shorter events, 30.3 us)
Async XLA Ops:
  1.6 22.6 %collective-permute-start.12 = (bf16[2,192,384]{2,1,0:T(8,128)(2,1)S(1)}, bf16[2,192,384]{2,1,0:T(8,128)(2,1)S(1)}, u32[]{:S(2)}, u32[]{:S(2)}) collective-permute-start(bf16[2,192,384]{2,1,0:T(8,128)(2,1)S(1)} %shard_map.111.refs_1_), channel_id=1, source_target_pairs={{0,1},{1,0},{2,3},{3,2},{4,5},{5,4},{6,7},{7,6},{8,9},{9,8},{10,11... | collective-permute-start | bytes 884744 | tf_op jit(solution)/shard_map/ppermute | solution.py:327
  5.6 23.3 %collective-permute-start = (bf16[3,192,384]{2,1,0:T(8,128)(2,1)S(1)}, bf16[3,192,384]{2,1,0:T(8,128)(2,1)S(1)}, u32[]{:S(2)}, u32[]{:S(2)}) collective-permute-start(bf16[3,192,384]{2,1,0:T(8,128)(2,1)S(1)} %shard_map.104.refs_0_), channel_id=1, source_target_pairs={{0,1},{1,0},{2,3},{3,2},{4,5},{5,4},{6,7},{7,6},{8,9},{9,8},{10,11... | collective-permute-start | bytes 1327112 | tf_op jit(solution)/shard_map/ppermute | solution.py:327
  6.5 17.7 %collective-permute-start.11 = (bf16[1,192,384]{2,1,0:T(8,128)(2,1)S(1)}, bf16[1,192,384]{2,1,0:T(8,128)(2,1)S(1)}, u32[]{:S(2)}, u32[]{:S(2)}) collective-permute-start(bf16[1,192,384]{2,1,0:T(8,128)(2,1)S(1)} %shard_map.110.refs_0_), channel_id=1, source_target_pairs={{0,1},{1,0},{2,3},{3,2},{4,5},{5,4},{6,7},{7,6},{8,9},{9,8},{10,11... | collective-permute-start | bytes 442376 | tf_op jit(solution)/shard_map/ppermute | solution.py:327
  27.1 16.3 %collective-permute-start.13 = (bf16[768,384]{1,0:T(8,128)(2,1)S(1)}, bf16[768,384]{1,0:T(8,128)(2,1)S(1)}, u32[]{:S(2)}, u32[]{:S(2)}) collective-permute-start(bf16[768,384]{1,0:T(8,128)(2,1)S(1)} %get-tuple-element.94), channel_id=1, source_target_pairs={{0,1},{1,0},{2,3},{3,2},{4,5},{5,4},{6,7},{7,6},{8,9},{9,8},{10,11... | collective-permute-start | bytes 1769480 | tf_op jit(solution)/shard_map/ppermute | solution.py:327
  31.7 35.8 %collective-permute-start.1 = (bf16[768,384]{1,0:T(8,128)(2,1)S(1)}, bf16[768,384]{1,0:T(8,128)(2,1)S(1)}, u32[]{:S(2)}, u32[]{:S(2)}) collective-permute-start(bf16[768,384]{1,0:T(8,128)(2,1)S(1)} %get-tuple-element.72), channel_id=1, source_target_pairs={{0,1},{1,0},{2,3},{3,2},{4,5},{5,4},{6,7},{7,6},{8,9},{9,8},{10,11... | collective-permute-start | bytes 1769480 | tf_op jit(solution)/shard_map/ppermute | solution.py:327
  33.6 32.5 %collective-permute-start.15 = (bf16[384,384]{1,0:T(8,128)(2,1)S(1)}, bf16[384,384]{1,0:T(8,128)(2,1)S(1)}, u32[]{:S(2)}, u32[]{:S(2)}) collective-permute-start(bf16[384,384]{1,0:T(8,128)(2,1)S(1)} %get-tuple-element.98), channel_id=1, source_target_pairs={{0,1},{1,0},{2,3},{3,2},{4,5},{5,4},{6,7},{7,6},{8,9},{9,8},{10,11... | collective-permute-start | bytes 884744 | tf_op jit(solution)/shard_map/ppermute | solution.py:327
  35.4 29.4 %collective-permute-start.17 = (bf16[192,384]{1,0:T(8,128)(2,1)S(1)}, bf16[192,384]{1,0:T(8,128)(2,1)S(1)}, u32[]{:S(2)}, u32[]{:S(2)}) collective-permute-start(bf16[192,384]{1,0:T(8,128)(2,1)S(1)} %collective-permute-done.5), channel_id=1, source_target_pairs={{4,0},{5,1}} | collective-permute-start | bytes 442376 | tf_op jit(solution)/shard_map/ppermute | solution.py:421
  44.0 44.3 %collective-permute-start.14 = (bf16[768,384]{1,0:T(8,128)(2,1)S(1)}, bf16[768,384]{1,0:T(8,128)(2,1)S(1)}, u32[]{:S(2)}, u32[]{:S(2)}) collective-permute-start(bf16[768,384]{1,0:T(8,128)(2,1)S(1)} %get-tuple-element.95.pgu_ref), channel_id=1, source_target_pairs={{0,2},{2,4},{4,6},{6,8},{8,10},{10,12},{12,14},{14,16},{16,18},{18... | collective-permute-start | bytes 1769480 | tf_op jit(solution)/shard_map/ppermute | solution.py:330
  45.4 31.4 %collective-permute-start.3 = (bf16[384,384]{1,0:T(8,128)(2,1)S(1)}, bf16[384,384]{1,0:T(8,128)(2,1)S(1)}, u32[]{:S(2)}, u32[]{:S(2)}) collective-permute-start(bf16[384,384]{1,0:T(8,128)(2,1)S(1)} %get-tuple-element.76), channel_id=1, source_target_pairs={{0,1},{1,0},{2,3},{3,2},{4,5},{5,4},{6,7},{7,6},{8,9},{9,8},{10,11... | collective-permute-start | bytes 884744 | tf_op jit(solution)/shard_map/ppermute | solution.py:327
  64.9 7.0 %collective-permute-start.18 = (bf16[192,384]{1,0:T(8,128)(2,1)S(1)}, bf16[192,384]{1,0:T(8,128)(2,1)S(1)}, u32[]{:S(2)}, u32[]{:S(2)}) collective-permute-start(bf16[192,384]{1,0:T(8,128)(2,1)S(1)} %collective-permute-done.5), channel_id=1, source_target_pairs={{8,0},{9,1}} | collective-permute-start | bytes 442376 | tf_op jit(solution)/shard_map/ppermute | solution.py:421
  66.2 7.9 %collective-permute-start.19 = (bf16[192,384]{1,0:T(8,128)(2,1)S(1)}, bf16[192,384]{1,0:T(8,128)(2,1)S(1)}, u32[]{:S(2)}, u32[]{:S(2)}) collective-permute-start(bf16[192,384]{1,0:T(8,128)(2,1)S(1)} %collective-permute-done.5), channel_id=1, source_target_pairs={{12,0},{13,1}} | collective-permute-start | bytes 442376 | tf_op jit(solution)/shard_map/ppermute | solution.py:421
  67.5 7.9 %collective-permute-start.6 = (bf16[192,384]{1,0:T(8,128)(2,1)S(1)}, bf16[192,384]{1,0:T(8,128)(2,1)S(1)}, u32[]{:S(2)}, u32[]{:S(2)}) collective-permute-start(bf16[192,384]{1,0:T(8,128)(2,1)S(1)} %collective-permute-done.5), channel_id=1, source_target_pairs={{16,0},{17,1}} | collective-permute-start | bytes 442376 | tf_op jit(solution)/shard_map/ppermute | solution.py:421
  71.9 26.7 %collective-permute-start.2 = (bf16[768,384]{1,0:T(8,128)(2,1)S(1)}, bf16[768,384]{1,0:T(8,128)(2,1)S(1)}, u32[]{:S(2)}, u32[]{:S(2)}) collective-permute-start(bf16[768,384]{1,0:T(8,128)(2,1)S(1)} %get-tuple-element.73.pgu_ref), channel_id=1, source_target_pairs={{0,2},{2,4},{4,6},{6,8},{8,10},{10,12},{12,14},{14,16},{16,18},{18... | collective-permute-start | bytes 1769480 | tf_op jit(solution)/shard_map/ppermute | solution.py:330
  74.1 12.8 %collective-permute-start.16 = (bf16[384,384]{1,0:T(8,128)(2,1)S(1)}, bf16[384,384]{1,0:T(8,128)(2,1)S(1)}, u32[]{:S(2)}, u32[]{:S(2)}) collective-permute-start(bf16[384,384]{1,0:T(8,128)(2,1)S(1)} %get-tuple-element.100.pdown_ref), channel_id=1, source_target_pairs={{0,2},{2,4},{4,6},{6,8},{8,10},{10,12},{12,14},{14,16},{16,18},{18... | collective-permute-start | bytes 884744 | tf_op jit(solution)/shard_map/ppermute | solution.py:330
  75.4 28.0 %collective-permute-start.20 = (bf16[1152,384]{1,0:T(8,128)(2,1)S(1)}, bf16[1152,384]{1,0:T(8,128)(2,1)S(1)}, u32[]{:S(2)}, u32[]{:S(2)}) collective-permute-start(bf16[1152,384]{1,0:T(8,128)(2,1)S(1)} %get-tuple-element.103), channel_id=1, source_target_pairs={{0,2},{2,4},{4,6},{6,8},{8,10},{10,12},{12,14},{14,16},{16,18},{18... | collective-permute-start | bytes 2654216 | tf_op jit(solution)/shard_map/ppermute | solution.py:330
  76.8 8.8 %collective-permute-start.7 = (bf16[192,384]{1,0:T(8,128)(2,1)S(1)}, bf16[192,384]{1,0:T(8,128)(2,1)S(1)}, u32[]{:S(2)}, u32[]{:S(2)}) collective-permute-start(bf16[192,384]{1,0:T(8,128)(2,1)S(1)} %collective-permute-done.5), channel_id=1, source_target_pairs={{20,0},{21,1}} | collective-permute-start | bytes 442376 | tf_op jit(solution)/shard_map/ppermute | solution.py:421
  85.6 13.0 %collective-permute-start.4 = (bf16[384,384]{1,0:T(8,128)(2,1)S(1)}, bf16[384,384]{1,0:T(8,128)(2,1)S(1)}, u32[]{:S(2)}, u32[]{:S(2)}) collective-permute-start(bf16[384,384]{1,0:T(8,128)(2,1)S(1)} %get-tuple-element.78.pdown_ref), channel_id=1, source_target_pairs={{0,2},{2,4},{4,6},{6,8},{8,10},{10,12},{12,14},{14,16},{16,18},{18... | collective-permute-start | bytes 884744 | tf_op jit(solution)/shard_map/ppermute | solution.py:330
  86.9 42.3 %collective-permute-start.9 = (bf16[1152,384]{1,0:T(8,128)(2,1)S(1)}, bf16[1152,384]{1,0:T(8,128)(2,1)S(1)}, u32[]{:S(2)}, u32[]{:S(2)}) collective-permute-start(bf16[1152,384]{1,0:T(8,128)(2,1)S(1)} %get-tuple-element.81), channel_id=1, source_target_pairs={{0,2},{2,4},{4,6},{6,8},{8,10},{10,12},{12,14},{14,16},{16,18},{18... | collective-permute-start | bytes 2654216 | tf_op jit(solution)/shard_map/ppermute | solution.py:330
  88.3 8.8 %collective-permute-start.8 = (bf16[192,384]{1,0:T(8,128)(2,1)S(1)}, bf16[192,384]{1,0:T(8,128)(2,1)S(1)}, u32[]{:S(2)}, u32[]{:S(2)}) collective-permute-start(bf16[192,384]{1,0:T(8,128)(2,1)S(1)} %collective-permute-done.5), channel_id=1, source_target_pairs={{24,0},{25,1}} | collective-permute-start | bytes 442376 | tf_op jit(solution)/shard_map/ppermute | solution.py:421
  97.1 16.2 %collective-permute-start.21 = (bf16[768,384]{1,0:T(8,128)(2,1)S(1)}, bf16[768,384]{1,0:T(8,128)(2,1)S(1)}, u32[]{:S(2)}, u32[]{:S(2)}) collective-permute-start(bf16[768,384]{1,0:T(8,128)(2,1)S(1)} %get-tuple-element.107), channel_id=1, source_target_pairs={{0,1},{1,0},{2,3},{3,2},{4,5},{5,4},{6,7},{7,6},{8,9},{9,8},{10,11... | collective-permute-start | bytes 1769480 | tf_op jit(solution)/shard_map/ppermute | solution.py:327
  101.3 28.0 %collective-permute-start.10 = (bf16[768,384]{1,0:T(8,128)(2,1)S(1)}, bf16[768,384]{1,0:T(8,128)(2,1)S(1)}, u32[]{:S(2)}, u32[]{:S(2)}) collective-permute-start(bf16[768,384]{1,0:T(8,128)(2,1)S(1)} %get-tuple-element.85), channel_id=1, source_target_pairs={{0,1},{1,0},{2,3},{3,2},{4,5},{5,4},{6,7},{7,6},{8,9},{9,8},{10,11... | collective-permute-start | bytes 1769480 | tf_op jit(solution)/shard_map/ppermute | solution.py:327
  101.9 25.7 %collective-permute-start.22 = (bf16[384,384]{1,0:T(8,128)(2,1)S(1)}, bf16[384,384]{1,0:T(8,128)(2,1)S(1)}, u32[]{:S(2)}, u32[]{:S(2)}) collective-permute-start(bf16[384,384]{1,0:T(8,128)(2,1)S(1)} %get-tuple-element.109), channel_id=1, source_target_pairs={{0,1},{1,0},{2,3},{3,2},{4,5},{5,4},{6,7},{7,6},{8,9},{9,8},{10,11... | collective-permute-start | bytes 884744 | tf_op jit(solution)/shard_map/ppermute | solution.py:327
  103.4 27.6 %collective-permute-start.24 = (bf16[256,384]{1,0:T(8,128)(2,1)S(1)}, bf16[256,384]{1,0:T(8,128)(2,1)S(1)}, u32[]{:S(2)}, u32[]{:S(2)}) collective-permute-start(bf16[256,384]{1,0:T(8,128)(2,1)S(1)} %get-tuple-element.118), channel_id=1, source_target_pairs={{0,1},{1,0},{2,3},{3,2},{4,5},{5,4},{6,7},{7,6},{8,9},{9,8},{10,11... | collective-permute-start | bytes 589832 | tf_op jit(solution)/shard_map/ppermute | solution.py:327
  113.3 19.0 %collective-permute-start.23 = (bf16[128,384]{1,0:T(8,128)(2,1)S(1)}, bf16[128,384]{1,0:T(8,128)(2,1)S(1)}, u32[]{:S(2)}, u32[]{:S(2)}) collective-permute-start(bf16[128,384]{1,0:T(8,128)(2,1)S(1)} %get-tuple-element.117), channel_id=1, source_target_pairs={{0,1},{1,0},{2,3},{3,2},{4,5},{5,4},{6,7},{7,6},{8,9},{9,8},{10,11... | collective-permute-start | bytes 294920 | tf_op jit(solution)/shard_map/ppermute | solution.py:327
  (3 other events, 32.6 us)
